TPU v7x, 32 devices: a whole 2x2x4 slice. The times are simulated.
32 devices in a mesh: lat: 4 (over y, core), lon: 8 (over z, x).
Axes of the slice: x: 2, y: 2, z: 4, core: 2. Of those that a mesh axis runs over, the one named last changes fastest.
Arguments:
- queries: bfloat16 [64, 128, 512], P('lat', 'lon'), may hold values from -6 to 6
- keys: bfloat16 [64, 128, 512], P('lat', 'lon'), may hold values from -6 to 6
- values: bfloat16 [64, 128, 512], P('lat', 'lon'), may hold values from -16 to 16
- rel_bias: float32 [8, 13, 13], replicated, may hold values from -4 to 4
- out_weight: bfloat16 [512, 1024], replicated, may hold values from -0.25 to 0.25
- cotangent: bfloat16 [64, 128, 1024], P('lat', 'lon'), may hold values from -16 to 16
Outputs:
- block_out: bfloat16 [64, 128, 1024], P('lat', 'lon')
- query_grad: bfloat16 [64, 128, 512], P('lat', 'lon')
- key_grad: bfloat16 [64, 128, 512], P('lat', 'lon')
- value_grad: bfloat16 [64, 128, 512], P('lat', 'lon')
- weight_grad: bfloat16 [512, 1024], replicated
- bias_grad: float32 [8, 13, 13], replicated
All inputs are finite; a program needn't handle non-finite values.
Results may differ from a plain program's by a relative error of at most 0.007.
Values may be sent and summed in bfloat16 or wider, within the bound.
No kernel may reach another device: no remote copies, remote signals or barrier semaphores. Data moves between devices by JAX's collectives and lax.ppermute only.
A program may use at most 128 MiB of HBM per device.

v0:
```python
import jax
import jax.numpy as jnp
from jax import lax
from jax.sharding import PartitionSpec as P

RAD = 6


def with_halo(block, sides, width, periodic):
    for axis, dim in sides:
        count = lax.axis_size(axis)
        forward = [(i, i + 1) for i in range(count - 1)]
        if periodic:
            forward.append((count - 1, 0))
        backward = [(target, source) for source, target in forward]
        low = lax.ppermute(
            lax.slice_in_dim(block, block.shape[dim] - width, None, axis=dim), axis, forward
        )
        high = lax.ppermute(lax.slice_in_dim(block, 0, width, axis=dim), axis, backward)
        block = jnp.concatenate([low, block, high], axis=dim)
    return block


def from_behind(block, axis, distance):
    devices = range(lax.axis_size(axis))
    route = [(i - distance, i) for i in devices if i - distance in devices]
    return lax.ppermute(block, axis, route)


def from_behind_2(value, axis, steps):
    count = lax.axis_size(axis)
    pairs = [(source, (source + steps) % count) for source in range(count)]
    return lax.ppermute(value, axis, pairs)


def relative_table(count_query, count_key):
    query_pos = jnp.arange(count_query, dtype=jnp.int32)
    key_pos = jnp.arange(count_key, dtype=jnp.int32)
    offset_pos = jnp.arange(2 * RAD + 1, dtype=jnp.int32)
    relative = key_pos[None, :] - query_pos[:, None]
    return (relative[:, :, None] == offset_pos[None, None, :]).astype(jnp.float32)


def shards(queries, keys, values, rel_bias, out_weight, cotangent):
    lat_dev, lon_dev, width = queries.shape
    heads = rel_bias.shape[0]
    head_size = width // heads
    outer_lat = lat_dev + 2 * RAD
    outer_lon = lon_dev + 2 * RAD
    count_query = lat_dev * lon_dev
    count_key = outer_lat * outer_lon
    tokens_all = count_query * lax.axis_size("lat") * lax.axis_size("lon")
    scale = head_size ** (-0.5)
    norm_factor = tokens_all ** (-0.5)
    paired = jnp.concatenate((keys, values), 2)
    widened = with_halo(paired, (("lon", 1),), RAD, True)
    outer = with_halo(widened, (("lat", 0),), RAD, False)
    outer_rows = outer.reshape(count_key, 2 * width)
    row_hot = relative_table(lat_dev, outer_lat)
    col_hot = relative_table(lon_dev, outer_lon)
    global_row = lax.axis_index("lat") * lat_dev + jnp.arange(outer_lat, dtype=jnp.int32) - RAD
    row_inside = ((global_row >= 0) & (global_row < lat_dev * lax.axis_size("lat"))).astype(
        jnp.float32
    )
    row_keep = row_hot * row_inside[None, :, None]
    bias_table = jnp.einsum(
        "hab,ika,jlb->hijkl", rel_bias, row_keep, col_hot, precision=lax.Precision.HIGHEST
    )
    keep_table = jnp.einsum("ika,jlb->ijkl", row_keep, col_hot, precision=lax.Precision.HIGHEST)
    keep_flat = keep_table.reshape(1, count_query, count_key) > 0.5
    masked_bias = jnp.where(keep_flat, bias_table.reshape(heads, count_query, count_key), -jnp.inf)
    query_heads = queries.reshape(count_query, heads, head_size).transpose(1, 0, 2)
    key_heads = outer_rows[:, :width].reshape(count_key, heads, head_size).transpose(1, 0, 2)
    value_heads = outer_rows[:, width:].reshape(count_key, heads, head_size).transpose(1, 0, 2)

    def weights_of(query_one, key_one, bias_one):
        scores = (
            lax.dot_general(
                query_one, key_one, (((1,), (1,)), ((), ())), preferred_element_type=jnp.float32
            )
            * scale
        )
        scores = scores + bias_one
        lifted = jnp.exp(scores - jnp.max(scores, -1, keepdims=True))
        return lifted / jnp.sum(lifted, -1, keepdims=True)

    def forward_head(items):
        query_one, key_one, value_one, bias_one = items
        probs = weights_of(query_one, key_one, bias_one)
        return jnp.dot(probs.astype(jnp.bfloat16), value_one, preferred_element_type=jnp.float32)

    mixed = lax.map(forward_head, (query_heads, key_heads, value_heads, masked_bias))
    attended = mixed.transpose(1, 0, 2).reshape(count_query, width).astype(jnp.bfloat16)
    block_out = jnp.dot(attended, out_weight, preferred_element_type=jnp.float32).astype(
        jnp.bfloat16
    )
    block_out = block_out.reshape(lat_dev, lon_dev, out_weight.shape[1])
    grad_rows = cotangent.reshape(count_query, cotangent.shape[2])
    attended_grad = lax.dot_general(
        grad_rows, out_weight, (((1,), (1,)), ((), ())), preferred_element_type=jnp.float32
    ).astype(jnp.bfloat16)
    weight_local = lax.dot_general(
        attended, grad_rows, (((0,), (0,)), ((), ())), preferred_element_type=jnp.float32
    )
    grad_heads = attended_grad.reshape(count_query, heads, head_size).transpose(1, 0, 2)

    def backward_head(items):
        query_one, key_one, value_one, grad_one, bias_one = items
        probs = weights_of(query_one, key_one, bias_one)
        rounded = probs.astype(jnp.bfloat16)
        slopes = lax.dot_general(
            grad_one, value_one, (((1,), (1,)), ((), ())), preferred_element_type=jnp.float32
        )
        inner_sum = jnp.sum(probs * slopes, -1, keepdims=True)
        score_grad = probs * (slopes - inner_sum)
        bias_part = jnp.einsum(
            "ijkl,ika,jlb->ab",
            score_grad.reshape(lat_dev, lon_dev, outer_lat, outer_lon),
            row_hot,
            col_hot,
            precision=lax.Precision.HIGHEST,
        )
        score_round = score_grad.astype(jnp.bfloat16)
        query_part = jnp.dot(score_round, key_one, preferred_element_type=jnp.float32) * scale
        key_part = (
            lax.dot_general(
                score_round, query_one, (((0,), (0,)), ((), ())), preferred_element_type=jnp.float32
            )
            * scale
        )
        value_part = lax.dot_general(
            rounded, grad_one, (((0,), (0,)), ((), ())), preferred_element_type=jnp.float32
        )
        return (query_part, key_part, value_part, bias_part)

    query_part, key_part, value_part, bias_local = lax.map(
        backward_head, (query_heads, key_heads, value_heads, grad_heads, masked_bias)
    )
    query_grad = query_part.transpose(1, 0, 2).reshape(lat_dev, lon_dev, width).astype(jnp.bfloat16)
    key_flat = key_part.transpose(1, 0, 2).reshape(count_key, width)
    value_flat = value_part.transpose(1, 0, 2).reshape(count_key, width)
    terms = jnp.concatenate((key_flat, value_flat), 1).reshape(outer_lat, outer_lon, 2 * width)
    top_rows = terms[:RAD]
    bottom_rows = terms[outer_lat - RAD :]
    middle = terms[RAD : RAD + lat_dev]
    from_below = from_behind(top_rows.astype(jnp.bfloat16), "lat", -1).astype(top_rows.dtype)
    from_above = from_behind(bottom_rows, "lat", 1)
    middle = middle.at[lat_dev - RAD :].add(from_below)
    middle = middle.at[:RAD].add(from_above)
    west_cols = middle[:, :RAD]
    east_cols = middle[:, outer_lon - RAD :]
    center = middle[:, RAD : RAD + lon_dev]
    from_east = from_behind_2(west_cols, "lon", -1)
    from_west = from_behind_2(east_cols, "lon", 1)
    center = center.at[:, lon_dev - RAD :].add(from_east)
    center = center.at[:, :RAD].add(from_west)
    key_grad = center[:, :, :width].astype(jnp.bfloat16)
    value_grad = center[:, :, width:].astype(jnp.bfloat16)
    weight_total, bias_total = lax.psum((weight_local, bias_local), ("lat", "lon"))
    weight_grad = (weight_total * norm_factor).astype(jnp.bfloat16)
    bias_grad = bias_total * norm_factor
    return (block_out, query_grad, key_grad, value_grad, weight_grad, bias_grad)


def solution(mesh):
    in_specs = (
        P("lat", "lon", None),
        P("lat", "lon", None),
        P("lat", "lon", None),
        P(),
        P(),
        P("lat", "lon", None),
    )
    out_specs = (
        P("lat", "lon", None),
        P("lat", "lon", None),
        P("lat", "lon", None),
        P("lat", "lon", None),
        P(),
        P(),
    )
    return jax.shard_map(shards, mesh=mesh, in_specs=in_specs, out_specs=out_specs, check_vma=False)
```

profile of v0, /device:TPU:1, one launch (start us, length us, event | category | flops | bytes accessed | tf_op | source)
XLA Modules:
  0.0 480.8 jit_solution(6144126483298326666)
XLA Ops:
  10.2 5.1 %collective-permute-start.1 = (bf16[16,6,1024]{2,1,0:T(8,128)(2,1)}, bf16[16,6,1024]{2,1,0:T(8,128)(2,1)S(1)}, u32[]{:S(2)}, u32[]{:S(2)}) collective-permute-start(bf16[16,6,1024]{2,1,0:T(8,128)(2,1)} %get-tuple-element.320), channel_id=1, source_target_pairs={{1,0},{2,1},{3,2},{4,3},{5,4},{6,5},{7,6},{0,7},{9,8},{10,9},{11,1... | collective-permute-start | bytes 589832 | tf_op jit(solution)/shard_map/ppermute | solution.py:19
  16.4 14.0 %convolution_bitcast_fusion.4 = f32[8,16,16,28,28]{4,3,2,0,1:T(8,128)S(1)} fusion(f32[16,28,8,13,1]{1,3,4,2,0:T(8,128)S(1)} %convolution_bitcast_fusion.5, s32[16,28]{1,0:T(8,128)S(1)} %iota_subtract_fusion), kind=kOutput, calls=%fused_computation.61 | convolution fusion | flops 250484416 | bytes 6610688 | tf_op jit(solution)/shard_map/hab,ika,jlb->hijkl/dot_general | solution.py:66
  30.4 13.2 %copy.37 = f32[8,16,16,28,28]{4,3,2,1,0:T(8,128)} copy(f32[8,16,16,28,28]{4,3,2,0,1:T(8,128)S(1)} %convolution_bitcast_fusion.4) | data formatting | bytes 12845056 | tf_op jit(solution)/shard_map/hab,ika,jlb->hijkl/transpose | solution.py:66
  43.7 28.1 %reshape.215 = f32[8,256,784]{2,1,0:T(8,128)} reshape(f32[8,16,16,28,28]{4,3,2,1,0:T(8,128)} %copy.37) | data formatting | bytes 12845056 | tf_op jit(solution)/shard_map/reshape | solution.py:71
  72.5 3.4 gt.20
  77.2 2.9 collective-permute-start.3
  80.1 3.4 collective-permute-start.2
  83.4 6.6 %broadcast_select_fusion = f32[8,256,784]{2,1,0:T(8,128)} fusion(f32[8,256,784]{2,1,0:T(8,128)} %reshape.215, pred[256,784]{1,0:T(8,128)(4,1)S(1)} %gt.20), kind=kLoop, calls=%fused_computation.70 | loop fusion | flops 1605632 | bytes 13045760 | tf_op jit(solution)/shard_map/jit(_where)/select_n | solution.py:71
  91.2 8.2 %copy.41 = f32[8,256,784]{1,2,0:T(8,128)} copy(f32[8,256,784]{2,1,0:T(8,128)} %broadcast_select_fusion) | data formatting | bytes 12845056 | tf_op jit(solution)/shard_map/while | solution.py:92
  103.9 2.4 fusion.65
  111.7 151.7 %while.34 = (s32[]{:T(128)}, bf16[8,256,64]{1,2,0:T(8,128)(2,1)S(1)}, f32[8,784,64]{1,2,0:T(8,128)}, f32[8,784,64]{1,2,0:T(8,128)}, f32[8,13,13]{2,0,1:T(8,128)S...) while((s32[]{:T(128)}, ...), condition=%wide.region_10.11_spmd.clone.clone, body=%wide.region_6.10_spmd.clone.clone.sunk | while | flops 164370688 | bytes 14238653 | solution.py:136
  119.9 6.0 %reshape.233 = f32[16,16,28,28]{3,2,1,0:T(8,128)} reshape(f32[256,784]{1,0:T(8,128)S(1)} %copy.64) | data formatting | bytes 1605632 | tf_op jit(solution)/shard_map/while/body/eval_jaxpr/reshape | solution.py:118
  126.0 4.3 convolution_bitcast_fusion.8
  138.9 6.0 %reshape.233 = f32[16,16,28,28]{3,2,1,0:T(8,128)} reshape(f32[256,784]{1,0:T(8,128)S(1)} %copy.64) | data formatting | bytes 1605632 | tf_op jit(solution)/shard_map/while/body/eval_jaxpr/reshape | solution.py:118
  144.9 4.3 convolution_bitcast_fusion.8
  157.9 6.0 %reshape.233 = f32[16,16,28,28]{3,2,1,0:T(8,128)} reshape(f32[256,784]{1,0:T(8,128)S(1)} %copy.64) | data formatting | bytes 1605632 | tf_op jit(solution)/shard_map/while/body/eval_jaxpr/reshape | solution.py:118
  163.9 4.3 convolution_bitcast_fusion.8
  176.8 6.0 %reshape.233 = f32[16,16,28,28]{3,2,1,0:T(8,128)} reshape(f32[256,784]{1,0:T(8,128)S(1)} %copy.64) | data formatting | bytes 1605632 | tf_op jit(solution)/shard_map/while/body/eval_jaxpr/reshape | solution.py:118
  182.9 4.3 convolution_bitcast_fusion.8
  195.8 6.0 %reshape.233 = f32[16,16,28,28]{3,2,1,0:T(8,128)} reshape(f32[256,784]{1,0:T(8,128)S(1)} %copy.64) | data formatting | bytes 1605632 | tf_op jit(solution)/shard_map/while/body/eval_jaxpr/reshape | solution.py:118
  201.8 4.3 convolution_bitcast_fusion.8
  214.8 6.0 %reshape.233 = f32[16,16,28,28]{3,2,1,0:T(8,128)} reshape(f32[256,784]{1,0:T(8,128)S(1)} %copy.64) | data formatting | bytes 1605632 | tf_op jit(solution)/shard_map/while/body/eval_jaxpr/reshape | solution.py:118
  220.8 4.3 convolution_bitcast_fusion.8
  233.7 6.0 %reshape.233 = f32[16,16,28,28]{3,2,1,0:T(8,128)} reshape(f32[256,784]{1,0:T(8,128)S(1)} %copy.64) | data formatting | bytes 1605632 | tf_op jit(solution)/shard_map/while/body/eval_jaxpr/reshape | solution.py:118
  239.7 4.3 convolution_bitcast_fusion.8
  252.7 6.0 %reshape.233 = f32[16,16,28,28]{3,2,1,0:T(8,128)} reshape(f32[256,784]{1,0:T(8,128)S(1)} %copy.64) | data formatting | bytes 1605632 | tf_op jit(solution)/shard_map/while/body/eval_jaxpr/reshape | solution.py:118
  258.7 4.3 convolution_bitcast_fusion.8
  263.4 1.8 copy.50
  265.3 2.7 copy.51
  267.9 2.2 pad_maximum_fusion.1
  271.7 28.9 %while.33 = (s32[]{:T(128)}, bf16[8,256,64]{1,2,0:T(8,128)(2,1)}, bf16[8,256,64]{2,1,0:T(8,128)(2,1)}, bf16[8,784,64]{2,1,0:T(8,128)(2,1)}, f32[8,256,784]{1,2,0...) while((s32[]{:T(128)}, bf16[8,256,64]{1,2,0:T(8,128)(2,1)}, bf16[8,256,64]{2,1,0:T(8,128)(2,1)}, ...), condition=%wide.region_5.6_spmd, body=%wide.region_2.5_spmd.sunk | while | flops 52985344 | bytes 3751509 | solution.py:92
  273.5 1.8 fusion.99
  277.1 1.8 fusion.99
  280.7 1.8 fusion.99
  284.3 1.8 fusion.99
  302.3 1.9 collective-permute-start.4
  305.2 3.6 collective-permute-start.5
  308.9 2.9 fusion.68
  311.8 2.6 fusion.49
  315.9 2.1 reshape.222
  318.0 39.6 %psum.15 = f32[8,13,13]{2,0,1:T(8,128)S(1)} all-reduce(f32[8,13,13]{2,0,1:T(8,128)S(1)} %get-tuple-element.181), channel_id=1, replica_groups=mesh['lat'=4,'lon'=8] {'lat','lon'}, use_global_device_ids=true, to_apply=%region_12.13 | all-reduce | flops 1352 | bytes 10816 | tf_op jit(solution)/shard_map/psum | solution.py:159
  362.5 1.9 collective-permute-start.6
  366.1 2.1 convert_element_type.73
  369.2 89.9 %all-reduce.2.cloned.1.call-done = f32[512,1024]{1,0:T(8,128)} async-done(((f32[512,1024]{1,0:T(8,128)}), f32[512,1024]{1,0:T(8,128)}) %all-reduce.2.cloned.1.call-update) | async-done | bytes 2097168 | tf_op jit(solution)/shard_map/psum | solution.py:159
  459.2 2.8 multiply_convert_fusion
  462.0 1.9 slice_add_fusion.2
  463.9 3.1 scatter-add.16
  468.2 3.5 scatter-add.19
  (181 shorter events, 124.0 us)
Async XLA Ops:
  7.2 92.2 %copy-start = (bf16[512,1024]{1,0:T(8,128)(2,1)S(1)}, bf16[512,1024]{1,0:T(8,128)(2,1)}, u32[]{:S(2)}) copy-start(bf16[512,1024]{1,0:T(8,128)(2,1)} %param.22) | copy-start | bytes 3145732
  7.2 8.1 %copy-start.10 = (f32[8,13,13]{2,0,1:T(8,128)S(1)}, f32[8,13,13]{2,0,1:T(8,128)}, u32[]{:S(2)}) copy-start(f32[8,13,13]{2,0,1:T(8,128)} %param.21) | copy-start | bytes 16228
  7.2 452.0 %all-reduce.2.cloned.1.call-start = ((), (), s32[]{:S(2)}) async-start(), calls=%async_computation | async-start | bytes 4194304 | tf_op jit(solution)/shard_map/psum | solution.py:159
  10.2 65.8 %collective-permute-start.1 = (bf16[16,6,1024]{2,1,0:T(8,128)(2,1)}, bf16[16,6,1024]{2,1,0:T(8,128)(2,1)S(1)}, u32[]{:S(2)}, u32[]{:S(2)}) collective-permute-start(bf16[16,6,1024]{2,1,0:T(8,128)(2,1)} %get-tuple-element.320), channel_id=1, source_target_pairs={{1,0},{2,1},{3,2},{4,3},{5,4},{6,5},{7,6},{0,7},{9,8},{10,9},{11,1... | collective-permute-start | bytes 589832 | tf_op jit(solution)/shard_map/ppermute | solution.py:19
  15.2 60.7 %collective-permute-start = (bf16[16,6,1024]{2,1,0:T(8,128)(2,1)}, bf16[16,6,1024]{2,1,0:T(8,128)(2,1)S(1)}, u32[]{:S(2)}, u32[]{:S(2)}) collective-permute-start(bf16[16,6,1024]{2,1,0:T(8,128)(2,1)} %get-tuple-element.319), channel_id=1, source_target_pairs={{0,1},{1,2},{2,3},{3,4},{4,5},{5,6},{6,7},{7,0},{8,9},{9,10},{10,1... | collective-permute-start | bytes 589832 | tf_op jit(solution)/shard_map/ppermute | solution.py:16
  75.9 14.1 %copy-start.5 = (bf16[16,6,1024]{2,1,0:T(8,128)(2,1)}, bf16[16,6,1024]{2,1,0:T(8,128)(2,1)S(1)}, u32[]{:S(2)}) copy-start(bf16[16,6,1024]{2,1,0:T(8,128)(2,1)S(1)} %collective-permute-done.1) | copy-start | bytes 589828
  76.0 14.1 %copy-start.6 = (bf16[16,6,1024]{2,1,0:T(8,128)(2,1)}, bf16[16,6,1024]{2,1,0:T(8,128)(2,1)S(1)}, u32[]{:S(2)}) copy-start(bf16[16,6,1024]{2,1,0:T(8,128)(2,1)S(1)} %collective-permute-done) | copy-start | bytes 589828
  77.2 23.6 %collective-permute-start.3 = (bf16[6,28,1024]{2,1,0:T(8,128)(2,1)}, bf16[6,28,1024]{2,1,0:T(8,128)(2,1)}, u32[]{:S(2)}, u32[]{:S(2)}) collective-permute-start(bf16[6,28,1024]{2,1,0:T(8,128)(2,1)} %get-tuple-element.316), channel_id=1, source_target_pairs={{8,0},{16,8},{24,16},{9,1},{17,9},{25,17},{10,2},{18,10},{26,18},{... | collective-permute-start | bytes 1032200 | tf_op jit(solution)/shard_map/ppermute | solution.py:19
  80.1 10.0 %copy-start.9 = (bf16[16,16,512]{2,1,0:T(8,128)(2,1)S(1)}, bf16[16,16,512]{2,1,0:T(8,128)(2,1)}, u32[]{:S(2)}) copy-start(bf16[16,16,512]{2,1,0:T(8,128)(2,1)} %param.18) | copy-start | bytes 786436
  80.1 20.7 %collective-permute-start.2 = (bf16[6,28,1024]{2,1,0:T(8,128)(2,1)}, bf16[6,28,1024]{2,1,0:T(8,128)(2,1)}, u32[]{:S(2)}, u32[]{:S(2)}) collective-permute-start(bf16[6,28,1024]{2,1,0:T(8,128)(2,1)} %get-tuple-element.315), channel_id=1, source_target_pairs={{0,8},{8,16},{16,24},{1,9},{9,17},{17,25},{2,10},{10,18},{18,26},{... | collective-permute-start | bytes 1032200 | tf_op jit(solution)/shard_map/ppermute | solution.py:16
  91.2 8.2 %copy-start.4 = (bf16[16,16,1024]{2,1,0:T(8,128)(2,1)S(1)}, bf16[16,16,1024]{2,1,0:T(8,128)(2,1)}, u32[]{:S(2)}) copy-start(bf16[16,16,1024]{2,1,0:T(8,128)(2,1)} %param.23) | copy-start | bytes 1572868
  263.4 1.9 copy-start.7
  267.9 2.2 copy-start.1
  302.3 56.5 %collective-permute-start.4 = (bf16[6,28,1024]{2,1,0:T(8,128)(2,1)}, bf16[6,28,1024]{2,1,0:T(8,128)(2,1)}, u32[]{:S(2)}, u32[]{:S(2)}) collective-permute-start(bf16[6,28,1024]{2,1,0:T(8,128)(2,1)} %convert_element_type.74), channel_id=1, source_target_pairs={{8,0},{16,8},{24,16},{9,1},{17,9},{25,17},{10,2},{18,10},{26,18},{... | collective-permute-start | bytes 1032200 | tf_op jit(solution)/shard_map/ppermute | solution.py:27
  305.2 54.8 %collective-permute-start.5 = (f32[6,28,1024]{2,1,0:T(8,128)}, f32[6,28,1024]{2,1,0:T(8,128)}, u32[]{:S(2)}, u32[]{:S(2)}) collective-permute-start(f32[6,28,1024]{2,1,0:T(8,128)} %slice.163), channel_id=1, source_target_pairs={{0,8},{8,16},{16,24},{1,9},{9,17},{17,25},{2,10},{10,18},{18,26},{... | collective-permute-start | bytes 2064392 | tf_op jit(solution)/shard_map/ppermute | solution.py:27
  315.9 41.7 %copy-start.3 = (bf16[8,256,64]{1,2,0:T(8,128)(2,1)S(1)}, bf16[8,256,64]{1,2,0:T(8,128)(2,1)}, u32[]{:S(2)}) copy-start(bf16[8,256,64]{1,2,0:T(8,128)(2,1)} %get-tuple-element.177) | copy-start | bytes 786436
  357.6 1.3 copy-start.2
  360.0 5.0 %copy-start.8 = (bf16[8,256,64]{1,2,0:T(8,128)(2,1)S(1)}, bf16[8,256,64]{1,2,0:T(8,128)(2,1)}, u32[]{:S(2)}) copy-start(bf16[8,256,64]{1,2,0:T(8,128)(2,1)} %copy-done.7) | copy-start | bytes 786436
  362.5 99.5 %collective-permute-start.6 = (f32[16,6,1024]{2,1,0:T(8,128)}, f32[16,6,1024]{2,1,0:T(8,128)}, u32[]{:S(2)}, u32[]{:S(2)}) collective-permute-start(f32[16,6,1024]{2,1,0:T(8,128)} %get-tuple-element.312), channel_id=1, source_target_pairs={{0,7},{1,0},{2,1},{3,2},{4,3},{5,4},{6,5},{7,6},{8,15},{9,8},{10,9... | collective-permute-start | bytes 1179656 | tf_op jit(solution)/shard_map/ppermute | solution.py:33
  369.2 97.7 %collective-permute-start.7 = (f32[16,6,1024]{2,1,0:T(8,128)}, f32[16,6,1024]{2,1,0:T(8,128)}, u32[]{:S(2)}, u32[]{:S(2)}) collective-permute-start(f32[16,6,1024]{2,1,0:T(8,128)} %get-tuple-element.311), channel_id=1, source_target_pairs={{0,1},{1,2},{2,3},{3,4},{4,5},{5,6},{6,7},{7,0},{8,9},{9,10},{10,1... | collective-permute-start | bytes 1179656 | tf_op jit(solution)/shard_map/ppermute | solution.py:33
Sparse Core Ops, SparseCore 0:
  318.2 140.9 all-reduce.1
where the time goes:
time: 486 us; the launch traced here: 481 us
  matrix products  144 us (30%)
  local copies, waits for them, and re-layouts  143 us (29%)
  waiting for transfers between devices  90 us (19%)
  blocking collectives  39.6 us (8%)
  other arithmetic  30.6 us (6%)
  starting transfers between devices  18.7 us (4%)
  between operations  14.4 us (3%)
    psum x1, waiting for transfers between devices, shards(): lax.psum((weight_local, bias_local), ('lat', 'lon'))  89.9 us
    reshape x8, local copies, waits for them, and re-layouts, backward_head(): score_grad.reshape(lat_dev, lon_dev, outer_lat, outer_lon)  48.2 us
    psum x1, blocking collectives, shards(): lax.psum((weight_local, bias_local), ('lat', 'lon'))  39.6 us
    dot_general x16, matrix products, backward_head(): jnp.einsum('ijkl,ika,jlb->ab', score_grad.reshape(lat_dev, lon_dev, outer...  36.5 us
    reshape x1, local copies, waits for them, and re-layouts, shards(): bias_table.reshape(heads, count_query, count_key)  28.1 us
    dot_general x16, matrix products, weights_of(): lax.dot_general(query_one, key_one, (((1,), (1,)), ((), ())), preferred_e...  25.5 us
    dot_general x2, matrix products, shards(): jnp.einsum('hab,ika,jlb->hijkl', rel_bias, row_keep, col_hot, precision=l...  15 us
    dot_general x8, matrix products, forward_head(): jnp.dot(probs.astype(jnp.bfloat16), value_one, preferred_element_type=jnp...  14.7 us
  transfers between devices with their start and end apart: 9, of which 1 were waited for; matrix products, arithmetic and copies ran while one was open for 22% of the time, Pallas kernels for 0%

commit v1 on v0

v1 whole, which is shorter than its diff:
```python
import functools

import jax
import jax.numpy as jnp
from jax import lax
from jax.experimental import pallas as pl
from jax.experimental.pallas import tpu as pltpu
from jax.sharding import PartitionSpec as P

RAD = 6
SPAN = 2 * RAD + 1
TILE = 4
GROUP = 4
NEG = -1e30
NT = (((1,), (1,)), ((), ()))
F32 = jnp.float32
BF16 = jnp.bfloat16


def dot(a, b):
    return jnp.dot(a, b, preferred_element_type=F32)


def dot_nt(a, b):
    return lax.dot_general(a, b, NT, preferred_element_type=F32)


def head_of_lane(shape, axis, head_size):
    return lax.broadcasted_iota(jnp.int32, shape, axis) // head_size


def spread_heads(tile, cols, head_size):
    lane = head_of_lane((cols, tile.shape[1]), 1, head_size)
    zero = jnp.zeros((cols, tile.shape[1]), tile.dtype)
    parts = []
    for i in range(TILE):
        rows = tile[i * cols : (i + 1) * cols]
        for h in range(GROUP):
            parts.append(jnp.where(lane == h, rows, zero))
    return jnp.concatenate(parts, 0)


def head_mask(cols, head_size):
    shape = (GROUP * head_size, TILE * GROUP * cols)
    feature = lax.broadcasted_iota(jnp.int32, shape, 0) // head_size
    column = (lax.broadcasted_iota(jnp.int32, shape, 1) // cols) % GROUP
    return feature == column


def picker(cols):
    shape = (TILE * cols, TILE * GROUP * cols)
    row = lax.broadcasted_iota(jnp.int32, shape, 0)
    col = lax.broadcasted_iota(jnp.int32, shape, 1)
    same = (row // cols == col // (GROUP * cols)) & (row % cols == col % cols)
    return same.astype(F32).astype(BF16)


def scores_of(k_win, q_bd, bias, first_row, rows_all, cols_pad):
    shape = (k_win.shape[0], q_bd.shape[0])
    row = first_row + lax.broadcasted_iota(jnp.int32, shape, 0) // cols_pad
    keep = (row >= 0) & (row < rows_all)
    return jnp.where(keep, dot_nt(k_win, q_bd) + bias, NEG)


def fwd_kernel(sizes, lat_ref, q_ref, k_ref, v_ref, bias_ref, out_ref, m_ref, l_ref, vt_ref):
    lat_dev, cols, cols_pad, head_size, rows_all = sizes
    scale = head_size ** (-0.5)
    vt_ref[...] = v_ref[...].T
    mask = head_mask(cols, head_size)
    pick = picker(cols)
    win = (TILE + 2 * RAD) * cols_pad
    for t in range(lat_dev // TILE):
        lo = t * TILE * cols_pad
        qs = pl.ds(t * TILE * cols, TILE * cols)
        q_bd = spread_heads(q_ref[qs, :] * jnp.asarray(scale, BF16), cols, head_size)
        first = lat_ref[0] * lat_dev + t * TILE - RAD
        st = scores_of(k_ref[pl.ds(lo, win), :], q_bd, bias_ref[...], first, rows_all, cols_pad)
        m = jnp.max(st, 0, keepdims=True)
        e = jnp.exp(st - m)
        total = jnp.sum(e, 0, keepdims=True)
        p = (e * (1.0 / total)).astype(BF16)
        ot = dot(vt_ref[:, pl.ds(lo, win)], p)
        ot = jnp.where(mask, ot, 0.0).astype(BF16)
        out_ref[qs, :] = dot_nt(pick, ot).astype(BF16)
        m_ref[0, t : t + 1, :] = m
        l_ref[0, t : t + 1, :] = 1.0 / total


def bwd_kernel(
    sizes, lat_ref, q_ref, g_ref, k_ref, v_ref, bias_ref, m_ref, l_ref,
    dq_ref, dk_ref, dv_ref, db_ref, kt_ref,
):
    lat_dev, cols, cols_pad, head_size, rows_all = sizes
    scale = head_size ** (-0.5)
    kt_ref[...] = k_ref[...].T
    mask = head_mask(cols, head_size)
    pick = picker(cols)
    win = (TILE + 2 * RAD) * cols_pad
    dk_ref[...] = jnp.zeros_like(dk_ref)
    dv_ref[...] = jnp.zeros_like(dv_ref)
    for t in range(lat_dev // TILE):
        lo = t * TILE * cols_pad
        qs = pl.ds(t * TILE * cols, TILE * cols)
        ws = pl.ds(lo, win)
        q_bd = spread_heads(q_ref[qs, :] * jnp.asarray(scale, BF16), cols, head_size)
        g_bd = spread_heads(g_ref[qs, :], cols, head_size)
        first = lat_ref[0] * lat_dev + t * TILE - RAD
        st = scores_of(k_ref[ws, :], q_bd, bias_ref[...], first, rows_all, cols_pad)
        p = jnp.exp(st - m_ref[0, t : t + 1, :]) * l_ref[0, t : t + 1, :]
        slope = dot_nt(v_ref[ws, :], g_bd)
        inner = jnp.sum(p * slope, 0, keepdims=True)
        sg = p * (slope - inner)
        if t == 0:
            db_ref[...] = sg
        else:
            db_ref[...] += sg
        sgb = sg.astype(BF16)
        dqt = jnp.where(mask, dot(kt_ref[:, ws], sgb) * scale, 0.0).astype(BF16)
        dq_ref[qs, :] = dot_nt(pick, dqt).astype(BF16)
        dk_ref[ws, :] += dot(sgb, q_bd)
        dv_ref[ws, :] += dot(p.astype(BF16), g_bd)


def bits_of(mesh_shape):
    order = []
    for axis in ("lat", "lon"):
        n = mesh_shape[axis]
        bit = 1
        while bit < n:
            order.append((axis, bit, n))
            bit *= 2
    return order


def swap(x, axis, bit, n):
    return lax.ppermute(x, axis, [(i, i ^ bit) for i in range(n)])


def split_f32(x):
    hi = lax.reduce_precision(x, 8, 7)
    return hi.astype(BF16), (x - hi).astype(BF16)


def reduce_all(weight, bias, mesh_shape):
    order = bits_of(mesh_shape)
    part = weight
    for axis, bit, n in order[:-1]:
        mine = (lax.axis_index(axis) // bit) % 2
        half = part.shape[0] // 2
        keep = lax.dynamic_slice_in_dim(part, mine * half, half, 0)
        send = lax.dynamic_slice_in_dim(part, (1 - mine) * half, half, 0)
        got = swap(send, axis, bit, n)
        part = (keep.astype(F32) + got.astype(F32)).astype(BF16)
    nb = bias.shape[0]
    for step, (axis, bit, n) in enumerate(order[::-1]):
        rows = part.shape[0]
        hi, lo = split_f32(bias)
        got = swap(jnp.concatenate([hi, lo, part], 0), axis, bit, n)
        bias = bias + (got[:nb].astype(F32) + got[nb : 2 * nb].astype(F32))
        other = got[2 * nb :]
        if step == 0:
            part = part.astype(F32) + other.astype(F32)
            part = part.astype(BF16)
        else:
            mine = (lax.axis_index(axis) // bit) % 2
            both = jnp.zeros((2 * rows, part.shape[1]), BF16)
            both = lax.dynamic_update_slice_in_dim(both, part, mine * rows, 0)
            part = lax.dynamic_update_slice_in_dim(both, other, (1 - mine) * rows, 0)
    return part, bias


def bias_tables(rel_bias, cols, cols_pad):
    heads = rel_bias.shape[0]
    slot = jnp.arange(cols_pad, dtype=jnp.int32)
    pos = jnp.where(
        slot < cols,
        slot + RAD,
        jnp.where(slot < cols + RAD, slot - cols, jnp.where(slot < cols + 2 * RAD, slot, -1000)),
    )
    offset = pos[:, None] - jnp.arange(cols, dtype=jnp.int32)[None, :]
    hot = (offset[None] == jnp.arange(SPAN, dtype=jnp.int32)[:, None, None]).astype(F32)
    table = jnp.einsum("hab,blj->alhj", rel_bias, hot, precision=lax.Precision.HIGHEST)
    inside = (offset >= 0) & (offset < SPAN)
    table = jnp.where(inside[None, :, None, :], table, NEG)
    table = table.reshape(SPAN, cols_pad, heads // GROUP, 1, GROUP * cols)
    edge = TILE - 1
    table = jnp.pad(table, ((edge, edge), (0, 0), (0, 0), (0, 0), (0, 0)), constant_values=NEG)
    rows = TILE + 2 * RAD
    full = jnp.concatenate([table[edge - i : edge - i + rows] for i in range(TILE)], 3)
    return full.reshape(rows * cols_pad, heads * TILE * cols), hot


def shards(mesh_shape, queries, keys, values, rel_bias, out_weight, cotangent):
    lat_dev, lon_dev, width = queries.shape
    heads = rel_bias.shape[0]
    head_size = width // heads
    groups = heads // GROUP
    lanes = GROUP * head_size
    n_lat, n_lon = mesh_shape["lat"], mesh_shape["lon"]
    cols_pad = 32
    outer_lat = lat_dev + 2 * RAD
    tokens = lat_dev * lon_dev
    norm_factor = (tokens * n_lat * n_lon) ** (-0.5)
    east = [(i, (i + 1) % n_lon) for i in range(n_lon)]
    west = [(i, (i - 1) % n_lon) for i in range(n_lon)]
    down = [(i, i + 1) for i in range(n_lat - 1)]
    up = [(i + 1, i) for i in range(n_lat - 1)]

    paired = jnp.concatenate((keys, values), 2)
    from_west = lax.ppermute(paired[:, lon_dev - RAD :], "lon", east)
    from_east = lax.ppermute(paired[:, :RAD], "lon", west)
    fill = jnp.zeros((lat_dev, cols_pad - lon_dev - 2 * RAD, 2 * width), BF16)
    wide = jnp.concatenate((paired, from_west, from_east, fill), 1)
    from_above = lax.ppermute(wide[lat_dev - RAD :], "lat", down)
    from_below = lax.ppermute(wide[:RAD], "lat", up)
    outer = jnp.concatenate((from_above, wide, from_below), 0)
    outer = outer.reshape(outer_lat * cols_pad, 2 * width)
    bias_full, hot = bias_tables(rel_bias, lon_dev, cols_pad)

    q_flat = queries.reshape(tokens, width)
    cot = cotangent.reshape(tokens, cotangent.shape[2])
    attended_grad = lax.dot_general(cot, out_weight, NT, preferred_element_type=F32).astype(BF16)
    lat_index = lax.axis_index("lat").astype(jnp.int32).reshape(1)

    sizes = (lat_dev, lon_dev, cols_pad, head_size, lat_dev * n_lat)
    win = (TILE + 2 * RAD) * cols_pad
    tiles = lat_dev // TILE
    lanes_q = TILE * GROUP * lon_dev
    n_keys = outer_lat * cols_pad
    smem = pl.BlockSpec(memory_space=pltpu.SMEM)
    tok_spec = pl.BlockSpec((tokens, lanes), lambda g: (0, g))
    k_spec = pl.BlockSpec((n_keys, lanes), lambda g: (0, g))
    v_spec = pl.BlockSpec((n_keys, lanes), lambda g: (0, g + groups))
    b_spec = pl.BlockSpec((win, lanes_q), lambda g: (0, g))
    s_spec = pl.BlockSpec((1, tiles, lanes_q), lambda g: (g, 0, 0))
    params = pltpu.CompilerParams(vmem_limit_bytes=40 << 20)
    attended, m, inv = pl.pallas_call(
        functools.partial(fwd_kernel, sizes),
        grid=(groups,),
        in_specs=[smem, tok_spec, k_spec, v_spec, b_spec],
        out_specs=[tok_spec, s_spec, s_spec],
        out_shape=[
            jax.ShapeDtypeStruct((tokens, width), BF16),
            jax.ShapeDtypeStruct((groups, tiles, lanes_q), F32),
            jax.ShapeDtypeStruct((groups, tiles, lanes_q), F32),
        ],
        scratch_shapes=[pltpu.VMEM((lanes, n_keys), BF16)],
        compiler_params=params,
        name="attend_fwd",
    )(lat_index, q_flat, outer, outer, bias_full)

    weight_local = lax.dot_general(
        attended, cot, (((0,), (0,)), ((), ())), preferred_element_type=F32
    ).astype(BF16)
    block_out = dot(attended, out_weight).astype(BF16)

    query_grad, dk, dv, db = pl.pallas_call(
        functools.partial(bwd_kernel, sizes),
        grid=(groups,),
        in_specs=[smem, tok_spec, tok_spec, k_spec, v_spec, b_spec, s_spec, s_spec],
        out_specs=[tok_spec, k_spec, k_spec, b_spec],
        out_shape=[
            jax.ShapeDtypeStruct((tokens, width), BF16),
            jax.ShapeDtypeStruct((n_keys, width), F32),
            jax.ShapeDtypeStruct((n_keys, width), F32),
            jax.ShapeDtypeStruct((win, groups * lanes_q), F32),
        ],
        scratch_shapes=[pltpu.VMEM((lanes, n_keys), BF16)],
        compiler_params=params,
        name="attend_bwd",
    )(lat_index, q_flat, attended_grad, outer, outer, bias_full, m, inv)

    terms = jnp.concatenate((dk, dv), 1).reshape(outer_lat, cols_pad, 2 * width)
    get_below = lax.ppermute(terms[:RAD].astype(BF16), "lat", up)
    get_above = lax.ppermute(terms[outer_lat - RAD :].astype(BF16), "lat", down)
    middle = terms[RAD : RAD + lat_dev]
    middle = middle.at[lat_dev - RAD :].add(get_below.astype(F32))
    middle = middle.at[:RAD].add(get_above.astype(F32))
    to_west = middle[:, lon_dev : lon_dev + RAD].astype(BF16)
    to_east = middle[:, lon_dev + RAD : lon_dev + 2 * RAD].astype(BF16)
    get_east = lax.ppermute(to_west, "lon", west)
    get_west = lax.ppermute(to_east, "lon", east)
    center = middle[:, :lon_dev]
    center = center.at[:, lon_dev - RAD :].add(get_east.astype(F32))
    center = center.at[:, :RAD].add(get_west.astype(F32))
    key_grad = center[:, :, :width].astype(BF16)
    value_grad = center[:, :, width:].astype(BF16)

    db = db.reshape(TILE + 2 * RAD, cols_pad, groups, TILE, GROUP * lon_dev)
    db = sum(db[i : i + SPAN, :, :, i] for i in range(TILE))
    db = db.reshape(SPAN, cols_pad, heads, lon_dev)
    bias_local = jnp.einsum("alhj,blj->hab", db, hot, precision=lax.Precision.HIGHEST)
    flat = bias_local.reshape(-1)
    packed = jnp.pad(flat, (0, 8 * 1024 - flat.shape[0])).reshape(8, 1024)
    weight_total, bias_total = reduce_all(weight_local, packed, mesh_shape)
    weight_grad = (weight_total.astype(F32) * norm_factor).astype(BF16)
    bias_grad = bias_total.reshape(-1)[: flat.shape[0]].reshape(rel_bias.shape) * norm_factor
    return (
        block_out.reshape(lat_dev, lon_dev, -1),
        query_grad.reshape(lat_dev, lon_dev, width),
        key_grad,
        value_grad,
        weight_grad,
        bias_grad,
    )


def solution(mesh):
    spec = P("lat", "lon", None)
    return jax.shard_map(
        functools.partial(shards, dict(mesh.shape)),
        mesh=mesh,
        in_specs=(spec, spec, spec, P(), P(), spec),
        out_specs=(spec, spec, spec, spec, P(), P()),
        check_vma=False,
    )
```

time: 486 us -> 130 us (0.27)
  matrix products: 144 us -> 4.65 us
  local copies, waits for them, and re-layouts: 143 us -> 27.3 us
  waiting for transfers between devices: 90 us -> 34.7 us
  blocking collectives: 39.6 us -> 0 us
  other arithmetic: 30.6 us -> 17.2 us
  Pallas kernels: 0 us -> 13.1 us
  between operations: 14.4 us -> 1.44 us
  starting transfers between devices: 18.7 us -> 30.6 us
    dot_general x77 -> x5, matrix products: 144 us -> 4.65 us  [the longest x1 1.92 us: shards(): jnp.einsum('alhj,blj->hab', db, hot, precision=lax.Precision.HIGHEST)]
    psum x1 -> x0, waiting for transfers between devices: 89.9 us -> none  [shards(): lax.psum((weight_local, bias_local), ('lat', 'lon'))]
    reshape x13 -> x4, local copies, waits for them, and re-layouts: 82.5 us -> 5.42 us  [the longest x1 2.78 us: bias_tables(): return (full.reshape(rows * cols_pad, heads * TILE * cols), hot)]
    psum x1 -> x0, blocking collectives: 39.6 us -> none  [shards(): lax.psum((weight_local, bias_local), ('lat', 'lon'))]
    ppermute x8 -> x17, waiting for transfers between devices: 0.02 us -> 34.7 us  [the longest x9 15.7 us: swap(): return lax.ppermute(x, axis, [(i, i ^ bit) for i in range(n)])]
    pallas_call x0 -> x2, Pallas kernels: none -> 13.1 us  [the longest x1 8.07 us: shards(): pl.pallas_call(functools.partial(bwd_kernel, sizes), grid=(groups,), in_s...]
    transpose x1, local copies, waits for them, and re-layouts: 13.2 us -> 0.16 us  [shards(): jnp.einsum('alhj,blj->hab', db, hot, precision=lax.Precision.HIGHEST)]
    while x4 -> x0, local copies, waits for them, and re-layouts: 12.4 us -> none  [shards(): lax.map(forward_head, (query_heads, key_heads, value_heads, masked_bias))]
  transfers between devices with their start and end apart: 9 -> 17, of which waited for: 1 -> 8; matrix products, arithmetic and copies ran while one was open for 22% -> 26% of each run, Pallas kernels for 0% -> 6%
where the time goes in v1:
time: 130 us; the launch traced here: 129 us
  waiting for transfers between devices  34.7 us (27%)
  starting transfers between devices  30.6 us (24%)
  local copies, waits for them, and re-layouts  27.3 us (21%)
  other arithmetic  17.2 us (13%)
  Pallas kernels  13.1 us (10%)
  matrix products  4.65 us (4%)
  between operations  1.44 us (1%)
    ppermute x9, waiting for transfers between devices, swap(): return lax.ppermute(x, axis, [(i, i ^ bit) for i in range(n)])  15.7 us
    ppermute x1, waiting for transfers between devices, shards(): get_east = lax.ppermute(to_west, 'lon', west)  11.4 us
    pallas_call x1, Pallas kernels, shards(): pl.pallas_call(functools.partial(bwd_kernel, sizes), grid=(groups,), in_s...  8.07 us
    ppermute x9, starting transfers between devices, swap(): return lax.ppermute(x, axis, [(i, i ^ bit) for i in range(n)])  7.54 us
    unnamed x28, local copies, waits for them, and re-layouts  7.26 us
    ppermute x1, waiting for transfers between devices, shards(): from_west = lax.ppermute(paired[:, lon_dev - RAD:], 'lon', east)  5.78 us
    ppermute x1, starting transfers between devices, shards(): get_above = lax.ppermute(terms[outer_lat - RAD:].astype(BF16), 'lat', down)  5.61 us
    pallas_call x1, Pallas kernels, shards(): pl.pallas_call(functools.partial(fwd_kernel, sizes), grid=(groups,), in_s...  5.01 us
  transfers between devices with their start and end apart: 17, of which 8 were waited for; matrix products, arithmetic and copies ran while one was open for 26% of the time, Pallas kernels for 6%

profile of v1, /device:TPU:1, one launch (start us, length us, event | category | flops | bytes accessed | tf_op | source)
XLA Modules:
  0.0 128.9 jit_solution(9379812943359615735)
XLA Ops:
  0.7 1.1 constant_dynamic-update-slice_fusion.1
  1.7 1.0 constant_dynamic-update-slice_fusion
  2.8 2.1 %collective-permute-start = (bf16[16,6,1024]{2,1,0:T(8,128)(2,1)S(1)}, bf16[16,6,1024]{2,1,0:T(8,128)(2,1)S(1)}, u32[]{:S(2)}, u32[]{:S(2)}) collective-permute-start(bf16[16,6,1024]{2,1,0:T(8,128)(2,1)S(1)} %get-tuple-element.92), channel_id=1, source_target_pairs={{0,1},{1,2},{2,3},{3,4},{4,5},{5,6},{6,7},{7,0},{8,9},{9,10},{10,1... | collective-permute-start | bytes 589832 | tf_op jit(solution)/shard_map/ppermute | solution.py:210
  4.9 3.1 %collective-permute-start.1 = (bf16[16,6,1024]{2,1,0:T(8,128)(2,1)S(1)}, bf16[16,6,1024]{2,1,0:T(8,128)(2,1)S(1)}, u32[]{:S(2)}, u32[]{:S(2)}) collective-permute-start(bf16[16,6,1024]{2,1,0:T(8,128)(2,1)S(1)} %get-tuple-element.93), channel_id=1, source_target_pairs={{0,7},{1,0},{2,1},{3,2},{4,3},{5,4},{6,5},{7,6},{8,15},{9,8},{10,9... | collective-permute-start | bytes 589832 | tf_op jit(solution)/shard_map/ppermute | solution.py:211
  9.7 5.8 %collective-permute-done = bf16[16,6,1024]{2,1,0:T(8,128)(2,1)S(1)} collective-permute-done((bf16[16,6,1024]{2,1,0:T(8,128)(2,1)S(1)}, bf16[16,6,1024]{2,1,0:T(8,128)(2,1)S(1)}, u32[]{:S(2)}, u32[]{:S(2)}) %collective-permute-start) | collective-permute-done | bytes 196640 | tf_op jit(solution)/shard_map/ppermute | solution.py:210
  15.5 1.9 %collective-permute-done.1 = bf16[16,6,1024]{2,1,0:T(8,128)(2,1)S(1)} collective-permute-done((bf16[16,6,1024]{2,1,0:T(8,128)(2,1)S(1)}, bf16[16,6,1024]{2,1,0:T(8,128)(2,1)S(1)}, u32[]{:S(2)}, u32[]{:S(2)}) %collective-permute-start.1) | collective-permute-done | bytes 196640 | tf_op jit(solution)/shard_map/ppermute | solution.py:211
  17.4 1.1 pad_maximum_fusion.6
  18.5 4.9 %collective-permute-start.2 = (bf16[6,32,1024]{2,1,0:T(8,128)(2,1)}, bf16[6,32,1024]{2,1,0:T(8,128)(2,1)}, u32[]{:S(2)}, u32[]{:S(2)}) collective-permute-start(bf16[6,32,1024]{2,1,0:T(8,128)(2,1)} %get-tuple-element.82), channel_id=1, source_target_pairs={{0,8},{8,16},{16,24},{1,9},{9,17},{17,25},{2,10},{10,18},{18,26},{... | collective-permute-start | bytes 1179656 | tf_op jit(solution)/shard_map/ppermute | solution.py:214
  23.4 2.1 %collective-permute-start.3 = (bf16[6,32,1024]{2,1,0:T(8,128)(2,1)}, bf16[6,32,1024]{2,1,0:T(8,128)(2,1)}, u32[]{:S(2)}, u32[]{:S(2)}) collective-permute-start(bf16[6,32,1024]{2,1,0:T(8,128)(2,1)} %get-tuple-element.83), channel_id=1, source_target_pairs={{8,0},{16,8},{24,16},{9,1},{17,9},{25,17},{10,2},{18,10},{26,18},{... | collective-permute-start | bytes 1179656 | tf_op jit(solution)/shard_map/ppermute | solution.py:215
  25.5 2.4 %pad_maximum_fusion = f32[16,32,2,4,64]{1,4,2,0,3:T(8,128)} fusion(f32[16,32,2,1,64]{1,4,2,0,3:T(8,128)S(1)} %get-tuple-element.89, f32[16,32,2,1,64]{1,4,2,0,3:T(8,128)S(1)} %get-tuple-element.88, f32[16,32,2,1,64]{1,4,2,0,3:T(8,128)S(1)} %get-tuple-element.87, f32[16,32,2,1,64]{1,4,2,0,3:T(8,128)S(1)} %get-tuple-element.86), kind=kLoop, calls=%fused_computation | loop fusion | flops 786432 | bytes 2097152 | tf_op jit(solution)/shard_map/concatenate | solution.py:189
  28.0 5.0 %copy.16 = f32[16,32,2,4,64]{4,3,2,1,0:T(4,128)} copy(f32[16,32,2,4,64]{1,4,2,0,3:T(8,128)} %pad_maximum_fusion) | data formatting | bytes 2097152 | tf_op jit(solution)/shard_map/concatenate | solution.py:189
  32.9 2.8 %reshape.245.bias_ref = f32[512,512]{1,0:T(8,128)S(1)} reshape(f32[16,32,2,4,64]{4,3,2,1,0:T(4,128)} %copy.16) | data formatting | bytes 2097152 | tf_op jit(solution)/shard_map/reshape | solution.py:190
  36.3 1.8 %pad_maximum_fusion.1 = bf16[28,32,1024]{2,1,0:T(8,128)(2,1)S(1)} fusion(bf16[6,32,1024]{2,1,0:T(8,128)(2,1)} %collective-permute-done.3, bf16[16,4,1024]{2,1,0:T(4,128)(2,1)S(1)} %broadcast_in_dim.36, bf16[16,6,1024]{2,1,0:T(8,128)(2,1)} %copy-done.9, bf16[16,6,1024]{2,1,0:T(8,128)(2,1)} %copy-done.8, ...), kind=kLoop, calls=%fused_computation.2 | loop fusion | flops 11010048 | bytes 3670016 | tf_op jit(solution)/shard_map/concatenate | solution.py:216
  38.1 5.0 %attend_fwd.1 = (bf16[256,512]{1,0:T(8,128)(2,1)S(1)}, f32[2,4,256]{2,1,0:T(4,128)S(1)}, f32[2,4,256]{2,1,0:T(4,128)S(1)}) custom-call(s32[1]{0:T(128)} %bitcast.lat_ref, bf16[256,512]{1,0:T(8,128)(2,1)S(1)} %bitcast.45, bf16[896,1024]{1,0:T(8,128)(2,1)S(1)} %bitcast.41, bf16[896,1024]{1,0:T(8,128)(2,1)S(1)} %bitcast.42, f32[512,512]{1,0:T(8,128)S(1)} %reshape.245.bias_ref), custom_call_target="tpu_custom_call" | custom-call | tf_op jit(solution)/shard_map/attend_fwd/pallas_call | solution.py:237
  43.6 0.9 constant_dynamic-slice_fusion.3
  44.8 8.1 %attend_bwd.1 = (bf16[256,512]{1,0:T(8,128)(2,1)}, f32[896,512]{1,0:T(8,128)S(1)}, f32[896,512]{1,0:T(8,128)S(1)}, f32[512,512]{1,0:T(8,128)S(1)}) custom-call(s32[1]{0:T(128)} %bitcast.lat_ref, bf16[256,512]{1,0:T(8,128)(2,1)S(1)} %bitcast.46, bf16[256,512]{1,0:T(8,128)(2,1)S(1)} %convolution_convert_fusion.2.g_ref, bf16[896,1024]{1,0:T(8,128)(2,1)S(1)} %bitcast.43, ...), custom_call_target="tpu_custom_call" | custom-call | tf_op jit(solution)/shard_map/attend_bwd/pallas_call | solution.py:257
  52.8 1.2 copy-done.1
  54.1 1.2 copy-done.3
  55.3 2.5 %reshape.250 = f32[16,32,2,4,64]{4,3,2,1,0:T(4,128)} reshape(f32[512,512]{1,0:T(8,128)S(1)} %get-tuple-element.67) | data formatting | bytes 2097152 | tf_op jit(solution)/shard_map/reshape | solution.py:289
  57.8 4.8 %slice_add_fusion.3 = f32[13,32,2,1,64]{4,3,2,1,0:T(1,128)S(1)} fusion(f32[16,32,2,4,64]{4,3,2,1,0:T(4,128)} %reshape.250), kind=kLoop, calls=%fused_computation.22 | loop fusion | flops 159744 | bytes 1064960 | tf_op jit(solution)/shard_map/add | solution.py:290
  62.6 1.1 copy.17
  63.7 1.9 %convolution_bitcast_fusion = f32[8,13,13]{1,2,0:T(8,128)S(1)} fusion(f32[13,32,8,16]{1,0,3,2:T(8,128)S(1)} %bitcast.48, s32[32,16]{0,1:T(8,128)S(1)} %iota_subtract_fusion), kind=kOutput, calls=%fused_computation.12 | convolution fusion | flops 8313344 | bytes 220448 | tf_op jit(solution)/shard_map/alhj,blj->hab/dot_general | solution.py:292
  66.0 1.9 %constant_dynamic-update-slice_fusion.3 = f32[896,1024]{1,0:T(8,128)S(1)} fusion(f32[896,512]{1,0:T(8,128)} %copy-done.3), kind=kLoop, calls=%fused_computation.70 | loop fusion | bytes 3670016
  68.4 0.9 copy-done.6
  69.3 1.2 add_convert_fusion
  70.6 1.7 %collective-permute-start.9 = (bf16[128,1024]{1,0:T(8,128)(2,1)S(1)}, bf16[128,1024]{1,0:T(8,128)(2,1)S(1)}, u32[]{:S(2)}, u32[]{:S(2)}) collective-permute-start(bf16[128,1024]{1,0:T(8,128)(2,1)S(1)} %constant_dynamic-slice_fusion.2), channel_id=1, source_target_pairs={{0,16},{8,24},{16,0},{24,8},{1,17},{9,25},{17,1},{25,9},{2,18},{10... | collective-permute-start | bytes 786440 | tf_op jit(solution)/shard_map/ppermute | solution.py:136
  72.2 1.2 convolution_convert_fusion.1
  73.5 5.1 %collective-permute-done.9 = bf16[128,1024]{1,0:T(8,128)(2,1)S(1)} collective-permute-done((bf16[128,1024]{1,0:T(8,128)(2,1)S(1)}, bf16[128,1024]{1,0:T(8,128)(2,1)S(1)}, u32[]{:S(2)}, u32[]{:S(2)}) %collective-permute-start.9) | collective-permute-done | bytes 262176 | tf_op jit(solution)/shard_map/ppermute | solution.py:136
  78.8 3.1 %collective-permute-start.4 = (bf16[6,32,1024]{2,1,0:T(8,128)(2,1)S(1)}, bf16[6,32,1024]{2,1,0:T(8,128)(2,1)S(1)}, u32[]{:S(2)}, u32[]{:S(2)}) collective-permute-start(bf16[6,32,1024]{2,1,0:T(8,128)(2,1)S(1)} %bitcast.55), channel_id=1, source_target_pairs={{8,0},{16,8},{24,16},{9,1},{17,9},{25,17},{10,2},{18,10},{26,18},{... | collective-permute-start | bytes 1179656 | tf_op jit(solution)/shard_map/ppermute | solution.py:274
  82.6 1.1 collective-permute-start.11
  83.9 5.6 %collective-permute-start.5 = (bf16[6,32,1024]{2,1,0:T(8,128)(2,1)S(1)}, bf16[6,32,1024]{2,1,0:T(8,128)(2,1)S(1)}, u32[]{:S(2)}, u32[]{:S(2)}) collective-permute-start(bf16[6,32,1024]{2,1,0:T(8,128)(2,1)S(1)} %bitcast.54), channel_id=1, source_target_pairs={{0,8},{8,16},{16,24},{1,9},{9,17},{17,25},{2,10},{10,18},{18,26},{... | collective-permute-start | bytes 1179656 | tf_op jit(solution)/shard_map/ppermute | solution.py:275
  89.6 2.4 %collective-permute-start.12 = (bf16[48,1024]{1,0:T(8,128)(2,1)S(1)}, bf16[48,1024]{1,0:T(8,128)(2,1)S(1)}, u32[]{:S(2)}, u32[]{:S(2)}) collective-permute-start(bf16[48,1024]{1,0:T(8,128)(2,1)S(1)} %pad_maximum_fusion.9), channel_id=1, source_target_pairs={{0,4},{1,5},{2,6},{3,7},{4,0},{5,1},{6,2},{7,3},{8,12},{9,13},{10,... | collective-permute-start | bytes 294920 | tf_op jit(solution)/shard_map/ppermute | solution.py:136
  92.1 5.3 %collective-permute-done.12 = bf16[48,1024]{1,0:T(8,128)(2,1)S(1)} collective-permute-done((bf16[48,1024]{1,0:T(8,128)(2,1)S(1)}, bf16[48,1024]{1,0:T(8,128)(2,1)S(1)}, u32[]{:S(2)}, u32[]{:S(2)}) %collective-permute-start.12) | collective-permute-done | bytes 98336 | tf_op jit(solution)/shard_map/ppermute | solution.py:136
  98.0 3.6 %collective-permute-done.13 = bf16[48,1024]{1,0:T(8,128)(2,1)S(1)} collective-permute-done((bf16[48,1024]{1,0:T(8,128)(2,1)S(1)}, bf16[48,1024]{1,0:T(8,128)(2,1)S(1)}, u32[]{:S(2)}, u32[]{:S(2)}) %collective-permute-start.13) | collective-permute-done | bytes 98336 | tf_op jit(solution)/shard_map/ppermute | solution.py:136
  101.7 0.8 fusion.16
  102.6 2.2 %collective-permute-start.6 = (bf16[16,6,1024]{2,1,0:T(8,128)(2,1)S(1)}, bf16[16,6,1024]{2,1,0:T(8,128)(2,1)S(1)}, u32[]{:S(2)}, u32[]{:S(2)}) collective-permute-start(bf16[16,6,1024]{2,1,0:T(8,128)(2,1)S(1)} %get-tuple-element.85), channel_id=1, source_target_pairs={{0,7},{1,0},{2,1},{3,2},{4,3},{5,4},{6,5},{7,6},{8,15},{9,8},{10,9... | collective-permute-start | bytes 589832 | tf_op jit(solution)/shard_map/ppermute | solution.py:281
  104.8 1.0 collective-permute-done.14
  106.0 11.4 %collective-permute-done.6 = bf16[16,6,1024]{2,1,0:T(8,128)(2,1)S(1)} collective-permute-done((bf16[16,6,1024]{2,1,0:T(8,128)(2,1)S(1)}, bf16[16,6,1024]{2,1,0:T(8,128)(2,1)S(1)}, u32[]{:S(2)}, u32[]{:S(2)}) %collective-permute-start.6) | collective-permute-done | bytes 196640 | tf_op jit(solution)/shard_map/ppermute | solution.py:281
  117.5 0.7 scatter-add.16
  118.3 0.8 reduce-precision_convert_fusion
  119.1 0.8 pad_maximum_fusion.2
  120.0 2.2 %collective-permute-start.16 = (bf16[272,1024]{1,0:T(8,128)(2,1)}, bf16[272,1024]{1,0:T(8,128)(2,1)}, u32[]{:S(2)}, u32[]{:S(2)}) collective-permute-start(bf16[272,1024]{1,0:T(8,128)(2,1)} %pad_maximum_fusion.2), channel_id=1, source_target_pairs={{0,8},{8,0},{16,24},{24,16},{1,9},{9,1},{17,25},{25,17},{2,10},{10... | collective-permute-start | bytes 1671176 | tf_op jit(solution)/shard_map/ppermute | solution.py:136
  122.1 1.0 slice_add_fusion.1
  123.2 0.8 scatter-add.19
  124.0 0.9 fusion.17
  125.1 0.7 add_bitcast_fusion
  126.7 1.1 slice_dynamic-update-slice_fusion
  127.7 1.2 multiply_convert_fusion
  (93 shorter events, 7.2 us)
Async XLA Ops:
  0.6 35.1 %copy-start = (bf16[512,1024]{1,0:T(8,128)(2,1)S(1)}, bf16[512,1024]{1,0:T(8,128)(2,1)}, u32[]{:S(2)}) copy-start(bf16[512,1024]{1,0:T(8,128)(2,1)} %param.18) | copy-start | bytes 3145732
  0.6 7.5 %copy-start.11 = (f32[8,13,13]{2,0,1:T(8,128)S(1)}, f32[8,13,13]{2,0,1:T(8,128)}, u32[]{:S(2)}) copy-start(f32[8,13,13]{2,0,1:T(8,128)} %param.17) | copy-start | bytes 16228
  2.8 12.7 %collective-permute-start = (bf16[16,6,1024]{2,1,0:T(8,128)(2,1)S(1)}, bf16[16,6,1024]{2,1,0:T(8,128)(2,1)S(1)}, u32[]{:S(2)}, u32[]{:S(2)}) collective-permute-start(bf16[16,6,1024]{2,1,0:T(8,128)(2,1)S(1)} %get-tuple-element.92), channel_id=1, source_target_pairs={{0,1},{1,2},{2,3},{3,4},{4,5},{5,6},{6,7},{7,0},{8,9},{9,10},{10,1... | collective-permute-start | bytes 589832 | tf_op jit(solution)/shard_map/ppermute | solution.py:210
  4.9 12.5 %collective-permute-start.1 = (bf16[16,6,1024]{2,1,0:T(8,128)(2,1)S(1)}, bf16[16,6,1024]{2,1,0:T(8,128)(2,1)S(1)}, u32[]{:S(2)}, u32[]{:S(2)}) collective-permute-start(bf16[16,6,1024]{2,1,0:T(8,128)(2,1)S(1)} %get-tuple-element.93), channel_id=1, source_target_pairs={{0,7},{1,0},{2,1},{3,2},{4,3},{5,4},{6,5},{7,6},{8,15},{9,8},{10,9... | collective-permute-start | bytes 589832 | tf_op jit(solution)/shard_map/ppermute | solution.py:211
  15.5 12.5 %copy-start.8 = (bf16[16,6,1024]{2,1,0:T(8,128)(2,1)}, bf16[16,6,1024]{2,1,0:T(8,128)(2,1)S(1)}, u32[]{:S(2)}) copy-start(bf16[16,6,1024]{2,1,0:T(8,128)(2,1)S(1)} %collective-permute-done) | copy-start | bytes 589828
  17.4 10.6 %copy-start.9 = (bf16[16,6,1024]{2,1,0:T(8,128)(2,1)}, bf16[16,6,1024]{2,1,0:T(8,128)(2,1)S(1)}, u32[]{:S(2)}) copy-start(bf16[16,6,1024]{2,1,0:T(8,128)(2,1)S(1)} %collective-permute-done.1) | copy-start | bytes 589828
  18.5 17.8 %collective-permute-start.2 = (bf16[6,32,1024]{2,1,0:T(8,128)(2,1)}, bf16[6,32,1024]{2,1,0:T(8,128)(2,1)}, u32[]{:S(2)}, u32[]{:S(2)}) collective-permute-start(bf16[6,32,1024]{2,1,0:T(8,128)(2,1)} %get-tuple-element.82), channel_id=1, source_target_pairs={{0,8},{8,16},{16,24},{1,9},{9,17},{17,25},{2,10},{10,18},{18,26},{... | collective-permute-start | bytes 1179656 | tf_op jit(solution)/shard_map/ppermute | solution.py:214
  23.4 12.9 %collective-permute-start.3 = (bf16[6,32,1024]{2,1,0:T(8,128)(2,1)}, bf16[6,32,1024]{2,1,0:T(8,128)(2,1)}, u32[]{:S(2)}, u32[]{:S(2)}) collective-permute-start(bf16[6,32,1024]{2,1,0:T(8,128)(2,1)} %get-tuple-element.83), channel_id=1, source_target_pairs={{8,0},{16,8},{24,16},{9,1},{17,9},{25,17},{10,2},{18,10},{26,18},{... | collective-permute-start | bytes 1179656 | tf_op jit(solution)/shard_map/ppermute | solution.py:215
  32.9 2.8 %copy-start.7 = (bf16[16,16,1024]{2,1,0:T(8,128)(2,1)S(1)}, bf16[16,16,1024]{2,1,0:T(8,128)(2,1)}, u32[]{:S(2)}) copy-start(bf16[16,16,1024]{2,1,0:T(8,128)(2,1)} %param.19) | copy-start | bytes 1572868
  36.3 1.9 %copy-start.4 = (bf16[16,16,512]{2,1,0:T(8,128)(2,1)S(1)}, bf16[16,16,512]{2,1,0:T(8,128)(2,1)}, u32[]{:S(2)}) copy-start(bf16[16,16,512]{2,1,0:T(8,128)(2,1)} %param.14) | copy-start | bytes 786436
  43.6 1.1 copy-start.5
  44.5 23.9 %collective-permute-start.8 = (bf16[256,1024]{1,0:T(8,128)(2,1)}, bf16[256,1024]{1,0:T(8,128)(2,1)}, u32[]{:S(2)}, u32[]{:S(2)}) collective-permute-start(bf16[256,1024]{1,0:T(8,128)(2,1)} %constant_dynamic-slice_fusion.3), channel_id=1, source_target_pairs={{0,8},{8,0},{16,24},{24,16},{1,9},{9,1},{17,25},{25,17},{2,10},{10... | collective-permute-start | bytes 1572872 | tf_op jit(solution)/shard_map/ppermute | solution.py:136
  52.8 1.2 copy-start.1
  54.1 1.3 copy-start.3
  65.7 2.2 %copy-start.2 = (f32[896,512]{1,0:T(8,128)S(1)}, f32[896,512]{1,0:T(8,128)}, u32[]{:S(2)}) copy-start(f32[896,512]{1,0:T(8,128)} %copy-done.1) | copy-start | bytes 5505028
  68.1 1.2 copy-start.6
  70.6 8.0 %collective-permute-start.9 = (bf16[128,1024]{1,0:T(8,128)(2,1)S(1)}, bf16[128,1024]{1,0:T(8,128)(2,1)S(1)}, u32[]{:S(2)}, u32[]{:S(2)}) collective-permute-start(bf16[128,1024]{1,0:T(8,128)(2,1)S(1)} %constant_dynamic-slice_fusion.2), channel_id=1, source_target_pairs={{0,16},{8,24},{16,0},{24,8},{1,17},{9,25},{17,1},{25,9},{2,18},{10... | collective-permute-start | bytes 786440 | tf_op jit(solution)/shard_map/ppermute | solution.py:136
  78.7 3.9 %collective-permute-start.10 = (bf16[64,1024]{1,0:T(8,128)(2,1)S(1)}, bf16[64,1024]{1,0:T(8,128)(2,1)S(1)}, u32[]{:S(2)}, u32[]{:S(2)}) collective-permute-start(bf16[64,1024]{1,0:T(8,128)(2,1)S(1)} %constant_dynamic-slice_fusion.1), channel_id=1, source_target_pairs={{0,1},{1,0},{2,3},{3,2},{4,5},{5,4},{6,7},{7,6},{8,9},{9,8},{10,11... | collective-permute-start | bytes 393224 | tf_op jit(solution)/shard_map/ppermute | solution.py:136
  78.8 13.1 %collective-permute-start.4 = (bf16[6,32,1024]{2,1,0:T(8,128)(2,1)S(1)}, bf16[6,32,1024]{2,1,0:T(8,128)(2,1)S(1)}, u32[]{:S(2)}, u32[]{:S(2)}) collective-permute-start(bf16[6,32,1024]{2,1,0:T(8,128)(2,1)S(1)} %bitcast.55), channel_id=1, source_target_pairs={{8,0},{16,8},{24,16},{9,1},{17,9},{25,17},{10,2},{18,10},{26,18},{... | collective-permute-start | bytes 1179656 | tf_op jit(solution)/shard_map/ppermute | solution.py:274
  82.6 6.9 %collective-permute-start.11 = (bf16[32,1024]{1,0:T(8,128)(2,1)S(1)}, bf16[32,1024]{1,0:T(8,128)(2,1)S(1)}, u32[]{:S(2)}, u32[]{:S(2)}) collective-permute-start(bf16[32,1024]{1,0:T(8,128)(2,1)S(1)} %constant_dynamic-slice_fusion), channel_id=1, source_target_pairs={{0,2},{1,3},{2,0},{3,1},{4,6},{5,7},{6,4},{7,5},{8,10},{9,11},{10,... | collective-permute-start | bytes 196616 | tf_op jit(solution)/shard_map/ppermute | solution.py:136
  83.9 13.7 %collective-permute-start.5 = (bf16[6,32,1024]{2,1,0:T(8,128)(2,1)S(1)}, bf16[6,32,1024]{2,1,0:T(8,128)(2,1)S(1)}, u32[]{:S(2)}, u32[]{:S(2)}) collective-permute-start(bf16[6,32,1024]{2,1,0:T(8,128)(2,1)S(1)} %bitcast.54), channel_id=1, source_target_pairs={{0,8},{8,16},{16,24},{1,9},{9,17},{17,25},{2,10},{10,18},{18,26},{... | collective-permute-start | bytes 1179656 | tf_op jit(solution)/shard_map/ppermute | solution.py:275
  89.6 7.8 %collective-permute-start.12 = (bf16[48,1024]{1,0:T(8,128)(2,1)S(1)}, bf16[48,1024]{1,0:T(8,128)(2,1)S(1)}, u32[]{:S(2)}, u32[]{:S(2)}) collective-permute-start(bf16[48,1024]{1,0:T(8,128)(2,1)S(1)} %pad_maximum_fusion.9), channel_id=1, source_target_pairs={{0,4},{1,5},{2,6},{3,7},{4,0},{5,1},{6,2},{7,3},{8,12},{9,13},{10,... | collective-permute-start | bytes 294920 | tf_op jit(solution)/shard_map/ppermute | solution.py:136
  97.5 4.0 %collective-permute-start.13 = (bf16[48,1024]{1,0:T(8,128)(2,1)S(1)}, bf16[48,1024]{1,0:T(8,128)(2,1)S(1)}, u32[]{:S(2)}, u32[]{:S(2)}) collective-permute-start(bf16[48,1024]{1,0:T(8,128)(2,1)S(1)} %pad_maximum_fusion.10), channel_id=1, source_target_pairs={{0,2},{1,3},{2,0},{3,1},{4,6},{5,7},{6,4},{7,5},{8,10},{9,11},{10,... | collective-permute-start | bytes 294920 | tf_op jit(solution)/shard_map/ppermute | solution.py:136
  101.6 4.2 %collective-permute-start.14 = (bf16[80,1024]{1,0:T(8,128)(2,1)S(1)}, bf16[80,1024]{1,0:T(8,128)(2,1)S(1)}, u32[]{:S(2)}, u32[]{:S(2)}) collective-permute-start(bf16[80,1024]{1,0:T(8,128)(2,1)S(1)} %pad_maximum_fusion.8), channel_id=1, source_target_pairs={{0,1},{1,0},{2,3},{3,2},{4,5},{5,4},{6,7},{7,6},{8,9},{9,8},{10,11... | collective-permute-start | bytes 491528 | tf_op jit(solution)/shard_map/ppermute | solution.py:136
  102.6 14.8 %collective-permute-start.6 = (bf16[16,6,1024]{2,1,0:T(8,128)(2,1)S(1)}, bf16[16,6,1024]{2,1,0:T(8,128)(2,1)S(1)}, u32[]{:S(2)}, u32[]{:S(2)}) collective-permute-start(bf16[16,6,1024]{2,1,0:T(8,128)(2,1)S(1)} %get-tuple-element.85), channel_id=1, source_target_pairs={{0,7},{1,0},{2,1},{3,2},{4,3},{5,4},{6,5},{7,6},{8,15},{9,8},{10,9... | collective-permute-start | bytes 589832 | tf_op jit(solution)/shard_map/ppermute | solution.py:281
  104.8 17.4 %collective-permute-start.7 = (bf16[16,6,1024]{2,1,0:T(8,128)(2,1)}, bf16[16,6,1024]{2,1,0:T(8,128)(2,1)}, u32[]{:S(2)}, u32[]{:S(2)}) collective-permute-start(bf16[16,6,1024]{2,1,0:T(8,128)(2,1)} %get-tuple-element.84), channel_id=1, source_target_pairs={{0,1},{1,2},{2,3},{3,4},{4,5},{5,6},{6,7},{7,0},{8,9},{9,10},{10,1... | collective-permute-start | bytes 589832 | tf_op jit(solution)/shard_map/ppermute | solution.py:282
  105.9 11.5 %copy-start.10 = (bf16[80,1024]{1,0:T(8,128)(2,1)}, bf16[80,1024]{1,0:T(8,128)(2,1)S(1)}, u32[]{:S(2)}) copy-start(bf16[80,1024]{1,0:T(8,128)(2,1)S(1)} %collective-permute-done.14) | copy-start | bytes 491524
  105.9 12.4 %collective-permute-start.15 = (bf16[144,1024]{1,0:T(8,128)(2,1)S(1)}, bf16[144,1024]{1,0:T(8,128)(2,1)S(1)}, u32[]{:S(2)}, u32[]{:S(2)}) collective-permute-start(bf16[144,1024]{1,0:T(8,128)(2,1)S(1)} %pad_maximum_fusion.7), channel_id=1, source_target_pairs={{0,16},{8,24},{16,0},{24,8},{1,17},{9,25},{17,1},{25,9},{2,18},{10... | collective-permute-start | bytes 884744 | tf_op jit(solution)/shard_map/ppermute | solution.py:136
  120.0 5.1 %collective-permute-start.16 = (bf16[272,1024]{1,0:T(8,128)(2,1)}, bf16[272,1024]{1,0:T(8,128)(2,1)}, u32[]{:S(2)}, u32[]{:S(2)}) collective-permute-start(bf16[272,1024]{1,0:T(8,128)(2,1)} %pad_maximum_fusion.2), channel_id=1, source_target_pairs={{0,8},{8,0},{16,24},{24,16},{1,9},{9,1},{17,25},{25,17},{2,10},{10... | collective-permute-start | bytes 1671176 | tf_op jit(solution)/shard_map/ppermute | solution.py:136

commit v2 on v1

v2 whole, which is shorter than its diff:
```python
import functools

import jax
import jax.numpy as jnp
from jax import lax
from jax.experimental import pallas as pl
from jax.experimental.pallas import tpu as pltpu
from jax.sharding import PartitionSpec as P

RAD = 6
SPAN = 2 * RAD + 1
TILE = 4
GROUP = 4
NEG = -1e30
NT = (((1,), (1,)), ((), ()))
F32 = jnp.float32
BF16 = jnp.bfloat16
SLOTS = 16
CORNER = 80


def dot(a, b):
    return jnp.dot(a, b, preferred_element_type=F32)


def dot_nt(a, b):
    return lax.dot_general(a, b, NT, preferred_element_type=F32)


def iota2(shape, axis):
    return lax.broadcasted_iota(jnp.int32, shape, axis)


def hot(mask):
    return mask.astype(F32).astype(BF16)


def spread_heads(tile, cols, head_size):
    lane = iota2((cols, tile.shape[1]), 1) // head_size
    zero = jnp.zeros((cols, tile.shape[1]), tile.dtype)
    parts = []
    for i in range(TILE):
        rows = tile[i * cols : (i + 1) * cols]
        for h in range(GROUP):
            parts.append(jnp.where(lane == h, rows, zero))
    return jnp.concatenate(parts, 0)


def head_mask(cols, head_size):
    shape = (GROUP * head_size, TILE * GROUP * cols)
    return iota2(shape, 0) // head_size == (iota2(shape, 1) // cols) % GROUP


def picker(cols):
    shape = (TILE * cols, TILE * GROUP * cols)
    row = iota2(shape, 0)
    col = iota2(shape, 1)
    return hot((row // cols == col // (GROUP * cols)) & (row % cols == col % cols))


def row_keep(first_row, rows_all, win, lanes, cols_pad):
    row = first_row + iota2((win, lanes), 0) // cols_pad
    return (row >= 0) & (row < rows_all)


def take_cols(rows, cols, first):
    shape = (rows * RAD, rows * cols)
    n = iota2(shape, 0)
    return hot(iota2(shape, 1) == (n // RAD) * cols + first + n % RAD)


def put_cols(rows, cols, first):
    shape = (rows * cols, rows * RAD)
    n = iota2(shape, 1)
    return hot(iota2(shape, 0) == (n // RAD) * cols + first + n % RAD)


def put_corner(cols):
    shape = (RAD * cols, CORNER)
    n = iota2(shape, 1)
    half = RAD * RAD
    m = jnp.where(n < half, n, n - half)
    target = (m // RAD) * cols + m % RAD + jnp.where(n < half, 0, RAD)
    return hot((iota2(shape, 0) == target) & (n < 2 * half))


def pack_kernel(rows, cols, k_ref, v_ref, east_ref, west_ref, down_ref, up_ref):
    pick_east = take_cols(rows, cols, cols - RAD)
    pick_west = take_cols(rows, cols, 0)
    edge = RAD * cols
    for i, ref in enumerate((k_ref, v_ref)):
        x = ref[...]
        east_ref[i] = dot(pick_east, x).astype(BF16)
        west_ref[i] = dot(pick_west, x).astype(BF16)
        down_ref[i] = x[(rows - RAD) * cols :]
        up_ref[i] = x[:edge]


def corner_kernel(rows, w_ref, e_ref, down_ref, up_ref):
    half = RAD * RAD
    shape = (CORNER, rows * RAD)
    n = iota2(shape, 0)
    src = iota2(shape, 1)
    for ref, first in ((down_ref, (rows - RAD) * RAD), (up_ref, 0)):
        pick_w = hot((src == first + n) & (n < half))
        pick_e = hot((src == first + n - half) & (n >= half) & (n < 2 * half))
        for i in range(2):
            ref[i] = (dot(pick_w, w_ref[i]) + dot(pick_e, e_ref[i])).astype(BF16)


def table_kernel(cols, cols_pad, rel_ref, out_ref, c_ref, r_ref):
    lanes = rel_ref.shape[1]
    half = lanes // 2
    shape = (cols_pad, lanes)
    offset = slot_offset(shape, cols)
    inside = (offset >= 0) & (offset < SPAN)
    for a in range(SPAN):
        tile = jnp.full(shape, NEG, F32)
        for b in range(SPAN):
            n = a * SPAN + b
            tile = jnp.where(offset == b, rel_ref[n : n + 1, :], tile)
        tile = jnp.where(inside, tile, NEG)
        c_ref[a] = tile
        r_ref[a] = pltpu.roll(tile, half, 1)
    low = iota2(shape, 1) < half
    blank = jnp.full(shape, NEG, F32)
    for g in range(2):
        first, second = (c_ref, r_ref) if g == 0 else (r_ref, c_ref)
        for pair in range(TILE // 2):
            i = 2 * pair
            lo = (g * TILE // 2 + pair) * lanes
            for k in range(TILE + 2 * RAD):
                a = k - i
                one = first[a] if 0 <= a < SPAN else blank
                two = second[a - 1] if 0 <= a - 1 < SPAN else blank
                out_ref[k * cols_pad : (k + 1) * cols_pad, lo : lo + lanes] = jnp.where(
                    low, one, two
                )


def slot_offset(shape, cols):
    slot = iota2(shape, 0)
    pos = jnp.where(slot < cols, slot + RAD, jnp.where(slot < cols + RAD, slot - cols, slot))
    pos = jnp.where(slot < cols + 2 * RAD, pos, -1000)
    return pos - iota2(shape, 1) % cols


def assemble(out_ref, i, rows, cols, cols_pad, own, refs):
    w_ref, e_ref, ao_ref, ac_ref, bo_ref, bc_ref = refs
    side = dot(put_cols(rows, SLOTS, 0), w_ref[i]) + dot(put_cols(rows, SLOTS, RAD), e_ref[i])
    side = side.astype(BF16)
    for r in range(rows):
        lo = (RAD + r) * cols_pad
        out_ref[lo : lo + cols, :] = own[r * cols : (r + 1) * cols, :]
        out_ref[lo + cols : lo + cols + SLOTS, :] = side[r * SLOTS : (r + 1) * SLOTS]
    put = put_corner(SLOTS)
    for first, o_ref, c_ref in ((0, ao_ref, ac_ref), (RAD + rows, bo_ref, bc_ref)):
        side = dot(put, c_ref[i]).astype(BF16)
        for r in range(RAD):
            lo = (first + r) * cols_pad
            out_ref[lo : lo + cols, :] = o_ref[i, r * cols : (r + 1) * cols, :]
            out_ref[lo + cols : lo + cols + SLOTS, :] = side[r * SLOTS : (r + 1) * SLOTS]


def fwd_kernel(
    sizes, info_ref, q_ref, k_ref, v_ref, w_ref, e_ref, ao_ref, ac_ref, bo_ref, bc_ref,
    bias_ref, cot_ref, out_ref, m_ref, l_ref, weight_ref, ko_ref, vo_ref, vt_ref, at_ref,
):
    lat_dev, cols, cols_pad, head_size, rows_all = sizes
    scale = head_size ** (-0.5)
    refs = (w_ref, e_ref, ao_ref, ac_ref, bo_ref, bc_ref)
    assemble(ko_ref, 0, lat_dev, cols, cols_pad, k_ref, refs)
    assemble(vo_ref, 1, lat_dev, cols, cols_pad, v_ref, refs)
    vt_ref[...] = vo_ref[...].T
    mask = head_mask(cols, head_size)
    pick = picker(cols)
    win = (TILE + 2 * RAD) * cols_pad
    for t in range(lat_dev // TILE):
        lo = t * TILE * cols_pad
        qs = pl.ds(t * TILE * cols, TILE * cols)
        q_bd = spread_heads(q_ref[qs, :] * jnp.asarray(scale, BF16), cols, head_size)
        first = info_ref[1] * lat_dev + t * TILE - RAD
        keep = row_keep(first, rows_all, win, q_bd.shape[0], cols_pad)
        st = jnp.where(keep, dot_nt(ko_ref[pl.ds(lo, win), :], q_bd) + bias_ref[...], NEG)
        m = jnp.max(st, 0, keepdims=True)
        e = jnp.exp(st - m)
        inv = 1.0 / jnp.sum(e, 0, keepdims=True)
        p = (e * inv).astype(BF16)
        ot = dot(vt_ref[:, pl.ds(lo, win)], p)
        ot = jnp.where(mask, ot, 0.0).astype(BF16)
        out_ref[qs, :] = dot_nt(pick, ot).astype(BF16)
        m_ref[t : t + 1, :] = m
        l_ref[t : t + 1, :] = inv
    at_ref[...] = out_ref[...].T
    weight_ref[...] = dot(at_ref[...], cot_ref[...]).astype(weight_ref.dtype)


def bwd_kernel(
    sizes, info_ref, q_ref, g_ref, k_ref, v_ref, w_ref, e_ref, ao_ref, ac_ref, bo_ref, bc_ref,
    bias_ref, ms_ref, ls_ref, mk_ref, lk_ref,
    dq_ref, top_ref, bot_ref, mid_ref, side_ref, x_ref,
    ko_ref, vo_ref, kt_ref, dk_ref, dv_ref, db_ref,
):
    lat_dev, cols, cols_pad, head_size, rows_all = sizes
    scale = head_size ** (-0.5)
    refs = (w_ref, e_ref, ao_ref, ac_ref, bo_ref, bc_ref)
    assemble(ko_ref, 0, lat_dev, cols, cols_pad, k_ref, refs)
    assemble(vo_ref, 1, lat_dev, cols, cols_pad, v_ref, refs)
    kt_ref[...] = ko_ref[...].T
    mask = head_mask(cols, head_size)
    pick = picker(cols)
    win = (TILE + 2 * RAD) * cols_pad
    sent = pl.program_id(0) == info_ref[0]
    dk_ref[...] = jnp.zeros_like(dk_ref)
    dv_ref[...] = jnp.zeros_like(dv_ref)
    for t in range(lat_dev // TILE):
        lo = t * TILE * cols_pad
        qs = pl.ds(t * TILE * cols, TILE * cols)
        ws = pl.ds(lo, win)
        q_bd = spread_heads(q_ref[qs, :] * jnp.asarray(scale, BF16), cols, head_size)
        g_bd = spread_heads(g_ref[qs, :], cols, head_size)
        first = info_ref[1] * lat_dev + t * TILE - RAD
        keep = row_keep(first, rows_all, win, q_bd.shape[0], cols_pad)
        st = jnp.where(keep, dot_nt(ko_ref[ws, :], q_bd) + bias_ref[...], NEG)
        m = jnp.where(sent, ms_ref[t : t + 1, :], mk_ref[t : t + 1, :])
        inv = jnp.where(sent, ls_ref[t : t + 1, :], lk_ref[t : t + 1, :])
        p = jnp.exp(st - m) * inv
        slope = dot_nt(vo_ref[ws, :], g_bd)
        inner = jnp.sum(p * slope, 0, keepdims=True)
        sg = p * (slope - inner)
        if t == 0:
            db_ref[...] = sg
        else:
            db_ref[...] += sg
        sgb = sg.astype(BF16)
        dqt = jnp.where(mask, dot(kt_ref[:, ws], sgb) * scale, 0.0).astype(BF16)
        dq_ref[qs, :] = dot_nt(pick, dqt).astype(BF16)
        dk_ref[ws, :] += dot(sgb, q_bd)
        dv_ref[ws, :] += dot(p.astype(BF16), g_bd)
    edge = RAD * cols_pad
    for i, ref in enumerate((dk_ref, dv_ref)):
        top_ref[i] = ref[:edge, :].astype(BF16)
        bot_ref[i] = ref[edge + lat_dev * cols_pad :, :].astype(BF16)
        for r in range(lat_dev):
            lo = (RAD + r) * cols_pad
            mid_ref[i, r * cols : (r + 1) * cols, :] = ref[lo : lo + cols, :]
            side_ref[i, r * SLOTS : (r + 1) * SLOTS, :] = ref[lo + cols : lo + cols_pad, :]
    half = GROUP * cols
    low = iota2((cols_pad, 2 * half), 1) < half
    for a in range(SPAN):
        total = jnp.zeros((cols_pad, 2 * half), F32)
        for pair in range(TILE // 2):
            i = 2 * pair
            lanes = slice(pair * 2 * half, (pair + 1) * 2 * half)
            one = db_ref[(a + i) * cols_pad : (a + i + 1) * cols_pad, lanes]
            two = db_ref[(a + i + 1) * cols_pad : (a + i + 2) * cols_pad, lanes]
            total = total + jnp.where(low, one, two)
        x_ref[0, a * cols_pad : (a + 1) * cols_pad, :] = total


def bias_kernel(cols, cols_pad, x_ref, out_ref, z_ref):
    lanes = x_ref.shape[2]
    half = lanes // 2
    shape = (cols_pad, lanes)
    low = iota2(shape, 1) < half
    offset = slot_offset(shape, cols)
    z_ref[...] = jnp.zeros_like(z_ref)
    for a in range(SPAN):
        rows = slice(a * cols_pad, (a + 1) * cols_pad)
        one = x_ref[0, rows, :]
        two = x_ref[1, rows, :]
        both = jnp.where(low, one + pltpu.roll(one, half, 1), two + pltpu.roll(two, half, 1))
        for b in range(SPAN):
            n = a * SPAN + b
            z_ref[n : n + 1, :] = jnp.sum(jnp.where(offset == b, both, 0.0), 0, keepdims=True)
    heads = out_ref.shape[0]
    pick = (iota2((heads, lanes), 1) // cols == iota2((heads, lanes), 0)).astype(F32)
    out_ref[...] = lax.dot_general(
        pick, z_ref[...], NT, precision=lax.Precision.HIGHEST, preferred_element_type=F32
    )


def lat_terms(ref, i, rows, cols, cols_pad, first):
    parts = []
    for r in range(RAD):
        lo = r * cols_pad + first
        parts.append(ref[i, lo : lo + cols, :])
    return jnp.concatenate(parts, 0).astype(F32)


def side_kernel(rows, cols, cols_pad, side_ref, a_ref, b_ref, west_ref, east_ref, s_ref):
    edge = RAD * SLOTS
    pick_west = take_cols(rows, SLOTS, 0)
    pick_east = take_cols(rows, SLOTS, RAD)
    for i in range(2):
        s_ref[...] = side_ref[i]
        s_ref[:edge, :] += lat_terms(a_ref, i, rows, SLOTS, cols_pad, cols)
        s_ref[(rows - RAD) * SLOTS :, :] += lat_terms(b_ref, i, rows, SLOTS, cols_pad, cols)
        x = s_ref[...].astype(BF16)
        west_ref[i] = dot(pick_west, x).astype(BF16)
        east_ref[i] = dot(pick_east, x).astype(BF16)


def join_kernel(rows, cols, cols_pad, mid_ref, a_ref, b_ref, w_ref, e_ref, k_ref, v_ref, s_ref):
    edge = RAD * cols
    put_west = put_cols(rows, cols, 0)
    put_east = put_cols(rows, cols, cols - RAD)
    for i, out_ref in enumerate((k_ref, v_ref)):
        s_ref[...] = mid_ref[i] + dot(put_west, w_ref[i]) + dot(put_east, e_ref[i])
        s_ref[:edge, :] += lat_terms(a_ref, i, rows, cols, cols_pad, 0)
        s_ref[(rows - RAD) * cols :, :] += lat_terms(b_ref, i, rows, cols, cols_pad, 0)
        out_ref[...] = s_ref[...].astype(BF16)


def bits_of(mesh_shape):
    order = []
    for axis in ("lat", "lon"):
        n = mesh_shape[axis]
        bit = 1
        while bit < n:
            order.append((axis, bit, n))
            bit *= 2
    return order


def swap(x, axis, bit, n):
    return lax.ppermute(x, axis, [(i, i ^ bit) for i in range(n)])


def split_f32(x):
    hi = lax.reduce_precision(x, 8, 7)
    return hi.astype(BF16), lax.reduce_precision(x - hi, 8, 7).astype(BF16)


def place_kernel(info_ref, own_ref, got_ref, out_ref):
    first = pl.program_id(0) == 0

    @pl.when(first)
    def _():
        out_ref[...] = own_ref[...]

    @pl.when(jnp.logical_not(first))
    def _():
        out_ref[...] = got_ref[...]


def reduce_all(send, keep, bias, mesh_shape, norm):
    order = bits_of(mesh_shape)
    axis, bit, n = order[0]
    part = keep + swap(send, axis, bit, n).astype(F32)
    for axis, bit, n in order[1:-1]:
        mine = (lax.axis_index(axis) // bit) % 2
        half = part.shape[0] // 2
        send = lax.dynamic_slice_in_dim(part, (1 - mine) * half, half, 0).astype(BF16)
        keep = lax.dynamic_slice_in_dim(part, mine * half, half, 0)
        part = keep + swap(send, axis, bit, n).astype(F32)
    heads, count = bias.shape
    width = part.shape[1]
    part = part.astype(BF16)
    for step, (axis, bit, n) in enumerate(order[::-1]):
        rows = part.shape[0]
        hi, lo = split_f32(bias)
        small = jnp.pad(jnp.concatenate([hi, lo], 1), ((0, 0), (0, width - 2 * count)))
        got = swap(jnp.concatenate([part, small], 0), axis, bit, n)
        near = hi.astype(F32) + lo.astype(F32)
        far = got[rows:, :count].astype(F32) + got[rows:, count : 2 * count].astype(F32)
        bias = near + far
        if step == 0:
            part = ((part.astype(F32) + got[:rows].astype(F32)) * norm).astype(BF16)
            continue
        mine = (lax.axis_index(axis) // bit) % 2
        if step < len(order) - 1:
            other = got[:rows]
            part = jnp.where(
                mine == 0,
                jnp.concatenate([part, other], 0),
                jnp.concatenate([other, part], 0),
            )
            continue
        whole = pl.BlockSpec((rows, width), lambda i, s: (0, 0))
        part = pl.pallas_call(
            place_kernel,
            grid_spec=pltpu.PrefetchScalarGridSpec(
                num_scalar_prefetch=1,
                grid=(2,),
                in_specs=[whole, whole],
                out_specs=pl.BlockSpec((rows, width), lambda i, s: (i ^ s[0], 0)),
            ),
            out_shape=jax.ShapeDtypeStruct((2 * rows, width), BF16),
            name="place",
        )(mine.astype(jnp.int32).reshape(1), part, got)
    return part, bias * norm


def shards(mesh_shape, queries, keys, values, rel_bias, out_weight, cotangent):
    lat_dev, lon_dev, width = queries.shape
    heads = rel_bias.shape[0]
    head_size = width // heads
    groups = heads // GROUP
    lanes = GROUP * head_size
    model = out_weight.shape[1]
    n_lat, n_lon = mesh_shape["lat"], mesh_shape["lon"]
    cols_pad = lon_dev + SLOTS
    outer_lat = lat_dev + 2 * RAD
    tokens = lat_dev * lon_dev
    norm = (tokens * n_lat * n_lon) ** (-0.5)
    east = [(i, (i + 1) % n_lon) for i in range(n_lon)]
    west = [(i, (i - 1) % n_lon) for i in range(n_lon)]
    down = [(i, i + 1) for i in range(n_lat - 1)]
    up = [(i + 1, i) for i in range(n_lat - 1)]
    win = (TILE + 2 * RAD) * cols_pad
    tiles = lat_dev // TILE
    lanes_q = TILE * GROUP * lon_dev
    n_keys = outer_lat * cols_pad
    n_side = lat_dev * RAD
    n_edge = RAD * lon_dev
    n_strip = RAD * cols_pad

    def shape(dims, dtype=BF16):
        return jax.ShapeDtypeStruct(dims, dtype)

    q_flat = queries.reshape(tokens, width)
    k_flat = keys.reshape(tokens, width)
    v_flat = values.reshape(tokens, width)
    cot = cotangent.reshape(tokens, model)

    to_east, to_west, to_down, to_up = pl.pallas_call(
        functools.partial(pack_kernel, lat_dev, lon_dev),
        out_shape=[shape((2, n_side, width))] * 2 + [shape((2, n_edge, width))] * 2,
        name="pack",
    )(k_flat, v_flat)
    from_west = lax.ppermute(to_east, "lon", east)
    from_east = lax.ppermute(to_west, "lon", west)
    above_own = lax.ppermute(to_down, "lat", down)
    below_own = lax.ppermute(to_up, "lat", up)
    corner_down, corner_up = pl.pallas_call(
        functools.partial(corner_kernel, lat_dev),
        out_shape=[shape((2, CORNER, width))] * 2,
        name="corner",
    )(from_west, from_east)
    above_corner = lax.ppermute(corner_down, "lat", down)
    below_corner = lax.ppermute(corner_up, "lat", up)

    rel = jnp.repeat(rel_bias.reshape(heads, SPAN * SPAN).T, lon_dev, axis=1)
    table = pl.pallas_call(
        functools.partial(table_kernel, lon_dev, cols_pad),
        out_shape=shape((win, groups * lanes_q), F32),
        scratch_shapes=[pltpu.VMEM((SPAN, cols_pad, heads * lon_dev), F32)] * 2,
        name="table",
    )(rel)
    attended_grad = dot_nt(cot, out_weight).astype(BF16)

    lat_index = lax.axis_index("lat").astype(jnp.int32)
    core = lat_index % 2
    sizes = (lat_dev, lon_dev, cols_pad, head_size, lat_dev * n_lat)
    params = pltpu.CompilerParams(vmem_limit_bytes=48 << 20)

    def forward(group, dtype):
        def part(rows):
            return pl.BlockSpec((2, rows, lanes), lambda i, s: (0, 0, s[0]))

        tok = pl.BlockSpec((tokens, lanes), lambda i, s: (0, s[0]))
        whole = pl.BlockSpec((tokens, lanes), lambda i, s: (0, 0))
        stat = pl.BlockSpec((tiles, lanes_q), lambda i, s: (0, 0))
        return pl.pallas_call(
            functools.partial(fwd_kernel, sizes),
            grid_spec=pltpu.PrefetchScalarGridSpec(
                num_scalar_prefetch=1,
                grid=(1,),
                in_specs=[tok, tok, tok, part(n_side), part(n_side), part(n_edge), part(CORNER)]
                + [part(n_edge), part(CORNER), pl.BlockSpec((win, lanes_q), lambda i, s: (0, s[0]))]
                + [pl.BlockSpec((tokens, model), lambda i, s: (0, 0))],
                out_specs=[whole, stat, stat, pl.BlockSpec((lanes, model), lambda i, s: (0, 0))],
                scratch_shapes=[pltpu.VMEM((n_keys, lanes), BF16)] * 2
                + [pltpu.VMEM((lanes, n_keys), BF16), pltpu.VMEM((lanes, tokens), BF16)],
            ),
            out_shape=[shape((tokens, lanes))]
            + [shape((tiles, lanes_q), F32)] * 2
            + [shape((lanes, model), dtype)],
            compiler_params=params,
            name="attend_fwd",
        )(
            jnp.stack([group, lat_index]), q_flat, k_flat, v_flat, from_west, from_east,
            above_own, above_corner, below_own, below_corner, table, cot,
        )

    att_s, m_s, l_s, weight_s = forward(1 - core, BF16)
    att_k, m_k, l_k, weight_k = forward(core, F32)

    low = jnp.where(core == 0, att_k, att_s)
    high = jnp.where(core == 0, att_s, att_k)
    attended = jnp.concatenate([low, high], 1)
    block_out = dot(attended, out_weight).astype(BF16)

    smem = pl.BlockSpec(memory_space=pltpu.SMEM)
    tok = pl.BlockSpec((tokens, lanes), lambda g: (0, g))
    stat = pl.BlockSpec((tiles, lanes_q), lambda g: (0, 0))

    def part(rows):
        return pl.BlockSpec((2, rows, lanes), lambda g: (0, 0, g))

    query_grad, top, bottom, mid, side, folded = pl.pallas_call(
        functools.partial(bwd_kernel, sizes),
        grid=(groups,),
        in_specs=[smem, tok, tok, tok, tok, part(n_side), part(n_side), part(n_edge)]
        + [part(CORNER), part(n_edge), part(CORNER)]
        + [pl.BlockSpec((win, lanes_q), lambda g: (0, g)), stat, stat, stat, stat],
        out_specs=[tok, part(n_strip), part(n_strip), part(tokens), part(tokens)]
        + [pl.BlockSpec((1, SPAN * cols_pad, 2 * GROUP * lon_dev), lambda g: (g, 0, 0))],
        out_shape=[shape((tokens, width))]
        + [shape((2, n_strip, width))] * 2
        + [shape((2, tokens, width), F32)] * 2
        + [shape((groups, SPAN * cols_pad, 2 * GROUP * lon_dev), F32)],
        scratch_shapes=[pltpu.VMEM((n_keys, lanes), BF16)] * 2
        + [pltpu.VMEM((lanes, n_keys), BF16)]
        + [pltpu.VMEM((n_keys, lanes), F32)] * 2
        + [pltpu.VMEM((win, lanes_q), F32)],
        compiler_params=params,
        name="attend_bwd",
    )(
        jnp.stack([1 - core, lat_index]), q_flat, attended_grad, k_flat, v_flat, from_west,
        from_east, above_own, above_corner, below_own, below_corner, table, m_s, l_s, m_k, l_k,
    )

    get_below = lax.ppermute(top, "lat", up)
    get_above = lax.ppermute(bottom, "lat", down)
    give_west, give_east = pl.pallas_call(
        functools.partial(side_kernel, lat_dev, lon_dev, cols_pad),
        out_shape=[shape((2, n_side, width))] * 2,
        scratch_shapes=[pltpu.VMEM((tokens, width), F32)],
        name="side",
    )(side, get_above, get_below)
    get_east = lax.ppermute(give_west, "lon", west)
    get_west = lax.ppermute(give_east, "lon", east)
    key_grad, value_grad = pl.pallas_call(
        functools.partial(join_kernel, lat_dev, lon_dev, cols_pad),
        out_shape=[shape((tokens, width))] * 2,
        scratch_shapes=[pltpu.VMEM((tokens, width), F32)],
        name="join",
    )(mid, get_above, get_below, get_west, get_east)

    count = SPAN * SPAN
    bias_local = pl.pallas_call(
        functools.partial(bias_kernel, lon_dev, cols_pad),
        out_shape=shape((heads, 256), F32),
        scratch_shapes=[pltpu.VMEM((256, heads * lon_dev), F32)],
        name="bias_fold",
    )(folded)
    weight_grad, bias_total = reduce_all(weight_s, weight_k, bias_local, mesh_shape, norm)
    bias_grad = bias_total[:, :count].reshape(rel_bias.shape)
    return (
        block_out.reshape(lat_dev, lon_dev, model),
        query_grad.reshape(queries.shape),
        key_grad.reshape(keys.shape),
        value_grad.reshape(values.shape),
        weight_grad,
        bias_grad,
    )


def solution(mesh):
    spec = P("lat", "lon", None)
    return jax.shard_map(
        functools.partial(shards, dict(mesh.shape)),
        mesh=mesh,
        in_specs=(spec, spec, spec, P(), P(), spec),
        out_specs=(spec, spec, spec, spec, P(), P()),
        check_vma=False,
    )
```

time: 130 us -> 129 us (level)
  Pallas kernels: 13.1 us -> 33.1 us
  other arithmetic: 17.2 us -> 3.64 us
  waiting for transfers between devices: 34.7 us -> 24.4 us
  starting transfers between devices: 30.6 us -> 40.8 us
  local copies, waits for them, and re-layouts: 27.3 us -> 23.3 us
  matrix products: 4.65 us -> 1.71 us
    pallas_call x1 -> x9, Pallas kernels: 5.01 us -> 23.9 us  [the longest x2 7.88 us: forward(): pl.pallas_call(functools.partial(fwd_kernel, sizes), grid_spec=pltpu.Pref...]
    unnamed x28 -> x96, local copies, waits for them, and re-layouts: 7.26 us -> 20.9 us
    ppermute x8 -> x10, waiting for transfers between devices: 19.1 us -> 8.02 us  [the longest x1 4.12 us: shards(): get_below = lax.ppermute(top, 'lat', up)]
    ppermute x8 -> x10, starting transfers between devices: 23.1 us -> 32.6 us  [the longest x1 8.45 us: shards(): get_above = lax.ppermute(bottom, 'lat', down)]
    concatenate x3 -> x0, local copies, waits for them, and re-layouts: 6.11 us -> none  [the longest x1 4.95 us: bias_tables(): jnp.concatenate([table[edge - i:edge - i + rows] for i in range(TILE)], 3)]
    reshape x4 -> x3, local copies, waits for them, and re-layouts: 5.42 us -> 0.9 us  [the longest x2 0.81 us: shards(): rel = jnp.repeat(rel_bias.reshape(heads, SPAN * SPAN).T, lon_dev, axis=1)]
    concatenate x7 -> x10, other arithmetic: 5.17 us -> 0.95 us  [the longest x5 0.93 us: reduce_all(): got = swap(jnp.concatenate([part, small], 0), axis, bit, n)]
    add x3, other arithmetic: 5.94 us -> 2.3 us  [reduce_all(): part = keep + swap(send, axis, bit, n).astype(F32)]
  transfers between devices with their start and end apart: 17 -> 19, of which waited for: 8 -> 10; matrix products, arithmetic and copies ran while one was open for 26% -> 4% of each run, Pallas kernels for 6% -> 19%
where the time goes in v2:
time: 129 us; the launch traced here: 128 us
  starting transfers between devices  40.8 us (32%)
  Pallas kernels  33.1 us (26%)
  waiting for transfers between devices  24.4 us (19%)
  local copies, waits for them, and re-layouts  23.3 us (18%)
  other arithmetic  3.64 us (3%)
  matrix products  1.71 us (1%)
    unnamed x96, local copies, waits for them, and re-layouts  20.9 us
    ppermute x9, waiting for transfers between devices, swap(): return lax.ppermute(x, axis, [(i, i ^ bit) for i in range(n)])  16.4 us
    pallas_call x1, Pallas kernels, shards(): pl.pallas_call(functools.partial(bwd_kernel, sizes), grid=(groups,), in_s...  9.15 us
    ppermute x1, starting transfers between devices, shards(): get_above = lax.ppermute(bottom, 'lat', down)  8.45 us
    ppermute x9, starting transfers between devices, swap(): return lax.ppermute(x, axis, [(i, i ^ bit) for i in range(n)])  8.16 us
    pallas_call x2, Pallas kernels, forward(): pl.pallas_call(functools.partial(fwd_kernel, sizes), grid_spec=pltpu.Pref...  7.88 us
    ppermute x1, starting transfers between devices, shards(): above_corner = lax.ppermute(corner_down, 'lat', down)  4.89 us
    ppermute x1, starting transfers between devices, shards(): above_own = lax.ppermute(to_down, 'lat', down)  4.17 us
  transfers between devices with their start and end apart: 19, of which 10 were waited for; matrix products, arithmetic and copies ran while one was open for 4% of the time, Pallas kernels for 19%

profile of v2, /device:TPU:1, one launch (start us, length us, event | category | flops | bytes accessed | tf_op | source)
XLA Modules:
  0.0 128.1 jit_solution(16607260589490930908)
XLA Ops:
  0.6 2.2 %pack.1 = (bf16[2,96,512]{2,1,0:T(8,128)(2,1)}, bf16[2,96,512]{2,1,0:T(8,128)(2,1)}, bf16[2,96,512]{2,1,0:T(8,128)(2,1)}, bf16[2,96,512]{2,1,0:T(8,128)(2,1)}) custom-call(bf16[256,512]{1,0:T(8,128)(2,1)} %bitcast.19, bf16[256,512]{1,0:T(8,128)(2,1)} %bitcast.23), custom_call_target="tpu_custom_call" | custom-call | tf_op jit(solution)/shard_map/pack/pallas_call | solution.py:427
  2.9 2.0 %collective-permute-start = (bf16[2,96,512]{2,1,0:T(8,128)(2,1)}, bf16[2,96,512]{2,1,0:T(8,128)(2,1)S(1)}, u32[]{:S(2)}, u32[]{:S(2)}) collective-permute-start(bf16[2,96,512]{2,1,0:T(8,128)(2,1)} %get-tuple-element.30), channel_id=1, source_target_pairs={{0,1},{1,2},{2,3},{3,4},{4,5},{5,6},{6,7},{7,0},{8,9},{9,10},{10,1... | collective-permute-start | bytes 589832 | tf_op jit(solution)/shard_map/ppermute | solution.py:432
  4.9 3.0 %collective-permute-start.1 = (bf16[2,96,512]{2,1,0:T(8,128)(2,1)}, bf16[2,96,512]{2,1,0:T(8,128)(2,1)S(1)}, u32[]{:S(2)}, u32[]{:S(2)}) collective-permute-start(bf16[2,96,512]{2,1,0:T(8,128)(2,1)} %get-tuple-element.31), channel_id=1, source_target_pairs={{0,7},{1,0},{2,1},{3,2},{4,3},{5,4},{6,5},{7,6},{8,15},{9,8},{10,9... | collective-permute-start | bytes 589832 | tf_op jit(solution)/shard_map/ppermute | solution.py:433
  8.0 4.2 %collective-permute-start.2 = (bf16[2,96,512]{2,1,0:T(8,128)(2,1)}, bf16[2,96,512]{2,1,0:T(8,128)(2,1)S(1)}, u32[]{:S(2)}, u32[]{:S(2)}) collective-permute-start(bf16[2,96,512]{2,1,0:T(8,128)(2,1)} %get-tuple-element.32), channel_id=1, source_target_pairs={{0,8},{8,16},{16,24},{1,9},{9,17},{17,25},{2,10},{10,18},{18,26},{... | collective-permute-start | bytes 589832 | tf_op jit(solution)/shard_map/ppermute | solution.py:434
  12.2 2.1 %collective-permute-start.4 = (bf16[2,96,512]{2,1,0:T(8,128)(2,1)}, bf16[2,96,512]{2,1,0:T(8,128)(2,1)S(1)}, u32[]{:S(2)}, u32[]{:S(2)}) collective-permute-start(bf16[2,96,512]{2,1,0:T(8,128)(2,1)} %get-tuple-element.34), channel_id=1, source_target_pairs={{8,0},{16,8},{24,16},{9,1},{17,9},{25,17},{10,2},{18,10},{26,18},{... | collective-permute-start | bytes 589832 | tf_op jit(solution)/shard_map/ppermute | solution.py:435
  15.6 2.0 %corner.1 = (bf16[2,80,512]{2,1,0:T(8,128)(2,1)}, bf16[2,80,512]{2,1,0:T(8,128)(2,1)}) custom-call(bf16[2,96,512]{2,1,0:T(8,128)(2,1)} %copy-done.6, bf16[2,96,512]{2,1,0:T(8,128)(2,1)} %copy-done.8), custom_call_target="tpu_custom_call" | custom-call | tf_op jit(solution)/shard_map/corner/pallas_call | solution.py:436
  17.6 4.9 %collective-permute-start.3 = (bf16[2,80,512]{2,1,0:T(8,128)(2,1)}, bf16[2,80,512]{2,1,0:T(8,128)(2,1)S(1)}, u32[]{:S(2)}, u32[]{:S(2)}) collective-permute-start(bf16[2,80,512]{2,1,0:T(8,128)(2,1)} %get-tuple-element.33), channel_id=1, source_target_pairs={{0,8},{8,16},{16,24},{1,9},{9,17},{17,25},{2,10},{10,18},{18,26},{... | collective-permute-start | bytes 491528 | tf_op jit(solution)/shard_map/ppermute | solution.py:441
  22.5 1.9 %collective-permute-start.5 = (bf16[2,80,512]{2,1,0:T(8,128)(2,1)}, bf16[2,80,512]{2,1,0:T(8,128)(2,1)S(1)}, u32[]{:S(2)}, u32[]{:S(2)}) collective-permute-start(bf16[2,80,512]{2,1,0:T(8,128)(2,1)} %get-tuple-element.35), channel_id=1, source_target_pairs={{8,0},{16,8},{24,16},{9,1},{17,9},{25,17},{10,2},{18,10},{26,18},{... | collective-permute-start | bytes 491528 | tf_op jit(solution)/shard_map/ppermute | solution.py:442
  26.1 2.1 %table.1.bias_ref = f32[512,512]{1,0:T(8,128)} custom-call(f32[169,128]{1,0:T(8,128)} %copy.14.rel_ref), custom_call_target="tpu_custom_call" | custom-call | tf_op jit(solution)/shard_map/table/pallas_call | solution.py:445
  31.1 1.2 copy-done.1
  32.3 0.9 copy-done.10
  33.3 0.9 copy-done.14
  34.2 0.9 copy-done.18
  35.1 0.9 copy-done.22
  36.1 0.9 copy-done.26
  37.0 4.3 %attend_fwd.3 = (bf16[256,256]{1,0:T(8,128)(2,1)S(1)}, f32[4,256]{1,0:T(4,128)S(1)}, f32[4,256]{1,0:T(4,128)S(1)}, bf16[256,1024]{1,0:T(8,128)(2,1)}) custom-call(s32[2]{0:T(128)S(1)} %get-tuple-element.81.info_ref, bf16[256,512]{1,0:T(8,128)(2,1)S(1)} %bitcast.27, bf16[256,512]{1,0:T(8,128)(2,1)S(1)} %bitcast.20, bf16[256,512]{1,0:T(8,128)(2,1)S(1)} %bitcast.24, ...), custom_call_target="tpu_custom_call" | custom-call | tf_op jit(solution)/shard_map/attend_fwd/pallas_call | solution.py:465
  41.9 0.9 copy-done.11
  42.9 0.9 copy-done.15
  43.8 0.9 copy-done.19
  44.7 0.9 copy-done.23
  45.7 0.9 copy-done.27
  46.6 3.5 %attend_fwd.2 = (bf16[256,256]{1,0:T(8,128)(2,1)S(1)}, f32[4,256]{1,0:T(4,128)S(1)}, f32[4,256]{1,0:T(4,128)S(1)}, f32[256,1024]{1,0:T(8,128)S(1)}) custom-call(s32[2]{0:T(128)S(1)} %get-tuple-element.80.info_ref, bf16[256,512]{1,0:T(8,128)(2,1)S(1)} %bitcast.28, bf16[256,512]{1,0:T(8,128)(2,1)S(1)} %bitcast.21, bf16[256,512]{1,0:T(8,128)(2,1)S(1)} %bitcast.25, ...), custom_call_target="tpu_custom_call" | custom-call | tf_op jit(solution)/shard_map/attend_fwd/pallas_call | solution.py:465
  50.2 1.2 convert_add_fusion
  52.2 1.9 %collective-permute-start.11 = (bf16[128,1024]{1,0:T(8,128)(2,1)}, bf16[128,1024]{1,0:T(8,128)(2,1)}, u32[]{:S(2)}, u32[]{:S(2)}) collective-permute-start(bf16[128,1024]{1,0:T(8,128)(2,1)} %dynamic-slice_convert_fusion), channel_id=1, source_target_pairs={{0,16},{8,24},{16,0},{24,8},{1,17},{9,25},{17,1},{25,9},{2,18},{10... | collective-permute-start | bytes 786440 | tf_op jit(solution)/shard_map/ppermute | solution.py:327
  54.7 9.2 %attend_bwd.1 = (bf16[256,512]{1,0:T(8,128)(2,1)}, bf16[2,192,512]{2,1,0:T(8,128)(2,1)S(1)}, bf16[2,192,512]{2,1,0:T(8,128)(2,1)S(1)}, f32[2,256,512]{2,1,0:T(8,...) custom-call(s32[2]{0:T(128)S(1)} %get-tuple-element.81.info_ref, bf16[256,512]{1,0:T(8,128)(2,1)S(1)} %bitcast.29, ...), custom_call_target="tpu_custom_call" | custom-call | tf_op jit(solution)/shard_map/attend_bwd/pallas_call | solution.py:502
  63.8 1.0 copy-done.29
  64.8 1.0 copy-done.30
  67.3 2.3 %bias_fold.1 = f32[8,256]{1,0:T(8,128)} custom-call(f32[2,416,128]{2,1,0:T(8,128)} %copy-done.31), custom_call_target="tpu_custom_call" | custom-call | tf_op jit(solution)/shard_map/bias_fold/pallas_call | solution.py:543
  69.6 1.0 convert_add_fusion.1
  71.4 4.2 %collective-permute-done.12 = bf16[64,1024]{1,0:T(8,128)(2,1)S(1)} collective-permute-done((bf16[64,1024]{1,0:T(8,128)(2,1)S(1)}, bf16[64,1024]{1,0:T(8,128)(2,1)S(1)}, u32[]{:S(2)}, u32[]{:S(2)}) %collective-permute-start.12) | collective-permute-done | bytes 131104 | tf_op jit(solution)/shard_map/ppermute | solution.py:327
  75.6 1.0 collective-permute-start.13
  76.6 2.2 %collective-permute-done.13 = bf16[32,1024]{1,0:T(8,128)(2,1)S(1)} collective-permute-done((bf16[32,1024]{1,0:T(8,128)(2,1)S(1)}, bf16[32,1024]{1,0:T(8,128)(2,1)S(1)}, u32[]{:S(2)}, u32[]{:S(2)}) %collective-permute-start.13) | collective-permute-done | bytes 65568 | tf_op jit(solution)/shard_map/ppermute | solution.py:327
  78.8 2.1 %collective-permute-start.14 = (bf16[40,1024]{1,0:T(8,128)(2,1)S(1)}, bf16[40,1024]{1,0:T(8,128)(2,1)S(1)}, u32[]{:S(2)}, u32[]{:S(2)}) collective-permute-start(bf16[40,1024]{1,0:T(8,128)(2,1)S(1)} %pad_maximum_fusion.3), channel_id=1, source_target_pairs={{0,4},{1,5},{2,6},{3,7},{4,0},{5,1},{6,2},{7,3},{8,12},{9,13},{10,... | collective-permute-start | bytes 245768 | tf_op jit(solution)/shard_map/ppermute | solution.py:327
  80.9 3.1 %collective-permute-done.14 = bf16[40,1024]{1,0:T(8,128)(2,1)S(1)} collective-permute-done((bf16[40,1024]{1,0:T(8,128)(2,1)S(1)}, bf16[40,1024]{1,0:T(8,128)(2,1)S(1)}, u32[]{:S(2)}, u32[]{:S(2)}) %collective-permute-start.14) | collective-permute-done | bytes 81952 | tf_op jit(solution)/shard_map/ppermute | solution.py:327
  84.5 3.0 %collective-permute-done.15 = bf16[40,1024]{1,0:T(8,128)(2,1)S(1)} collective-permute-done((bf16[40,1024]{1,0:T(8,128)(2,1)S(1)}, bf16[40,1024]{1,0:T(8,128)(2,1)S(1)}, u32[]{:S(2)}, u32[]{:S(2)}) %collective-permute-start.15) | collective-permute-done | bytes 81952 | tf_op jit(solution)/shard_map/ppermute | solution.py:327
  87.6 4.0 %collective-permute-done.16 = bf16[72,1024]{1,0:T(8,128)(2,1)S(1)} collective-permute-done((bf16[72,1024]{1,0:T(8,128)(2,1)S(1)}, bf16[72,1024]{1,0:T(8,128)(2,1)S(1)}, u32[]{:S(2)}, u32[]{:S(2)}) %collective-permute-start.16) | collective-permute-done | bytes 147488 | tf_op jit(solution)/shard_map/ppermute | solution.py:327
  92.6 8.4 %collective-permute-start.6 = (bf16[2,192,512]{2,1,0:T(8,128)(2,1)S(1)}, bf16[2,192,512]{2,1,0:T(8,128)(2,1)S(1)}, u32[]{:S(2)}, u32[]{:S(2)}) collective-permute-start(bf16[2,192,512]{2,1,0:T(8,128)(2,1)S(1)} %copy-done.37), channel_id=1, source_target_pairs={{0,8},{8,16},{16,24},{1,9},{9,17},{17,25},{2,10},{10,18},{18,26},{... | collective-permute-start | bytes 1179656 | tf_op jit(solution)/shard_map/ppermute | solution.py:526
  101.0 1.9 %collective-permute-start.7 = (bf16[2,192,512]{2,1,0:T(8,128)(2,1)S(1)}, bf16[2,192,512]{2,1,0:T(8,128)(2,1)}, u32[]{:S(2)}, u32[]{:S(2)}) collective-permute-start(bf16[2,192,512]{2,1,0:T(8,128)(2,1)S(1)} %get-tuple-element.45), channel_id=1, source_target_pairs={{8,0},{16,8},{24,16},{9,1},{17,9},{25,17},{10,2},{18,10},{26,18},{... | collective-permute-start | bytes 1179656 | tf_op jit(solution)/shard_map/ppermute | solution.py:525
  103.8 0.9 pad_maximum_fusion
  104.7 1.1 collective-permute-start.18
  106.1 4.1 %collective-permute-done.7.b_ref = bf16[2,192,512]{2,1,0:T(8,128)(2,1)} collective-permute-done((bf16[2,192,512]{2,1,0:T(8,128)(2,1)S(1)}, bf16[2,192,512]{2,1,0:T(8,128)(2,1)}, u32[]{:S(2)}, u32[]{:S(2)}) %collective-permute-start.7) | collective-permute-done | bytes 393248 | tf_op jit(solution)/shard_map/ppermute | solution.py:525
  110.2 2.5 %side.1 = (bf16[2,96,512]{2,1,0:T(8,128)(2,1)}, bf16[2,96,512]{2,1,0:T(8,128)(2,1)}) custom-call(f32[2,256,512]{2,1,0:T(8,128)} %copy-done.29, bf16[2,192,512]{2,1,0:T(8,128)(2,1)} %copy-done.39, bf16[2,192,512]{2,1,0:T(8,128)(2,1)} %collective-permute-done.7.b_ref), custom_call_target="tpu_custom_call" | custom-call | tf_op jit(solution)/shard_map/side/pallas_call | solution.py:527
  112.7 4.2 %collective-permute-start.9 = (bf16[2,96,512]{2,1,0:T(8,128)(2,1)}, bf16[2,96,512]{2,1,0:T(8,128)(2,1)S(1)}, u32[]{:S(2)}, u32[]{:S(2)}) collective-permute-start(bf16[2,96,512]{2,1,0:T(8,128)(2,1)} %get-tuple-element.48), channel_id=1, source_target_pairs={{0,7},{1,0},{2,1},{3,2},{4,3},{5,4},{6,5},{7,6},{8,15},{9,8},{10,9... | collective-permute-start | bytes 589832 | tf_op jit(solution)/shard_map/ppermute | solution.py:533
  116.8 1.2 convolution_convert_fusion
  118.1 2.1 %collective-permute-done.8.w_ref = bf16[2,96,512]{2,1,0:T(8,128)(2,1)S(1)} collective-permute-done((bf16[2,96,512]{2,1,0:T(8,128)(2,1)}, bf16[2,96,512]{2,1,0:T(8,128)(2,1)S(1)}, u32[]{:S(2)}, u32[]{:S(2)}) %collective-permute-start.8) | collective-permute-done | bytes 196640 | tf_op jit(solution)/shard_map/ppermute | solution.py:534
  120.2 0.9 collective-permute-done.9.e_ref
  121.8 2.7 %join.1 = (bf16[256,512]{1,0:T(8,128)(2,1)}, bf16[256,512]{1,0:T(8,128)(2,1)}) custom-call(f32[2,256,512]{2,1,0:T(8,128)} %copy-done.30, bf16[2,192,512]{2,1,0:T(8,128)(2,1)} %copy-done.39, bf16[2,192,512]{2,1,0:T(8,128)(2,1)} %collective-permute-done.7.b_ref, bf16[2,96,512]{2,1,0:T(8,128)(2,1)} %copy-done.40, bf16[2,96,512]{2,1,0:T(8,128)(2,1)} %copy-done.41), custom_call_target="tpu_custom_call" | custom-call | tf_op jit(solution)/shard_map/join/pallas_call | solution.py:535
  125.9 2.2 %place.1 = bf16[512,1024]{1,0:T(8,128)(2,1)} custom-call(s32[1]{0:T(128)} %bitcast.info_ref, bf16[256,1024]{1,0:T(8,128)(2,1)} %copy-done.38, bf16[264,1024]{1,0:T(8,128)(2,1)} %collective-permute-done.18.got_ref), custom_call_target="tpu_custom_call" | custom-call | tf_op jit(solution)/shard_map/place/pallas_call | solution.py:381
  (135 shorter events, 14.9 us)
Async XLA Ops:
  0.6 53.5 %copy-start = (bf16[512,1024]{1,0:T(8,128)(2,1)S(1)}, bf16[512,1024]{1,0:T(8,128)(2,1)}, u32[]{:S(2)}) copy-start(bf16[512,1024]{1,0:T(8,128)(2,1)} %param.10) | copy-start | bytes 3145732
  2.9 11.4 %collective-permute-start = (bf16[2,96,512]{2,1,0:T(8,128)(2,1)}, bf16[2,96,512]{2,1,0:T(8,128)(2,1)S(1)}, u32[]{:S(2)}, u32[]{:S(2)}) collective-permute-start(bf16[2,96,512]{2,1,0:T(8,128)(2,1)} %get-tuple-element.30), channel_id=1, source_target_pairs={{0,1},{1,2},{2,3},{3,4},{4,5},{5,6},{6,7},{7,0},{8,9},{9,10},{10,1... | collective-permute-start | bytes 589832 | tf_op jit(solution)/shard_map/ppermute | solution.py:432
  4.9 9.9 %collective-permute-start.1 = (bf16[2,96,512]{2,1,0:T(8,128)(2,1)}, bf16[2,96,512]{2,1,0:T(8,128)(2,1)S(1)}, u32[]{:S(2)}, u32[]{:S(2)}) collective-permute-start(bf16[2,96,512]{2,1,0:T(8,128)(2,1)} %get-tuple-element.31), channel_id=1, source_target_pairs={{0,7},{1,0},{2,1},{3,2},{4,3},{5,4},{6,5},{7,6},{8,15},{9,8},{10,9... | collective-permute-start | bytes 589832 | tf_op jit(solution)/shard_map/ppermute | solution.py:433
  8.0 20.4 %collective-permute-start.2 = (bf16[2,96,512]{2,1,0:T(8,128)(2,1)}, bf16[2,96,512]{2,1,0:T(8,128)(2,1)S(1)}, u32[]{:S(2)}, u32[]{:S(2)}) collective-permute-start(bf16[2,96,512]{2,1,0:T(8,128)(2,1)} %get-tuple-element.32), channel_id=1, source_target_pairs={{0,8},{8,16},{16,24},{1,9},{9,17},{17,25},{2,10},{10,18},{18,26},{... | collective-permute-start | bytes 589832 | tf_op jit(solution)/shard_map/ppermute | solution.py:434
  12.1 18.9 %copy-start.3 = (bf16[16,16,1024]{2,1,0:T(8,128)(2,1)S(1)}, bf16[16,16,1024]{2,1,0:T(8,128)(2,1)}, u32[]{:S(2)}) copy-start(bf16[16,16,1024]{2,1,0:T(8,128)(2,1)} %param.11) | copy-start | bytes 1572868
  12.1 18.9 %copy-start.4 = (bf16[16,16,512]{2,1,0:T(8,128)(2,1)S(1)}, bf16[16,16,512]{2,1,0:T(8,128)(2,1)}, u32[]{:S(2)}) copy-start(bf16[16,16,512]{2,1,0:T(8,128)(2,1)} %param.7) | copy-start | bytes 786436
  12.2 18.9 %copy-start.5 = (bf16[16,16,512]{2,1,0:T(8,128)(2,1)S(1)}, bf16[16,16,512]{2,1,0:T(8,128)(2,1)}, u32[]{:S(2)}) copy-start(bf16[16,16,512]{2,1,0:T(8,128)(2,1)} %param.8) | copy-start | bytes 786436
  12.2 16.9 %collective-permute-start.4 = (bf16[2,96,512]{2,1,0:T(8,128)(2,1)}, bf16[2,96,512]{2,1,0:T(8,128)(2,1)S(1)}, u32[]{:S(2)}, u32[]{:S(2)}) collective-permute-start(bf16[2,96,512]{2,1,0:T(8,128)(2,1)} %get-tuple-element.34), channel_id=1, source_target_pairs={{8,0},{16,8},{24,16},{9,1},{17,9},{25,17},{10,2},{18,10},{26,18},{... | collective-permute-start | bytes 589832 | tf_op jit(solution)/shard_map/ppermute | solution.py:435
  17.6 13.5 %copy-start.7 = (bf16[2,96,512]{2,1,0:T(8,128)(2,1)S(1)}, bf16[2,96,512]{2,1,0:T(8,128)(2,1)}, u32[]{:S(2)}) copy-start(bf16[2,96,512]{2,1,0:T(8,128)(2,1)} %copy-done.6) | copy-start | bytes 589828
  17.6 13.5 %copy-start.9 = (bf16[2,96,512]{2,1,0:T(8,128)(2,1)S(1)}, bf16[2,96,512]{2,1,0:T(8,128)(2,1)}, u32[]{:S(2)}) copy-start(bf16[2,96,512]{2,1,0:T(8,128)(2,1)} %copy-done.8) | copy-start | bytes 589828
  17.6 12.1 %collective-permute-start.3 = (bf16[2,80,512]{2,1,0:T(8,128)(2,1)}, bf16[2,80,512]{2,1,0:T(8,128)(2,1)S(1)}, u32[]{:S(2)}, u32[]{:S(2)}) collective-permute-start(bf16[2,80,512]{2,1,0:T(8,128)(2,1)} %get-tuple-element.33), channel_id=1, source_target_pairs={{0,8},{8,16},{16,24},{1,9},{9,17},{17,25},{2,10},{10,18},{18,26},{... | collective-permute-start | bytes 491528 | tf_op jit(solution)/shard_map/ppermute | solution.py:441
  22.5 7.9 %collective-permute-start.5 = (bf16[2,80,512]{2,1,0:T(8,128)(2,1)}, bf16[2,80,512]{2,1,0:T(8,128)(2,1)S(1)}, u32[]{:S(2)}, u32[]{:S(2)}) collective-permute-start(bf16[2,80,512]{2,1,0:T(8,128)(2,1)} %get-tuple-element.35), channel_id=1, source_target_pairs={{8,0},{16,8},{24,16},{9,1},{17,9},{25,17},{10,2},{18,10},{26,18},{... | collective-permute-start | bytes 491528 | tf_op jit(solution)/shard_map/ppermute | solution.py:442
  31.1 1.2 copy-start.1
  32.3 0.9 copy-start.10
  33.3 0.9 copy-start.14
  34.2 0.9 copy-start.18
  37.0 5.0 %copy-start.2 = (f32[512,512]{1,0:T(8,128)S(1)}, f32[512,512]{1,0:T(8,128)}, u32[]{:S(2)}) copy-start(f32[512,512]{1,0:T(8,128)} %table.1.bias_ref) | copy-start | bytes 3145732
  41.9 8.2 %collective-permute-start.10 = (bf16[256,1024]{1,0:T(8,128)(2,1)}, bf16[256,1024]{1,0:T(8,128)(2,1)}, u32[]{:S(2)}, u32[]{:S(2)}) collective-permute-start(bf16[256,1024]{1,0:T(8,128)(2,1)} %get-tuple-element.52), channel_id=1, source_target_pairs={{0,8},{8,0},{16,24},{24,16},{1,9},{9,1},{17,25},{25,17},{2,10},{10... | collective-permute-start | bytes 1572872 | tf_op jit(solution)/shard_map/ppermute | solution.py:327
  41.9 1.0 copy-start.11
  42.9 0.9 copy-start.15
  50.1 1.3 copy-start.34
  52.2 2.4 %copy-start.12 = (bf16[16,16,512]{2,1,0:T(8,128)(2,1)S(1)}, bf16[16,16,512]{2,1,0:T(8,128)(2,1)}, u32[]{:S(2)}) copy-start(bf16[16,16,512]{2,1,0:T(8,128)(2,1)} %param.6) | copy-start | bytes 786436
  52.2 2.5 %copy-start.16 = (bf16[2,96,512]{2,1,0:T(8,128)(2,1)S(1)}, bf16[2,96,512]{2,1,0:T(8,128)(2,1)}, u32[]{:S(2)}) copy-start(bf16[2,96,512]{2,1,0:T(8,128)(2,1)} %copy-done.13) | copy-start | bytes 589828
  52.2 2.5 %copy-start.20 = (bf16[2,96,512]{2,1,0:T(8,128)(2,1)S(1)}, bf16[2,96,512]{2,1,0:T(8,128)(2,1)}, u32[]{:S(2)}) copy-start(bf16[2,96,512]{2,1,0:T(8,128)(2,1)} %copy-done.17) | copy-start | bytes 589828
  52.2 2.5 %copy-start.24 = (bf16[2,80,512]{2,1,0:T(8,128)(2,1)S(1)}, bf16[2,80,512]{2,1,0:T(8,128)(2,1)}, u32[]{:S(2)}) copy-start(bf16[2,80,512]{2,1,0:T(8,128)(2,1)} %copy-done.21) | copy-start | bytes 491524
  52.2 2.5 %copy-start.28 = (bf16[2,80,512]{2,1,0:T(8,128)(2,1)S(1)}, bf16[2,80,512]{2,1,0:T(8,128)(2,1)}, u32[]{:S(2)}) copy-start(bf16[2,80,512]{2,1,0:T(8,128)(2,1)} %copy-done.25) | copy-start | bytes 491524
  52.2 17.4 %collective-permute-start.11 = (bf16[128,1024]{1,0:T(8,128)(2,1)}, bf16[128,1024]{1,0:T(8,128)(2,1)}, u32[]{:S(2)}, u32[]{:S(2)}) collective-permute-start(bf16[128,1024]{1,0:T(8,128)(2,1)} %dynamic-slice_convert_fusion), channel_id=1, source_target_pairs={{0,16},{8,24},{16,0},{24,8},{1,17},{9,25},{17,1},{25,9},{2,18},{10... | collective-permute-start | bytes 786440 | tf_op jit(solution)/shard_map/ppermute | solution.py:327
  63.8 1.0 copy-start.29
  64.8 1.0 copy-start.30
  69.6 1.8 %copy-start.46 = (f32[8,256]{1,0:T(8,128)S(1)}, f32[8,256]{1,0:T(8,128)}, u32[]{:S(2)}) copy-start(f32[8,256]{1,0:T(8,128)} %bias_fold.1) | copy-start | bytes 24580
  70.6 4.9 %collective-permute-start.12 = (bf16[64,1024]{1,0:T(8,128)(2,1)S(1)}, bf16[64,1024]{1,0:T(8,128)(2,1)S(1)}, u32[]{:S(2)}, u32[]{:S(2)}) collective-permute-start(bf16[64,1024]{1,0:T(8,128)(2,1)S(1)} %dynamic-slice_convert_fusion.1), channel_id=1, source_target_pairs={{0,1},{1,0},{2,3},{3,2},{4,5},{5,4},{6,7},{7,6},{8,9},{9,8},{10,11... | collective-permute-start | bytes 393224 | tf_op jit(solution)/shard_map/ppermute | solution.py:327
  75.6 3.2 %collective-permute-start.13 = (bf16[32,1024]{1,0:T(8,128)(2,1)S(1)}, bf16[32,1024]{1,0:T(8,128)(2,1)S(1)}, u32[]{:S(2)}, u32[]{:S(2)}) collective-permute-start(bf16[32,1024]{1,0:T(8,128)(2,1)S(1)} %dynamic-slice_convert_fusion.2), channel_id=1, source_target_pairs={{0,2},{1,3},{2,0},{3,1},{4,6},{5,7},{6,4},{7,5},{8,10},{9,11},{10,... | collective-permute-start | bytes 196616 | tf_op jit(solution)/shard_map/ppermute | solution.py:327
  78.8 5.1 %collective-permute-start.14 = (bf16[40,1024]{1,0:T(8,128)(2,1)S(1)}, bf16[40,1024]{1,0:T(8,128)(2,1)S(1)}, u32[]{:S(2)}, u32[]{:S(2)}) collective-permute-start(bf16[40,1024]{1,0:T(8,128)(2,1)S(1)} %pad_maximum_fusion.3), channel_id=1, source_target_pairs={{0,4},{1,5},{2,6},{3,7},{4,0},{5,1},{6,2},{7,3},{8,12},{9,13},{10,... | collective-permute-start | bytes 245768 | tf_op jit(solution)/shard_map/ppermute | solution.py:327
  84.0 3.4 %collective-permute-start.15 = (bf16[40,1024]{1,0:T(8,128)(2,1)S(1)}, bf16[40,1024]{1,0:T(8,128)(2,1)S(1)}, u32[]{:S(2)}, u32[]{:S(2)}) collective-permute-start(bf16[40,1024]{1,0:T(8,128)(2,1)S(1)} %pad_maximum_fusion.4), channel_id=1, source_target_pairs={{0,2},{1,3},{2,0},{3,1},{4,6},{5,7},{6,4},{7,5},{8,10},{9,11},{10,... | collective-permute-start | bytes 245768 | tf_op jit(solution)/shard_map/ppermute | solution.py:327
  84.5 8.1 %copy-start.37 = (bf16[2,192,512]{2,1,0:T(8,128)(2,1)S(1)}, bf16[2,192,512]{2,1,0:T(8,128)(2,1)}, u32[]{:S(2)}) copy-start(bf16[2,192,512]{2,1,0:T(8,128)(2,1)} %copy-done.36) | copy-start | bytes 1179652
  87.5 4.1 %collective-permute-start.16 = (bf16[72,1024]{1,0:T(8,128)(2,1)S(1)}, bf16[72,1024]{1,0:T(8,128)(2,1)S(1)}, u32[]{:S(2)}, u32[]{:S(2)}) collective-permute-start(bf16[72,1024]{1,0:T(8,128)(2,1)S(1)} %pad_maximum_fusion.2), channel_id=1, source_target_pairs={{0,1},{1,0},{2,3},{3,2},{4,5},{5,4},{6,7},{7,6},{8,9},{9,8},{10,11... | collective-permute-start | bytes 442376 | tf_op jit(solution)/shard_map/ppermute | solution.py:327
  91.7 11.2 %collective-permute-start.17 = (bf16[136,1024]{1,0:T(8,128)(2,1)S(1)}, bf16[136,1024]{1,0:T(8,128)(2,1)S(1)}, u32[]{:S(2)}, u32[]{:S(2)}) collective-permute-start(bf16[136,1024]{1,0:T(8,128)(2,1)S(1)} %pad_maximum_fusion.1), channel_id=1, source_target_pairs={{0,16},{8,24},{16,0},{24,8},{1,17},{9,25},{17,1},{25,9},{2,18},{10... | collective-permute-start | bytes 835592 | tf_op jit(solution)/shard_map/ppermute | solution.py:327
  92.6 13.5 %collective-permute-start.6 = (bf16[2,192,512]{2,1,0:T(8,128)(2,1)S(1)}, bf16[2,192,512]{2,1,0:T(8,128)(2,1)S(1)}, u32[]{:S(2)}, u32[]{:S(2)}) collective-permute-start(bf16[2,192,512]{2,1,0:T(8,128)(2,1)S(1)} %copy-done.37), channel_id=1, source_target_pairs={{0,8},{8,16},{16,24},{1,9},{9,17},{17,25},{2,10},{10,18},{18,26},{... | collective-permute-start | bytes 1179656 | tf_op jit(solution)/shard_map/ppermute | solution.py:526
  101.0 9.2 %collective-permute-start.7 = (bf16[2,192,512]{2,1,0:T(8,128)(2,1)S(1)}, bf16[2,192,512]{2,1,0:T(8,128)(2,1)}, u32[]{:S(2)}, u32[]{:S(2)}) collective-permute-start(bf16[2,192,512]{2,1,0:T(8,128)(2,1)S(1)} %get-tuple-element.45), channel_id=1, source_target_pairs={{8,0},{16,8},{24,16},{9,1},{17,9},{25,17},{10,2},{18,10},{26,18},{... | collective-permute-start | bytes 1179656 | tf_op jit(solution)/shard_map/ppermute | solution.py:525
  103.6 2.1 %copy-start.33 = (bf16[256,256]{1,0:T(8,128)(2,1)S(1)}, bf16[256,256]{1,0:T(8,128)(2,1)}, u32[]{:S(2)}) copy-start(bf16[256,256]{1,0:T(8,128)(2,1)} %copy-done.32) | copy-start | bytes 393220
  103.6 2.1 %copy-start.35 = (bf16[256,256]{1,0:T(8,128)(2,1)S(1)}, bf16[256,256]{1,0:T(8,128)(2,1)}, u32[]{:S(2)}) copy-start(bf16[256,256]{1,0:T(8,128)(2,1)} %copy-done.34) | copy-start | bytes 393220
  103.8 8.9 %copy-start.38 = (bf16[256,1024]{1,0:T(8,128)(2,1)}, bf16[256,1024]{1,0:T(8,128)(2,1)S(1)}, u32[]{:S(2)}) copy-start(bf16[256,1024]{1,0:T(8,128)(2,1)S(1)} %maximum_select_fusion.own_ref) | copy-start | bytes 1572868
  104.7 19.8 %collective-permute-start.18 = (bf16[264,1024]{1,0:T(8,128)(2,1)}, bf16[264,1024]{1,0:T(8,128)(2,1)}, u32[]{:S(2)}, u32[]{:S(2)}) collective-permute-start(bf16[264,1024]{1,0:T(8,128)(2,1)} %pad_maximum_fusion), channel_id=1, source_target_pairs={{0,8},{8,0},{16,24},{24,16},{1,9},{9,1},{17,25},{25,17},{2,10},{10... | collective-permute-start | bytes 1622024 | tf_op jit(solution)/shard_map/ppermute | solution.py:327
  106.1 4.1 %copy-start.39 = (bf16[2,192,512]{2,1,0:T(8,128)(2,1)}, bf16[2,192,512]{2,1,0:T(8,128)(2,1)S(1)}, u32[]{:S(2)}) copy-start(bf16[2,192,512]{2,1,0:T(8,128)(2,1)S(1)} %collective-permute-done.6.a_ref) | copy-start | bytes 1179652
  112.7 7.5 %collective-permute-start.8 = (bf16[2,96,512]{2,1,0:T(8,128)(2,1)}, bf16[2,96,512]{2,1,0:T(8,128)(2,1)S(1)}, u32[]{:S(2)}, u32[]{:S(2)}) collective-permute-start(bf16[2,96,512]{2,1,0:T(8,128)(2,1)} %get-tuple-element.47), channel_id=1, source_target_pairs={{0,1},{1,2},{2,3},{3,4},{4,5},{5,6},{6,7},{7,0},{8,9},{9,10},{10,1... | collective-permute-start | bytes 589832 | tf_op jit(solution)/shard_map/ppermute | solution.py:534
  112.7 8.4 %collective-permute-start.9 = (bf16[2,96,512]{2,1,0:T(8,128)(2,1)}, bf16[2,96,512]{2,1,0:T(8,128)(2,1)S(1)}, u32[]{:S(2)}, u32[]{:S(2)}) collective-permute-start(bf16[2,96,512]{2,1,0:T(8,128)(2,1)} %get-tuple-element.48), channel_id=1, source_target_pairs={{0,7},{1,0},{2,1},{3,2},{4,3},{5,4},{6,5},{7,6},{8,15},{9,8},{10,9... | collective-permute-start | bytes 589832 | tf_op jit(solution)/shard_map/ppermute | solution.py:533
  121.7 3.4 %copy-start.43 = (bf16[8,256]{1,0:T(8,128)(2,1)S(1)}, bf16[8,256]{1,0:T(8,128)(2,1)}, u32[]{:S(2)}) copy-start(bf16[8,256]{1,0:T(8,128)(2,1)} %copy-done.42) | copy-start | bytes 12292
  121.7 3.4 %copy-start.45 = (bf16[8,256]{1,0:T(8,128)(2,1)S(1)}, bf16[8,256]{1,0:T(8,128)(2,1)}, u32[]{:S(2)}) copy-start(bf16[8,256]{1,0:T(8,128)(2,1)} %copy-done.44) | copy-start | bytes 12292
  (18 other events, 13.5 us)

commit v3 on v2

v3 whole, which is shorter than its diff:
```python
import functools

import jax
import jax.numpy as jnp
from jax import lax
from jax.experimental import pallas as pl
from jax.experimental.pallas import tpu as pltpu
from jax.sharding import PartitionSpec as P

RAD = 6
SPAN = 2 * RAD + 1
TILE = 4
GROUP = 4
NEG = -1e30
NT = (((1,), (1,)), ((), ()))
F32 = jnp.float32
BF16 = jnp.bfloat16
SLOTS = 16
CORNER = 80
MIB = 1 << 20


def dot(a, b):
    return jnp.dot(a, b, preferred_element_type=F32)


def dot_nt(a, b):
    return lax.dot_general(a, b, NT, preferred_element_type=F32)


def room(mib):
    return pltpu.CompilerParams(vmem_limit_bytes=mib * MIB)


def iota2(shape, axis):
    return lax.broadcasted_iota(jnp.int32, shape, axis)


def hot(mask):
    return mask.astype(F32).astype(BF16)


def spread_heads(tile, cols, head_size):
    lane = iota2((cols, tile.shape[1]), 1) // head_size
    zero = jnp.zeros((cols, tile.shape[1]), tile.dtype)
    parts = []
    for i in range(TILE):
        rows = tile[i * cols : (i + 1) * cols]
        for h in range(GROUP):
            parts.append(jnp.where(lane == h, rows, zero))
    return jnp.concatenate(parts, 0)


def head_mask(cols, head_size):
    shape = (GROUP * head_size, TILE * GROUP * cols)
    return iota2(shape, 0) // head_size == (iota2(shape, 1) // cols) % GROUP


def picker(cols):
    shape = (TILE * cols, TILE * GROUP * cols)
    row = iota2(shape, 0)
    col = iota2(shape, 1)
    return hot((row // cols == col // (GROUP * cols)) & (row % cols == col % cols))


def row_keep(first_row, rows_all, win, lanes, cols_pad):
    row = first_row + iota2((win, lanes), 0) // cols_pad
    return (row >= 0) & (row < rows_all)


def take_cols(rows, cols, first):
    shape = (rows * RAD, rows * cols)
    n = iota2(shape, 0)
    return hot(iota2(shape, 1) == (n // RAD) * cols + first + n % RAD)


def put_cols(rows, cols, first):
    shape = (rows * cols, rows * RAD)
    n = iota2(shape, 1)
    return hot(iota2(shape, 0) == (n // RAD) * cols + first + n % RAD)


def put_corner(cols):
    shape = (RAD * cols, CORNER)
    n = iota2(shape, 1)
    half = RAD * RAD
    m = jnp.where(n < half, n, n - half)
    target = (m // RAD) * cols + m % RAD + jnp.where(n < half, 0, RAD)
    return hot((iota2(shape, 0) == target) & (n < 2 * half))


def pack_kernel(
    rows, cols, k_hbm, v_hbm, east_ref, west_ref, down_ref, up_ref, x_ref, sem_ref
):
    copies = [
        pltpu.make_async_copy(ref, x_ref.at[i], sem_ref.at[i])
        for i, ref in enumerate((k_hbm, v_hbm))
    ]
    for copy in copies:
        copy.start()
    pick_east = take_cols(rows, cols, cols - RAD)
    pick_west = take_cols(rows, cols, 0)
    edge = RAD * cols
    for i, copy in enumerate(copies):
        copy.wait()
        x = x_ref[i]
        east_ref[i] = dot(pick_east, x).astype(BF16)
        west_ref[i] = dot(pick_west, x).astype(BF16)
        down_ref[i] = x[(rows - RAD) * cols :]
        up_ref[i] = x[:edge]


def corner_kernel(rows, w_ref, e_ref, down_ref, up_ref):
    half = RAD * RAD
    shape = (CORNER, rows * RAD)
    n = iota2(shape, 0)
    src = iota2(shape, 1)
    for ref, first in ((down_ref, (rows - RAD) * RAD), (up_ref, 0)):
        pick_w = hot((src == first + n) & (n < half))
        pick_e = hot((src == first + n - half) & (n >= half) & (n < 2 * half))
        for i in range(2):
            ref[i] = (dot(pick_w, w_ref[i]) + dot(pick_e, e_ref[i])).astype(BF16)


def prepare_kernel(
    cols, cols_pad, rel_ref, cot_ref, w_ref, out_ref, grad_ref, c_ref, r_ref
):
    grad_ref[...] = dot_nt(cot_ref[...], w_ref[...]).astype(BF16)
    heads = rel_ref.shape[0]
    lanes = heads * cols
    half = lanes // 2
    shape = (cols_pad, lanes)
    offset = slot_offset(shape, cols)
    inside = (offset >= 0) & (offset < SPAN)
    head = iota2((1, lanes), 1) // cols
    for a in range(SPAN):
        tile = jnp.full(shape, NEG, F32)
        for b in range(SPAN):
            row = jnp.full((1, lanes), rel_ref[0, a, b], F32)
            for h in range(1, heads):
                row = jnp.where(head == h, rel_ref[h, a, b], row)
            tile = jnp.where(offset == b, row, tile)
        tile = jnp.where(inside, tile, NEG)
        c_ref[a] = tile
        r_ref[a] = pltpu.roll(tile, half, 1)
    low = iota2(shape, 1) < half
    blank = jnp.full(shape, NEG, F32)
    for g in range(2):
        first, second = (c_ref, r_ref) if g == 0 else (r_ref, c_ref)
        for pair in range(TILE // 2):
            i = 2 * pair
            lo = (g * TILE // 2 + pair) * lanes
            for k in range(TILE + 2 * RAD):
                a = k - i
                one = first[a] if 0 <= a < SPAN else blank
                two = second[a - 1] if 0 <= a - 1 < SPAN else blank
                out_ref[k * cols_pad : (k + 1) * cols_pad, lo : lo + lanes] = jnp.where(
                    low, one, two
                )


def slot_offset(shape, cols):
    slot = iota2(shape, 0)
    pos = jnp.where(slot < cols, slot + RAD, jnp.where(slot < cols + RAD, slot - cols, slot))
    pos = jnp.where(slot < cols + 2 * RAD, pos, -1000)
    return pos - iota2(shape, 1) % cols


def assemble(out_ref, i, rows, cols, cols_pad, own, refs, group):
    w_ref, e_ref, ao_ref, ac_ref, bo_ref, bc_ref = refs
    side = dot(put_cols(rows, SLOTS, 0), w_ref[i, :, group])
    side = (side + dot(put_cols(rows, SLOTS, RAD), e_ref[i, :, group])).astype(BF16)
    for r in range(rows):
        lo = (RAD + r) * cols_pad
        out_ref[lo : lo + cols, :] = own[r * cols : (r + 1) * cols, group]
        out_ref[lo + cols : lo + cols + SLOTS, :] = side[r * SLOTS : (r + 1) * SLOTS]
    put = put_corner(SLOTS)
    for first, o_ref, c_ref in ((0, ao_ref, ac_ref), (RAD + rows, bo_ref, bc_ref)):
        side = dot(put, c_ref[i, :, group]).astype(BF16)
        for r in range(RAD):
            lo = (first + r) * cols_pad
            out_ref[lo : lo + cols, :] = o_ref[i, r * cols : (r + 1) * cols, group]
            out_ref[lo + cols : lo + cols + SLOTS, :] = side[r * SLOTS : (r + 1) * SLOTS]


def group_lanes(group, lanes):
    return pl.ds(pl.multiple_of(group * lanes, lanes), lanes)


def fwd_kernel(
    sizes, n, info_ref, q_ref, k_ref, v_ref, w_ref, e_ref, ao_ref, ac_ref, bo_ref, bc_ref,
    bias_ref, cot_ref, out_ref, weight_ref, p_ref, ko_ref, vo_ref, vt_ref, at_ref,
):
    lat_dev, cols, cols_pad, head_size, rows_all = sizes
    scale = head_size ** (-0.5)
    group = group_lanes(info_ref[n], GROUP * head_size)
    refs = (w_ref, e_ref, ao_ref, ac_ref, bo_ref, bc_ref)
    assemble(ko_ref, 0, lat_dev, cols, cols_pad, k_ref, refs, group)
    assemble(vo_ref, 1, lat_dev, cols, cols_pad, v_ref, refs, group)
    vt_ref[...] = vo_ref[...].T
    mask = head_mask(cols, head_size)
    pick = picker(cols)
    win = (TILE + 2 * RAD) * cols_pad
    for t in range(lat_dev // TILE):
        lo = t * TILE * cols_pad
        qs = pl.ds(t * TILE * cols, TILE * cols)
        q_bd = spread_heads(q_ref[qs, group] * jnp.asarray(scale, BF16), cols, head_size)
        first = info_ref[1] * lat_dev + t * TILE - RAD
        keep = row_keep(first, rows_all, win, q_bd.shape[0], cols_pad)
        st = dot_nt(ko_ref[pl.ds(lo, win), :], q_bd) + bias_ref[:, group]
        st = jnp.where(keep, st, NEG)
        m = jnp.max(st, 0, keepdims=True)
        e = jnp.exp(st - m)
        p = e * (1.0 / jnp.sum(e, 0, keepdims=True))
        p_ref[t] = p
        ot = dot(vt_ref[:, pl.ds(lo, win)], p.astype(BF16))
        ot = jnp.where(mask, ot, 0.0).astype(BF16)
        out_ref[qs, :] = dot_nt(pick, ot).astype(BF16)
    at_ref[...] = out_ref[...].T
    weight_ref[...] = dot(at_ref[...], cot_ref[...]).astype(weight_ref.dtype)


def bwd_kernel(
    sizes, info_ref, q_ref, g_ref, ps_ref, ks_ref, vs_ref, pk_ref, kk_ref, vk_ref,
    dq_ref, top_ref, bot_ref, mid_ref, side_ref, x_ref,
    kt_ref, dk_ref, dv_ref, db_ref,
):
    lat_dev, cols, cols_pad, head_size, rows_all = sizes
    scale = head_size ** (-0.5)
    mask = head_mask(cols, head_size)
    pick = picker(cols)
    win = (TILE + 2 * RAD) * cols_pad
    half = GROUP * cols
    low = iota2((cols_pad, 2 * half), 1) < half
    for step, (p_ref, k_ref, v_ref) in enumerate(
        ((ps_ref, ks_ref, vs_ref), (pk_ref, kk_ref, vk_ref))
    ):
        which = info_ref[0] if step == 0 else 1 - info_ref[0]
        group = group_lanes(which, GROUP * head_size)
        kt_ref[...] = k_ref[...].T
        dk_ref[...] = jnp.zeros_like(dk_ref)
        dv_ref[...] = jnp.zeros_like(dv_ref)
        for t in range(lat_dev // TILE):
            lo = t * TILE * cols_pad
            qs = pl.ds(t * TILE * cols, TILE * cols)
            ws = pl.ds(lo, win)
            q_bd = spread_heads(q_ref[qs, group] * jnp.asarray(scale, BF16), cols, head_size)
            g_bd = spread_heads(g_ref[qs, group], cols, head_size)
            p = p_ref[t]
            slope = dot_nt(v_ref[ws, :], g_bd)
            inner = jnp.sum(p * slope, 0, keepdims=True)
            sg = p * (slope - inner)
            if t == 0:
                db_ref[...] = sg
            else:
                db_ref[...] += sg
            sgb = sg.astype(BF16)
            dqt = jnp.where(mask, dot(kt_ref[:, ws], sgb) * scale, 0.0).astype(BF16)
            dq_ref[qs, group] = dot_nt(pick, dqt).astype(BF16)
            dk_ref[ws, :] += dot(sgb, q_bd)
            dv_ref[ws, :] += dot(p.astype(BF16), g_bd)
        edge = RAD * cols_pad
        for i, ref in enumerate((dk_ref, dv_ref)):
            top_ref[i, :, group] = ref[:edge, :].astype(BF16)
            bot_ref[i, :, group] = ref[edge + lat_dev * cols_pad :, :].astype(BF16)
            for r in range(lat_dev):
                lo = (RAD + r) * cols_pad
                mid_ref[i, r * cols : (r + 1) * cols, group] = ref[lo : lo + cols, :]
                side_ref[i, r * SLOTS : (r + 1) * SLOTS, group] = ref[lo + cols : lo + cols_pad, :]
        for a in range(SPAN):
            total = jnp.zeros((cols_pad, 2 * half), F32)
            for pair in range(TILE // 2):
                i = 2 * pair
                lanes = slice(pair * 2 * half, (pair + 1) * 2 * half)
                one = db_ref[(a + i) * cols_pad : (a + i + 1) * cols_pad, lanes]
                two = db_ref[(a + i + 1) * cols_pad : (a + i + 2) * cols_pad, lanes]
                total = total + jnp.where(low, one, two)
            x_ref[which, a * cols_pad : (a + 1) * cols_pad, :] = total


def bias_kernel(cols, cols_pad, x_ref, out_ref, z_ref):
    lanes = x_ref.shape[2]
    half = lanes // 2
    shape = (cols_pad, lanes)
    low = iota2(shape, 1) < half
    offset = slot_offset(shape, cols)
    z_ref[...] = jnp.zeros_like(z_ref)
    for a in range(SPAN):
        rows = slice(a * cols_pad, (a + 1) * cols_pad)
        one = x_ref[0, rows, :]
        two = x_ref[1, rows, :]
        both = jnp.where(low, one + pltpu.roll(one, half, 1), two + pltpu.roll(two, half, 1))
        for b in range(SPAN):
            n = a * SPAN + b
            z_ref[n : n + 1, :] = jnp.sum(jnp.where(offset == b, both, 0.0), 0, keepdims=True)
    heads = out_ref.shape[0]
    pick = (iota2((heads, lanes), 1) // cols == iota2((heads, lanes), 0)).astype(F32)
    out_ref[...] = lax.dot_general(
        pick, z_ref[...], NT, precision=lax.Precision.HIGHEST, preferred_element_type=F32
    )


def lat_terms(ref, i, rows, cols, cols_pad, first):
    parts = []
    for r in range(RAD):
        lo = r * cols_pad + first
        parts.append(ref[i, lo : lo + cols, :])
    return jnp.concatenate(parts, 0).astype(F32)


def side_kernel(rows, cols, cols_pad, side_ref, a_ref, b_ref, west_ref, east_ref, s_ref):
    edge = RAD * SLOTS
    pick_west = take_cols(rows, SLOTS, 0)
    pick_east = take_cols(rows, SLOTS, RAD)
    for i in range(2):
        s_ref[...] = side_ref[i]
        s_ref[:edge, :] += lat_terms(a_ref, i, rows, SLOTS, cols_pad, cols)
        s_ref[(rows - RAD) * SLOTS :, :] += lat_terms(b_ref, i, rows, SLOTS, cols_pad, cols)
        x = s_ref[...].astype(BF16)
        west_ref[i] = dot(pick_west, x).astype(BF16)
        east_ref[i] = dot(pick_east, x).astype(BF16)


def join_kernel(rows, cols, cols_pad, mid_ref, a_ref, b_ref, w_ref, e_ref, k_ref, v_ref, s_ref):
    edge = RAD * cols
    put_west = put_cols(rows, cols, 0)
    put_east = put_cols(rows, cols, cols - RAD)
    for i, out_ref in enumerate((k_ref, v_ref)):
        s_ref[...] = mid_ref[i] + dot(put_west, w_ref[i]) + dot(put_east, e_ref[i])
        s_ref[:edge, :] += lat_terms(a_ref, i, rows, cols, cols_pad, 0)
        s_ref[(rows - RAD) * cols :, :] += lat_terms(b_ref, i, rows, cols, cols_pad, 0)
        out_ref[...] = s_ref[...].astype(BF16)


def bits_of(mesh_shape):
    order = []
    for axis in ("lat", "lon"):
        bit = 1
        while bit < mesh_shape[axis]:
            order.append((axis, bit))
            bit *= 2
    return order


def rounds_of(mesh_shape):
    first, *rest = bits_of(mesh_shape)
    *middle, last = rest
    turned = middle[1:] + middle[:1]
    return [(first, first)] + list(zip(middle, turned)) + [(last, last)]


def partner_pairs(mesh_shape, bits):
    n_lat, n_lon = mesh_shape["lat"], mesh_shape["lon"]
    pairs = []
    for i in range(n_lat):
        axis, bit = bits[i % 2]
        for j in range(n_lon):
            a, b = (i ^ bit, j) if axis == "lat" else (i, j ^ bit)
            pairs.append((i * n_lon + j, a * n_lon + b))
    return pairs


def swap(x, mesh_shape, bits):
    return lax.ppermute(x, ("lat", "lon"), partner_pairs(mesh_shape, bits))


def my_bit(bits):
    def of(axis, bit):
        return (lax.axis_index(axis) // bit) % 2

    odd = lax.axis_index("lat") % 2
    return jnp.where(odd == 0, of(*bits[0]), of(*bits[1]))


def put_bias(ref, rows, bias):
    heads, count = bias.shape
    high = bias.astype(BF16)
    ref[rows:, :count] = high
    ref[rows:, count : 2 * count] = (bias - high.astype(F32)).astype(BF16)
    ref[rows:, 2 * count :] = jnp.zeros((heads, ref.shape[1] - 2 * count), BF16)


def get_bias(ref, rows, count):
    return ref[rows:, :count].astype(F32) + ref[rows:, count : 2 * count].astype(F32)


def halve_kernel(n, info_ref, keep_ref, got_ref, send_ref, out_ref):
    half = send_ref.shape[0]
    low = keep_ref[:half, :] + got_ref[:half, :].astype(F32)
    high = keep_ref[half:, :] + got_ref[half:, :].astype(F32)
    lower = info_ref[n] == 0
    send_ref[...] = jnp.where(lower, high, low).astype(BF16)
    out_ref[...] = jnp.where(lower, low, high)


def meet_kernel(keep_ref, got_ref, bias_ref, out_ref):
    rows = keep_ref.shape[0]
    out_ref[:rows, :] = (keep_ref[...] + got_ref[...].astype(F32)).astype(BF16)
    put_bias(out_ref, rows, bias_ref[...])


def total_kernel(norm, count, heads, own_ref, got_ref, out_ref):
    rows = own_ref.shape[0] - heads
    total = own_ref[:rows, :].astype(F32) + got_ref[:rows, :].astype(F32)
    out_ref[:rows, :] = (total * norm).astype(BF16)
    put_bias(out_ref, rows, get_bias(own_ref, rows, count) + get_bias(got_ref, rows, count))


def grow_kernel(n, count, heads, info_ref, own_ref, got_ref, out_ref):
    rows = own_ref.shape[0] - heads
    lower = info_ref[n] == 0
    own = own_ref[:rows, :]
    got = got_ref[:rows, :]
    out_ref[:rows, :] = jnp.where(lower, own, got)
    out_ref[rows : 2 * rows, :] = jnp.where(lower, got, own)
    put_bias(out_ref, 2 * rows, get_bias(own_ref, rows, count) + get_bias(got_ref, rows, count))


def last_kernel(n, norm, count, info_ref, own_ref, got_ref, out_ref, bias_ref):
    rows = out_ref.shape[0] // 2
    lower = info_ref[n] == 0
    own = own_ref[:rows, :]
    got = got_ref[:rows, :]
    out_ref[:rows, :] = jnp.where(lower, own, got)
    out_ref[rows:, :] = jnp.where(lower, got, own)
    bias = (get_bias(own_ref, rows, count) + get_bias(got_ref, rows, count)) * norm
    for a in range(SPAN):
        bias_ref[:, a, :] = bias[:, a * SPAN : (a + 1) * SPAN]


def project_kernel(info_ref, s_ref, k_ref, w_ref, out_ref):
    rows = s_ref.shape[1]
    first = pl.ds(pl.multiple_of(info_ref[0] * rows, rows), rows)
    second = pl.ds(pl.multiple_of((1 - info_ref[0]) * rows, rows), rows)
    out = dot(s_ref[...], w_ref[first, :]) + dot(k_ref[...], w_ref[second, :])
    out_ref[...] = out.astype(BF16)


def shards(mesh_shape, queries, keys, values, rel_bias, out_weight, cotangent):
    lat_dev, lon_dev, width = queries.shape
    heads = rel_bias.shape[0]
    head_size = width // heads
    groups = heads // GROUP
    lanes = GROUP * head_size
    model = out_weight.shape[1]
    n_lat, n_lon = mesh_shape["lat"], mesh_shape["lon"]
    cols_pad = lon_dev + SLOTS
    outer_lat = lat_dev + 2 * RAD
    tokens = lat_dev * lon_dev
    norm = (tokens * n_lat * n_lon) ** (-0.5)
    east = [(i, (i + 1) % n_lon) for i in range(n_lon)]
    west = [(i, (i - 1) % n_lon) for i in range(n_lon)]
    down = [(i, i + 1) for i in range(n_lat - 1)]
    up = [(i + 1, i) for i in range(n_lat - 1)]
    win = (TILE + 2 * RAD) * cols_pad
    tiles = lat_dev // TILE
    lanes_q = TILE * GROUP * lon_dev
    n_keys = outer_lat * cols_pad
    n_side = lat_dev * RAD
    n_edge = RAD * lon_dev
    n_strip = RAD * cols_pad

    def shape(dims, dtype=BF16):
        return jax.ShapeDtypeStruct(dims, dtype)

    q_flat = queries.reshape(tokens, width)
    k_flat = keys.reshape(tokens, width)
    v_flat = values.reshape(tokens, width)
    cot = cotangent.reshape(tokens, model)

    lat_index = lax.axis_index("lat").astype(jnp.int32)
    core = lat_index % 2
    rounds = rounds_of(mesh_shape)
    facts = [1 - core, lat_index, core] + [my_bit(bits) for bits in rounds]
    info = jnp.stack([x.astype(jnp.int32) for x in facts])
    smem = pl.BlockSpec(memory_space=pltpu.SMEM)
    vmem = pl.BlockSpec(memory_space=pltpu.VMEM)
    hbm = pl.BlockSpec(memory_space=pltpu.HBM)

    to_east, to_west, to_down, to_up = pl.pallas_call(
        functools.partial(pack_kernel, lat_dev, lon_dev),
        in_specs=[hbm, hbm],
        out_shape=[shape((2, n_side, width))] * 2 + [shape((2, n_edge, width))] * 2,
        scratch_shapes=[pltpu.VMEM((2, tokens, width), BF16), pltpu.SemaphoreType.DMA((2,))],
        compiler_params=room(4),
        name="pack",
    )(k_flat, v_flat)
    from_west = lax.ppermute(to_east, "lon", east)
    from_east = lax.ppermute(to_west, "lon", west)
    above_own = lax.ppermute(to_down, "lat", down)
    below_own = lax.ppermute(to_up, "lat", up)
    sizes = (lat_dev, lon_dev, cols_pad, head_size, lat_dev * n_lat)
    table, attended_grad = pl.pallas_call(
        functools.partial(prepare_kernel, lon_dev, cols_pad),
        in_specs=[smem, vmem, vmem],
        out_shape=[shape((win, groups * lanes_q), F32), shape((tokens, width))],
        scratch_shapes=[pltpu.VMEM((SPAN, cols_pad, heads * lon_dev), F32)] * 2,
        compiler_params=room(6),
        name="prepare",
    )(rel_bias, cot, out_weight)
    from_west, from_east, table = lax.optimization_barrier((from_west, from_east, table))
    corner_down, corner_up = pl.pallas_call(
        functools.partial(corner_kernel, lat_dev),
        out_shape=[shape((2, CORNER, width))] * 2,
        compiler_params=room(4),
        name="corner",
    )(from_west, from_east)
    above_corner = lax.ppermute(corner_down, "lat", down)
    below_corner = lax.ppermute(corner_up, "lat", up)

    probs = (tiles, win, lanes_q)
    outer = (n_keys, lanes)

    def forward(n, dtype):
        return pl.pallas_call(
            functools.partial(fwd_kernel, sizes, n),
            in_specs=[smem] + [vmem] * 11,
            out_shape=[shape((tokens, lanes)), shape((lanes, model), dtype), shape(probs, F32)]
            + [shape(outer)] * 2,
            scratch_shapes=[pltpu.VMEM((lanes, n_keys), BF16), pltpu.VMEM((lanes, tokens), BF16)],
            compiler_params=room(8),
            name="attend_fwd",
        )(
            info, q_flat, k_flat, v_flat, from_west, from_east,
            above_own, above_corner, below_own, below_corner, table, cot,
        )

    def step_call(kernel, name, outs, *operands):
        scalars = [smem if x.dtype == jnp.int32 else vmem for x in operands]
        return pl.pallas_call(
            kernel, in_specs=scalars, out_shape=outs, compiler_params=room(4), name=name
        )(*operands)

    att_s, weight_s, p_s, k_s, v_s = forward(0, BF16)
    got = swap(weight_s, mesh_shape, rounds[0])
    att_k, keep, p_k, k_k, v_k = forward(2, F32)

    def halve(keep, got, number):
        half = (keep.shape[0] // 2, model)
        outs = [shape(half), shape(half, F32)]
        kernel = functools.partial(halve_kernel, 3 + number)
        return step_call(kernel, "halve", outs, info, keep, got)

    send, keep = halve(keep, got, 1)
    info_b, send = lax.optimization_barrier((info, send))
    got = swap(send, mesh_shape, rounds[1])

    query_grad, top, bottom, mid, side, folded = pl.pallas_call(
        functools.partial(bwd_kernel, sizes),
        in_specs=[smem] + [vmem] * 8,
        out_shape=[shape((tokens, width))]
        + [shape((2, n_strip, width))] * 2
        + [shape((2, tokens, width), F32)] * 2
        + [shape((groups, SPAN * cols_pad, 2 * GROUP * lon_dev), F32)],
        scratch_shapes=[pltpu.VMEM((lanes, n_keys), BF16)]
        + [pltpu.VMEM((n_keys, lanes), F32)] * 2
        + [pltpu.VMEM((win, lanes_q), F32)],
        compiler_params=room(10),
        name="attend_bwd",
    )(info_b, q_flat, attended_grad, p_s, k_s, v_s, p_k, k_k, v_k)

    get_below = lax.ppermute(top, "lat", up)
    get_above = lax.ppermute(bottom, "lat", down)
    for number in range(2, len(rounds) - 1):
        send, keep = halve(keep, got, number)
        if number == 3:
            send, get_below, get_above = lax.optimization_barrier((send, get_below, get_above))
        got = swap(send, mesh_shape, rounds[number])

    give_west, give_east = pl.pallas_call(
        functools.partial(side_kernel, lat_dev, lon_dev, cols_pad),
        out_shape=[shape((2, n_side, width))] * 2,
        scratch_shapes=[pltpu.VMEM((tokens, width), F32)],
        compiler_params=room(6),
        name="side",
    )(side, get_above, get_below)
    get_east = lax.ppermute(give_west, "lon", west)
    get_west = lax.ppermute(give_east, "lon", east)

    count = 256
    bias_local = pl.pallas_call(
        functools.partial(bias_kernel, lon_dev, cols_pad),
        out_shape=shape((heads, count), F32),
        scratch_shapes=[pltpu.VMEM((count, heads * lon_dev), F32)],
        compiler_params=room(4),
        name="bias_fold",
    )(folded)
    note = shape((keep.shape[0] + heads, model))
    message = step_call(meet_kernel, "meet", note, keep, got, bias_local)
    got = swap(message, mesh_shape, rounds[-1])
    kernel = functools.partial(total_kernel, norm, count, heads)
    message = step_call(kernel, "total", note, message, got)
    for number in range(len(rounds) - 2, 0, -1):
        if number == 2:
            message, get_east, get_west = lax.optimization_barrier((message, get_east, get_west))
        got = swap(message, mesh_shape, rounds[number])
        note = shape((2 * message.shape[0] - heads, model))
        kernel = functools.partial(grow_kernel, 3 + number, count, heads)
        message = step_call(kernel, "grow", note, info, message, got)

    key_grad, value_grad = pl.pallas_call(
        functools.partial(join_kernel, lat_dev, lon_dev, cols_pad),
        out_shape=[shape((tokens, width))] * 2,
        scratch_shapes=[pltpu.VMEM((tokens, width), F32)],
        compiler_params=room(6),
        name="join",
    )(mid, get_above, get_below, get_west, get_east)
    block_out = pl.pallas_call(
        project_kernel,
        in_specs=[smem] + [vmem] * 3,
        out_shape=shape((tokens, model)),
        compiler_params=room(6),
        name="project",
    )(info, att_s, att_k, out_weight)

    got = swap(message, mesh_shape, rounds[0])
    weight_grad, bias_grad = step_call(
        functools.partial(last_kernel, 3, norm, count),
        "last",
        [shape((width, model)), shape(rel_bias.shape, F32)],
        info, message, got,
    )
    return (
        block_out.reshape(lat_dev, lon_dev, model),
        query_grad.reshape(queries.shape),
        key_grad.reshape(keys.shape),
        value_grad.reshape(values.shape),
        weight_grad,
        bias_grad,
    )


def solution(mesh):
    spec = P("lat", "lon", None)
    return jax.shard_map(
        functools.partial(shards, dict(mesh.shape)),
        mesh=mesh,
        in_specs=(spec, spec, spec, P(), P(), spec),
        out_specs=(spec, spec, spec, spec, P(), P()),
        check_vma=False,
    )
```

time: 129 us -> 97.9 us (0.76)
  local copies, waits for them, and re-layouts: 23.3 us -> 5.8 us
  starting transfers between devices: 40.8 us -> 35.1 us
  Pallas kernels: 33.1 us -> 27.6 us
  other arithmetic: 3.64 us -> 0 us
  waiting for transfers between devices: 24.4 us -> 27.4 us
  matrix products: 1.71 us -> 0 us
    unnamed x96 -> x24, local copies, waits for them, and re-layouts: 20.9 us -> 5.71 us
    ppermute x1, starting transfers between devices: 8.45 us -> 3.97 us  [shards(): get_above = lax.ppermute(bottom, 'lat', down)]
    ppermute x9, waiting for transfers between devices: 16.4 us -> 20.8 us  [swap(): return lax.ppermute(x, ('lat', 'lon'), partner_pairs(mesh_shape, bits))]
    ppermute x1, waiting for transfers between devices: 0.01 us -> 4.3 us  [shards(): below_corner = lax.ppermute(corner_up, 'lat', up)]
    ppermute x1, starting transfers between devices: 4.16 us -> 1.61 us  [shards(): get_east = lax.ppermute(give_west, 'lon', west)]
    ppermute x9, starting transfers between devices: 8.16 us -> 10.7 us  [swap(): return lax.ppermute(x, ('lat', 'lon'), partner_pairs(mesh_shape, bits))]
    add x3 -> x0, other arithmetic: 2.3 us -> none  [reduce_all(): part = keep + swap(send, axis, bit, n).astype(F32)]
    ppermute x1, waiting for transfers between devices: 4.12 us -> 1.88 us  [shards(): get_below = lax.ppermute(top, 'lat', up)]
  transfers between devices with their start and end apart: 19 -> 19, of which waited for: 10 -> 9; matrix products, arithmetic and copies ran while one was open for 4% -> 1% of each run, Pallas kernels for 19% -> 20%
where the time goes in v3:
time: 97.9 us; the launch traced here: 97 us
  starting transfers between devices  35.1 us (36%)
  Pallas kernels  27.6 us (28%)
  waiting for transfers between devices  27.4 us (28%)
  local copies, waits for them, and re-layouts  5.8 us (6%)
  between operations  1.03 us (1%)
    ppermute x9, waiting for transfers between devices, swap(): return lax.ppermute(x, ('lat', 'lon'), partner_pairs(mesh_shape, bits))  20.8 us
    ppermute x9, starting transfers between devices, swap(): return lax.ppermute(x, ('lat', 'lon'), partner_pairs(mesh_shape, bits))  10.7 us
    pallas_call x2, Pallas kernels, forward(): pl.pallas_call(functools.partial(fwd_kernel, sizes, n), in_specs=[smem] +...  7.24 us
    pallas_call x1, Pallas kernels, shards(): pl.pallas_call(functools.partial(bwd_kernel, sizes), in_specs=[smem] + [v...  6.36 us
    unnamed x24, local copies, waits for them, and re-layouts  5.71 us
    pallas_call x9, Pallas kernels, step_call(): pl.pallas_call(kernel, in_specs=scalars, out_shape=outs, compiler_params=...  5.4 us
    ppermute x1, waiting for transfers between devices, shards(): below_corner = lax.ppermute(corner_up, 'lat', up)  4.3 us
    ppermute x1, starting transfers between devices, shards(): above_own = lax.ppermute(to_down, 'lat', down)  4.11 us
  transfers between devices with their start and end apart: 19, of which 9 were waited for; matrix products, arithmetic and copies ran while one was open for 1% of the time, Pallas kernels for 20%

profile of v3, /device:TPU:1, one launch (start us, length us, event | category | flops | bytes accessed | tf_op | source)
XLA Modules:
  0.0 97.0 jit_solution(3899344804959643513)
XLA Ops:
  0.7 1.0 %copy-done.4 = bf16[16,16,512]{2,1,0:T(8,128)(2,1)S(1)} copy-done((bf16[16,16,512]{2,1,0:T(8,128)(2,1)S(1)}, bf16[16,16,512]{2,1,0:T(8,128)(2,1)}, u32[]{:S(2)}) %copy-start.4) | copy-done | bytes 262168
  1.7 0.9 copy-done.6
  2.6 1.1 %pack.1 = (bf16[2,96,512]{2,1,0:T(8,128)(2,1)S(1)}, bf16[2,96,512]{2,1,0:T(8,128)(2,1)S(1)}, bf16[2,96,512]{2,1,0:T(8,128)(2,1)}, bf16[2,96,512]{2,1,0:T(8,128)(2,1)}) custom-call(bf16[256,512]{1,0:T(8,128)(2,1)S(1)} %bitcast.18, bf16[256,512]{1,0:T(8,128)(2,1)S(1)} %bitcast.21), custom_call_target="tpu_custom_call" | custom-call | tf_op jit(solution)/shard_map/pack/pallas_call | solution.py:480
  3.7 2.1 %collective-permute-start = (bf16[2,96,512]{2,1,0:T(8,128)(2,1)S(1)}, bf16[2,96,512]{2,1,0:T(8,128)(2,1)S(1)}, u32[]{:S(2)}, u32[]{:S(2)}) collective-permute-start(bf16[2,96,512]{2,1,0:T(8,128)(2,1)S(1)} %get-tuple-element.53), channel_id=1, source_target_pairs={{0,1},{1,2},{2,3},{3,4},{4,5},{5,6},{6,7},{7,0},{8,9},{9,10},{10,1... | collective-permute-start | bytes 589832 | tf_op jit(solution)/shard_map/ppermute | solution.py:488
  5.8 3.1 %collective-permute-start.1 = (bf16[2,96,512]{2,1,0:T(8,128)(2,1)S(1)}, bf16[2,96,512]{2,1,0:T(8,128)(2,1)S(1)}, u32[]{:S(2)}, u32[]{:S(2)}) collective-permute-start(bf16[2,96,512]{2,1,0:T(8,128)(2,1)S(1)} %get-tuple-element.54), channel_id=1, source_target_pairs={{0,7},{1,0},{2,1},{3,2},{4,3},{5,4},{6,5},{7,6},{8,15},{9,8},{10,9... | collective-permute-start | bytes 589832 | tf_op jit(solution)/shard_map/ppermute | solution.py:489
  8.9 4.1 %collective-permute-start.2 = (bf16[2,96,512]{2,1,0:T(8,128)(2,1)}, bf16[2,96,512]{2,1,0:T(8,128)(2,1)S(1)}, u32[]{:S(2)}, u32[]{:S(2)}) collective-permute-start(bf16[2,96,512]{2,1,0:T(8,128)(2,1)} %get-tuple-element.58), channel_id=1, source_target_pairs={{0,8},{8,16},{16,24},{1,9},{9,17},{17,25},{2,10},{10,18},{18,26},{... | collective-permute-start | bytes 589832 | tf_op jit(solution)/shard_map/ppermute | solution.py:490
  13.0 1.9 %collective-permute-start.4 = (bf16[2,96,512]{2,1,0:T(8,128)(2,1)}, bf16[2,96,512]{2,1,0:T(8,128)(2,1)S(1)}, u32[]{:S(2)}, u32[]{:S(2)}) collective-permute-start(bf16[2,96,512]{2,1,0:T(8,128)(2,1)} %get-tuple-element.60), channel_id=1, source_target_pairs={{8,0},{16,8},{24,16},{9,1},{17,9},{25,17},{10,2},{18,10},{26,18},{... | collective-permute-start | bytes 589832 | tf_op jit(solution)/shard_map/ppermute | solution.py:491
  14.9 0.8 copy.12.rel_ref
  15.8 1.0 %copy-done = bf16[16,16,1024]{2,1,0:T(8,128)(2,1)S(1)} copy-done((bf16[16,16,1024]{2,1,0:T(8,128)(2,1)S(1)}, bf16[16,16,1024]{2,1,0:T(8,128)(2,1)}, u32[]{:S(2)}) %copy-start) | copy-done | bytes 524312
  16.8 1.2 %copy-done.2 = bf16[512,1024]{1,0:T(8,128)(2,1)S(1)} copy-done((bf16[512,1024]{1,0:T(8,128)(2,1)S(1)}, bf16[512,1024]{1,0:T(8,128)(2,1)}, u32[]{:S(2)}) %copy-start.2) | copy-done | bytes 1048600
  18.0 2.6 %prepare.1 = (f32[512,512]{1,0:T(8,128)S(1)}, bf16[256,512]{1,0:T(8,128)(2,1)S(1)}) custom-call(f32[8,13,13]{2,1,0:T(8,128)S(1)} %copy.12.rel_ref, bf16[256,1024]{1,0:T(8,128)(2,1)S(1)} %bitcast.15, bf16[512,1024]{1,0:T(8,128)(2,1)S(1)} %copy-done.2), custom_call_target="tpu_custom_call" | custom-call | tf_op jit(solution)/shard_map/prepare/pallas_call | solution.py:493
  20.7 1.0 %corner.1 = (bf16[2,80,512]{2,1,0:T(8,128)(2,1)}, bf16[2,80,512]{2,1,0:T(8,128)(2,1)}) custom-call(bf16[2,96,512]{2,1,0:T(8,128)(2,1)S(1)} %collective-permute-done.w_ref, bf16[2,96,512]{2,1,0:T(8,128)(2,1)S(1)} %collective-permute-done.1.e_ref), custom_call_target="tpu_custom_call" | custom-call | tf_op jit(solution)/shard_map/corner/pallas_call | solution.py:502
  21.7 3.6 %collective-permute-start.3 = (bf16[2,80,512]{2,1,0:T(8,128)(2,1)}, bf16[2,80,512]{2,1,0:T(8,128)(2,1)S(1)}, u32[]{:S(2)}, u32[]{:S(2)}) collective-permute-start(bf16[2,80,512]{2,1,0:T(8,128)(2,1)} %get-tuple-element.59), channel_id=1, source_target_pairs={{0,8},{8,16},{16,24},{1,9},{9,17},{17,25},{2,10},{10,18},{18,26},{... | collective-permute-start | bytes 491528 | tf_op jit(solution)/shard_map/ppermute | solution.py:508
  25.3 1.9 %collective-permute-start.5 = (bf16[2,80,512]{2,1,0:T(8,128)(2,1)}, bf16[2,80,512]{2,1,0:T(8,128)(2,1)S(1)}, u32[]{:S(2)}, u32[]{:S(2)}) collective-permute-start(bf16[2,80,512]{2,1,0:T(8,128)(2,1)} %get-tuple-element.61), channel_id=1, source_target_pairs={{8,0},{16,8},{24,16},{9,1},{17,9},{25,17},{10,2},{18,10},{26,18},{... | collective-permute-start | bytes 491528 | tf_op jit(solution)/shard_map/ppermute | solution.py:509
  27.3 0.1 stack.32.info_ref
  27.4 0.4 collective-permute-done.3.ac_ref
  27.9 4.3 %collective-permute-done.5.bc_ref = bf16[2,80,512]{2,1,0:T(8,128)(2,1)S(1)} collective-permute-done((bf16[2,80,512]{2,1,0:T(8,128)(2,1)}, bf16[2,80,512]{2,1,0:T(8,128)(2,1)S(1)}, u32[]{:S(2)}, u32[]{:S(2)}) %collective-permute-start.5) | collective-permute-done | bytes 163872 | tf_op jit(solution)/shard_map/ppermute | solution.py:509
  32.2 3.6 %attend_fwd.2 = (bf16[256,256]{1,0:T(8,128)(2,1)S(1)}, bf16[256,1024]{1,0:T(8,128)(2,1)S(1)}, f32[4,512,256]{2,1,0:T(8,128)S(1)}, bf16[896,256]{1,0:T(8,128)(2,1)S(1)}, bf16[896,256]{1,0:T(8,128)(2,1)S(1)}) custom-call(s32[8]{0:T(128)S(1)} %stack.32.info_ref, bf16[256,512]{1,0:T(8,128)(2,1)S(1)} %bitcast.24, bf16[256,512]{1,0:T(8,128)(2,1)S(1)} %bitcast.19, ...), custom_call_target="tpu_custom_call" | custom-call | tf_op jit(solution)/shard_map/attend_fwd/pallas_call | solution.py:515
  35.8 0.1 collective-permute-start.6
  35.9 3.6 %attend_fwd.3 = (bf16[256,256]{1,0:T(8,128)(2,1)S(1)}, f32[256,1024]{1,0:T(8,128)S(1)}, f32[4,512,256]{2,1,0:T(8,128)S(1)}, bf16[896,256]{1,0:T(8,128)(2,1)S(1)}, bf16[896,256]{1,0:T(8,128)(2,1)S(1)}) custom-call(s32[8]{0:T(128)S(1)} %stack.32.info_ref, bf16[256,512]{1,0:T(8,128)(2,1)S(1)} %bitcast.25, bf16[256,512]{1,0:T(8,128)(2,1)S(1)} %bitcast.20, ...), custom_call_target="tpu_custom_call" | custom-call | tf_op jit(solution)/shard_map/attend_fwd/pallas_call | solution.py:515
  39.5 0.7 halve.3
  40.3 6.4 %attend_bwd.1 = (bf16[256,512]{1,0:T(8,128)(2,1)}, bf16[2,192,512]{2,1,0:T(8,128)(2,1)S(1)}, bf16[2,192,512]{2,1,0:T(8,128)(2,1)S(1)}, f32[2,256,512]{2,1,0:T(8,...) custom-call(s32[8]{0:T(128)S(1)} %stack.32.info_ref, bf16[256,512]{1,0:T(8,128)(2,1)S(1)} %bitcast.26, ...), custom_call_target="tpu_custom_call" | custom-call | tf_op jit(solution)/shard_map/attend_bwd/pallas_call | solution.py:548
  46.7 4.0 %collective-permute-start.10 = (bf16[2,192,512]{2,1,0:T(8,128)(2,1)S(1)}, bf16[2,192,512]{2,1,0:T(8,128)(2,1)S(1)}, u32[]{:S(2)}, u32[]{:S(2)}) collective-permute-start(bf16[2,192,512]{2,1,0:T(8,128)(2,1)S(1)} %get-tuple-element.84), channel_id=1, source_target_pairs={{0,8},{8,16},{16,24},{1,9},{9,17},{17,25},{2,10},{10,18},{18,26},{... | collective-permute-start | bytes 1179656 | tf_op jit(solution)/shard_map/ppermute | solution.py:563
  50.7 2.1 %collective-permute-start.9 = (bf16[2,192,512]{2,1,0:T(8,128)(2,1)S(1)}, bf16[2,192,512]{2,1,0:T(8,128)(2,1)S(1)}, u32[]{:S(2)}, u32[]{:S(2)}) collective-permute-start(bf16[2,192,512]{2,1,0:T(8,128)(2,1)S(1)} %get-tuple-element.83), channel_id=1, source_target_pairs={{8,0},{16,8},{24,16},{9,1},{17,9},{25,17},{10,2},{18,10},{26,18},{... | collective-permute-start | bytes 1179656 | tf_op jit(solution)/shard_map/ppermute | solution.py:562
  52.8 0.6 halve.4
  53.4 0.1 collective-permute-start.8
  53.5 3.8 %collective-permute-done.8.got_ref = bf16[64,1024]{1,0:T(8,128)(2,1)S(1)} collective-permute-done((bf16[64,1024]{1,0:T(8,128)(2,1)S(1)}, bf16[64,1024]{1,0:T(8,128)(2,1)S(1)}, u32[]{:S(2)}, u32[]{:S(2)}) %collective-permute-start.8) | collective-permute-done | bytes 131104 | tf_op jit(solution)/shard_map/ppermute | solution.py:364
  57.3 0.6 halve.5
  57.9 1.9 %collective-permute-done.9.b_ref = bf16[2,192,512]{2,1,0:T(8,128)(2,1)S(1)} collective-permute-done((bf16[2,192,512]{2,1,0:T(8,128)(2,1)S(1)}, bf16[2,192,512]{2,1,0:T(8,128)(2,1)S(1)}, u32[]{:S(2)}, u32[]{:S(2)}) %collective-permute-start.9) | collective-permute-done | bytes 393248 | tf_op jit(solution)/shard_map/ppermute | solution.py:562
  59.8 0.3 side.1
  60.1 1.6 %collective-permute-start.14 = (bf16[2,96,512]{2,1,0:T(8,128)(2,1)S(1)}, bf16[2,96,512]{2,1,0:T(8,128)(2,1)S(1)}, u32[]{:S(2)}, u32[]{:S(2)}) collective-permute-start(bf16[2,96,512]{2,1,0:T(8,128)(2,1)S(1)} %get-tuple-element.91), channel_id=1, source_target_pairs={{0,7},{1,0},{2,1},{3,2},{4,3},{5,4},{6,5},{7,6},{8,15},{9,8},{10,9... | collective-permute-start | bytes 589832 | tf_op jit(solution)/shard_map/ppermute | solution.py:577
  61.7 0.7 bias_fold.1.bias_ref
  62.4 0.5 collective-permute-done.11.got_ref
  62.9 0.9 collective-permute-start.12
  63.8 6.1 %collective-permute-done.12.got_ref = bf16[40,1024]{1,0:T(8,128)(2,1)S(1)} collective-permute-done((bf16[40,1024]{1,0:T(8,128)(2,1)S(1)}, bf16[40,1024]{1,0:T(8,128)(2,1)S(1)}, u32[]{:S(2)}, u32[]{:S(2)}) %collective-permute-start.12) | collective-permute-done | bytes 81952 | tf_op jit(solution)/shard_map/ppermute | solution.py:364
  70.0 3.6 %collective-permute-done.13.got_ref = bf16[40,1024]{1,0:T(8,128)(2,1)S(1)} collective-permute-done((bf16[40,1024]{1,0:T(8,128)(2,1)S(1)}, bf16[40,1024]{1,0:T(8,128)(2,1)S(1)}, u32[]{:S(2)}, u32[]{:S(2)}) %collective-permute-start.13) | collective-permute-done | bytes 81952 | tf_op jit(solution)/shard_map/ppermute | solution.py:364
  73.6 0.6 grow.3.own_ref
  74.2 1.2 %collective-permute-start.16 = (bf16[72,1024]{1,0:T(8,128)(2,1)S(1)}, bf16[72,1024]{1,0:T(8,128)(2,1)S(1)}, u32[]{:S(2)}, u32[]{:S(2)}) collective-permute-start(bf16[72,1024]{1,0:T(8,128)(2,1)S(1)} %grow.3.own_ref), channel_id=1, source_target_pairs={{0,1},{1,0},{2,3},{3,2},{4,5},{5,4},{6,7},{7,6},{8,10},{9,11},{10,... | collective-permute-start | bytes 442376 | tf_op jit(solution)/shard_map/ppermute | solution.py:364
  75.4 2.8 %collective-permute-done.16.got_ref = bf16[72,1024]{1,0:T(8,128)(2,1)S(1)} collective-permute-done((bf16[72,1024]{1,0:T(8,128)(2,1)S(1)}, bf16[72,1024]{1,0:T(8,128)(2,1)S(1)}, u32[]{:S(2)}, u32[]{:S(2)}) %collective-permute-start.16) | collective-permute-done | bytes 147488 | tf_op jit(solution)/shard_map/ppermute | solution.py:364
  78.2 0.6 grow.4.own_ref
  78.8 3.5 %collective-permute-start.17 = (bf16[136,1024]{1,0:T(8,128)(2,1)S(1)}, bf16[136,1024]{1,0:T(8,128)(2,1)S(1)}, u32[]{:S(2)}, u32[]{:S(2)}) collective-permute-start(bf16[136,1024]{1,0:T(8,128)(2,1)S(1)} %grow.4.own_ref), channel_id=1, source_target_pairs={{0,16},{1,17},{2,18},{3,19},{4,20},{5,21},{6,22},{7,23},{8,9},{9,8... | collective-permute-start | bytes 835592 | tf_op jit(solution)/shard_map/ppermute | solution.py:364
  82.3 3.9 %collective-permute-done.17.got_ref = bf16[136,1024]{1,0:T(8,128)(2,1)S(1)} collective-permute-done((bf16[136,1024]{1,0:T(8,128)(2,1)S(1)}, bf16[136,1024]{1,0:T(8,128)(2,1)S(1)}, u32[]{:S(2)}, u32[]{:S(2)}) %collective-permute-start.17) | collective-permute-done | bytes 278560 | tf_op jit(solution)/shard_map/ppermute | solution.py:364
  86.2 0.6 grow.5.own_ref
  86.8 4.9 %collective-permute-start.18 = (bf16[264,1024]{1,0:T(8,128)(2,1)S(1)}, bf16[264,1024]{1,0:T(8,128)(2,1)S(1)}, u32[]{:S(2)}, u32[]{:S(2)}) collective-permute-start(bf16[264,1024]{1,0:T(8,128)(2,1)S(1)} %grow.5.own_ref), channel_id=1, source_target_pairs={{0,8},{1,9},{2,10},{3,11},{4,12},{5,13},{6,14},{7,15},{8,0},{9,1},... | collective-permute-start | bytes 1622024 | tf_op jit(solution)/shard_map/ppermute | solution.py:364
  91.7 1.8 %project.1 = bf16[256,1024]{1,0:T(8,128)(2,1)} custom-call(s32[8]{0:T(128)S(1)} %stack.32.info_ref, bf16[256,256]{1,0:T(8,128)(2,1)S(1)} %get-tuple-element.63.s_ref, bf16[256,256]{1,0:T(8,128)(2,1)S(1)} %get-tuple-element.64.k_ref, bf16[512,1024]{1,0:T(8,128)(2,1)S(1)} %copy-done.3), custom_call_target="tpu_custom_call" | custom-call | tf_op jit(solution)/shard_map/project/pallas_call | solution.py:608
  93.4 1.1 %join.1 = (bf16[256,512]{1,0:T(8,128)(2,1)}, bf16[256,512]{1,0:T(8,128)(2,1)}) custom-call(f32[2,256,512]{2,1,0:T(8,128)S(1)} %get-tuple-element.77.mid_ref, bf16[2,192,512]{2,1,0:T(8,128)(2,1)S(1)} %collective-permute-done.10.a_ref, bf16[2,192,512]{2,1,0:T(8,128)(2,1)S(1)} %collective-permute-done.9.b_ref, ...), custom_call_target="tpu_custom_call" | custom-call | tf_op jit(solution)/shard_map/join/pallas_call | solution.py:601
  94.6 1.8 %last.1 = (bf16[512,1024]{1,0:T(8,128)(2,1)}, f32[8,13,13]{2,1,0:T(8,128)S(1)}) custom-call(s32[8]{0:T(128)S(1)} %stack.32.info_ref, bf16[264,1024]{1,0:T(8,128)(2,1)S(1)} %grow.5.own_ref, bf16[264,1024]{1,0:T(8,128)(2,1)S(1)} %collective-permute-done.18.got_ref), custom_call_target="tpu_custom_call" | custom-call | tf_op jit(solution)/shard_map/last/pallas_call | solution.py:530
  96.3 0.6 copy.13
  (34 shorter events, 0.3 us)
Async XLA Ops:
  0.6 31.5 %copy-start.1 = (bf16[16,16,1024]{2,1,0:T(8,128)(2,1)S(1)}, bf16[16,16,1024]{2,1,0:T(8,128)(2,1)}, u32[]{:S(2)}) copy-start(bf16[16,16,1024]{2,1,0:T(8,128)(2,1)} %param.11) | copy-start | bytes 1572868
  0.6 1.0 %copy-start.4 = (bf16[16,16,512]{2,1,0:T(8,128)(2,1)S(1)}, bf16[16,16,512]{2,1,0:T(8,128)(2,1)}, u32[]{:S(2)}) copy-start(bf16[16,16,512]{2,1,0:T(8,128)(2,1)} %param.7) | copy-start | bytes 786436
  1.7 0.9 copy-start.6
  3.7 17.0 %collective-permute-start = (bf16[2,96,512]{2,1,0:T(8,128)(2,1)S(1)}, bf16[2,96,512]{2,1,0:T(8,128)(2,1)S(1)}, u32[]{:S(2)}, u32[]{:S(2)}) collective-permute-start(bf16[2,96,512]{2,1,0:T(8,128)(2,1)S(1)} %get-tuple-element.53), channel_id=1, source_target_pairs={{0,1},{1,2},{2,3},{3,4},{4,5},{5,6},{6,7},{7,0},{8,9},{9,10},{10,1... | collective-permute-start | bytes 589832 | tf_op jit(solution)/shard_map/ppermute | solution.py:488
  5.8 14.9 %collective-permute-start.1 = (bf16[2,96,512]{2,1,0:T(8,128)(2,1)S(1)}, bf16[2,96,512]{2,1,0:T(8,128)(2,1)S(1)}, u32[]{:S(2)}, u32[]{:S(2)}) collective-permute-start(bf16[2,96,512]{2,1,0:T(8,128)(2,1)S(1)} %get-tuple-element.54), channel_id=1, source_target_pairs={{0,7},{1,0},{2,1},{3,2},{4,3},{5,4},{6,5},{7,6},{8,15},{9,8},{10,9... | collective-permute-start | bytes 589832 | tf_op jit(solution)/shard_map/ppermute | solution.py:489
  8.9 18.6 %collective-permute-start.2 = (bf16[2,96,512]{2,1,0:T(8,128)(2,1)}, bf16[2,96,512]{2,1,0:T(8,128)(2,1)S(1)}, u32[]{:S(2)}, u32[]{:S(2)}) collective-permute-start(bf16[2,96,512]{2,1,0:T(8,128)(2,1)} %get-tuple-element.58), channel_id=1, source_target_pairs={{0,8},{8,16},{16,24},{1,9},{9,17},{17,25},{2,10},{10,18},{18,26},{... | collective-permute-start | bytes 589832 | tf_op jit(solution)/shard_map/ppermute | solution.py:490
  13.0 14.4 %collective-permute-start.4 = (bf16[2,96,512]{2,1,0:T(8,128)(2,1)}, bf16[2,96,512]{2,1,0:T(8,128)(2,1)S(1)}, u32[]{:S(2)}, u32[]{:S(2)}) collective-permute-start(bf16[2,96,512]{2,1,0:T(8,128)(2,1)} %get-tuple-element.60), channel_id=1, source_target_pairs={{8,0},{16,8},{24,16},{9,1},{17,9},{25,17},{10,2},{18,10},{26,18},{... | collective-permute-start | bytes 589832 | tf_op jit(solution)/shard_map/ppermute | solution.py:491
  15.7 1.0 %copy-start = (bf16[16,16,1024]{2,1,0:T(8,128)(2,1)S(1)}, bf16[16,16,1024]{2,1,0:T(8,128)(2,1)}, u32[]{:S(2)}) copy-start(bf16[16,16,1024]{2,1,0:T(8,128)(2,1)} %param.11) | copy-start | bytes 1572868
  16.8 1.2 %copy-start.2 = (bf16[512,1024]{1,0:T(8,128)(2,1)S(1)}, bf16[512,1024]{1,0:T(8,128)(2,1)}, u32[]{:S(2)}) copy-start(bf16[512,1024]{1,0:T(8,128)(2,1)} %w_ref.3) | copy-start | bytes 3145732
  18.0 14.2 %copy-start.5 = (bf16[16,16,512]{2,1,0:T(8,128)(2,1)S(1)}, bf16[16,16,512]{2,1,0:T(8,128)(2,1)}, u32[]{:S(2)}) copy-start(bf16[16,16,512]{2,1,0:T(8,128)(2,1)} %param.7) | copy-start | bytes 786436
  18.0 14.2 %copy-start.7 = (bf16[16,16,512]{2,1,0:T(8,128)(2,1)S(1)}, bf16[16,16,512]{2,1,0:T(8,128)(2,1)}, u32[]{:S(2)}) copy-start(bf16[16,16,512]{2,1,0:T(8,128)(2,1)} %param.8) | copy-start | bytes 786436
  18.0 14.2 %copy-start.8 = (bf16[16,16,512]{2,1,0:T(8,128)(2,1)S(1)}, bf16[16,16,512]{2,1,0:T(8,128)(2,1)}, u32[]{:S(2)}) copy-start(bf16[16,16,512]{2,1,0:T(8,128)(2,1)} %param.6) | copy-start | bytes 786436
  20.7 4.7 %copy-start.9 = (bf16[256,512]{1,0:T(8,128)(2,1)}, bf16[256,512]{1,0:T(8,128)(2,1)S(1)}, u32[]{:S(2)}) copy-start(bf16[256,512]{1,0:T(8,128)(2,1)S(1)} %get-tuple-element.69.g_ref) | copy-start | bytes 786436
  21.7 6.2 %collective-permute-start.3 = (bf16[2,80,512]{2,1,0:T(8,128)(2,1)}, bf16[2,80,512]{2,1,0:T(8,128)(2,1)S(1)}, u32[]{:S(2)}, u32[]{:S(2)}) collective-permute-start(bf16[2,80,512]{2,1,0:T(8,128)(2,1)} %get-tuple-element.59), channel_id=1, source_target_pairs={{0,8},{8,16},{16,24},{1,9},{9,17},{17,25},{2,10},{10,18},{18,26},{... | collective-permute-start | bytes 491528 | tf_op jit(solution)/shard_map/ppermute | solution.py:508
  25.3 6.8 %collective-permute-start.5 = (bf16[2,80,512]{2,1,0:T(8,128)(2,1)}, bf16[2,80,512]{2,1,0:T(8,128)(2,1)S(1)}, u32[]{:S(2)}, u32[]{:S(2)}) collective-permute-start(bf16[2,80,512]{2,1,0:T(8,128)(2,1)} %get-tuple-element.61), channel_id=1, source_target_pairs={{8,0},{16,8},{24,16},{9,1},{17,9},{25,17},{10,2},{18,10},{26,18},{... | collective-permute-start | bytes 491528 | tf_op jit(solution)/shard_map/ppermute | solution.py:509
  35.8 4.5 %copy-start.10 = (bf16[256,512]{1,0:T(8,128)(2,1)S(1)}, bf16[256,512]{1,0:T(8,128)(2,1)}, u32[]{:S(2)}) copy-start(bf16[256,512]{1,0:T(8,128)(2,1)} %copy-done.9) | copy-start | bytes 786436
  35.8 3.7 %collective-permute-start.6 = (bf16[256,1024]{1,0:T(8,128)(2,1)S(1)}, bf16[256,1024]{1,0:T(8,128)(2,1)S(1)}, u32[]{:S(2)}, u32[]{:S(2)}) collective-permute-start(bf16[256,1024]{1,0:T(8,128)(2,1)S(1)} %get-tuple-element.66), channel_id=1, source_target_pairs={{0,8},{1,9},{2,10},{3,11},{4,12},{5,13},{6,14},{7,15},{8,0},{9,1},... | collective-permute-start | bytes 1572872 | tf_op jit(solution)/shard_map/ppermute | solution.py:364
  40.3 12.5 %collective-permute-start.7 = (bf16[128,1024]{1,0:T(8,128)(2,1)S(1)}, bf16[128,1024]{1,0:T(8,128)(2,1)S(1)}, u32[]{:S(2)}, u32[]{:S(2)}) collective-permute-start(bf16[128,1024]{1,0:T(8,128)(2,1)S(1)} %get-tuple-element.79), channel_id=1, source_target_pairs={{0,16},{1,17},{2,18},{3,19},{4,20},{5,21},{6,22},{7,23},{8,9},{9,8... | collective-permute-start | bytes 786440 | tf_op jit(solution)/shard_map/ppermute | solution.py:364
  46.7 11.2 %collective-permute-start.10 = (bf16[2,192,512]{2,1,0:T(8,128)(2,1)S(1)}, bf16[2,192,512]{2,1,0:T(8,128)(2,1)S(1)}, u32[]{:S(2)}, u32[]{:S(2)}) collective-permute-start(bf16[2,192,512]{2,1,0:T(8,128)(2,1)S(1)} %get-tuple-element.84), channel_id=1, source_target_pairs={{0,8},{8,16},{16,24},{1,9},{9,17},{17,25},{2,10},{10,18},{18,26},{... | collective-permute-start | bytes 1179656 | tf_op jit(solution)/shard_map/ppermute | solution.py:563
  50.7 9.1 %collective-permute-start.9 = (bf16[2,192,512]{2,1,0:T(8,128)(2,1)S(1)}, bf16[2,192,512]{2,1,0:T(8,128)(2,1)S(1)}, u32[]{:S(2)}, u32[]{:S(2)}) collective-permute-start(bf16[2,192,512]{2,1,0:T(8,128)(2,1)S(1)} %get-tuple-element.83), channel_id=1, source_target_pairs={{8,0},{16,8},{24,16},{9,1},{17,9},{25,17},{10,2},{18,10},{26,18},{... | collective-permute-start | bytes 1179656 | tf_op jit(solution)/shard_map/ppermute | solution.py:562
  53.4 3.9 %collective-permute-start.8 = (bf16[64,1024]{1,0:T(8,128)(2,1)S(1)}, bf16[64,1024]{1,0:T(8,128)(2,1)S(1)}, u32[]{:S(2)}, u32[]{:S(2)}) collective-permute-start(bf16[64,1024]{1,0:T(8,128)(2,1)S(1)} %get-tuple-element.81), channel_id=1, source_target_pairs={{0,1},{1,0},{2,3},{3,2},{4,5},{5,4},{6,7},{7,6},{8,10},{9,11},{10,... | collective-permute-start | bytes 393224 | tf_op jit(solution)/shard_map/ppermute | solution.py:364
  59.8 3.1 %collective-permute-start.11 = (bf16[32,1024]{1,0:T(8,128)(2,1)S(1)}, bf16[32,1024]{1,0:T(8,128)(2,1)S(1)}, u32[]{:S(2)}, u32[]{:S(2)}) collective-permute-start(bf16[32,1024]{1,0:T(8,128)(2,1)S(1)} %get-tuple-element.88), channel_id=1, source_target_pairs={{0,2},{1,3},{2,0},{3,1},{4,6},{5,7},{6,4},{7,5},{8,24},{9,25},{10,... | collective-permute-start | bytes 196616 | tf_op jit(solution)/shard_map/ppermute | solution.py:364
  59.8 31.9 %copy-start.3 = (bf16[512,1024]{1,0:T(8,128)(2,1)S(1)}, bf16[512,1024]{1,0:T(8,128)(2,1)}, u32[]{:S(2)}) copy-start(bf16[512,1024]{1,0:T(8,128)(2,1)} %w_ref.3) | copy-start | bytes 3145732
  60.1 14.0 %collective-permute-start.14 = (bf16[2,96,512]{2,1,0:T(8,128)(2,1)S(1)}, bf16[2,96,512]{2,1,0:T(8,128)(2,1)S(1)}, u32[]{:S(2)}, u32[]{:S(2)}) collective-permute-start(bf16[2,96,512]{2,1,0:T(8,128)(2,1)S(1)} %get-tuple-element.91), channel_id=1, source_target_pairs={{0,7},{1,0},{2,1},{3,2},{4,3},{5,4},{6,5},{7,6},{8,15},{9,8},{10,9... | collective-permute-start | bytes 589832 | tf_op jit(solution)/shard_map/ppermute | solution.py:577
  61.7 12.4 %collective-permute-start.15 = (bf16[2,96,512]{2,1,0:T(8,128)(2,1)S(1)}, bf16[2,96,512]{2,1,0:T(8,128)(2,1)S(1)}, u32[]{:S(2)}, u32[]{:S(2)}) collective-permute-start(bf16[2,96,512]{2,1,0:T(8,128)(2,1)S(1)} %get-tuple-element.92), channel_id=1, source_target_pairs={{0,1},{1,2},{2,3},{3,4},{4,5},{5,6},{6,7},{7,0},{8,9},{9,10},{10,1... | collective-permute-start | bytes 589832 | tf_op jit(solution)/shard_map/ppermute | solution.py:578
  62.9 7.0 %collective-permute-start.12 = (bf16[40,1024]{1,0:T(8,128)(2,1)S(1)}, bf16[40,1024]{1,0:T(8,128)(2,1)S(1)}, u32[]{:S(2)}, u32[]{:S(2)}) collective-permute-start(bf16[40,1024]{1,0:T(8,128)(2,1)S(1)} %meet.1.own_ref), channel_id=1, source_target_pairs={{0,4},{1,5},{2,6},{3,7},{4,0},{5,1},{6,2},{7,3},{8,12},{9,13},{10,... | collective-permute-start | bytes 245768 | tf_op jit(solution)/shard_map/ppermute | solution.py:364
  69.9 3.7 %collective-permute-start.13 = (bf16[40,1024]{1,0:T(8,128)(2,1)S(1)}, bf16[40,1024]{1,0:T(8,128)(2,1)S(1)}, u32[]{:S(2)}, u32[]{:S(2)}) collective-permute-start(bf16[40,1024]{1,0:T(8,128)(2,1)S(1)} %total.1.own_ref), channel_id=1, source_target_pairs={{0,2},{1,3},{2,0},{3,1},{4,6},{5,7},{6,4},{7,5},{8,24},{9,25},{10,... | collective-permute-start | bytes 245768 | tf_op jit(solution)/shard_map/ppermute | solution.py:364
  74.2 4.1 %collective-permute-start.16 = (bf16[72,1024]{1,0:T(8,128)(2,1)S(1)}, bf16[72,1024]{1,0:T(8,128)(2,1)S(1)}, u32[]{:S(2)}, u32[]{:S(2)}) collective-permute-start(bf16[72,1024]{1,0:T(8,128)(2,1)S(1)} %grow.3.own_ref), channel_id=1, source_target_pairs={{0,1},{1,0},{2,3},{3,2},{4,5},{5,4},{6,7},{7,6},{8,10},{9,11},{10,... | collective-permute-start | bytes 442376 | tf_op jit(solution)/shard_map/ppermute | solution.py:364
  78.8 7.4 %collective-permute-start.17 = (bf16[136,1024]{1,0:T(8,128)(2,1)S(1)}, bf16[136,1024]{1,0:T(8,128)(2,1)S(1)}, u32[]{:S(2)}, u32[]{:S(2)}) collective-permute-start(bf16[136,1024]{1,0:T(8,128)(2,1)S(1)} %grow.4.own_ref), channel_id=1, source_target_pairs={{0,16},{1,17},{2,18},{3,19},{4,20},{5,21},{6,22},{7,23},{8,9},{9,8... | collective-permute-start | bytes 835592 | tf_op jit(solution)/shard_map/ppermute | solution.py:364
  86.8 7.8 %collective-permute-start.18 = (bf16[264,1024]{1,0:T(8,128)(2,1)S(1)}, bf16[264,1024]{1,0:T(8,128)(2,1)S(1)}, u32[]{:S(2)}, u32[]{:S(2)}) collective-permute-start(bf16[264,1024]{1,0:T(8,128)(2,1)S(1)} %grow.5.own_ref), channel_id=1, source_target_pairs={{0,8},{1,9},{2,10},{3,11},{4,12},{5,13},{6,14},{7,15},{8,0},{9,1},... | collective-permute-start | bytes 1622024 | tf_op jit(solution)/shard_map/ppermute | solution.py:364

commit v4 on v3

v4 whole, which is shorter than its diff:
```python
import functools

import jax
import jax.numpy as jnp
from jax import lax
from jax.experimental import pallas as pl
from jax.experimental.pallas import tpu as pltpu
from jax.sharding import PartitionSpec as P

RAD = 6
SPAN = 2 * RAD + 1
TILE = 4
GROUP = 4
NEG = -1e30
NT = (((1,), (1,)), ((), ()))
F32 = jnp.float32
BF16 = jnp.bfloat16
SLOTS = 16
CORNER = 80
MIB = 1 << 20


def dot(a, b):
    return jnp.dot(a, b, preferred_element_type=F32)


def dot_nt(a, b):
    return lax.dot_general(a, b, NT, preferred_element_type=F32)


def in_hbm(x):
    return pltpu.with_memory_space_constraint(x, pltpu.HBM)


def room(mib):
    return pltpu.CompilerParams(vmem_limit_bytes=mib * MIB)


def iota2(shape, axis):
    return lax.broadcasted_iota(jnp.int32, shape, axis)


def hot(mask):
    return mask.astype(F32).astype(BF16)


def over(x, n):
    if n & (n - 1) == 0:
        return x >> (n.bit_length() - 1), x & (n - 1)
    return x // n, x % n


def down_iota(n):
    return iota2((n, 1), 0)


def along_iota(n):
    return iota2((1, n), 1)


def spread_heads(tile, cols, head_size):
    lane = over(iota2((cols, tile.shape[1]), 1), head_size)[0]
    zero = jnp.zeros((cols, tile.shape[1]), tile.dtype)
    parts = []
    for i in range(TILE):
        rows = tile[i * cols : (i + 1) * cols]
        for h in range(GROUP):
            parts.append(jnp.where(lane == h, rows, zero))
    return jnp.concatenate(parts, 0)


def head_mask(cols, head_size):
    shape = (GROUP * head_size, TILE * GROUP * cols)
    column = over(over(iota2(shape, 1), cols)[0], GROUP)[1]
    return over(iota2(shape, 0), head_size)[0] == column


def picker(cols):
    row_i, row_j = over(down_iota(TILE * cols), cols)
    high, col_j = over(along_iota(TILE * GROUP * cols), cols)
    return hot((row_i == over(high, GROUP)[0]) & (row_j == col_j))


def keep_rows(st, first_row, rows_all, cols_pad):
    parts = []
    for k in range(TILE + 2 * RAD):
        row = first_row + k
        inside = (row >= 0) & (row < rows_all)
        parts.append(jnp.where(inside, st[k * cols_pad : (k + 1) * cols_pad], NEG))
    return jnp.concatenate(parts, 0)


def take_cols(rows, cols, first):
    r, c = over(down_iota(rows * RAD), RAD)
    return hot(along_iota(rows * cols) == r * cols + first + c)


def put_cols(rows, cols, first):
    r, c = over(along_iota(rows * RAD), RAD)
    return hot(down_iota(rows * cols) == r * cols + first + c)


def put_corner(cols):
    n = along_iota(CORNER)
    half = RAD * RAD
    r, c = over(jnp.where(n < half, n, n - half), RAD)
    target = r * cols + c + jnp.where(n < half, 0, RAD)
    return hot((down_iota(RAD * cols) == target) & (n < 2 * half))


def pack_kernel(
    rows, cols, k_hbm, v_hbm, east_ref, west_ref, down_ref, up_ref, x_ref, sem_ref
):
    copies = [
        pltpu.make_async_copy(ref, x_ref.at[i], sem_ref.at[i])
        for i, ref in enumerate((k_hbm, v_hbm))
    ]
    for copy in copies:
        copy.start()
    pick_east = take_cols(rows, cols, cols - RAD)
    pick_west = take_cols(rows, cols, 0)
    edge = RAD * cols
    for i, copy in enumerate(copies):
        copy.wait()
        x = x_ref[i]
        east_ref[i] = dot(pick_east, x).astype(BF16)
        west_ref[i] = dot(pick_west, x).astype(BF16)
        down_ref[i] = x[(rows - RAD) * cols :]
        up_ref[i] = x[:edge]


def corner_kernel(rows, cols, w_ref, e_ref, own_down_ref, own_up_ref, down_ref, up_ref):
    half = RAD * RAD
    edge = RAD * cols
    n = down_iota(CORNER)
    src = along_iota(rows * RAD)
    for ref, own_ref, first in (
        (down_ref, own_down_ref, (rows - RAD) * RAD), (up_ref, own_up_ref, 0)
    ):
        pick_w = hot((src == first + n) & (n < half))
        pick_e = hot((src == first + n - half) & (n >= half) & (n < 2 * half))
        for i in range(2):
            side = dot(pick_w, w_ref[i]) + dot(pick_e, e_ref[i])
            ref[i, :edge, :] = own_ref[i]
            ref[i, edge:, :] = side.astype(BF16)


def prepare_kernel(
    cols, cols_pad, rel_ref, cot_hbm, w_hbm, out_ref, grad_ref, c_ref, r_ref, cot_ref, w_ref,
    sem_ref,
):
    copies = [
        pltpu.make_async_copy(cot_hbm, cot_ref, sem_ref.at[0]),
        pltpu.make_async_copy(w_hbm, w_ref, sem_ref.at[1]),
    ]
    for copy in copies:
        copy.start()
    heads = rel_ref.shape[1]
    lanes = heads * cols
    half = lanes // 2
    shape = (cols_pad, lanes)
    offset = slot_offset(shape, cols)
    inside = (offset >= 0) & (offset < SPAN)
    head = over(iota2((1, lanes), 1), cols)[0]
    for a in range(SPAN):
        tile = jnp.full(shape, NEG, F32)
        for b in range(SPAN):
            row = jnp.full((1, lanes), rel_ref[a, 0, b], F32)
            for h in range(1, heads):
                row = jnp.where(head == h, rel_ref[a, h, b], row)
            tile = jnp.where(offset == b, row, tile)
        tile = jnp.where(inside, tile, NEG)
        c_ref[a] = tile
        r_ref[a] = pltpu.roll(tile, half, 1)
    low = iota2(shape, 1) < half
    blank = jnp.full(shape, NEG, F32)
    for g in range(2):
        first, second = (c_ref, r_ref) if g == 0 else (r_ref, c_ref)
        for pair in range(TILE // 2):
            i = 2 * pair
            lo = (g * TILE // 2 + pair) * lanes
            for k in range(TILE + 2 * RAD):
                a = k - i
                one = first[a] if 0 <= a < SPAN else blank
                two = second[a - 1] if 0 <= a - 1 < SPAN else blank
                out_ref[k * cols_pad : (k + 1) * cols_pad, lo : lo + lanes] = jnp.where(
                    low, one, two
                )
    for copy in copies:
        copy.wait()
    grad_ref[...] = dot_nt(cot_ref[...], w_ref[...]).astype(BF16)


def slot_offset(shape, cols):
    slot = iota2(shape, 0)
    pos = jnp.where(slot < cols, slot + RAD, jnp.where(slot < cols + RAD, slot - cols, slot))
    pos = jnp.where(slot < cols + 2 * RAD, pos, -1000)
    return pos - over(iota2(shape, 1), cols)[1]


def assemble(out_ref, i, rows, cols, cols_pad, own, refs, group):
    w_ref, e_ref, a_ref, b_ref = refs
    edge = RAD * cols
    side = dot(put_cols(rows, SLOTS, 0), w_ref[i, :, group])
    side = (side + dot(put_cols(rows, SLOTS, RAD), e_ref[i, :, group])).astype(BF16)
    for r in range(rows):
        lo = (RAD + r) * cols_pad
        out_ref[lo : lo + cols, :] = own[r * cols : (r + 1) * cols, group]
        out_ref[lo + cols : lo + cols + SLOTS, :] = side[r * SLOTS : (r + 1) * SLOTS]
    put = put_corner(SLOTS)
    for first, o_ref in ((0, a_ref), (RAD + rows, b_ref)):
        side = dot(put, o_ref[i, edge:, group]).astype(BF16)
        for r in range(RAD):
            lo = (first + r) * cols_pad
            out_ref[lo : lo + cols, :] = o_ref[i, r * cols : (r + 1) * cols, group]
            out_ref[lo + cols : lo + cols + SLOTS, :] = side[r * SLOTS : (r + 1) * SLOTS]


def group_lanes(group, lanes):
    return pl.ds(pl.multiple_of(group * lanes, lanes), lanes)


def fwd_kernel(
    sizes, n, info_ref, q_ref, k_ref, v_ref, w_ref, e_ref, a_ref, b_ref,
    bias_ref, cot_ref, out_ref, weight_ref, p_ref, ko_ref, vo_ref, vt_ref, at_ref,
):
    lat_dev, cols, cols_pad, head_size, rows_all = sizes
    scale = head_size ** (-0.5)
    group = group_lanes(info_ref[n], GROUP * head_size)
    refs = (w_ref, e_ref, a_ref, b_ref)
    assemble(ko_ref, 0, lat_dev, cols, cols_pad, k_ref, refs, group)
    assemble(vo_ref, 1, lat_dev, cols, cols_pad, v_ref, refs, group)
    vt_ref[...] = vo_ref[...].T
    mask = head_mask(cols, head_size)
    pick = picker(cols)
    win = (TILE + 2 * RAD) * cols_pad
    for t in range(lat_dev // TILE):
        lo = t * TILE * cols_pad
        qs = pl.ds(t * TILE * cols, TILE * cols)
        q_bd = spread_heads(q_ref[qs, group] * jnp.asarray(scale, BF16), cols, head_size)
        first = info_ref[1] * lat_dev + t * TILE - RAD
        st = dot_nt(ko_ref[pl.ds(lo, win), :], q_bd) + bias_ref[:, group]
        st = keep_rows(st, first, rows_all, cols_pad)
        m = jnp.max(st, 0, keepdims=True)
        e = jnp.exp(st - m)
        p = e * (1.0 / jnp.sum(e, 0, keepdims=True))
        p_ref[t] = p
        ot = dot(vt_ref[:, pl.ds(lo, win)], p.astype(BF16))
        ot = jnp.where(mask, ot, 0.0).astype(BF16)
        out_ref[qs, :] = dot_nt(pick, ot).astype(BF16)
    at_ref[...] = out_ref[...].T
    weight_ref[...] = dot(at_ref[...], cot_ref[...]).astype(weight_ref.dtype)


def bwd_kernel(sizes, n, info_ref, q_ref, g_ref, p_ref, k_ref, v_ref, *refs):
    dq_ref, top_ref, bot_ref, mid_ref, side_ref, x_ref, kt_ref, dk_ref, dv_ref, db_ref = refs[-10:]
    before = refs[:-10]
    lat_dev, cols, cols_pad, head_size, rows_all = sizes
    scale = head_size ** (-0.5)
    mask = head_mask(cols, head_size)
    pick = picker(cols)
    win = (TILE + 2 * RAD) * cols_pad
    half = GROUP * cols
    low = iota2((cols_pad, 2 * half), 1) < half
    which = info_ref[n]
    group = group_lanes(which, GROUP * head_size)
    mine = group if before else slice(None)
    if before:
        other = group_lanes(1 - which, GROUP * head_size)
        dq_ref[:, other] = before[0][...]
        top_ref[:, :, other] = before[1][...]
        bot_ref[:, :, other] = before[2][...]
    kt_ref[...] = k_ref[...].T
    dk_ref[...] = jnp.zeros_like(dk_ref)
    dv_ref[...] = jnp.zeros_like(dv_ref)
    for t in range(lat_dev // TILE):
        lo = t * TILE * cols_pad
        qs = pl.ds(t * TILE * cols, TILE * cols)
        ws = pl.ds(lo, win)
        q_bd = spread_heads(q_ref[qs, group] * jnp.asarray(scale, BF16), cols, head_size)
        g_bd = spread_heads(g_ref[qs, group], cols, head_size)
        p = p_ref[t]
        slope = dot_nt(v_ref[ws, :], g_bd)
        inner = jnp.sum(p * slope, 0, keepdims=True)
        sg = p * (slope - inner)
        if t == 0:
            db_ref[...] = sg
        else:
            db_ref[...] += sg
        sgb = sg.astype(BF16)
        dqt = jnp.where(mask, dot(kt_ref[:, ws], sgb) * scale, 0.0).astype(BF16)
        dq_ref[qs, mine] = dot_nt(pick, dqt).astype(BF16)
        dk_ref[ws, :] += dot(sgb, q_bd)
        dv_ref[ws, :] += dot(p.astype(BF16), g_bd)
    edge = RAD * cols_pad
    for i, ref in enumerate((dk_ref, dv_ref)):
        top_ref[i, :, mine] = ref[:edge, :].astype(BF16)
        bot_ref[i, :, mine] = ref[edge + lat_dev * cols_pad :, :].astype(BF16)
        for r in range(lat_dev):
            lo = (RAD + r) * cols_pad
            mid_ref[i, r * cols : (r + 1) * cols, :] = ref[lo : lo + cols, :]
            side_ref[i, r * SLOTS : (r + 1) * SLOTS, :] = ref[lo + cols : lo + cols_pad, :]
    for a in range(SPAN):
        total = jnp.zeros((cols_pad, 2 * half), F32)
        for pair in range(TILE // 2):
            i = 2 * pair
            lanes = slice(pair * 2 * half, (pair + 1) * 2 * half)
            one = db_ref[(a + i) * cols_pad : (a + i + 1) * cols_pad, lanes]
            two = db_ref[(a + i + 1) * cols_pad : (a + i + 2) * cols_pad, lanes]
            total = total + jnp.where(low, one, two)
        x_ref[a * cols_pad : (a + 1) * cols_pad, :] = total


def bias_kernel(cols, cols_pad, info_ref, xs_ref, xk_ref, out_ref, z_ref):
    lanes = xs_ref.shape[1]
    half = lanes // 2
    shape = (cols_pad, lanes)
    low = (over(iota2(shape, 1), half)[0] == info_ref[0])
    offset = slot_offset(shape, cols)
    z_ref[...] = jnp.zeros_like(z_ref)
    for a in range(SPAN):
        rows = slice(a * cols_pad, (a + 1) * cols_pad)
        one = xs_ref[rows, :]
        two = xk_ref[rows, :]
        both = jnp.where(low, one + pltpu.roll(one, half, 1), two + pltpu.roll(two, half, 1))
        for b in range(SPAN):
            n = a * SPAN + b
            z_ref[n : n + 1, :] = jnp.sum(jnp.where(offset == b, both, 0.0), 0, keepdims=True)
    heads = out_ref.shape[0]
    pick = (over(iota2((heads, lanes), 1), cols)[0] == iota2((heads, lanes), 0)).astype(F32)
    out_ref[...] = lax.dot_general(
        pick, z_ref[...], NT, precision=lax.Precision.HIGHEST, preferred_element_type=F32
    )


def lat_terms(ref, i, rows, cols, cols_pad, first):
    parts = []
    for r in range(RAD):
        lo = r * cols_pad + first
        parts.append(ref[i, lo : lo + cols, :])
    return jnp.concatenate(parts, 0).astype(F32)


def both_groups(info_ref, dst_ref, i, s_ref, k_ref):
    lanes = s_ref.shape[2]
    dst_ref[:, group_lanes(info_ref[0], lanes)] = s_ref[i]
    dst_ref[:, group_lanes(1 - info_ref[0], lanes)] = k_ref[i]


def side_kernel(
    rows, cols, cols_pad, info_ref, ss_ref, sk_ref, a_ref, b_ref, west_ref, east_ref, s_ref
):
    edge = RAD * SLOTS
    pick_west = take_cols(rows, SLOTS, 0)
    pick_east = take_cols(rows, SLOTS, RAD)
    for i in range(2):
        both_groups(info_ref, s_ref, i, ss_ref, sk_ref)
        s_ref[:edge, :] += lat_terms(a_ref, i, rows, SLOTS, cols_pad, cols)
        s_ref[(rows - RAD) * SLOTS :, :] += lat_terms(b_ref, i, rows, SLOTS, cols_pad, cols)
        x = s_ref[...].astype(BF16)
        west_ref[i] = dot(pick_west, x).astype(BF16)
        east_ref[i] = dot(pick_east, x).astype(BF16)


def join_kernel(
    rows, cols, cols_pad, info_ref, ms_ref, mk_ref, a_ref, b_ref, w_ref, e_ref,
    k_ref, v_ref, s_ref,
):
    edge = RAD * cols
    put_west = put_cols(rows, cols, 0)
    put_east = put_cols(rows, cols, cols - RAD)
    for i, out_ref in enumerate((k_ref, v_ref)):
        both_groups(info_ref, s_ref, i, ms_ref, mk_ref)
        s_ref[...] += dot(put_west, w_ref[i]) + dot(put_east, e_ref[i])
        s_ref[:edge, :] += lat_terms(a_ref, i, rows, cols, cols_pad, 0)
        s_ref[(rows - RAD) * cols :, :] += lat_terms(b_ref, i, rows, cols, cols_pad, 0)
        out_ref[...] = s_ref[...].astype(BF16)


def bits_of(mesh_shape):
    order = []
    for axis in ("lat", "lon"):
        bit = 1
        while bit < mesh_shape[axis]:
            order.append((axis, bit))
            bit *= 2
    return order


def rounds_of(mesh_shape):
    first, *rest = bits_of(mesh_shape)
    middle, ends = rest[:-2], rest[-2:]
    turned = middle[1:] + middle[:1]
    return [(first, first)] + list(zip(middle, turned)), list(zip(ends, ends[::-1]))


def partner_pairs(mesh_shape, bits):
    n_lat, n_lon = mesh_shape["lat"], mesh_shape["lon"]
    pairs = []
    for i in range(n_lat):
        axis, bit = bits[i % 2]
        for j in range(n_lon):
            a, b = (i ^ bit, j) if axis == "lat" else (i, j ^ bit)
            pairs.append((i * n_lon + j, a * n_lon + b))
    return pairs


def swap(x, mesh_shape, bits):
    return lax.ppermute(x, ("lat", "lon"), partner_pairs(mesh_shape, bits))


def my_bit(bits):
    def of(axis, bit):
        return (lax.axis_index(axis) // bit) % 2

    odd = lax.axis_index("lat") % 2
    return jnp.where(odd == 0, of(*bits[0]), of(*bits[1]))


def put_bias(ref, rows, bias):
    heads, count = bias.shape
    high = bias.astype(BF16)
    ref[rows:, :count] = high
    ref[rows:, count : 2 * count] = (bias - high.astype(F32)).astype(BF16)
    ref[rows:, 2 * count :] = jnp.zeros((heads, ref.shape[1] - 2 * count), BF16)


def get_bias(ref, rows, count):
    return ref[rows:, :count].astype(F32) + ref[rows:, count : 2 * count].astype(F32)


def halve_kernel(n, info_ref, keep_ref, got_ref, send_ref, out_ref):
    half = send_ref.shape[0]
    low = keep_ref[:half, :] + got_ref[:half, :].astype(F32)
    high = keep_ref[half:, :] + got_ref[half:, :].astype(F32)
    lower = info_ref[n] == 0
    send_ref[...] = jnp.where(lower, high, low).astype(BF16)
    out_ref[...] = jnp.where(lower, low, high)


def meet_kernel(keep_ref, got_ref, bias_ref, out_ref):
    rows = keep_ref.shape[0]
    out_ref[:rows, :] = (keep_ref[...] + got_ref[...].astype(F32)).astype(BF16)
    put_bias(out_ref, rows, bias_ref[...])


def total_kernel(norm, count, heads, own_ref, got_ref, out_ref):
    rows = own_ref.shape[0] - heads
    total = own_ref[:rows, :].astype(F32) + got_ref[:rows, :].astype(F32)
    out_ref[:rows, :] = (total if norm is None else total * norm).astype(BF16)
    put_bias(out_ref, rows, get_bias(own_ref, rows, count) + get_bias(got_ref, rows, count))


def grow_kernel(n, count, heads, info_ref, own_ref, got_ref, out_ref):
    rows = own_ref.shape[0] - heads
    lower = info_ref[n] == 0
    own = own_ref[:rows, :]
    got = got_ref[:rows, :]
    out_ref[:rows, :] = jnp.where(lower, own, got)
    out_ref[rows : 2 * rows, :] = jnp.where(lower, got, own)
    put_bias(out_ref, 2 * rows, get_bias(own_ref, rows, count) + get_bias(got_ref, rows, count))


def last_kernel(n, norm, count, info_ref, own_ref, got_ref, out_ref, bias_ref):
    rows = out_ref.shape[0] // 2
    lower = info_ref[n] == 0
    own = own_ref[:rows, :]
    got = got_ref[:rows, :]
    out_ref[:rows, :] = jnp.where(lower, own, got)
    out_ref[rows:, :] = jnp.where(lower, got, own)
    bias = (get_bias(own_ref, rows, count) + get_bias(got_ref, rows, count)) * norm
    for a in range(SPAN):
        bias_ref[a] = bias[:, a * SPAN : (a + 1) * SPAN]


def project_kernel(info_ref, s_ref, k_ref, w_ref, out_ref):
    rows = s_ref.shape[1]
    first = pl.ds(pl.multiple_of(info_ref[0] * rows, rows), rows)
    second = pl.ds(pl.multiple_of((1 - info_ref[0]) * rows, rows), rows)
    out = dot(s_ref[...], w_ref[first, :]) + dot(k_ref[...], w_ref[second, :])
    out_ref[...] = out.astype(BF16)


def shards(mesh_shape, queries, keys, values, rel_bias, out_weight, cotangent):
    lat_dev, lon_dev, width = queries.shape
    heads = rel_bias.shape[0]
    head_size = width // heads
    groups = heads // GROUP
    lanes = GROUP * head_size
    model = out_weight.shape[1]
    n_lat, n_lon = mesh_shape["lat"], mesh_shape["lon"]
    cols_pad = lon_dev + SLOTS
    outer_lat = lat_dev + 2 * RAD
    tokens = lat_dev * lon_dev
    norm = (tokens * n_lat * n_lon) ** (-0.5)
    east = [(i, (i + 1) % n_lon) for i in range(n_lon)]
    west = [(i, (i - 1) % n_lon) for i in range(n_lon)]
    down = [(i, i + 1) for i in range(n_lat - 1)]
    up = [(i + 1, i) for i in range(n_lat - 1)]
    win = (TILE + 2 * RAD) * cols_pad
    tiles = lat_dev // TILE
    lanes_q = TILE * GROUP * lon_dev
    n_keys = outer_lat * cols_pad
    n_side = lat_dev * RAD
    n_edge = RAD * lon_dev
    n_strip = RAD * cols_pad

    def shape(dims, dtype=BF16):
        return jax.ShapeDtypeStruct(dims, dtype)

    q_flat = queries.reshape(tokens, width)
    k_flat = keys.reshape(tokens, width)
    v_flat = values.reshape(tokens, width)
    cot = cotangent.reshape(tokens, model)

    lat_index = lax.axis_index("lat").astype(jnp.int32)
    core = lat_index % 2
    rounds, ends = rounds_of(mesh_shape)
    facts = [1 - core, lat_index, core] + [my_bit(bits) for bits in rounds]
    info = jnp.stack([x.astype(jnp.int32) for x in facts])
    smem = pl.BlockSpec(memory_space=pltpu.SMEM)
    vmem = pl.BlockSpec(memory_space=pltpu.VMEM)
    hbm = pl.BlockSpec(memory_space=pltpu.HBM)

    to_east, to_west, to_down, to_up = pl.pallas_call(
        functools.partial(pack_kernel, lat_dev, lon_dev),
        in_specs=[hbm, hbm],
        out_shape=[shape((2, n_side, width))] * 2 + [shape((2, n_edge, width))] * 2,
        scratch_shapes=[pltpu.VMEM((2, tokens, width), BF16), pltpu.SemaphoreType.DMA((2,))],
        compiler_params=room(4),
        name="pack",
    )(in_hbm(k_flat), in_hbm(v_flat))
    from_west = lax.ppermute(to_east, "lon", east)
    from_east = lax.ppermute(to_west, "lon", west)
    sizes = (lat_dev, lon_dev, cols_pad, head_size, lat_dev * n_lat)
    table, attended_grad = pl.pallas_call(
        functools.partial(prepare_kernel, lon_dev, cols_pad),
        in_specs=[smem, hbm, hbm],
        out_shape=[shape((win, groups * lanes_q), F32), shape((tokens, width))],
        scratch_shapes=[pltpu.VMEM((SPAN, cols_pad, heads * lon_dev), F32)] * 2
        + [pltpu.VMEM((tokens, model), BF16), pltpu.VMEM((width, model), BF16)]
        + [pltpu.SemaphoreType.DMA((2,))],
        compiler_params=room(6),
        name="prepare",
    )(rel_bias.transpose(1, 0, 2), in_hbm(cot), in_hbm(out_weight))
    from_west, from_east, table = lax.optimization_barrier((from_west, from_east, table))
    corner_down, corner_up = pl.pallas_call(
        functools.partial(corner_kernel, lat_dev, lon_dev),
        out_shape=[shape((2, n_edge + CORNER, width))] * 2,
        compiler_params=room(4),
        name="corner",
    )(from_west, from_east, to_down, to_up)
    from_above = lax.ppermute(corner_down, "lat", down)
    from_below = lax.ppermute(corner_up, "lat", up)

    probs = (tiles, win, lanes_q)
    outer = (n_keys, lanes)

    def forward(n, dtype):
        return pl.pallas_call(
            functools.partial(fwd_kernel, sizes, n),
            in_specs=[smem] + [vmem] * 9,
            out_shape=[shape((tokens, lanes)), shape((lanes, model), dtype), shape(probs, F32)]
            + [shape(outer)] * 2,
            scratch_shapes=[pltpu.VMEM((lanes, n_keys), BF16), pltpu.VMEM((lanes, tokens), BF16)],
            compiler_params=room(8),
            name="attend_fwd",
        )(
            info, q_flat, k_flat, v_flat, from_west, from_east,
            from_above, from_below, table, cot,
        )

    def step_call(kernel, name, outs, *operands):
        scalars = [smem if x.dtype == jnp.int32 else vmem for x in operands]
        return pl.pallas_call(
            kernel, in_specs=scalars, out_shape=outs, compiler_params=room(4), name=name
        )(*operands)

    att_s, weight_s, p_s, k_s, v_s = forward(0, BF16)
    got = swap(weight_s, mesh_shape, rounds[0])
    att_k, keep, p_k, k_k, v_k = forward(2, F32)

    def halve(keep, got, number):
        half = (keep.shape[0] // 2, model)
        outs = [shape(half), shape(half, F32)]
        kernel = functools.partial(halve_kernel, 3 + number)
        return step_call(kernel, "halve", outs, info, keep, got)

    send, keep = halve(keep, got, 1)
    def backward(n, info, p, k, v, *before):
        size = width if before else lanes
        return pl.pallas_call(
            functools.partial(bwd_kernel, sizes, n),
            in_specs=[smem] + [vmem] * (5 + len(before)),
            out_shape=[shape((tokens, size))]
            + [shape((2, n_strip, size))] * 2
            + [shape((2, tokens, lanes), F32)] * 2
            + [shape((SPAN * cols_pad, 2 * GROUP * lon_dev), F32)],
            scratch_shapes=[pltpu.VMEM((lanes, n_keys), BF16)]
            + [pltpu.VMEM((n_keys, lanes), F32)] * 2
            + [pltpu.VMEM((win, lanes_q), F32)],
            compiler_params=room(10),
            name="attend_bwd",
        )(info, q_flat, attended_grad, p, k, v, *before)

    info_b, send = lax.optimization_barrier((info, send))
    got = swap(send, mesh_shape, rounds[1])
    *before, mid_s, side_s, fold_s = backward(0, info_b, p_s, k_s, v_s)
    for number in range(2, len(rounds)):
        send, keep = halve(keep, got, number)
        if number == 2:
            info_b, send = lax.optimization_barrier((info, send))
        got = swap(send, mesh_shape, rounds[number])
    after = backward(2, info_b, p_k, k_k, v_k, *before)
    query_grad, top, bottom, mid_k, side_k, fold_k = after
    get_below = lax.ppermute(top, "lat", up)
    get_above = lax.ppermute(bottom, "lat", down)

    count = 256
    bias_local = pl.pallas_call(
        functools.partial(bias_kernel, lon_dev, cols_pad),
        in_specs=[smem, vmem, vmem],
        out_shape=shape((heads, count), F32),
        scratch_shapes=[pltpu.VMEM((count, heads * lon_dev), F32)],
        compiler_params=room(4),
        name="bias_fold",
    )(info, fold_s, fold_k)
    block_out = pl.pallas_call(
        project_kernel,
        in_specs=[smem] + [vmem] * 3,
        out_shape=shape((tokens, model)),
        compiler_params=room(6),
        name="project",
    )(info, att_s, att_k, out_weight)
    note = shape((keep.shape[0] + heads, model))
    message = step_call(meet_kernel, "meet", note, keep, got, bias_local)
    got = swap(message, mesh_shape, ends[0])
    kernel = functools.partial(total_kernel, None, count, heads)
    message = step_call(kernel, "total", note, message, got)
    message, get_below, get_above, block_out = lax.optimization_barrier(
        (message, get_below, get_above, block_out)
    )
    got = swap(message, mesh_shape, ends[1])
    give_west, give_east = pl.pallas_call(
        functools.partial(side_kernel, lat_dev, lon_dev, cols_pad),
        in_specs=[smem] + [vmem] * 4,
        out_shape=[shape((2, n_side, width))] * 2,
        scratch_shapes=[pltpu.VMEM((tokens, width), F32)],
        compiler_params=room(6),
        name="side",
    )(info, side_s, side_k, get_above, get_below)
    get_east = lax.ppermute(give_west, "lon", west)
    get_west = lax.ppermute(give_east, "lon", east)
    kernel = functools.partial(total_kernel, norm, count, heads)
    message = step_call(kernel, "total", note, message, got)
    message, give_west, give_east = lax.optimization_barrier((message, give_west, give_east))

    for number in range(len(rounds) - 1, 0, -1):
        if number == 1:
            message, get_east, get_west = lax.optimization_barrier((message, get_east, get_west))
        got = swap(message, mesh_shape, rounds[number])
        note = shape((2 * message.shape[0] - heads, model))
        kernel = functools.partial(grow_kernel, 3 + number, count, heads)
        message = step_call(kernel, "grow", note, info, message, got)
    key_grad, value_grad = pl.pallas_call(
        functools.partial(join_kernel, lat_dev, lon_dev, cols_pad),
        in_specs=[smem] + [vmem] * 6,
        out_shape=[shape((tokens, width))] * 2,
        scratch_shapes=[pltpu.VMEM((tokens, width), F32)],
        compiler_params=room(6),
        name="join",
    )(info, mid_s, mid_k, get_above, get_below, get_west, get_east)
    got = swap(message, mesh_shape, rounds[0])
    weight_grad, bias_grad = step_call(
        functools.partial(last_kernel, 3, norm, count),
        "last",
        [shape((width, model)), shape((SPAN, heads, SPAN), F32)],
        info, message, got,
    )
    return (
        block_out.reshape(lat_dev, lon_dev, model),
        query_grad.reshape(queries.shape),
        key_grad.reshape(keys.shape),
        value_grad.reshape(values.shape),
        weight_grad,
        bias_grad.transpose(1, 0, 2),
    )


def solution(mesh):
    spec = P("lat", "lon", None)
    return jax.shard_map(
        functools.partial(shards, dict(mesh.shape)),
        mesh=mesh,
        in_specs=(spec, spec, spec, P(), P(), spec),
        out_specs=(spec, spec, spec, spec, P(), P()),
        check_vma=False,
    )
```

time: 97.9 us -> 92 us (0.940)
  local copies, waits for them, and re-layouts: 5.8 us -> 0.93 us
  Pallas kernels: 27.6 us -> 30.8 us
  waiting for transfers between devices: 27.4 us -> 25.3 us
  starting transfers between devices: 35.1 us -> 33.6 us
    ppermute x9 -> x8, waiting for transfers between devices: 20.8 us -> 15.9 us  [swap(): return lax.ppermute(x, ('lat', 'lon'), partner_pairs(mesh_shape, bits))]
    unnamed x24 -> x16, local copies, waits for them, and re-layouts: 5.71 us -> 0.85 us
    ppermute x4 -> x2, starting transfers between devices: 11.6 us -> 6.81 us  [the longest x1 4.89 us: shards(): from_above = lax.ppermute(corner_down, 'lat', down)]
    ppermute x9 -> x8, starting transfers between devices: 10.7 us -> 13.6 us  [swap(): return lax.ppermute(x, ('lat', 'lon'), partner_pairs(mesh_shape, bits))]
    ppermute x4 -> x2, waiting for transfers between devices: 4.73 us -> 6.89 us  [the longest x1 4.3 us: shards(): from_below = lax.ppermute(corner_up, 'lat', up)]
    ppermute x1, waiting for transfers between devices: 1.88 us -> 0.01 us  [shards(): get_below = lax.ppermute(top, 'lat', up)]
    ppermute x1, waiting for transfers between devices: 0.01 us -> 1.86 us  [shards(): from_east = lax.ppermute(to_west, 'lon', west)]
    pallas_call x3 -> x4, Pallas kernels: 8 us -> 9.53 us  [the longest x2 7.25 us: backward(): pl.pallas_call(functools.partial(bwd_kernel, sizes, n), in_specs=[smem] +...]
  transfers between devices with their start and end apart: 19 -> 16, of which waited for: 9 -> 9; matrix products, arithmetic and copies ran while one was open for 1% -> 0% of each run, Pallas kernels for 20% -> 19%
where the time goes in v4:
time: 92 us; the launch traced here: 91.6 us
  starting transfers between devices  33.6 us (37%)
  Pallas kernels  30.8 us (33%)
  waiting for transfers between devices  25.3 us (28%)
  between operations  0.95 us (1%)
  local copies, waits for them, and re-layouts  0.93 us (1%)
    ppermute x8, waiting for transfers between devices, swap(): return lax.ppermute(x, ('lat', 'lon'), partner_pairs(mesh_shape, bits))  15.9 us
    ppermute x8, starting transfers between devices, swap(): return lax.ppermute(x, ('lat', 'lon'), partner_pairs(mesh_shape, bits))  13.6 us
    pallas_call x2, Pallas kernels, backward(): pl.pallas_call(functools.partial(bwd_kernel, sizes, n), in_specs=[smem] +...  7.25 us
    pallas_call x2, Pallas kernels, forward(): pl.pallas_call(functools.partial(fwd_kernel, sizes, n), in_specs=[smem] +...  7.2 us
    ppermute x1, starting transfers between devices, shards(): from_above = lax.ppermute(corner_down, 'lat', down)  4.89 us
    ppermute x1, waiting for transfers between devices, shards(): from_below = lax.ppermute(corner_up, 'lat', up)  4.3 us
    pallas_call x8, Pallas kernels, step_call(): pl.pallas_call(kernel, in_specs=scalars, out_shape=outs, compiler_params=...  4.19 us
    pallas_call x1, Pallas kernels, shards(): pl.pallas_call(functools.partial(prepare_kernel, lon_dev, cols_pad), in_s...  3.86 us
  transfers between devices with their start and end apart: 16, of which 9 were waited for; matrix products, arithmetic and copies ran while one was open for 0% of the time, Pallas kernels for 19%

profile of v4, /device:TPU:1, one launch (start us, length us, event | category | flops | bytes accessed | tf_op | source)
XLA Modules:
  0.0 91.6 jit_solution(11745455810571284428)
XLA Ops:
  0.7 0.0 copy-start
  0.7 1.5 %pack.1 = (bf16[2,96,512]{2,1,0:T(8,128)(2,1)S(1)}, bf16[2,96,512]{2,1,0:T(8,128)(2,1)S(1)}, bf16[2,96,512]{2,1,0:T(8,128)(2,1)S(1)}, bf16[2,96,512]{2,1,0:T(8,128)(2,1)S(1)}) custom-call(bf16[256,512]{1,0:T(8,128)(2,1)} %bitcast.22, bf16[256,512]{1,0:T(8,128)(2,1)} %bitcast.25), custom_call_target="tpu_custom_call" | custom-call | tf_op jit(solution)/shard_map/pack/pallas_call | solution.py:525
  2.2 2.1 %collective-permute-start = (bf16[2,96,512]{2,1,0:T(8,128)(2,1)S(1)}, bf16[2,96,512]{2,1,0:T(8,128)(2,1)S(1)}, u32[]{:S(2)}, u32[]{:S(2)}) collective-permute-start(bf16[2,96,512]{2,1,0:T(8,128)(2,1)S(1)} %get-tuple-element.61), channel_id=1, source_target_pairs={{0,1},{1,2},{2,3},{3,4},{4,5},{5,6},{6,7},{7,0},{8,9},{9,10},{10,1... | collective-permute-start | bytes 589832 | tf_op jit(solution)/shard_map/ppermute | solution.py:533
  4.3 3.1 %collective-permute-start.1 = (bf16[2,96,512]{2,1,0:T(8,128)(2,1)S(1)}, bf16[2,96,512]{2,1,0:T(8,128)(2,1)S(1)}, u32[]{:S(2)}, u32[]{:S(2)}) collective-permute-start(bf16[2,96,512]{2,1,0:T(8,128)(2,1)S(1)} %get-tuple-element.62), channel_id=1, source_target_pairs={{0,7},{1,0},{2,1},{3,2},{4,3},{5,4},{6,5},{7,6},{8,15},{9,8},{10,9... | collective-permute-start | bytes 589832 | tf_op jit(solution)/shard_map/ppermute | solution.py:534
  7.4 0.8 copy-done.7
  8.2 3.9 %prepare.1 = (f32[512,512]{1,0:T(8,128)S(1)}, bf16[256,512]{1,0:T(8,128)(2,1)S(1)}) custom-call(f32[13,8,13]{2,1,0:T(8,128)S(1)} %bitcast.28, bf16[256,1024]{1,0:T(8,128)(2,1)} %bitcast.15, bf16[512,1024]{1,0:T(8,128)(2,1)} %w_ref.1), custom_call_target="tpu_custom_call" | custom-call | tf_op jit(solution)/shard_map/prepare/pallas_call | solution.py:536
  12.1 0.0 copy-start.5
  12.1 0.0 collective-permute-done.w_ref
  12.1 1.9 %collective-permute-done.1.e_ref = bf16[2,96,512]{2,1,0:T(8,128)(2,1)S(1)} collective-permute-done((bf16[2,96,512]{2,1,0:T(8,128)(2,1)S(1)}, bf16[2,96,512]{2,1,0:T(8,128)(2,1)S(1)}, u32[]{:S(2)}, u32[]{:S(2)}) %collective-permute-start.1) | collective-permute-done | bytes 196640 | tf_op jit(solution)/shard_map/ppermute | solution.py:534
  14.0 1.1 %corner.1 = (bf16[2,176,512]{2,1,0:T(8,128)(2,1)}, bf16[2,176,512]{2,1,0:T(8,128)(2,1)}) custom-call(bf16[2,96,512]{2,1,0:T(8,128)(2,1)S(1)} %collective-permute-done.w_ref, bf16[2,96,512]{2,1,0:T(8,128)(2,1)S(1)} %collective-permute-done.1.e_ref, bf16[2,96,512]{2,1,0:T(8,128)(2,1)S(1)} %get-tuple-element.66.own_down_ref, ...), custom_call_target="tpu_custom_call" | custom-call | tf_op jit(solution)/shard_map/corner/pallas_call | solution.py:547
  15.0 4.9 %collective-permute-start.2 = (bf16[2,176,512]{2,1,0:T(8,128)(2,1)}, bf16[2,176,512]{2,1,0:T(8,128)(2,1)S(1)}, u32[]{:S(2)}, u32[]{:S(2)}) collective-permute-start(bf16[2,176,512]{2,1,0:T(8,128)(2,1)} %get-tuple-element.68), channel_id=1, source_target_pairs={{0,8},{8,16},{16,24},{1,9},{9,17},{17,25},{2,10},{10,18},{18,26},{... | collective-permute-start | bytes 1081352 | tf_op jit(solution)/shard_map/ppermute | solution.py:553
  20.0 1.9 %collective-permute-start.3 = (bf16[2,176,512]{2,1,0:T(8,128)(2,1)}, bf16[2,176,512]{2,1,0:T(8,128)(2,1)S(1)}, u32[]{:S(2)}, u32[]{:S(2)}) collective-permute-start(bf16[2,176,512]{2,1,0:T(8,128)(2,1)} %get-tuple-element.69), channel_id=1, source_target_pairs={{8,0},{16,8},{24,16},{9,1},{17,9},{25,17},{10,2},{18,10},{26,18},{... | collective-permute-start | bytes 1081352 | tf_op jit(solution)/shard_map/ppermute | solution.py:554
  21.9 0.1 stack.24.info_ref
  22.0 2.6 %collective-permute-done.2.a_ref = bf16[2,176,512]{2,1,0:T(8,128)(2,1)S(1)} collective-permute-done((bf16[2,176,512]{2,1,0:T(8,128)(2,1)}, bf16[2,176,512]{2,1,0:T(8,128)(2,1)S(1)}, u32[]{:S(2)}, u32[]{:S(2)}) %collective-permute-start.2) | collective-permute-done | bytes 360480 | tf_op jit(solution)/shard_map/ppermute | solution.py:553
  24.6 4.3 %collective-permute-done.3.b_ref = bf16[2,176,512]{2,1,0:T(8,128)(2,1)S(1)} collective-permute-done((bf16[2,176,512]{2,1,0:T(8,128)(2,1)}, bf16[2,176,512]{2,1,0:T(8,128)(2,1)S(1)}, u32[]{:S(2)}, u32[]{:S(2)}) %collective-permute-start.3) | collective-permute-done | bytes 360480 | tf_op jit(solution)/shard_map/ppermute | solution.py:554
  28.9 3.6 %attend_fwd.3 = (bf16[256,256]{1,0:T(8,128)(2,1)S(1)}, bf16[256,1024]{1,0:T(8,128)(2,1)S(1)}, f32[4,512,256]{2,1,0:T(8,128)S(1)}, bf16[896,256]{1,0:T(8,128)(2,1)S(1)}, bf16[896,256]{1,0:T(8,128)(2,1)S(1)}) custom-call(s32[6]{0:T(128)S(1)} %stack.24.info_ref, bf16[256,512]{1,0:T(8,128)(2,1)S(1)} %bitcast.18, bf16[256,512]{1,0:T(8,128)(2,1)S(1)} %bitcast.23, ...), custom_call_target="tpu_custom_call" | custom-call | tf_op jit(solution)/shard_map/attend_fwd/pallas_call | solution.py:560
  32.5 0.0 copy-start.6
  32.5 0.1 collective-permute-start.4
  32.6 3.6 %attend_fwd.2 = (bf16[256,256]{1,0:T(8,128)(2,1)S(1)}, f32[256,1024]{1,0:T(8,128)S(1)}, f32[4,512,256]{2,1,0:T(8,128)S(1)}, bf16[896,256]{1,0:T(8,128)(2,1)S(1)}, bf16[896,256]{1,0:T(8,128)(2,1)S(1)}) custom-call(s32[6]{0:T(128)S(1)} %stack.24.info_ref, bf16[256,512]{1,0:T(8,128)(2,1)S(1)} %bitcast.19, bf16[256,512]{1,0:T(8,128)(2,1)S(1)} %bitcast.24, ...), custom_call_target="tpu_custom_call" | custom-call | tf_op jit(solution)/shard_map/attend_fwd/pallas_call | solution.py:560
  36.2 0.7 halve.2
  36.9 0.1 collective-permute-start.5
  37.0 3.3 %attend_bwd.2 = (bf16[256,256]{1,0:T(8,128)(2,1)S(1)}, bf16[2,192,256]{2,1,0:T(8,128)(2,1)S(1)}, bf16[2,192,256]{2,1,0:T(8,128)(2,1)S(1)}, f32[2,256,256]{2,1,0:...) custom-call(s32[6]{0:T(128)S(1)} %stack.24.info_ref, bf16[256,512]{1,0:T(8,128)(2,1)S(1)} %bitcast.20, ...), custom_call_target="tpu_custom_call" | custom-call | tf_op jit(solution)/shard_map/attend_bwd/pallas_call | solution.py:592
  40.4 2.2 %collective-permute-done.5.got_ref = bf16[128,1024]{1,0:T(8,128)(2,1)S(1)} collective-permute-done((bf16[128,1024]{1,0:T(8,128)(2,1)S(1)}, bf16[128,1024]{1,0:T(8,128)(2,1)S(1)}, u32[]{:S(2)}, u32[]{:S(2)}) %collective-permute-start.5) | collective-permute-done | bytes 262176 | tf_op jit(solution)/shard_map/ppermute | solution.py:409
  42.5 0.6 halve.3
  43.1 0.0 copy-start.1
  43.2 3.9 %attend_bwd.3 = (bf16[256,512]{1,0:T(8,128)(2,1)}, bf16[2,192,512]{2,1,0:T(8,128)(2,1)S(1)}, bf16[2,192,512]{2,1,0:T(8,128)(2,1)S(1)}, f32[2,256,256]{2,1,0:T(8,...) custom-call(s32[6]{0:T(128)S(1)} %stack.24.info_ref, bf16[256,512]{1,0:T(8,128)(2,1)S(1)} %bitcast.21, ...), custom_call_target="tpu_custom_call" | custom-call | tf_op jit(solution)/shard_map/attend_bwd/pallas_call | solution.py:592
  47.1 3.2 %collective-permute-start.8 = (bf16[2,192,512]{2,1,0:T(8,128)(2,1)S(1)}, bf16[2,192,512]{2,1,0:T(8,128)(2,1)S(1)}, u32[]{:S(2)}, u32[]{:S(2)}) collective-permute-start(bf16[2,192,512]{2,1,0:T(8,128)(2,1)S(1)} %get-tuple-element.93), channel_id=1, source_target_pairs={{8,0},{16,8},{24,16},{9,1},{17,9},{25,17},{10,2},{18,10},{26,18},{... | collective-permute-start | bytes 1179656 | tf_op jit(solution)/shard_map/ppermute | solution.py:616
  50.3 2.5 %collective-permute-start.9 = (bf16[2,192,512]{2,1,0:T(8,128)(2,1)S(1)}, bf16[2,192,512]{2,1,0:T(8,128)(2,1)S(1)}, u32[]{:S(2)}, u32[]{:S(2)}) collective-permute-start(bf16[2,192,512]{2,1,0:T(8,128)(2,1)S(1)} %get-tuple-element.94), channel_id=1, source_target_pairs={{0,8},{8,16},{16,24},{1,9},{9,17},{17,25},{2,10},{10,18},{18,26},{... | collective-permute-start | bytes 1179656 | tf_op jit(solution)/shard_map/ppermute | solution.py:617
  52.8 0.1 collective-permute-start.6
  52.9 1.2 %bias_fold.1.bias_ref = f32[8,256]{1,0:T(8,128)S(1)} custom-call(s32[6]{0:T(128)S(1)} %stack.24.info_ref, f32[416,128]{1,0:T(8,128)S(1)} %get-tuple-element.84.xs_ref, f32[416,128]{1,0:T(8,128)S(1)} %get-tuple-element.92.xk_ref), custom_call_target="tpu_custom_call" | custom-call | tf_op jit(solution)/shard_map/bias_fold/pallas_call | solution.py:620
  54.1 4.6 %collective-permute-done.6.got_ref = bf16[64,1024]{1,0:T(8,128)(2,1)S(1)} collective-permute-done((bf16[64,1024]{1,0:T(8,128)(2,1)S(1)}, bf16[64,1024]{1,0:T(8,128)(2,1)S(1)}, u32[]{:S(2)}, u32[]{:S(2)}) %collective-permute-start.6) | collective-permute-done | bytes 131104 | tf_op jit(solution)/shard_map/ppermute | solution.py:409
  58.8 2.1 %collective-permute-start.7 = (bf16[72,1024]{1,0:T(8,128)(2,1)S(1)}, bf16[72,1024]{1,0:T(8,128)(2,1)S(1)}, u32[]{:S(2)}, u32[]{:S(2)}) collective-permute-start(bf16[72,1024]{1,0:T(8,128)(2,1)S(1)} %meet.1.own_ref), channel_id=1, source_target_pairs={{0,2},{1,3},{2,0},{3,1},{4,6},{5,7},{6,4},{7,5},{8,12},{9,13},{10,... | collective-permute-start | bytes 442376 | tf_op jit(solution)/shard_map/ppermute | solution.py:409
  60.8 1.8 %project.1 = bf16[256,1024]{1,0:T(8,128)(2,1)} custom-call(s32[6]{0:T(128)S(1)} %stack.24.info_ref, bf16[256,256]{1,0:T(8,128)(2,1)S(1)} %get-tuple-element.95.s_ref, bf16[256,256]{1,0:T(8,128)(2,1)S(1)} %get-tuple-element.96.k_ref, bf16[512,1024]{1,0:T(8,128)(2,1)S(1)} %copy-done.1), custom_call_target="tpu_custom_call" | custom-call | tf_op jit(solution)/shard_map/project/pallas_call | solution.py:628
  62.6 2.0 %collective-permute-done.7.got_ref = bf16[72,1024]{1,0:T(8,128)(2,1)S(1)} collective-permute-done((bf16[72,1024]{1,0:T(8,128)(2,1)S(1)}, bf16[72,1024]{1,0:T(8,128)(2,1)S(1)}, u32[]{:S(2)}, u32[]{:S(2)}) %collective-permute-start.7) | collective-permute-done | bytes 147488 | tf_op jit(solution)/shard_map/ppermute | solution.py:409
  64.7 0.0 collective-permute-done.9.a_ref
  64.7 1.6 %collective-permute-start.10 = (bf16[72,1024]{1,0:T(8,128)(2,1)S(1)}, bf16[72,1024]{1,0:T(8,128)(2,1)S(1)}, u32[]{:S(2)}, u32[]{:S(2)}) collective-permute-start(bf16[72,1024]{1,0:T(8,128)(2,1)S(1)} %total.2.own_ref), channel_id=1, source_target_pairs={{0,4},{1,5},{2,6},{3,7},{4,0},{5,1},{6,2},{7,3},{8,10},{9,11},{10,... | collective-permute-start | bytes 442376 | tf_op jit(solution)/shard_map/ppermute | solution.py:409
  66.2 0.9 %side.1 = (bf16[2,96,512]{2,1,0:T(8,128)(2,1)S(1)}, bf16[2,96,512]{2,1,0:T(8,128)(2,1)S(1)}) custom-call(s32[6]{0:T(128)S(1)} %stack.24.info_ref, f32[2,256,256]{2,1,0:T(8,128)S(1)} %get-tuple-element.104.ss_ref, f32[2,256,256]{2,1,0:T(8,128)S(1)} %get-tuple-element.105.sk_ref, bf16[2,192,512]{2,1,0:T(8,128)(2,1)S(1)} %collective-permute-done.9.a_ref, ...), custom_call_target="tpu_custom_call" | custom-call | tf_op jit(solution)/shard_map/side/pallas_call | solution.py:644
  67.2 2.3 %collective-permute-start.12 = (bf16[2,96,512]{2,1,0:T(8,128)(2,1)S(1)}, bf16[2,96,512]{2,1,0:T(8,128)(2,1)S(1)}, u32[]{:S(2)}, u32[]{:S(2)}) collective-permute-start(bf16[2,96,512]{2,1,0:T(8,128)(2,1)S(1)} %get-tuple-element.106), channel_id=1, source_target_pairs={{0,7},{1,0},{2,1},{3,2},{4,3},{5,4},{6,5},{7,6},{8,15},{9,8},{10,9... | collective-permute-start | bytes 589832 | tf_op jit(solution)/shard_map/ppermute | solution.py:652
  69.5 4.5 %collective-permute-start.11 = (bf16[72,1024]{1,0:T(8,128)(2,1)S(1)}, bf16[72,1024]{1,0:T(8,128)(2,1)S(1)}, u32[]{:S(2)}, u32[]{:S(2)}) collective-permute-start(bf16[72,1024]{1,0:T(8,128)(2,1)S(1)} %total.3.own_ref), channel_id=1, source_target_pairs={{0,1},{1,0},{2,3},{3,2},{4,5},{5,4},{6,7},{7,6},{8,24},{9,25},{10,... | collective-permute-start | bytes 442376 | tf_op jit(solution)/shard_map/ppermute | solution.py:409
  74.0 2.8 %collective-permute-done.11.got_ref = bf16[72,1024]{1,0:T(8,128)(2,1)S(1)} collective-permute-done((bf16[72,1024]{1,0:T(8,128)(2,1)S(1)}, bf16[72,1024]{1,0:T(8,128)(2,1)S(1)}, u32[]{:S(2)}, u32[]{:S(2)}) %collective-permute-start.11) | collective-permute-done | bytes 147488 | tf_op jit(solution)/shard_map/ppermute | solution.py:409
  76.8 0.6 grow.2.own_ref
  77.4 0.7 collective-permute-done.13.w_ref
  78.1 1.9 %collective-permute-start.14 = (bf16[136,1024]{1,0:T(8,128)(2,1)S(1)}, bf16[136,1024]{1,0:T(8,128)(2,1)S(1)}, u32[]{:S(2)}, u32[]{:S(2)}) collective-permute-start(bf16[136,1024]{1,0:T(8,128)(2,1)S(1)} %grow.2.own_ref), channel_id=1, source_target_pairs={{0,16},{1,17},{2,18},{3,19},{4,20},{5,21},{6,22},{7,23},{8,9},{9,8... | collective-permute-start | bytes 835592 | tf_op jit(solution)/shard_map/ppermute | solution.py:409
  80.0 4.2 %collective-permute-done.14.got_ref = bf16[136,1024]{1,0:T(8,128)(2,1)S(1)} collective-permute-done((bf16[136,1024]{1,0:T(8,128)(2,1)S(1)}, bf16[136,1024]{1,0:T(8,128)(2,1)S(1)}, u32[]{:S(2)}, u32[]{:S(2)}) %collective-permute-start.14) | collective-permute-done | bytes 278560 | tf_op jit(solution)/shard_map/ppermute | solution.py:409
  84.2 0.6 grow.3.own_ref
  84.8 3.4 %collective-permute-start.15 = (bf16[264,1024]{1,0:T(8,128)(2,1)S(1)}, bf16[264,1024]{1,0:T(8,128)(2,1)S(1)}, u32[]{:S(2)}, u32[]{:S(2)}) collective-permute-start(bf16[264,1024]{1,0:T(8,128)(2,1)S(1)} %grow.3.own_ref), channel_id=1, source_target_pairs={{0,8},{1,9},{2,10},{3,11},{4,12},{5,13},{6,14},{7,15},{8,0},{9,1},... | collective-permute-start | bytes 1622024 | tf_op jit(solution)/shard_map/ppermute | solution.py:409
  88.2 1.7 %join.1 = (bf16[256,512]{1,0:T(8,128)(2,1)}, bf16[256,512]{1,0:T(8,128)(2,1)}) custom-call(s32[6]{0:T(128)S(1)} %stack.24.info_ref, f32[2,256,256]{2,1,0:T(8,128)S(1)} %get-tuple-element.99.ms_ref, f32[2,256,256]{2,1,0:T(8,128)S(1)} %get-tuple-element.100.mk_ref, bf16[2,192,512]{2,1,0:T(8,128)(2,1)S(1)} %collective-permute-done.9.a_ref, ...), custom_call_target="tpu_custom_call" | custom-call | tf_op jit(solution)/shard_map/join/pallas_call | solution.py:665
  89.9 1.6 %last.1 = (bf16[512,1024]{1,0:T(8,128)(2,1)}, f32[13,8,13]{2,1,0:T(8,128)}) custom-call(s32[6]{0:T(128)S(1)} %stack.24.info_ref, bf16[264,1024]{1,0:T(8,128)(2,1)S(1)} %grow.3.own_ref, bf16[264,1024]{1,0:T(8,128)(2,1)S(1)} %collective-permute-done.15.got_ref), custom_call_target="tpu_custom_call" | custom-call | tf_op jit(solution)/shard_map/last/pallas_call | solution.py:575
  (20 shorter events, 0.2 us)
Async XLA Ops:
  0.6 28.3 %copy-start.4 = (bf16[16,16,512]{2,1,0:T(8,128)(2,1)S(1)}, bf16[16,16,512]{2,1,0:T(8,128)(2,1)}, u32[]{:S(2)}) copy-start(bf16[16,16,512]{2,1,0:T(8,128)(2,1)} %param.8) | copy-start | bytes 786436
  0.6 28.3 %copy-start.3 = (bf16[16,16,512]{2,1,0:T(8,128)(2,1)S(1)}, bf16[16,16,512]{2,1,0:T(8,128)(2,1)}, u32[]{:S(2)}) copy-start(bf16[16,16,512]{2,1,0:T(8,128)(2,1)} %param.7) | copy-start | bytes 786436
  0.7 28.3 %copy-start = (bf16[16,16,1024]{2,1,0:T(8,128)(2,1)S(1)}, bf16[16,16,1024]{2,1,0:T(8,128)(2,1)}, u32[]{:S(2)}) copy-start(bf16[16,16,1024]{2,1,0:T(8,128)(2,1)} %param.11) | copy-start | bytes 1572868
  0.7 28.3 %copy-start.2 = (bf16[16,16,512]{2,1,0:T(8,128)(2,1)S(1)}, bf16[16,16,512]{2,1,0:T(8,128)(2,1)}, u32[]{:S(2)}) copy-start(bf16[16,16,512]{2,1,0:T(8,128)(2,1)} %param.6) | copy-start | bytes 786436
  2.2 9.9 %collective-permute-start = (bf16[2,96,512]{2,1,0:T(8,128)(2,1)S(1)}, bf16[2,96,512]{2,1,0:T(8,128)(2,1)S(1)}, u32[]{:S(2)}, u32[]{:S(2)}) collective-permute-start(bf16[2,96,512]{2,1,0:T(8,128)(2,1)S(1)} %get-tuple-element.61), channel_id=1, source_target_pairs={{0,1},{1,2},{2,3},{3,4},{4,5},{5,6},{6,7},{7,0},{8,9},{9,10},{10,1... | collective-permute-start | bytes 589832 | tf_op jit(solution)/shard_map/ppermute | solution.py:533
  4.3 9.7 %collective-permute-start.1 = (bf16[2,96,512]{2,1,0:T(8,128)(2,1)S(1)}, bf16[2,96,512]{2,1,0:T(8,128)(2,1)S(1)}, u32[]{:S(2)}, u32[]{:S(2)}) collective-permute-start(bf16[2,96,512]{2,1,0:T(8,128)(2,1)S(1)} %get-tuple-element.62), channel_id=1, source_target_pairs={{0,7},{1,0},{2,1},{3,2},{4,3},{5,4},{6,5},{7,6},{8,15},{9,8},{10,9... | collective-permute-start | bytes 589832 | tf_op jit(solution)/shard_map/ppermute | solution.py:534
  7.4 0.8 copy-start.7
  12.1 7.9 %copy-start.5 = (bf16[256,512]{1,0:T(8,128)(2,1)}, bf16[256,512]{1,0:T(8,128)(2,1)S(1)}, u32[]{:S(2)}) copy-start(bf16[256,512]{1,0:T(8,128)(2,1)S(1)} %get-tuple-element.80.g_ref) | copy-start | bytes 786436
  15.0 9.6 %collective-permute-start.2 = (bf16[2,176,512]{2,1,0:T(8,128)(2,1)}, bf16[2,176,512]{2,1,0:T(8,128)(2,1)S(1)}, u32[]{:S(2)}, u32[]{:S(2)}) collective-permute-start(bf16[2,176,512]{2,1,0:T(8,128)(2,1)} %get-tuple-element.68), channel_id=1, source_target_pairs={{0,8},{8,16},{16,24},{1,9},{9,17},{17,25},{2,10},{10,18},{18,26},{... | collective-permute-start | bytes 1081352 | tf_op jit(solution)/shard_map/ppermute | solution.py:553
  20.0 9.0 %collective-permute-start.3 = (bf16[2,176,512]{2,1,0:T(8,128)(2,1)}, bf16[2,176,512]{2,1,0:T(8,128)(2,1)S(1)}, u32[]{:S(2)}, u32[]{:S(2)}) collective-permute-start(bf16[2,176,512]{2,1,0:T(8,128)(2,1)} %get-tuple-element.69), channel_id=1, source_target_pairs={{8,0},{16,8},{24,16},{9,1},{17,9},{25,17},{10,2},{18,10},{26,18},{... | collective-permute-start | bytes 1081352 | tf_op jit(solution)/shard_map/ppermute | solution.py:554
  32.5 4.5 %copy-start.6 = (bf16[256,512]{1,0:T(8,128)(2,1)S(1)}, bf16[256,512]{1,0:T(8,128)(2,1)}, u32[]{:S(2)}) copy-start(bf16[256,512]{1,0:T(8,128)(2,1)} %copy-done.5) | copy-start | bytes 786436
  32.5 3.7 %collective-permute-start.4 = (bf16[256,1024]{1,0:T(8,128)(2,1)S(1)}, bf16[256,1024]{1,0:T(8,128)(2,1)S(1)}, u32[]{:S(2)}, u32[]{:S(2)}) collective-permute-start(bf16[256,1024]{1,0:T(8,128)(2,1)S(1)} %get-tuple-element.72), channel_id=1, source_target_pairs={{0,8},{1,9},{2,10},{3,11},{4,12},{5,13},{6,14},{7,15},{8,0},{9,1},... | collective-permute-start | bytes 1572872 | tf_op jit(solution)/shard_map/ppermute | solution.py:409
  36.9 5.6 %collective-permute-start.5 = (bf16[128,1024]{1,0:T(8,128)(2,1)S(1)}, bf16[128,1024]{1,0:T(8,128)(2,1)S(1)}, u32[]{:S(2)}, u32[]{:S(2)}) collective-permute-start(bf16[128,1024]{1,0:T(8,128)(2,1)S(1)} %get-tuple-element.75), channel_id=1, source_target_pairs={{0,16},{1,17},{2,18},{3,19},{4,20},{5,21},{6,22},{7,23},{8,9},{9,8... | collective-permute-start | bytes 786440 | tf_op jit(solution)/shard_map/ppermute | solution.py:409
  43.1 17.7 %copy-start.1 = (bf16[512,1024]{1,0:T(8,128)(2,1)S(1)}, bf16[512,1024]{1,0:T(8,128)(2,1)}, u32[]{:S(2)}) copy-start(bf16[512,1024]{1,0:T(8,128)(2,1)} %w_ref.1) | copy-start | bytes 3145732
  47.1 17.6 %collective-permute-start.8 = (bf16[2,192,512]{2,1,0:T(8,128)(2,1)S(1)}, bf16[2,192,512]{2,1,0:T(8,128)(2,1)S(1)}, u32[]{:S(2)}, u32[]{:S(2)}) collective-permute-start(bf16[2,192,512]{2,1,0:T(8,128)(2,1)S(1)} %get-tuple-element.93), channel_id=1, source_target_pairs={{8,0},{16,8},{24,16},{9,1},{17,9},{25,17},{10,2},{18,10},{26,18},{... | collective-permute-start | bytes 1179656 | tf_op jit(solution)/shard_map/ppermute | solution.py:616
  50.3 14.4 %collective-permute-start.9 = (bf16[2,192,512]{2,1,0:T(8,128)(2,1)S(1)}, bf16[2,192,512]{2,1,0:T(8,128)(2,1)S(1)}, u32[]{:S(2)}, u32[]{:S(2)}) collective-permute-start(bf16[2,192,512]{2,1,0:T(8,128)(2,1)S(1)} %get-tuple-element.94), channel_id=1, source_target_pairs={{0,8},{8,16},{16,24},{1,9},{9,17},{17,25},{2,10},{10,18},{18,26},{... | collective-permute-start | bytes 1179656 | tf_op jit(solution)/shard_map/ppermute | solution.py:617
  52.8 5.9 %collective-permute-start.6 = (bf16[64,1024]{1,0:T(8,128)(2,1)S(1)}, bf16[64,1024]{1,0:T(8,128)(2,1)S(1)}, u32[]{:S(2)}, u32[]{:S(2)}) collective-permute-start(bf16[64,1024]{1,0:T(8,128)(2,1)S(1)} %get-tuple-element.78), channel_id=1, source_target_pairs={{0,1},{1,0},{2,3},{3,2},{4,5},{5,4},{6,7},{7,6},{8,24},{9,25},{10,... | collective-permute-start | bytes 393224 | tf_op jit(solution)/shard_map/ppermute | solution.py:409
  58.8 5.8 %collective-permute-start.7 = (bf16[72,1024]{1,0:T(8,128)(2,1)S(1)}, bf16[72,1024]{1,0:T(8,128)(2,1)S(1)}, u32[]{:S(2)}, u32[]{:S(2)}) collective-permute-start(bf16[72,1024]{1,0:T(8,128)(2,1)S(1)} %meet.1.own_ref), channel_id=1, source_target_pairs={{0,2},{1,3},{2,0},{3,1},{4,6},{5,7},{6,4},{7,5},{8,12},{9,13},{10,... | collective-permute-start | bytes 442376 | tf_op jit(solution)/shard_map/ppermute | solution.py:409
  64.7 4.8 %collective-permute-start.10 = (bf16[72,1024]{1,0:T(8,128)(2,1)S(1)}, bf16[72,1024]{1,0:T(8,128)(2,1)S(1)}, u32[]{:S(2)}, u32[]{:S(2)}) collective-permute-start(bf16[72,1024]{1,0:T(8,128)(2,1)S(1)} %total.2.own_ref), channel_id=1, source_target_pairs={{0,4},{1,5},{2,6},{3,7},{4,0},{5,1},{6,2},{7,3},{8,10},{9,11},{10,... | collective-permute-start | bytes 442376 | tf_op jit(solution)/shard_map/ppermute | solution.py:409
  67.2 10.2 %collective-permute-start.12 = (bf16[2,96,512]{2,1,0:T(8,128)(2,1)S(1)}, bf16[2,96,512]{2,1,0:T(8,128)(2,1)S(1)}, u32[]{:S(2)}, u32[]{:S(2)}) collective-permute-start(bf16[2,96,512]{2,1,0:T(8,128)(2,1)S(1)} %get-tuple-element.106), channel_id=1, source_target_pairs={{0,7},{1,0},{2,1},{3,2},{4,3},{5,4},{6,5},{7,6},{8,15},{9,8},{10,9... | collective-permute-start | bytes 589832 | tf_op jit(solution)/shard_map/ppermute | solution.py:652
  69.5 8.6 %collective-permute-start.13 = (bf16[2,96,512]{2,1,0:T(8,128)(2,1)S(1)}, bf16[2,96,512]{2,1,0:T(8,128)(2,1)S(1)}, u32[]{:S(2)}, u32[]{:S(2)}) collective-permute-start(bf16[2,96,512]{2,1,0:T(8,128)(2,1)S(1)} %get-tuple-element.107), channel_id=1, source_target_pairs={{0,1},{1,2},{2,3},{3,4},{4,5},{5,6},{6,7},{7,0},{8,9},{9,10},{10,1... | collective-permute-start | bytes 589832 | tf_op jit(solution)/shard_map/ppermute | solution.py:653
  69.5 7.3 %collective-permute-start.11 = (bf16[72,1024]{1,0:T(8,128)(2,1)S(1)}, bf16[72,1024]{1,0:T(8,128)(2,1)S(1)}, u32[]{:S(2)}, u32[]{:S(2)}) collective-permute-start(bf16[72,1024]{1,0:T(8,128)(2,1)S(1)} %total.3.own_ref), channel_id=1, source_target_pairs={{0,1},{1,0},{2,3},{3,2},{4,5},{5,4},{6,7},{7,6},{8,24},{9,25},{10,... | collective-permute-start | bytes 442376 | tf_op jit(solution)/shard_map/ppermute | solution.py:409
  78.1 6.1 %collective-permute-start.14 = (bf16[136,1024]{1,0:T(8,128)(2,1)S(1)}, bf16[136,1024]{1,0:T(8,128)(2,1)S(1)}, u32[]{:S(2)}, u32[]{:S(2)}) collective-permute-start(bf16[136,1024]{1,0:T(8,128)(2,1)S(1)} %grow.2.own_ref), channel_id=1, source_target_pairs={{0,16},{1,17},{2,18},{3,19},{4,20},{5,21},{6,22},{7,23},{8,9},{9,8... | collective-permute-start | bytes 835592 | tf_op jit(solution)/shard_map/ppermute | solution.py:409
  84.8 5.1 %collective-permute-start.15 = (bf16[264,1024]{1,0:T(8,128)(2,1)S(1)}, bf16[264,1024]{1,0:T(8,128)(2,1)S(1)}, u32[]{:S(2)}, u32[]{:S(2)}) collective-permute-start(bf16[264,1024]{1,0:T(8,128)(2,1)S(1)} %grow.3.own_ref), channel_id=1, source_target_pairs={{0,8},{1,9},{2,10},{3,11},{4,12},{5,13},{6,14},{7,15},{8,0},{9,1},... | collective-permute-start | bytes 1622024 | tf_op jit(solution)/shard_map/ppermute | solution.py:409

commit v5 on v4

--- a/solution.py
+++ b/solution.py
@@ -109,7 +109,7 @@
 
 
 def pack_kernel(
-    rows, cols, k_hbm, v_hbm, east_ref, west_ref, down_ref, up_ref, x_ref, sem_ref
+    rows, cols, info_ref, k_hbm, v_hbm, east_ref, west_ref, a_ref, b_ref, x_ref, sem_ref
 ):
     copies = [
         pltpu.make_async_copy(ref, x_ref.at[i], sem_ref.at[i])
@@ -120,29 +120,34 @@
     pick_east = take_cols(rows, cols, cols - RAD)
     pick_west = take_cols(rows, cols, 0)
     edge = RAD * cols
+    odd = info_ref[2] == 1
     for i, copy in enumerate(copies):
         copy.wait()
         x = x_ref[i]
         east_ref[i] = dot(pick_east, x).astype(BF16)
         west_ref[i] = dot(pick_west, x).astype(BF16)
-        down_ref[i] = x[(rows - RAD) * cols :]
-        up_ref[i] = x[:edge]
-
-
-def corner_kernel(rows, cols, w_ref, e_ref, own_down_ref, own_up_ref, down_ref, up_ref):
+        down = x[(rows - RAD) * cols :]
+        up = x[:edge]
+        a_ref[i] = jnp.where(odd, up, down)
+        b_ref[i] = jnp.where(odd, down, up)
+
+
+def corner_kernel(rows, own, info_ref, w_ref, e_ref, *refs):
+    out_ref = refs[-1]
     half = RAD * RAD
-    edge = RAD * cols
     n = down_iota(CORNER)
     src = along_iota(rows * RAD)
-    for ref, own_ref, first in (
-        (down_ref, own_down_ref, (rows - RAD) * RAD), (up_ref, own_up_ref, 0)
-    ):
-        pick_w = hot((src == first + n) & (n < half))
-        pick_e = hot((src == first + n - half) & (n >= half) & (n < 2 * half))
-        for i in range(2):
-            side = dot(pick_w, w_ref[i]) + dot(pick_e, e_ref[i])
-            ref[i, :edge, :] = own_ref[i]
-            ref[i, edge:, :] = side.astype(BF16)
+    odd = info_ref[2] == 1
+    up = odd if own else jnp.logical_not(odd)
+    first = jnp.where(up, 0, (rows - RAD) * RAD)
+    pick_w = hot((src == first + n) & (n < half))
+    pick_e = hot((src == first + n - half) & (n >= half) & (n < 2 * half))
+    for i in range(2):
+        side = dot(pick_w, w_ref[i]) + dot(pick_e, e_ref[i])
+        edge = out_ref.shape[1] - CORNER
+        if own:
+            out_ref[i, :edge, :] = refs[0][i]
+        out_ref[i, edge:, :] = side.astype(BF16)
 
 
 def prepare_kernel(
@@ -198,8 +203,8 @@
     return pos - over(iota2(shape, 1), cols)[1]
 
 
-def assemble(out_ref, i, rows, cols, cols_pad, own, refs, group):
-    w_ref, e_ref, a_ref, b_ref = refs
+def assemble(out_ref, i, rows, cols, cols_pad, own, refs, group, odd):
+    w_ref, e_ref, a_ref, b_ref, c_ref = refs
     edge = RAD * cols
     side = dot(put_cols(rows, SLOTS, 0), w_ref[i, :, group])
     side = (side + dot(put_cols(rows, SLOTS, RAD), e_ref[i, :, group])).astype(BF16)
@@ -208,12 +213,18 @@
         out_ref[lo : lo + cols, :] = own[r * cols : (r + 1) * cols, group]
         out_ref[lo + cols : lo + cols + SLOTS, :] = side[r * SLOTS : (r + 1) * SLOTS]
     put = put_corner(SLOTS)
-    for first, o_ref in ((0, a_ref), (RAD + rows, b_ref)):
-        side = dot(put, o_ref[i, edge:, group]).astype(BF16)
+    below = (RAD + rows) * cols_pad
+    corner_a = a_ref[i, edge:, group]
+    for first, o_ref, corner in (
+        (jnp.where(odd, 0, below), a_ref, corner_a),
+        (jnp.where(odd, below, 0), b_ref, c_ref[i, :, group]),
+    ):
+        side = dot(put, corner).astype(BF16)
         for r in range(RAD):
-            lo = (first + r) * cols_pad
-            out_ref[lo : lo + cols, :] = o_ref[i, r * cols : (r + 1) * cols, group]
-            out_ref[lo + cols : lo + cols + SLOTS, :] = side[r * SLOTS : (r + 1) * SLOTS]
+            lo = pl.multiple_of(first + r * cols_pad, cols_pad)
+            out_ref[pl.ds(lo, cols), :] = o_ref[i, r * cols : (r + 1) * cols, group]
+            lo = pl.multiple_of(first + r * cols_pad + cols, cols)
+            out_ref[pl.ds(lo, SLOTS), :] = side[r * SLOTS : (r + 1) * SLOTS]
 
 
 def group_lanes(group, lanes):
@@ -221,15 +232,16 @@
 
 
 def fwd_kernel(
-    sizes, n, info_ref, q_ref, k_ref, v_ref, w_ref, e_ref, a_ref, b_ref,
+    sizes, n, info_ref, q_ref, k_ref, v_ref, w_ref, e_ref, a_ref, b_ref, c_ref,
     bias_ref, cot_ref, out_ref, weight_ref, p_ref, ko_ref, vo_ref, vt_ref, at_ref,
 ):
     lat_dev, cols, cols_pad, head_size, rows_all = sizes
     scale = head_size ** (-0.5)
     group = group_lanes(info_ref[n], GROUP * head_size)
-    refs = (w_ref, e_ref, a_ref, b_ref)
-    assemble(ko_ref, 0, lat_dev, cols, cols_pad, k_ref, refs, group)
-    assemble(vo_ref, 1, lat_dev, cols, cols_pad, v_ref, refs, group)
+    refs = (w_ref, e_ref, a_ref, b_ref, c_ref)
+    odd = info_ref[2] == 1
+    assemble(ko_ref, 0, lat_dev, cols, cols_pad, k_ref, refs, group, odd)
+    assemble(vo_ref, 1, lat_dev, cols, cols_pad, v_ref, refs, group, odd)
     vt_ref[...] = vo_ref[...].T
     mask = head_mask(cols, head_size)
     pick = picker(cols)
@@ -253,7 +265,7 @@
 
 
 def bwd_kernel(sizes, n, info_ref, q_ref, g_ref, p_ref, k_ref, v_ref, *refs):
-    dq_ref, top_ref, bot_ref, mid_ref, side_ref, x_ref, kt_ref, dk_ref, dv_ref, db_ref = refs[-10:]
+    dq_ref, sa_ref, sb_ref, mid_ref, side_ref, x_ref, kt_ref, dk_ref, dv_ref, db_ref = refs[-10:]
     before = refs[:-10]
     lat_dev, cols, cols_pad, head_size, rows_all = sizes
     scale = head_size ** (-0.5)
@@ -268,8 +280,8 @@
     if before:
         other = group_lanes(1 - which, GROUP * head_size)
         dq_ref[:, other] = before[0][...]
-        top_ref[:, :, other] = before[1][...]
-        bot_ref[:, :, other] = before[2][...]
+        sa_ref[:, :, other] = before[1][...]
+        sb_ref[:, :, other] = before[2][...]
     kt_ref[...] = k_ref[...].T
     dk_ref[...] = jnp.zeros_like(dk_ref)
     dv_ref[...] = jnp.zeros_like(dv_ref)
@@ -293,9 +305,13 @@
         dk_ref[ws, :] += dot(sgb, q_bd)
         dv_ref[ws, :] += dot(p.astype(BF16), g_bd)
     edge = RAD * cols_pad
+    odd = info_ref[2] == 1
+    low_rows = edge + lat_dev * cols_pad
+    first_a = pl.multiple_of(jnp.where(odd, 0, low_rows), cols_pad)
+    first_b = pl.multiple_of(jnp.where(odd, low_rows, 0), cols_pad)
     for i, ref in enumerate((dk_ref, dv_ref)):
-        top_ref[i, :, mine] = ref[:edge, :].astype(BF16)
-        bot_ref[i, :, mine] = ref[edge + lat_dev * cols_pad :, :].astype(BF16)
+        sa_ref[i, :, mine] = ref[pl.ds(first_a, edge), :].astype(BF16)
+        sb_ref[i, :, mine] = ref[pl.ds(first_b, edge), :].astype(BF16)
         for r in range(lat_dev):
             lo = (RAD + r) * cols_pad
             mid_ref[i, r * cols : (r + 1) * cols, :] = ref[lo : lo + cols, :]
@@ -341,6 +357,12 @@
     return jnp.concatenate(parts, 0).astype(F32)
 
 
+def strips(info_ref, rows, cols):
+    odd = info_ref[2] == 1
+    last = (rows - RAD) * cols
+    return [pl.multiple_of(jnp.where(odd, x, last - x), cols) for x in (0, last)]
+
+
 def both_groups(info_ref, dst_ref, i, s_ref, k_ref):
     lanes = s_ref.shape[2]
     dst_ref[:, group_lanes(info_ref[0], lanes)] = s_ref[i]
@@ -355,8 +377,8 @@
     pick_east = take_cols(rows, SLOTS, RAD)
     for i in range(2):
         both_groups(info_ref, s_ref, i, ss_ref, sk_ref)
-        s_ref[:edge, :] += lat_terms(a_ref, i, rows, SLOTS, cols_pad, cols)
-        s_ref[(rows - RAD) * SLOTS :, :] += lat_terms(b_ref, i, rows, SLOTS, cols_pad, cols)
+        for ref, first in zip((a_ref, b_ref), strips(info_ref, rows, SLOTS)):
+            s_ref[pl.ds(first, edge), :] += lat_terms(ref, i, rows, SLOTS, cols_pad, cols)
         x = s_ref[...].astype(BF16)
         west_ref[i] = dot(pick_west, x).astype(BF16)
         east_ref[i] = dot(pick_east, x).astype(BF16)
@@ -372,8 +394,8 @@
     for i, out_ref in enumerate((k_ref, v_ref)):
         both_groups(info_ref, s_ref, i, ms_ref, mk_ref)
         s_ref[...] += dot(put_west, w_ref[i]) + dot(put_east, e_ref[i])
-        s_ref[:edge, :] += lat_terms(a_ref, i, rows, cols, cols_pad, 0)
-        s_ref[(rows - RAD) * cols :, :] += lat_terms(b_ref, i, rows, cols, cols_pad, 0)
+        for ref, first in zip((a_ref, b_ref), strips(info_ref, rows, cols)):
+            s_ref[pl.ds(first, edge), :] += lat_terms(ref, i, rows, cols, cols_pad, 0)
         out_ref[...] = s_ref[...].astype(BF16)
 
 
@@ -495,8 +517,9 @@
     norm = (tokens * n_lat * n_lon) ** (-0.5)
     east = [(i, (i + 1) % n_lon) for i in range(n_lon)]
     west = [(i, (i - 1) % n_lon) for i in range(n_lon)]
-    down = [(i, i + 1) for i in range(n_lat - 1)]
-    up = [(i + 1, i) for i in range(n_lat - 1)]
+    pair_a = [(i, i ^ 1) for i in range(n_lat)]
+    pair_b = [(i, i + 1) for i in range(1, n_lat - 1, 2)]
+    pair_b = pair_b + [(j, i) for i, j in pair_b]
     win = (TILE + 2 * RAD) * cols_pad
     tiles = lat_dev // TILE
     lanes_q = TILE * GROUP * lon_dev
@@ -522,16 +545,17 @@
     vmem = pl.BlockSpec(memory_space=pltpu.VMEM)
     hbm = pl.BlockSpec(memory_space=pltpu.HBM)
 
-    to_east, to_west, to_down, to_up = pl.pallas_call(
+    to_east, to_west, own_a, own_b = pl.pallas_call(
         functools.partial(pack_kernel, lat_dev, lon_dev),
-        in_specs=[hbm, hbm],
+        in_specs=[smem, hbm, hbm],
         out_shape=[shape((2, n_side, width))] * 2 + [shape((2, n_edge, width))] * 2,
         scratch_shapes=[pltpu.VMEM((2, tokens, width), BF16), pltpu.SemaphoreType.DMA((2,))],
         compiler_params=room(4),
         name="pack",
-    )(in_hbm(k_flat), in_hbm(v_flat))
+    )(info, in_hbm(k_flat), in_hbm(v_flat))
     from_west = lax.ppermute(to_east, "lon", east)
     from_east = lax.ppermute(to_west, "lon", west)
+    from_b = lax.ppermute(own_b, "lat", pair_b)
     sizes = (lat_dev, lon_dev, cols_pad, head_size, lat_dev * n_lat)
     table, attended_grad = pl.pallas_call(
         functools.partial(prepare_kernel, lon_dev, cols_pad),
@@ -543,23 +567,30 @@
         compiler_params=room(6),
         name="prepare",
     )(rel_bias.transpose(1, 0, 2), in_hbm(cot), in_hbm(out_weight))
-    from_west, from_east, table = lax.optimization_barrier((from_west, from_east, table))
-    corner_down, corner_up = pl.pallas_call(
-        functools.partial(corner_kernel, lat_dev, lon_dev),
-        out_shape=[shape((2, n_edge + CORNER, width))] * 2,
-        compiler_params=room(4),
-        name="corner",
-    )(from_west, from_east, to_down, to_up)
-    from_above = lax.ppermute(corner_down, "lat", down)
-    from_below = lax.ppermute(corner_up, "lat", up)
-
+    from_west, from_east, from_b, table = lax.optimization_barrier(
+        (from_west, from_east, from_b, table)
+    )
+
+    def corner(rows, *own):
+        return pl.pallas_call(
+            functools.partial(corner_kernel, lat_dev, bool(own)),
+            in_specs=[smem] + [vmem] * (2 + len(own)),
+            out_shape=shape((2, rows, width)),
+            compiler_params=room(4),
+            name="corner",
+        )(info, from_west, from_east, *own)
+
+    corner_b = corner(CORNER)
+    corner_b, own_a = lax.optimization_barrier((corner_b, own_a))
+    side_b = lax.ppermute(corner_b, "lat", pair_b)
+    from_a = lax.ppermute(corner(n_edge + CORNER, own_a), "lat", pair_a)
     probs = (tiles, win, lanes_q)
     outer = (n_keys, lanes)
 
     def forward(n, dtype):
         return pl.pallas_call(
             functools.partial(fwd_kernel, sizes, n),
-            in_specs=[smem] + [vmem] * 9,
+            in_specs=[smem] + [vmem] * 10,
             out_shape=[shape((tokens, lanes)), shape((lanes, model), dtype), shape(probs, F32)]
             + [shape(outer)] * 2,
             scratch_shapes=[pltpu.VMEM((lanes, n_keys), BF16), pltpu.VMEM((lanes, tokens), BF16)],
@@ -567,7 +598,7 @@
             name="attend_fwd",
         )(
             info, q_flat, k_flat, v_flat, from_west, from_east,
-            from_above, from_below, table, cot,
+            from_a, from_b, side_b, table, cot,
         )
 
     def step_call(kernel, name, outs, *operands):
@@ -606,15 +637,17 @@
     info_b, send = lax.optimization_barrier((info, send))
     got = swap(send, mesh_shape, rounds[1])
     *before, mid_s, side_s, fold_s = backward(0, info_b, p_s, k_s, v_s)
+    got, fold_s = lax.optimization_barrier((got, fold_s))
     for number in range(2, len(rounds)):
         send, keep = halve(keep, got, number)
         if number == 2:
             info_b, send = lax.optimization_barrier((info, send))
         got = swap(send, mesh_shape, rounds[number])
     after = backward(2, info_b, p_k, k_k, v_k, *before)
-    query_grad, top, bottom, mid_k, side_k, fold_k = after
-    get_below = lax.ppermute(top, "lat", up)
-    get_above = lax.ppermute(bottom, "lat", down)
+    query_grad, strip_a, strip_b, mid_k, side_k, fold_k = after
+    got, strip_a, strip_b, fold_k = lax.optimization_barrier((got, strip_a, strip_b, fold_k))
+    get_b = lax.ppermute(strip_b, "lat", pair_b)
+    get_a = lax.ppermute(strip_a, "lat", pair_a)
 
     count = 256
     bias_local = pl.pallas_call(
@@ -637,8 +670,8 @@
     got = swap(message, mesh_shape, ends[0])
     kernel = functools.partial(total_kernel, None, count, heads)
     message = step_call(kernel, "total", note, message, got)
-    message, get_below, get_above, block_out = lax.optimization_barrier(
-        (message, get_below, get_above, block_out)
+    message, get_a, get_b, block_out = lax.optimization_barrier(
+        (message, get_a, get_b, block_out)
     )
     got = swap(message, mesh_shape, ends[1])
     give_west, give_east = pl.pallas_call(
@@ -648,7 +681,7 @@
         scratch_shapes=[pltpu.VMEM((tokens, width), F32)],
         compiler_params=room(6),
         name="side",
-    )(info, side_s, side_k, get_above, get_below)
+    )(info, side_s, side_k, get_a, get_b)
     get_east = lax.ppermute(give_west, "lon", west)
     get_west = lax.ppermute(give_east, "lon", east)
     kernel = functools.partial(total_kernel, norm, count, heads)
@@ -669,7 +702,7 @@
         scratch_shapes=[pltpu.VMEM((tokens, width), F32)],
         compiler_params=room(6),
         name="join",
-    )(info, mid_s, mid_k, get_above, get_below, get_west, get_east)
+    )(info, mid_s, mid_k, get_a, get_b, get_west, get_east)
     got = swap(message, mesh_shape, rounds[0])
     weight_grad, bias_grad = step_call(
         functools.partial(last_kernel, 3, norm, count),

time: 92 us -> 83.3 us (0.905)
  waiting for transfers between devices: 25.3 us -> 20.3 us
  starting transfers between devices: 33.6 us -> 28.7 us
  Pallas kernels: 30.8 us -> 32.1 us
    ppermute x8, starting transfers between devices: 13.6 us -> 9.84 us  [swap(): return lax.ppermute(x, ('lat', 'lon'), partner_pairs(mesh_shape, bits))]
    ppermute x4 -> x5, waiting for transfers between devices: 6.9 us -> 4.01 us  [the longest x1 4 us: shards(): side_b = lax.ppermute(corner_b, 'lat', pair_b)]
    ppermute x4 -> x5, starting transfers between devices: 12.5 us -> 10.7 us  [the longest x1 4.11 us: shards(): from_b = lax.ppermute(own_b, 'lat', pair_b)]
    ppermute x1, waiting for transfers between devices: 1.86 us -> 0.01 us  [shards(): from_east = lax.ppermute(to_west, 'lon', west)]
    ppermute x8, waiting for transfers between devices: 15.9 us -> 14.9 us  [swap(): return lax.ppermute(x, ('lat', 'lon'), partner_pairs(mesh_shape, bits))]
  transfers between devices with their start and end apart: 16 -> 17, of which waited for: 9 -> 7; matrix products, arithmetic and copies ran while one was open for 0% -> 0% of each run, Pallas kernels for 19% -> 26%
where the time goes in v5:
time: 83.3 us; the launch traced here: 83 us
  Pallas kernels  32.1 us (39%)
  starting transfers between devices  28.7 us (34%)
  waiting for transfers between devices  20.3 us (24%)
  between operations  0.95 us (1%)
  local copies, waits for them, and re-layouts  0.92 us (1%)
    ppermute x8, waiting for transfers between devices, swap(): return lax.ppermute(x, ('lat', 'lon'), partner_pairs(mesh_shape, bits))  14.9 us
    ppermute x8, starting transfers between devices, swap(): return lax.ppermute(x, ('lat', 'lon'), partner_pairs(mesh_shape, bits))  9.84 us
    pallas_call x2, Pallas kernels, backward(): pl.pallas_call(functools.partial(bwd_kernel, sizes, n), in_specs=[smem] +...  7.36 us
    pallas_call x2, Pallas kernels, forward(): pl.pallas_call(functools.partial(fwd_kernel, sizes, n), in_specs=[smem] +...  7.22 us
    pallas_call x8, Pallas kernels, step_call(): pl.pallas_call(kernel, in_specs=scalars, out_shape=outs, compiler_params=...  4.22 us
    ppermute x1, starting transfers between devices, shards(): from_b = lax.ppermute(own_b, 'lat', pair_b)  4.11 us
    ppermute x1, waiting for transfers between devices, shards(): side_b = lax.ppermute(corner_b, 'lat', pair_b)  4 us
    pallas_call x1, Pallas kernels, shards(): pl.pallas_call(functools.partial(prepare_kernel, lon_dev, cols_pad), in_s...  3.86 us
  transfers between devices with their start and end apart: 17, of which 7 were waited for; matrix products, arithmetic and copies ran while one was open for 0% of the time, Pallas kernels for 26%

profile of v5, /device:TPU:1, one launch (start us, length us, event | category | flops | bytes accessed | tf_op | source)
XLA Modules:
  0.0 83.0 jit_solution(10875138519074202450)
XLA Ops:
  0.6 0.0 copy-start.4
  0.6 0.0 copy-start.3
  0.7 0.0 copy-start
  0.7 0.1 stack.24.info_ref
  0.8 2.0 %pack.1 = (bf16[2,96,512]{2,1,0:T(8,128)(2,1)S(1)}, bf16[2,96,512]{2,1,0:T(8,128)(2,1)S(1)}, bf16[2,96,512]{2,1,0:T(8,128)(2,1)S(1)}, bf16[2,96,512]{2,1,0:T(8,128)(2,1)S(1)}) custom-call(s32[6]{0:T(128)S(1)} %stack.24.info_ref, bf16[256,512]{1,0:T(8,128)(2,1)} %bitcast.22, bf16[256,512]{1,0:T(8,128)(2,1)} %bitcast.25), custom_call_target="tpu_custom_call" | custom-call | tf_op jit(solution)/shard_map/pack/pallas_call | solution.py:548
  2.8 2.1 %collective-permute-start = (bf16[2,96,512]{2,1,0:T(8,128)(2,1)S(1)}, bf16[2,96,512]{2,1,0:T(8,128)(2,1)S(1)}, u32[]{:S(2)}, u32[]{:S(2)}) collective-permute-start(bf16[2,96,512]{2,1,0:T(8,128)(2,1)S(1)} %get-tuple-element.68), channel_id=1, source_target_pairs={{0,1},{1,2},{2,3},{3,4},{4,5},{5,6},{6,7},{7,0},{8,9},{9,10},{10,1... | collective-permute-start | bytes 589832 | tf_op jit(solution)/shard_map/ppermute | solution.py:556
  4.9 3.1 %collective-permute-start.1 = (bf16[2,96,512]{2,1,0:T(8,128)(2,1)S(1)}, bf16[2,96,512]{2,1,0:T(8,128)(2,1)S(1)}, u32[]{:S(2)}, u32[]{:S(2)}) collective-permute-start(bf16[2,96,512]{2,1,0:T(8,128)(2,1)S(1)} %get-tuple-element.69), channel_id=1, source_target_pairs={{0,7},{1,0},{2,1},{3,2},{4,3},{5,4},{6,5},{7,6},{8,15},{9,8},{10,9... | collective-permute-start | bytes 589832 | tf_op jit(solution)/shard_map/ppermute | solution.py:557
  8.0 4.1 %collective-permute-start.2 = (bf16[2,96,512]{2,1,0:T(8,128)(2,1)S(1)}, bf16[2,96,512]{2,1,0:T(8,128)(2,1)S(1)}, u32[]{:S(2)}, u32[]{:S(2)}) collective-permute-start(bf16[2,96,512]{2,1,0:T(8,128)(2,1)S(1)} %get-tuple-element.70), channel_id=1, source_target_pairs={{8,16},{16,8},{9,17},{17,9},{10,18},{18,10},{11,19},{19,11},{12,20... | collective-permute-start | bytes 589832 | tf_op jit(solution)/shard_map/ppermute | solution.py:558
  12.1 0.0 copy-start.5
  12.1 0.8 copy-done.5
  12.9 3.9 %prepare.1 = (f32[512,512]{1,0:T(8,128)S(1)}, bf16[256,512]{1,0:T(8,128)(2,1)S(1)}) custom-call(f32[13,8,13]{2,1,0:T(8,128)S(1)} %bitcast.28, bf16[256,1024]{1,0:T(8,128)(2,1)} %bitcast.15, bf16[512,1024]{1,0:T(8,128)(2,1)} %w_ref.1), custom_call_target="tpu_custom_call" | custom-call | tf_op jit(solution)/shard_map/prepare/pallas_call | solution.py:560
  16.8 0.0 collective-permute-done.w_ref
  16.8 0.8 corner.2
  17.6 0.8 corner.3
  18.4 0.1 collective-permute-start.3
  18.4 2.6 %collective-permute-start.4 = (bf16[2,80,512]{2,1,0:T(8,128)(2,1)S(1)}, bf16[2,80,512]{2,1,0:T(8,128)(2,1)S(1)}, u32[]{:S(2)}, u32[]{:S(2)}) collective-permute-start(bf16[2,80,512]{2,1,0:T(8,128)(2,1)S(1)} %corner.2), channel_id=1, source_target_pairs={{8,16},{16,8},{9,17},{17,9},{10,18},{18,10},{11,19},{19,11},{12,20... | collective-permute-start | bytes 491528 | tf_op jit(solution)/shard_map/ppermute | solution.py:585
  21.1 4.0 %collective-permute-done.4.c_ref = bf16[2,80,512]{2,1,0:T(8,128)(2,1)S(1)} collective-permute-done((bf16[2,80,512]{2,1,0:T(8,128)(2,1)S(1)}, bf16[2,80,512]{2,1,0:T(8,128)(2,1)S(1)}, u32[]{:S(2)}, u32[]{:S(2)}) %collective-permute-start.4) | collective-permute-done | bytes 163872 | tf_op jit(solution)/shard_map/ppermute | solution.py:585
  25.1 3.6 %attend_fwd.3 = (bf16[256,256]{1,0:T(8,128)(2,1)S(1)}, bf16[256,1024]{1,0:T(8,128)(2,1)S(1)}, f32[4,512,256]{2,1,0:T(8,128)S(1)}, bf16[896,256]{1,0:T(8,128)(2,1)S(1)}, bf16[896,256]{1,0:T(8,128)(2,1)S(1)}) custom-call(s32[6]{0:T(128)S(1)} %stack.24.info_ref, bf16[256,512]{1,0:T(8,128)(2,1)S(1)} %bitcast.18, bf16[256,512]{1,0:T(8,128)(2,1)S(1)} %bitcast.23, ...), custom_call_target="tpu_custom_call" | custom-call | tf_op jit(solution)/shard_map/attend_fwd/pallas_call | solution.py:591
  28.7 0.1 collective-permute-start.5
  28.8 3.6 %attend_fwd.2 = (bf16[256,256]{1,0:T(8,128)(2,1)S(1)}, f32[256,1024]{1,0:T(8,128)S(1)}, f32[4,512,256]{2,1,0:T(8,128)S(1)}, bf16[896,256]{1,0:T(8,128)(2,1)S(1)}, bf16[896,256]{1,0:T(8,128)(2,1)S(1)}) custom-call(s32[6]{0:T(128)S(1)} %stack.24.info_ref, bf16[256,512]{1,0:T(8,128)(2,1)S(1)} %bitcast.19, bf16[256,512]{1,0:T(8,128)(2,1)S(1)} %bitcast.24, ...), custom_call_target="tpu_custom_call" | custom-call | tf_op jit(solution)/shard_map/attend_fwd/pallas_call | solution.py:591
  32.4 0.7 halve.2
  33.1 0.1 collective-permute-start.6
  33.2 3.4 %attend_bwd.2 = (bf16[256,256]{1,0:T(8,128)(2,1)S(1)}, bf16[2,192,256]{2,1,0:T(8,128)(2,1)S(1)}, bf16[2,192,256]{2,1,0:T(8,128)(2,1)S(1)}, f32[2,256,256]{2,1,0:...) custom-call(s32[6]{0:T(128)S(1)} %stack.24.info_ref, bf16[256,512]{1,0:T(8,128)(2,1)S(1)} %bitcast.20, ...), custom_call_target="tpu_custom_call" | custom-call | tf_op jit(solution)/shard_map/attend_bwd/pallas_call | solution.py:623
  36.6 2.1 %collective-permute-done.6.got_ref = bf16[128,1024]{1,0:T(8,128)(2,1)S(1)} collective-permute-done((bf16[128,1024]{1,0:T(8,128)(2,1)S(1)}, bf16[128,1024]{1,0:T(8,128)(2,1)S(1)}, u32[]{:S(2)}, u32[]{:S(2)}) %collective-permute-start.6) | collective-permute-done | bytes 262176 | tf_op jit(solution)/shard_map/ppermute | solution.py:431
  38.7 0.6 halve.3
  39.3 0.9 %collective-permute-start.7 = (bf16[64,1024]{1,0:T(8,128)(2,1)S(1)}, bf16[64,1024]{1,0:T(8,128)(2,1)S(1)}, u32[]{:S(2)}, u32[]{:S(2)}) collective-permute-start(bf16[64,1024]{1,0:T(8,128)(2,1)S(1)} %get-tuple-element.93), channel_id=1, source_target_pairs={{0,1},{1,0},{2,3},{3,2},{4,5},{5,4},{6,7},{7,6},{8,24},{9,25},{10,... | collective-permute-start | bytes 393224 | tf_op jit(solution)/shard_map/ppermute | solution.py:431
  40.2 3.9 %attend_bwd.3 = (bf16[256,512]{1,0:T(8,128)(2,1)}, bf16[2,192,512]{2,1,0:T(8,128)(2,1)S(1)}, bf16[2,192,512]{2,1,0:T(8,128)(2,1)S(1)}, f32[2,256,256]{2,1,0:T(8,...) custom-call(s32[6]{0:T(128)S(1)} %stack.24.info_ref, bf16[256,512]{1,0:T(8,128)(2,1)S(1)} %bitcast.21, ...), custom_call_target="tpu_custom_call" | custom-call | tf_op jit(solution)/shard_map/attend_bwd/pallas_call | solution.py:623
  44.2 1.5 %collective-permute-start.9 = (bf16[2,192,512]{2,1,0:T(8,128)(2,1)S(1)}, bf16[2,192,512]{2,1,0:T(8,128)(2,1)S(1)}, u32[]{:S(2)}, u32[]{:S(2)}) collective-permute-start(bf16[2,192,512]{2,1,0:T(8,128)(2,1)S(1)} %get-tuple-element.107), channel_id=1, source_target_pairs={{0,8},{8,0},{16,24},{24,16},{1,9},{9,1},{17,25},{25,17},{2,10},{10... | collective-permute-start | bytes 1179656 | tf_op jit(solution)/shard_map/ppermute | solution.py:650
  45.7 2.3 %collective-permute-start.10 = (bf16[2,192,512]{2,1,0:T(8,128)(2,1)S(1)}, bf16[2,192,512]{2,1,0:T(8,128)(2,1)S(1)}, u32[]{:S(2)}, u32[]{:S(2)}) collective-permute-start(bf16[2,192,512]{2,1,0:T(8,128)(2,1)S(1)} %get-tuple-element.108), channel_id=1, source_target_pairs={{8,16},{16,8},{9,17},{17,9},{10,18},{18,10},{11,19},{19,11},{12,20... | collective-permute-start | bytes 1179656 | tf_op jit(solution)/shard_map/ppermute | solution.py:649
  48.0 1.2 %bias_fold.1.bias_ref = f32[8,256]{1,0:T(8,128)S(1)} custom-call(s32[6]{0:T(128)S(1)} %stack.24.info_ref, f32[416,128]{1,0:T(8,128)S(1)} %get-tuple-element.105.xs_ref, f32[416,128]{1,0:T(8,128)S(1)} %get-tuple-element.106.xk_ref), custom_call_target="tpu_custom_call" | custom-call | tf_op jit(solution)/shard_map/bias_fold/pallas_call | solution.py:653
  49.2 0.1 meet.1.own_ref
  49.3 2.1 %collective-permute-start.8 = (bf16[72,1024]{1,0:T(8,128)(2,1)S(1)}, bf16[72,1024]{1,0:T(8,128)(2,1)S(1)}, u32[]{:S(2)}, u32[]{:S(2)}) collective-permute-start(bf16[72,1024]{1,0:T(8,128)(2,1)S(1)} %meet.1.own_ref), channel_id=1, source_target_pairs={{0,2},{1,3},{2,0},{3,1},{4,6},{5,7},{6,4},{7,5},{8,12},{9,13},{10,... | collective-permute-start | bytes 442376 | tf_op jit(solution)/shard_map/ppermute | solution.py:431
  51.3 1.8 %project.1 = bf16[256,1024]{1,0:T(8,128)(2,1)} custom-call(s32[6]{0:T(128)S(1)} %stack.24.info_ref, bf16[256,256]{1,0:T(8,128)(2,1)S(1)} %get-tuple-element.109.s_ref, bf16[256,256]{1,0:T(8,128)(2,1)S(1)} %get-tuple-element.110.k_ref, bf16[512,1024]{1,0:T(8,128)(2,1)S(1)} %copy-done.1), custom_call_target="tpu_custom_call" | custom-call | tf_op jit(solution)/shard_map/project/pallas_call | solution.py:661
  53.1 2.7 %collective-permute-done.8.got_ref = bf16[72,1024]{1,0:T(8,128)(2,1)S(1)} collective-permute-done((bf16[72,1024]{1,0:T(8,128)(2,1)S(1)}, bf16[72,1024]{1,0:T(8,128)(2,1)S(1)}, u32[]{:S(2)}, u32[]{:S(2)}) %collective-permute-start.8) | collective-permute-done | bytes 147488 | tf_op jit(solution)/shard_map/ppermute | solution.py:431
  55.9 0.4 collective-permute-start.11
  56.3 1.1 %side.1 = (bf16[2,96,512]{2,1,0:T(8,128)(2,1)S(1)}, bf16[2,96,512]{2,1,0:T(8,128)(2,1)S(1)}) custom-call(s32[6]{0:T(128)S(1)} %stack.24.info_ref, f32[2,256,256]{2,1,0:T(8,128)S(1)} %get-tuple-element.118.ss_ref, f32[2,256,256]{2,1,0:T(8,128)S(1)} %get-tuple-element.119.sk_ref, bf16[2,192,512]{2,1,0:T(8,128)(2,1)S(1)} %collective-permute-done.9.a_ref, ...), custom_call_target="tpu_custom_call" | custom-call | tf_op jit(solution)/shard_map/side/pallas_call | solution.py:677
  57.4 3.0 %collective-permute-start.13 = (bf16[2,96,512]{2,1,0:T(8,128)(2,1)S(1)}, bf16[2,96,512]{2,1,0:T(8,128)(2,1)S(1)}, u32[]{:S(2)}, u32[]{:S(2)}) collective-permute-start(bf16[2,96,512]{2,1,0:T(8,128)(2,1)S(1)} %get-tuple-element.120), channel_id=1, source_target_pairs={{0,7},{1,0},{2,1},{3,2},{4,3},{5,4},{6,5},{7,6},{8,15},{9,8},{10,9... | collective-permute-start | bytes 589832 | tf_op jit(solution)/shard_map/ppermute | solution.py:685
  60.4 1.9 %collective-permute-done.11.got_ref = bf16[72,1024]{1,0:T(8,128)(2,1)S(1)} collective-permute-done((bf16[72,1024]{1,0:T(8,128)(2,1)S(1)}, bf16[72,1024]{1,0:T(8,128)(2,1)S(1)}, u32[]{:S(2)}, u32[]{:S(2)}) %collective-permute-start.11) | collective-permute-done | bytes 147488 | tf_op jit(solution)/shard_map/ppermute | solution.py:431
  62.4 0.1 collective-permute-start.12
  62.5 4.3 %collective-permute-done.12.got_ref = bf16[72,1024]{1,0:T(8,128)(2,1)S(1)} collective-permute-done((bf16[72,1024]{1,0:T(8,128)(2,1)S(1)}, bf16[72,1024]{1,0:T(8,128)(2,1)S(1)}, u32[]{:S(2)}, u32[]{:S(2)}) %collective-permute-start.12) | collective-permute-done | bytes 147488 | tf_op jit(solution)/shard_map/ppermute | solution.py:431
  66.8 0.6 grow.2.own_ref
  67.4 1.4 %collective-permute-done.14.w_ref = bf16[2,96,512]{2,1,0:T(8,128)(2,1)S(1)} collective-permute-done((bf16[2,96,512]{2,1,0:T(8,128)(2,1)S(1)}, bf16[2,96,512]{2,1,0:T(8,128)(2,1)S(1)}, u32[]{:S(2)}, u32[]{:S(2)}) %collective-permute-start.14) | collective-permute-done | bytes 196640 | tf_op jit(solution)/shard_map/ppermute | solution.py:686
  68.7 2.2 %collective-permute-start.15 = (bf16[136,1024]{1,0:T(8,128)(2,1)S(1)}, bf16[136,1024]{1,0:T(8,128)(2,1)S(1)}, u32[]{:S(2)}, u32[]{:S(2)}) collective-permute-start(bf16[136,1024]{1,0:T(8,128)(2,1)S(1)} %grow.2.own_ref), channel_id=1, source_target_pairs={{0,16},{1,17},{2,18},{3,19},{4,20},{5,21},{6,22},{7,23},{8,9},{9,8... | collective-permute-start | bytes 835592 | tf_op jit(solution)/shard_map/ppermute | solution.py:431
  70.9 3.9 %collective-permute-done.15.got_ref = bf16[136,1024]{1,0:T(8,128)(2,1)S(1)} collective-permute-done((bf16[136,1024]{1,0:T(8,128)(2,1)S(1)}, bf16[136,1024]{1,0:T(8,128)(2,1)S(1)}, u32[]{:S(2)}, u32[]{:S(2)}) %collective-permute-start.15) | collective-permute-done | bytes 278560 | tf_op jit(solution)/shard_map/ppermute | solution.py:431
  74.9 0.6 grow.3.own_ref
  75.4 4.0 %collective-permute-start.16 = (bf16[264,1024]{1,0:T(8,128)(2,1)S(1)}, bf16[264,1024]{1,0:T(8,128)(2,1)S(1)}, u32[]{:S(2)}, u32[]{:S(2)}) collective-permute-start(bf16[264,1024]{1,0:T(8,128)(2,1)S(1)} %grow.3.own_ref), channel_id=1, source_target_pairs={{0,8},{1,9},{2,10},{3,11},{4,12},{5,13},{6,14},{7,15},{8,0},{9,1},... | collective-permute-start | bytes 1622024 | tf_op jit(solution)/shard_map/ppermute | solution.py:431
  79.5 1.9 %join.1 = (bf16[256,512]{1,0:T(8,128)(2,1)}, bf16[256,512]{1,0:T(8,128)(2,1)}) custom-call(s32[6]{0:T(128)S(1)} %stack.24.info_ref, f32[2,256,256]{2,1,0:T(8,128)S(1)} %get-tuple-element.113.ms_ref, f32[2,256,256]{2,1,0:T(8,128)S(1)} %get-tuple-element.114.mk_ref, bf16[2,192,512]{2,1,0:T(8,128)(2,1)S(1)} %collective-permute-done.9.a_ref, ...), custom_call_target="tpu_custom_call" | custom-call | tf_op jit(solution)/shard_map/join/pallas_call | solution.py:698
  81.4 1.6 %last.1 = (bf16[512,1024]{1,0:T(8,128)(2,1)}, f32[13,8,13]{2,1,0:T(8,128)}) custom-call(s32[6]{0:T(128)S(1)} %stack.24.info_ref, bf16[264,1024]{1,0:T(8,128)(2,1)S(1)} %grow.3.own_ref, bf16[264,1024]{1,0:T(8,128)(2,1)S(1)} %collective-permute-done.16.got_ref), custom_call_target="tpu_custom_call" | custom-call | tf_op jit(solution)/shard_map/last/pallas_call | solution.py:606
  (19 shorter events, 0.1 us)
Async XLA Ops:
  0.6 24.5 %copy-start.4 = (bf16[16,16,512]{2,1,0:T(8,128)(2,1)S(1)}, bf16[16,16,512]{2,1,0:T(8,128)(2,1)}, u32[]{:S(2)}) copy-start(bf16[16,16,512]{2,1,0:T(8,128)(2,1)} %param.8) | copy-start | bytes 786436
  0.6 24.4 %copy-start.3 = (bf16[16,16,512]{2,1,0:T(8,128)(2,1)S(1)}, bf16[16,16,512]{2,1,0:T(8,128)(2,1)}, u32[]{:S(2)}) copy-start(bf16[16,16,512]{2,1,0:T(8,128)(2,1)} %param.7) | copy-start | bytes 786436
  0.7 24.4 %copy-start = (bf16[16,16,1024]{2,1,0:T(8,128)(2,1)S(1)}, bf16[16,16,1024]{2,1,0:T(8,128)(2,1)}, u32[]{:S(2)}) copy-start(bf16[16,16,1024]{2,1,0:T(8,128)(2,1)} %param.11) | copy-start | bytes 1572868
  0.7 24.4 %copy-start.2 = (bf16[16,16,512]{2,1,0:T(8,128)(2,1)S(1)}, bf16[16,16,512]{2,1,0:T(8,128)(2,1)}, u32[]{:S(2)}) copy-start(bf16[16,16,512]{2,1,0:T(8,128)(2,1)} %param.6) | copy-start | bytes 786436
  2.8 14.0 %collective-permute-start = (bf16[2,96,512]{2,1,0:T(8,128)(2,1)S(1)}, bf16[2,96,512]{2,1,0:T(8,128)(2,1)S(1)}, u32[]{:S(2)}, u32[]{:S(2)}) collective-permute-start(bf16[2,96,512]{2,1,0:T(8,128)(2,1)S(1)} %get-tuple-element.68), channel_id=1, source_target_pairs={{0,1},{1,2},{2,3},{3,4},{4,5},{5,6},{6,7},{7,0},{8,9},{9,10},{10,1... | collective-permute-start | bytes 589832 | tf_op jit(solution)/shard_map/ppermute | solution.py:556
  4.9 11.9 %collective-permute-start.1 = (bf16[2,96,512]{2,1,0:T(8,128)(2,1)S(1)}, bf16[2,96,512]{2,1,0:T(8,128)(2,1)S(1)}, u32[]{:S(2)}, u32[]{:S(2)}) collective-permute-start(bf16[2,96,512]{2,1,0:T(8,128)(2,1)S(1)} %get-tuple-element.69), channel_id=1, source_target_pairs={{0,7},{1,0},{2,1},{3,2},{4,3},{5,4},{6,5},{7,6},{8,15},{9,8},{10,9... | collective-permute-start | bytes 589832 | tf_op jit(solution)/shard_map/ppermute | solution.py:557
  8.0 8.8 %collective-permute-start.2 = (bf16[2,96,512]{2,1,0:T(8,128)(2,1)S(1)}, bf16[2,96,512]{2,1,0:T(8,128)(2,1)S(1)}, u32[]{:S(2)}, u32[]{:S(2)}) collective-permute-start(bf16[2,96,512]{2,1,0:T(8,128)(2,1)S(1)} %get-tuple-element.70), channel_id=1, source_target_pairs={{8,16},{16,8},{9,17},{17,9},{10,18},{18,10},{11,19},{19,11},{12,20... | collective-permute-start | bytes 589832 | tf_op jit(solution)/shard_map/ppermute | solution.py:558
  12.1 0.8 copy-start.5
  18.4 6.7 %collective-permute-start.3 = (bf16[2,176,512]{2,1,0:T(8,128)(2,1)S(1)}, bf16[2,176,512]{2,1,0:T(8,128)(2,1)S(1)}, u32[]{:S(2)}, u32[]{:S(2)}) collective-permute-start(bf16[2,176,512]{2,1,0:T(8,128)(2,1)S(1)} %corner.3), channel_id=1, source_target_pairs={{0,8},{8,0},{16,24},{24,16},{1,9},{9,1},{17,25},{25,17},{2,10},{10... | collective-permute-start | bytes 1081352 | tf_op jit(solution)/shard_map/ppermute | solution.py:586
  18.4 6.6 %collective-permute-start.4 = (bf16[2,80,512]{2,1,0:T(8,128)(2,1)S(1)}, bf16[2,80,512]{2,1,0:T(8,128)(2,1)S(1)}, u32[]{:S(2)}, u32[]{:S(2)}) collective-permute-start(bf16[2,80,512]{2,1,0:T(8,128)(2,1)S(1)} %corner.2), channel_id=1, source_target_pairs={{8,16},{16,8},{9,17},{17,9},{10,18},{18,10},{11,19},{19,11},{12,20... | collective-permute-start | bytes 491528 | tf_op jit(solution)/shard_map/ppermute | solution.py:585
  28.7 3.7 %collective-permute-start.5 = (bf16[256,1024]{1,0:T(8,128)(2,1)S(1)}, bf16[256,1024]{1,0:T(8,128)(2,1)S(1)}, u32[]{:S(2)}, u32[]{:S(2)}) collective-permute-start(bf16[256,1024]{1,0:T(8,128)(2,1)S(1)} %get-tuple-element.80), channel_id=1, source_target_pairs={{0,8},{1,9},{2,10},{3,11},{4,12},{5,13},{6,14},{7,15},{8,0},{9,1},... | collective-permute-start | bytes 1572872 | tf_op jit(solution)/shard_map/ppermute | solution.py:431
  33.1 5.6 %collective-permute-start.6 = (bf16[128,1024]{1,0:T(8,128)(2,1)S(1)}, bf16[128,1024]{1,0:T(8,128)(2,1)S(1)}, u32[]{:S(2)}, u32[]{:S(2)}) collective-permute-start(bf16[128,1024]{1,0:T(8,128)(2,1)S(1)} %get-tuple-element.83), channel_id=1, source_target_pairs={{0,16},{1,17},{2,18},{3,19},{4,20},{5,21},{6,22},{7,23},{8,9},{9,8... | collective-permute-start | bytes 786440 | tf_op jit(solution)/shard_map/ppermute | solution.py:431
  39.3 4.8 %collective-permute-start.7 = (bf16[64,1024]{1,0:T(8,128)(2,1)S(1)}, bf16[64,1024]{1,0:T(8,128)(2,1)S(1)}, u32[]{:S(2)}, u32[]{:S(2)}) collective-permute-start(bf16[64,1024]{1,0:T(8,128)(2,1)S(1)} %get-tuple-element.93), channel_id=1, source_target_pairs={{0,1},{1,0},{2,3},{3,2},{4,5},{5,4},{6,7},{7,6},{8,24},{9,25},{10,... | collective-permute-start | bytes 393224 | tf_op jit(solution)/shard_map/ppermute | solution.py:431
  40.2 11.1 %copy-start.1 = (bf16[512,1024]{1,0:T(8,128)(2,1)S(1)}, bf16[512,1024]{1,0:T(8,128)(2,1)}, u32[]{:S(2)}) copy-start(bf16[512,1024]{1,0:T(8,128)(2,1)} %w_ref.1) | copy-start | bytes 3145732
  44.2 11.7 %collective-permute-start.9 = (bf16[2,192,512]{2,1,0:T(8,128)(2,1)S(1)}, bf16[2,192,512]{2,1,0:T(8,128)(2,1)S(1)}, u32[]{:S(2)}, u32[]{:S(2)}) collective-permute-start(bf16[2,192,512]{2,1,0:T(8,128)(2,1)S(1)} %get-tuple-element.107), channel_id=1, source_target_pairs={{0,8},{8,0},{16,24},{24,16},{1,9},{9,1},{17,25},{25,17},{2,10},{10... | collective-permute-start | bytes 1179656 | tf_op jit(solution)/shard_map/ppermute | solution.py:650
  45.7 10.2 %collective-permute-start.10 = (bf16[2,192,512]{2,1,0:T(8,128)(2,1)S(1)}, bf16[2,192,512]{2,1,0:T(8,128)(2,1)S(1)}, u32[]{:S(2)}, u32[]{:S(2)}) collective-permute-start(bf16[2,192,512]{2,1,0:T(8,128)(2,1)S(1)} %get-tuple-element.108), channel_id=1, source_target_pairs={{8,16},{16,8},{9,17},{17,9},{10,18},{18,10},{11,19},{19,11},{12,20... | collective-permute-start | bytes 1179656 | tf_op jit(solution)/shard_map/ppermute | solution.py:649
  49.3 6.5 %collective-permute-start.8 = (bf16[72,1024]{1,0:T(8,128)(2,1)S(1)}, bf16[72,1024]{1,0:T(8,128)(2,1)S(1)}, u32[]{:S(2)}, u32[]{:S(2)}) collective-permute-start(bf16[72,1024]{1,0:T(8,128)(2,1)S(1)} %meet.1.own_ref), channel_id=1, source_target_pairs={{0,2},{1,3},{2,0},{3,1},{4,6},{5,7},{6,4},{7,5},{8,12},{9,13},{10,... | collective-permute-start | bytes 442376 | tf_op jit(solution)/shard_map/ppermute | solution.py:431
  55.9 6.5 %collective-permute-start.11 = (bf16[72,1024]{1,0:T(8,128)(2,1)S(1)}, bf16[72,1024]{1,0:T(8,128)(2,1)S(1)}, u32[]{:S(2)}, u32[]{:S(2)}) collective-permute-start(bf16[72,1024]{1,0:T(8,128)(2,1)S(1)} %total.2.own_ref), channel_id=1, source_target_pairs={{0,4},{1,5},{2,6},{3,7},{4,0},{5,1},{6,2},{7,3},{8,10},{9,11},{10,... | collective-permute-start | bytes 442376 | tf_op jit(solution)/shard_map/ppermute | solution.py:431
  57.4 9.9 %collective-permute-start.13 = (bf16[2,96,512]{2,1,0:T(8,128)(2,1)S(1)}, bf16[2,96,512]{2,1,0:T(8,128)(2,1)S(1)}, u32[]{:S(2)}, u32[]{:S(2)}) collective-permute-start(bf16[2,96,512]{2,1,0:T(8,128)(2,1)S(1)} %get-tuple-element.120), channel_id=1, source_target_pairs={{0,7},{1,0},{2,1},{3,2},{4,3},{5,4},{6,5},{7,6},{8,15},{9,8},{10,9... | collective-permute-start | bytes 589832 | tf_op jit(solution)/shard_map/ppermute | solution.py:685
  60.4 8.3 %collective-permute-start.14 = (bf16[2,96,512]{2,1,0:T(8,128)(2,1)S(1)}, bf16[2,96,512]{2,1,0:T(8,128)(2,1)S(1)}, u32[]{:S(2)}, u32[]{:S(2)}) collective-permute-start(bf16[2,96,512]{2,1,0:T(8,128)(2,1)S(1)} %get-tuple-element.121), channel_id=1, source_target_pairs={{0,1},{1,2},{2,3},{3,4},{4,5},{5,6},{6,7},{7,0},{8,9},{9,10},{10,1... | collective-permute-start | bytes 589832 | tf_op jit(solution)/shard_map/ppermute | solution.py:686
  62.4 4.4 %collective-permute-start.12 = (bf16[72,1024]{1,0:T(8,128)(2,1)S(1)}, bf16[72,1024]{1,0:T(8,128)(2,1)S(1)}, u32[]{:S(2)}, u32[]{:S(2)}) collective-permute-start(bf16[72,1024]{1,0:T(8,128)(2,1)S(1)} %total.3.own_ref), channel_id=1, source_target_pairs={{0,1},{1,0},{2,3},{3,2},{4,5},{5,4},{6,7},{7,6},{8,24},{9,25},{10,... | collective-permute-start | bytes 442376 | tf_op jit(solution)/shard_map/ppermute | solution.py:431
  68.7 6.1 %collective-permute-start.15 = (bf16[136,1024]{1,0:T(8,128)(2,1)S(1)}, bf16[136,1024]{1,0:T(8,128)(2,1)S(1)}, u32[]{:S(2)}, u32[]{:S(2)}) collective-permute-start(bf16[136,1024]{1,0:T(8,128)(2,1)S(1)} %grow.2.own_ref), channel_id=1, source_target_pairs={{0,16},{1,17},{2,18},{3,19},{4,20},{5,21},{6,22},{7,23},{8,9},{9,8... | collective-permute-start | bytes 835592 | tf_op jit(solution)/shard_map/ppermute | solution.py:431
  75.4 5.9 %collective-permute-start.16 = (bf16[264,1024]{1,0:T(8,128)(2,1)S(1)}, bf16[264,1024]{1,0:T(8,128)(2,1)S(1)}, u32[]{:S(2)}, u32[]{:S(2)}) collective-permute-start(bf16[264,1024]{1,0:T(8,128)(2,1)S(1)} %grow.3.own_ref), channel_id=1, source_target_pairs={{0,8},{1,9},{2,10},{3,11},{4,12},{5,13},{6,14},{7,15},{8,0},{9,1},... | collective-permute-start | bytes 1622024 | tf_op jit(solution)/shard_map/ppermute | solution.py:431

commit v6 on v5

--- a/solution.py
+++ b/solution.py
@@ -132,22 +132,23 @@
         b_ref[i] = jnp.where(odd, down, up)
 
 
-def corner_kernel(rows, own, info_ref, w_ref, e_ref, *refs):
-    out_ref = refs[-1]
+def corner_kernel(rows, cols, info_ref, w_ref, e_ref, own_ref, a_ref, b_ref):
     half = RAD * RAD
+    edge = RAD * cols
     n = down_iota(CORNER)
     src = along_iota(rows * RAD)
     odd = info_ref[2] == 1
-    up = odd if own else jnp.logical_not(odd)
-    first = jnp.where(up, 0, (rows - RAD) * RAD)
-    pick_w = hot((src == first + n) & (n < half))
-    pick_e = hot((src == first + n - half) & (n >= half) & (n < 2 * half))
-    for i in range(2):
-        side = dot(pick_w, w_ref[i]) + dot(pick_e, e_ref[i])
-        edge = out_ref.shape[1] - CORNER
-        if own:
-            out_ref[i, :edge, :] = refs[0][i]
-        out_ref[i, edge:, :] = side.astype(BF16)
+    last = (rows - RAD) * RAD
+    a_ref[:, :edge, :] = own_ref[...]
+    for ref, lo, first in (
+        (b_ref, 0, jnp.where(odd, last, 0)),
+        (a_ref, edge, jnp.where(odd, 0, last)),
+    ):
+        pick_w = hot((src == first + n) & (n < half))
+        pick_e = hot((src == first + n - half) & (n >= half) & (n < 2 * half))
+        for i in range(2):
+            side = dot(pick_w, w_ref[i]) + dot(pick_e, e_ref[i])
+            ref[i, lo:, :] = side.astype(BF16)
 
 
 def prepare_kernel(
@@ -281,7 +282,6 @@
         other = group_lanes(1 - which, GROUP * head_size)
         dq_ref[:, other] = before[0][...]
         sa_ref[:, :, other] = before[1][...]
-        sb_ref[:, :, other] = before[2][...]
     kt_ref[...] = k_ref[...].T
     dk_ref[...] = jnp.zeros_like(dk_ref)
     dv_ref[...] = jnp.zeros_like(dv_ref)
@@ -311,7 +311,7 @@
     first_b = pl.multiple_of(jnp.where(odd, low_rows, 0), cols_pad)
     for i, ref in enumerate((dk_ref, dv_ref)):
         sa_ref[i, :, mine] = ref[pl.ds(first_a, edge), :].astype(BF16)
-        sb_ref[i, :, mine] = ref[pl.ds(first_b, edge), :].astype(BF16)
+        sb_ref[i] = ref[pl.ds(first_b, edge), :].astype(BF16)
         for r in range(lat_dev):
             lo = (RAD + r) * cols_pad
             mid_ref[i, r * cols : (r + 1) * cols, :] = ref[lo : lo + cols, :]
@@ -363,29 +363,35 @@
     return [pl.multiple_of(jnp.where(odd, x, last - x), cols) for x in (0, last)]
 
 
-def both_groups(info_ref, dst_ref, i, s_ref, k_ref):
-    lanes = s_ref.shape[2]
-    dst_ref[:, group_lanes(info_ref[0], lanes)] = s_ref[i]
-    dst_ref[:, group_lanes(1 - info_ref[0], lanes)] = k_ref[i]
+def both_lanes(info_ref, lanes):
+    return group_lanes(info_ref[0], lanes), group_lanes(1 - info_ref[0], lanes)
+
+
+def both_groups(info_ref, dst_ref, i, *refs):
+    for ref, group in zip(refs, both_lanes(info_ref, refs[0].shape[2])):
+        dst_ref[:, group] = ref[i]
 
 
 def side_kernel(
-    rows, cols, cols_pad, info_ref, ss_ref, sk_ref, a_ref, b_ref, west_ref, east_ref, s_ref
+    rows, cols, cols_pad, info_ref, ss_ref, sk_ref, a_ref, bk_ref, bs_ref, west_ref, east_ref,
+    s_ref,
 ):
     edge = RAD * SLOTS
     pick_west = take_cols(rows, SLOTS, 0)
     pick_east = take_cols(rows, SLOTS, RAD)
     for i in range(2):
         both_groups(info_ref, s_ref, i, ss_ref, sk_ref)
-        for ref, first in zip((a_ref, b_ref), strips(info_ref, rows, SLOTS)):
-            s_ref[pl.ds(first, edge), :] += lat_terms(ref, i, rows, SLOTS, cols_pad, cols)
+        first_a, first_b = strips(info_ref, rows, SLOTS)
+        s_ref[pl.ds(first_a, edge), :] += lat_terms(a_ref, i, rows, SLOTS, cols_pad, cols)
+        for ref, group in zip((bk_ref, bs_ref), both_lanes(info_ref, bs_ref.shape[2])):
+            s_ref[pl.ds(first_b, edge), group] += lat_terms(ref, i, rows, SLOTS, cols_pad, cols)
         x = s_ref[...].astype(BF16)
         west_ref[i] = dot(pick_west, x).astype(BF16)
         east_ref[i] = dot(pick_east, x).astype(BF16)
 
 
 def join_kernel(
-    rows, cols, cols_pad, info_ref, ms_ref, mk_ref, a_ref, b_ref, w_ref, e_ref,
+    rows, cols, cols_pad, info_ref, ms_ref, mk_ref, a_ref, bk_ref, bs_ref, w_ref, e_ref,
     k_ref, v_ref, s_ref,
 ):
     edge = RAD * cols
@@ -394,8 +400,10 @@
     for i, out_ref in enumerate((k_ref, v_ref)):
         both_groups(info_ref, s_ref, i, ms_ref, mk_ref)
         s_ref[...] += dot(put_west, w_ref[i]) + dot(put_east, e_ref[i])
-        for ref, first in zip((a_ref, b_ref), strips(info_ref, rows, cols)):
-            s_ref[pl.ds(first, edge), :] += lat_terms(ref, i, rows, cols, cols_pad, 0)
+        first_a, first_b = strips(info_ref, rows, cols)
+        s_ref[pl.ds(first_a, edge), :] += lat_terms(a_ref, i, rows, cols, cols_pad, 0)
+        for ref, group in zip((bk_ref, bs_ref), both_lanes(info_ref, bs_ref.shape[2])):
+            s_ref[pl.ds(first_b, edge), group] += lat_terms(ref, i, rows, cols, cols_pad, 0)
         out_ref[...] = s_ref[...].astype(BF16)
 
 
@@ -571,19 +579,15 @@
         (from_west, from_east, from_b, table)
     )
 
-    def corner(rows, *own):
-        return pl.pallas_call(
-            functools.partial(corner_kernel, lat_dev, bool(own)),
-            in_specs=[smem] + [vmem] * (2 + len(own)),
-            out_shape=shape((2, rows, width)),
-            compiler_params=room(4),
-            name="corner",
-        )(info, from_west, from_east, *own)
-
-    corner_b = corner(CORNER)
-    corner_b, own_a = lax.optimization_barrier((corner_b, own_a))
+    corner_a, corner_b = pl.pallas_call(
+        functools.partial(corner_kernel, lat_dev, lon_dev),
+        in_specs=[smem] + [vmem] * 3,
+        out_shape=[shape((2, n_edge + CORNER, width)), shape((2, CORNER, width))],
+        compiler_params=room(4),
+        name="corner",
+    )(info, from_west, from_east, own_a)
     side_b = lax.ppermute(corner_b, "lat", pair_b)
-    from_a = lax.ppermute(corner(n_edge + CORNER, own_a), "lat", pair_a)
+    from_a = lax.ppermute(corner_a, "lat", pair_a)
     probs = (tiles, win, lanes_q)
     outer = (n_keys, lanes)
 
@@ -623,8 +627,8 @@
         return pl.pallas_call(
             functools.partial(bwd_kernel, sizes, n),
             in_specs=[smem] + [vmem] * (5 + len(before)),
-            out_shape=[shape((tokens, size))]
-            + [shape((2, n_strip, size))] * 2
+            out_shape=[shape((tokens, size)), shape((2, n_strip, size))]
+            + [shape((2, n_strip, lanes))]
             + [shape((2, tokens, lanes), F32)] * 2
             + [shape((SPAN * cols_pad, 2 * GROUP * lon_dev), F32)],
             scratch_shapes=[pltpu.VMEM((lanes, n_keys), BF16)]
@@ -636,8 +640,9 @@
 
     info_b, send = lax.optimization_barrier((info, send))
     got = swap(send, mesh_shape, rounds[1])
-    *before, mid_s, side_s, fold_s = backward(0, info_b, p_s, k_s, v_s)
+    *before, strip_s, mid_s, side_s, fold_s = backward(0, info_b, p_s, k_s, v_s)
     got, fold_s = lax.optimization_barrier((got, fold_s))
+    get_s = lax.ppermute(strip_s, "lat", pair_b)
     for number in range(2, len(rounds)):
         send, keep = halve(keep, got, number)
         if number == 2:
@@ -645,9 +650,7 @@
         got = swap(send, mesh_shape, rounds[number])
     after = backward(2, info_b, p_k, k_k, v_k, *before)
     query_grad, strip_a, strip_b, mid_k, side_k, fold_k = after
-    got, strip_a, strip_b, fold_k = lax.optimization_barrier((got, strip_a, strip_b, fold_k))
-    get_b = lax.ppermute(strip_b, "lat", pair_b)
-    get_a = lax.ppermute(strip_a, "lat", pair_a)
+    got, fold_k, get_s = lax.optimization_barrier((got, fold_k, get_s))
 
     count = 256
     bias_local = pl.pallas_call(
@@ -667,21 +670,22 @@
     )(info, att_s, att_k, out_weight)
     note = shape((keep.shape[0] + heads, model))
     message = step_call(meet_kernel, "meet", note, keep, got, bias_local)
+    message, strip_a, strip_b = lax.optimization_barrier((message, strip_a, strip_b))
+    get_b = lax.ppermute(strip_b, "lat", pair_b)
+    get_a = lax.ppermute(strip_a, "lat", pair_a)
     got = swap(message, mesh_shape, ends[0])
     kernel = functools.partial(total_kernel, None, count, heads)
     message = step_call(kernel, "total", note, message, got)
-    message, get_a, get_b, block_out = lax.optimization_barrier(
-        (message, get_a, get_b, block_out)
-    )
+    message, block_out = lax.optimization_barrier((message, block_out))
     got = swap(message, mesh_shape, ends[1])
     give_west, give_east = pl.pallas_call(
         functools.partial(side_kernel, lat_dev, lon_dev, cols_pad),
-        in_specs=[smem] + [vmem] * 4,
+        in_specs=[smem] + [vmem] * 5,
         out_shape=[shape((2, n_side, width))] * 2,
         scratch_shapes=[pltpu.VMEM((tokens, width), F32)],
         compiler_params=room(6),
         name="side",
-    )(info, side_s, side_k, get_a, get_b)
+    )(info, side_s, side_k, get_a, get_b, get_s)
     get_east = lax.ppermute(give_west, "lon", west)
     get_west = lax.ppermute(give_east, "lon", east)
     kernel = functools.partial(total_kernel, norm, count, heads)
@@ -692,17 +696,19 @@
         if number == 1:
             message, get_east, get_west = lax.optimization_barrier((message, get_east, get_west))
         got = swap(message, mesh_shape, rounds[number])
+        if number == 1:
+            key_grad, value_grad = pl.pallas_call(
+                functools.partial(join_kernel, lat_dev, lon_dev, cols_pad),
+                in_specs=[smem] + [vmem] * 7,
+                out_shape=[shape((tokens, width))] * 2,
+                scratch_shapes=[pltpu.VMEM((tokens, width), F32)],
+                compiler_params=room(6),
+                name="join",
+            )(info, mid_s, mid_k, get_a, get_b, get_s, get_west, get_east)
+            got, key_grad = lax.optimization_barrier((got, key_grad))
         note = shape((2 * message.shape[0] - heads, model))
         kernel = functools.partial(grow_kernel, 3 + number, count, heads)
         message = step_call(kernel, "grow", note, info, message, got)
-    key_grad, value_grad = pl.pallas_call(
-        functools.partial(join_kernel, lat_dev, lon_dev, cols_pad),
-        in_specs=[smem] + [vmem] * 6,
-        out_shape=[shape((tokens, width))] * 2,
-        scratch_shapes=[pltpu.VMEM((tokens, width), F32)],
-        compiler_params=room(6),
-        name="join",
-    )(info, mid_s, mid_k, get_a, get_b, get_west, get_east)
     got = swap(message, mesh_shape, rounds[0])
     weight_grad, bias_grad = step_call(
         functools.partial(last_kernel, 3, norm, count),

time: 83.3 us -> 81.1 us (0.974)
  waiting for transfers between devices: 20.3 us -> 16.3 us
  starting transfers between devices: 28.7 us -> 30.8 us
    ppermute x8, waiting for transfers between devices: 14.9 us -> 7.87 us  [swap(): return lax.ppermute(x, ('lat', 'lon'), partner_pairs(mesh_shape, bits))]
    ppermute x1 -> x2, starting transfers between devices: 0.07 us -> 4.27 us  [the longest x1 4.2 us: shards(): get_s = lax.ppermute(strip_s, 'lat', pair_b)]
    ppermute x1, waiting for transfers between devices: 1.37 us -> 3 us  [shards(): get_west = lax.ppermute(give_east, 'lon', east)]
    ppermute x1, waiting for transfers between devices: 0.01 us -> 1.39 us  [shards(): get_b = lax.ppermute(strip_b, 'lat', pair_b)]
    ppermute x1, starting transfers between devices: 3.04 us -> 1.68 us  [shards(): get_east = lax.ppermute(give_west, 'lon', west)]
    ppermute x1, starting transfers between devices: 1.54 us -> 0.28 us  [shards(): get_a = lax.ppermute(strip_a, 'lat', pair_a)]
  transfers between devices with their start and end apart: 17 -> 18, of which waited for: 7 -> 8; matrix products, arithmetic and copies ran while one was open for 0% -> 0% of each run, Pallas kernels for 26% -> 26%
where the time goes in v6:
time: 81.1 us; the launch traced here: 80.2 us
  Pallas kernels  31.3 us (39%)
  starting transfers between devices  30.8 us (38%)
  waiting for transfers between devices  16.3 us (20%)
  between operations  0.96 us (1%)
  local copies, waits for them, and re-layouts  0.92 us (1%)
    ppermute x8, starting transfers between devices, swap(): return lax.ppermute(x, ('lat', 'lon'), partner_pairs(mesh_shape, bits))  9.83 us
    ppermute x8, waiting for transfers between devices, swap(): return lax.ppermute(x, ('lat', 'lon'), partner_pairs(mesh_shape, bits))  7.87 us
    pallas_call x2, Pallas kernels, backward(): pl.pallas_call(functools.partial(bwd_kernel, sizes, n), in_specs=[smem] +...  7.34 us
    pallas_call x2, Pallas kernels, forward(): pl.pallas_call(functools.partial(fwd_kernel, sizes, n), in_specs=[smem] +...  7.22 us
    pallas_call x8, Pallas kernels, step_call(): pl.pallas_call(kernel, in_specs=scalars, out_shape=outs, compiler_params=...  4.22 us
    ppermute x1, starting transfers between devices, shards(): get_s = lax.ppermute(strip_s, 'lat', pair_b)  4.2 us
    ppermute x1, starting transfers between devices, shards(): from_b = lax.ppermute(own_b, 'lat', pair_b)  4.1 us
    ppermute x1, waiting for transfers between devices, shards(): side_b = lax.ppermute(corner_b, 'lat', pair_b)  4 us
  transfers between devices with their start and end apart: 18, of which 8 were waited for; matrix products, arithmetic and copies ran while one was open for 0% of the time, Pallas kernels for 26%

profile of v6, /device:TPU:1, one launch (start us, length us, event | category | flops | bytes accessed | tf_op | source)
XLA Modules:
  0.0 80.2 jit_solution(6591784690291641798)
XLA Ops:
  0.6 0.0 copy-start.4
  0.6 0.0 copy-start.3
  0.7 0.1 stack.24.info_ref
  0.8 2.0 %pack.1 = (bf16[2,96,512]{2,1,0:T(8,128)(2,1)S(1)}, bf16[2,96,512]{2,1,0:T(8,128)(2,1)S(1)}, bf16[2,96,512]{2,1,0:T(8,128)(2,1)S(1)}, bf16[2,96,512]{2,1,0:T(8,128)(2,1)S(1)}) custom-call(s32[6]{0:T(128)S(1)} %stack.24.info_ref, bf16[256,512]{1,0:T(8,128)(2,1)} %bitcast.22, bf16[256,512]{1,0:T(8,128)(2,1)} %bitcast.25), custom_call_target="tpu_custom_call" | custom-call | tf_op jit(solution)/shard_map/pack/pallas_call | solution.py:556
  2.8 2.1 %collective-permute-start = (bf16[2,96,512]{2,1,0:T(8,128)(2,1)S(1)}, bf16[2,96,512]{2,1,0:T(8,128)(2,1)S(1)}, u32[]{:S(2)}, u32[]{:S(2)}) collective-permute-start(bf16[2,96,512]{2,1,0:T(8,128)(2,1)S(1)} %get-tuple-element.70), channel_id=1, source_target_pairs={{0,1},{1,2},{2,3},{3,4},{4,5},{5,6},{6,7},{7,0},{8,9},{9,10},{10,1... | collective-permute-start | bytes 589832 | tf_op jit(solution)/shard_map/ppermute | solution.py:564
  4.9 3.1 %collective-permute-start.1 = (bf16[2,96,512]{2,1,0:T(8,128)(2,1)S(1)}, bf16[2,96,512]{2,1,0:T(8,128)(2,1)S(1)}, u32[]{:S(2)}, u32[]{:S(2)}) collective-permute-start(bf16[2,96,512]{2,1,0:T(8,128)(2,1)S(1)} %get-tuple-element.71), channel_id=1, source_target_pairs={{0,7},{1,0},{2,1},{3,2},{4,3},{5,4},{6,5},{7,6},{8,15},{9,8},{10,9... | collective-permute-start | bytes 589832 | tf_op jit(solution)/shard_map/ppermute | solution.py:565
  8.0 4.1 %collective-permute-start.2 = (bf16[2,96,512]{2,1,0:T(8,128)(2,1)S(1)}, bf16[2,96,512]{2,1,0:T(8,128)(2,1)S(1)}, u32[]{:S(2)}, u32[]{:S(2)}) collective-permute-start(bf16[2,96,512]{2,1,0:T(8,128)(2,1)S(1)} %get-tuple-element.72), channel_id=1, source_target_pairs={{8,16},{16,8},{9,17},{17,9},{10,18},{18,10},{11,19},{19,11},{12,20... | collective-permute-start | bytes 589832 | tf_op jit(solution)/shard_map/ppermute | solution.py:566
  12.1 0.0 copy-start.5
  12.1 0.8 copy-done.5
  12.9 3.9 %prepare.1 = (f32[512,512]{1,0:T(8,128)S(1)}, bf16[256,512]{1,0:T(8,128)(2,1)S(1)}) custom-call(f32[13,8,13]{2,1,0:T(8,128)S(1)} %bitcast.28, bf16[256,1024]{1,0:T(8,128)(2,1)} %bitcast.15, bf16[512,1024]{1,0:T(8,128)(2,1)} %w_ref.1), custom_call_target="tpu_custom_call" | custom-call | tf_op jit(solution)/shard_map/prepare/pallas_call | solution.py:568
  16.8 0.9 %corner.1 = (bf16[2,176,512]{2,1,0:T(8,128)(2,1)S(1)}, bf16[2,80,512]{2,1,0:T(8,128)(2,1)S(1)}) custom-call(s32[6]{0:T(128)S(1)} %stack.24.info_ref, bf16[2,96,512]{2,1,0:T(8,128)(2,1)S(1)} %collective-permute-done.w_ref, bf16[2,96,512]{2,1,0:T(8,128)(2,1)S(1)} %collective-permute-done.1.e_ref, bf16[2,96,512]{2,1,0:T(8,128)(2,1)S(1)} %get-tuple-element.76.own_ref), custom_call_target="tpu_custom_call" | custom-call | tf_op jit(solution)/shard_map/corner/pallas_call | solution.py:582
  17.7 0.1 collective-permute-start.3
  17.8 2.6 %collective-permute-start.4 = (bf16[2,80,512]{2,1,0:T(8,128)(2,1)S(1)}, bf16[2,80,512]{2,1,0:T(8,128)(2,1)S(1)}, u32[]{:S(2)}, u32[]{:S(2)}) collective-permute-start(bf16[2,80,512]{2,1,0:T(8,128)(2,1)S(1)} %get-tuple-element.79), channel_id=1, source_target_pairs={{8,16},{16,8},{9,17},{17,9},{10,18},{18,10},{11,19},{19,11},{12,20... | collective-permute-start | bytes 491528 | tf_op jit(solution)/shard_map/ppermute | solution.py:589
  20.4 4.0 %collective-permute-done.4.c_ref = bf16[2,80,512]{2,1,0:T(8,128)(2,1)S(1)} collective-permute-done((bf16[2,80,512]{2,1,0:T(8,128)(2,1)S(1)}, bf16[2,80,512]{2,1,0:T(8,128)(2,1)S(1)}, u32[]{:S(2)}, u32[]{:S(2)}) %collective-permute-start.4) | collective-permute-done | bytes 163872 | tf_op jit(solution)/shard_map/ppermute | solution.py:589
  24.4 3.6 %attend_fwd.3 = (bf16[256,256]{1,0:T(8,128)(2,1)S(1)}, bf16[256,1024]{1,0:T(8,128)(2,1)S(1)}, f32[4,512,256]{2,1,0:T(8,128)S(1)}, bf16[896,256]{1,0:T(8,128)(2,1)S(1)}, bf16[896,256]{1,0:T(8,128)(2,1)S(1)}) custom-call(s32[6]{0:T(128)S(1)} %stack.24.info_ref, bf16[256,512]{1,0:T(8,128)(2,1)S(1)} %bitcast.18, bf16[256,512]{1,0:T(8,128)(2,1)S(1)} %bitcast.23, ...), custom_call_target="tpu_custom_call" | custom-call | tf_op jit(solution)/shard_map/attend_fwd/pallas_call | solution.py:595
  28.0 0.1 collective-permute-start.5
  28.1 3.6 %attend_fwd.2 = (bf16[256,256]{1,0:T(8,128)(2,1)S(1)}, f32[256,1024]{1,0:T(8,128)S(1)}, f32[4,512,256]{2,1,0:T(8,128)S(1)}, bf16[896,256]{1,0:T(8,128)(2,1)S(1)}, bf16[896,256]{1,0:T(8,128)(2,1)S(1)}) custom-call(s32[6]{0:T(128)S(1)} %stack.24.info_ref, bf16[256,512]{1,0:T(8,128)(2,1)S(1)} %bitcast.19, bf16[256,512]{1,0:T(8,128)(2,1)S(1)} %bitcast.24, ...), custom_call_target="tpu_custom_call" | custom-call | tf_op jit(solution)/shard_map/attend_fwd/pallas_call | solution.py:595
  31.7 0.7 halve.2
  32.4 0.1 collective-permute-start.6
  32.5 3.4 %attend_bwd.2 = (bf16[256,256]{1,0:T(8,128)(2,1)S(1)}, bf16[2,192,256]{2,1,0:T(8,128)(2,1)S(1)}, bf16[2,192,256]{2,1,0:T(8,128)(2,1)S(1)}, f32[2,256,256]{2,1,0:...) custom-call(s32[6]{0:T(128)S(1)} %stack.24.info_ref, bf16[256,512]{1,0:T(8,128)(2,1)S(1)} %bitcast.20, ...), custom_call_target="tpu_custom_call" | custom-call | tf_op jit(solution)/shard_map/attend_bwd/pallas_call | solution.py:627
  35.9 4.2 %collective-permute-start.8 = (bf16[2,192,256]{2,1,0:T(8,128)(2,1)S(1)}, bf16[2,192,256]{2,1,0:T(8,128)(2,1)S(1)}, u32[]{:S(2)}, u32[]{:S(2)}) collective-permute-start(bf16[2,192,256]{2,1,0:T(8,128)(2,1)S(1)} %get-tuple-element.103), channel_id=1, source_target_pairs={{8,16},{16,8},{9,17},{17,9},{10,18},{18,10},{11,19},{19,11},{12,20... | collective-permute-start | bytes 589832 | tf_op jit(solution)/shard_map/ppermute | solution.py:645
  40.1 0.6 halve.3
  40.8 0.1 collective-permute-start.7
  40.8 0.0 copy-start.1
  40.9 3.9 %attend_bwd.3 = (bf16[256,512]{1,0:T(8,128)(2,1)}, bf16[2,192,512]{2,1,0:T(8,128)(2,1)S(1)}, bf16[2,192,256]{2,1,0:T(8,128)(2,1)S(1)}, f32[2,256,256]{2,1,0:T(8,...) custom-call(s32[6]{0:T(128)S(1)} %stack.24.info_ref, bf16[256,512]{1,0:T(8,128)(2,1)S(1)} %bitcast.21, ...), custom_call_target="tpu_custom_call" | custom-call | tf_op jit(solution)/shard_map/attend_bwd/pallas_call | solution.py:627
  44.8 1.2 %bias_fold.1.bias_ref = f32[8,256]{1,0:T(8,128)S(1)} custom-call(s32[6]{0:T(128)S(1)} %stack.24.info_ref, f32[416,128]{1,0:T(8,128)S(1)} %get-tuple-element.105.xs_ref, f32[416,128]{1,0:T(8,128)S(1)} %get-tuple-element.106.xk_ref), custom_call_target="tpu_custom_call" | custom-call | tf_op jit(solution)/shard_map/bias_fold/pallas_call | solution.py:656
  46.0 0.1 meet.1.own_ref
  46.1 0.3 collective-permute-start.11
  46.3 1.6 %collective-permute-start.9 = (bf16[72,1024]{1,0:T(8,128)(2,1)S(1)}, bf16[72,1024]{1,0:T(8,128)(2,1)S(1)}, u32[]{:S(2)}, u32[]{:S(2)}) collective-permute-start(bf16[72,1024]{1,0:T(8,128)(2,1)S(1)} %meet.1.own_ref), channel_id=1, source_target_pairs={{0,2},{1,3},{2,0},{3,1},{4,6},{5,7},{6,4},{7,5},{8,12},{9,13},{10,... | collective-permute-start | bytes 442376 | tf_op jit(solution)/shard_map/ppermute | solution.py:439
  47.9 2.8 %collective-permute-start.12 = (bf16[2,192,256]{2,1,0:T(8,128)(2,1)S(1)}, bf16[2,192,256]{2,1,0:T(8,128)(2,1)S(1)}, u32[]{:S(2)}, u32[]{:S(2)}) collective-permute-start(bf16[2,192,256]{2,1,0:T(8,128)(2,1)S(1)} %get-tuple-element.118), channel_id=1, source_target_pairs={{8,16},{16,8},{9,17},{17,9},{10,18},{18,10},{11,19},{19,11},{12,20... | collective-permute-start | bytes 589832 | tf_op jit(solution)/shard_map/ppermute | solution.py:674
  50.7 1.8 %project.1 = bf16[256,1024]{1,0:T(8,128)(2,1)} custom-call(s32[6]{0:T(128)S(1)} %stack.24.info_ref, bf16[256,256]{1,0:T(8,128)(2,1)S(1)} %get-tuple-element.110.s_ref, bf16[256,256]{1,0:T(8,128)(2,1)S(1)} %get-tuple-element.111.k_ref, bf16[512,1024]{1,0:T(8,128)(2,1)S(1)} %copy-done.1), custom_call_target="tpu_custom_call" | custom-call | tf_op jit(solution)/shard_map/project/pallas_call | solution.py:664
  52.5 0.3 collective-permute-done.9.got_ref
  52.9 0.7 collective-permute-start.10
  53.5 1.4 %collective-permute-done.12.bk_ref = bf16[2,192,256]{2,1,0:T(8,128)(2,1)S(1)} collective-permute-done((bf16[2,192,256]{2,1,0:T(8,128)(2,1)S(1)}, bf16[2,192,256]{2,1,0:T(8,128)(2,1)S(1)}, u32[]{:S(2)}, u32[]{:S(2)}) %collective-permute-start.12) | collective-permute-done | bytes 196640 | tf_op jit(solution)/shard_map/ppermute | solution.py:674
  54.9 1.0 %side.1 = (bf16[2,96,512]{2,1,0:T(8,128)(2,1)S(1)}, bf16[2,96,512]{2,1,0:T(8,128)(2,1)S(1)}) custom-call(s32[6]{0:T(128)S(1)} %stack.24.info_ref, f32[2,256,256]{2,1,0:T(8,128)S(1)} %get-tuple-element.115.ss_ref, f32[2,256,256]{2,1,0:T(8,128)S(1)} %get-tuple-element.116.sk_ref, bf16[2,192,512]{2,1,0:T(8,128)(2,1)S(1)} %collective-permute-done.11.a_ref, ...), custom_call_target="tpu_custom_call" | custom-call | tf_op jit(solution)/shard_map/side/pallas_call | solution.py:681
  55.9 1.7 %collective-permute-start.14 = (bf16[2,96,512]{2,1,0:T(8,128)(2,1)S(1)}, bf16[2,96,512]{2,1,0:T(8,128)(2,1)S(1)}, u32[]{:S(2)}, u32[]{:S(2)}) collective-permute-start(bf16[2,96,512]{2,1,0:T(8,128)(2,1)S(1)} %get-tuple-element.120), channel_id=1, source_target_pairs={{0,7},{1,0},{2,1},{3,2},{4,3},{5,4},{6,5},{7,6},{8,15},{9,8},{10,9... | collective-permute-start | bytes 589832 | tf_op jit(solution)/shard_map/ppermute | solution.py:689
  57.6 0.7 collective-permute-done.10.got_ref
  58.4 1.2 %collective-permute-start.13 = (bf16[72,1024]{1,0:T(8,128)(2,1)S(1)}, bf16[72,1024]{1,0:T(8,128)(2,1)S(1)}, u32[]{:S(2)}, u32[]{:S(2)}) collective-permute-start(bf16[72,1024]{1,0:T(8,128)(2,1)S(1)} %total.3.own_ref), channel_id=1, source_target_pairs={{0,1},{1,0},{2,3},{3,2},{4,5},{5,4},{6,7},{7,6},{8,24},{9,25},{10,... | collective-permute-start | bytes 442376 | tf_op jit(solution)/shard_map/ppermute | solution.py:439
  59.6 3.1 %collective-permute-done.13.got_ref = bf16[72,1024]{1,0:T(8,128)(2,1)S(1)} collective-permute-done((bf16[72,1024]{1,0:T(8,128)(2,1)S(1)}, bf16[72,1024]{1,0:T(8,128)(2,1)S(1)}, u32[]{:S(2)}, u32[]{:S(2)}) %collective-permute-start.13) | collective-permute-done | bytes 147488 | tf_op jit(solution)/shard_map/ppermute | solution.py:439
  62.7 0.6 grow.2.own_ref
  63.3 3.0 %collective-permute-done.15.w_ref = bf16[2,96,512]{2,1,0:T(8,128)(2,1)S(1)} collective-permute-done((bf16[2,96,512]{2,1,0:T(8,128)(2,1)S(1)}, bf16[2,96,512]{2,1,0:T(8,128)(2,1)S(1)}, u32[]{:S(2)}, u32[]{:S(2)}) %collective-permute-start.15) | collective-permute-done | bytes 196640 | tf_op jit(solution)/shard_map/ppermute | solution.py:690
  66.3 2.2 %collective-permute-start.16 = (bf16[136,1024]{1,0:T(8,128)(2,1)S(1)}, bf16[136,1024]{1,0:T(8,128)(2,1)S(1)}, u32[]{:S(2)}, u32[]{:S(2)}) collective-permute-start(bf16[136,1024]{1,0:T(8,128)(2,1)S(1)} %grow.2.own_ref), channel_id=1, source_target_pairs={{0,16},{1,17},{2,18},{3,19},{4,20},{5,21},{6,22},{7,23},{8,9},{9,8... | collective-permute-start | bytes 835592 | tf_op jit(solution)/shard_map/ppermute | solution.py:439
  68.5 1.8 %join.1 = (bf16[256,512]{1,0:T(8,128)(2,1)}, bf16[256,512]{1,0:T(8,128)(2,1)}) custom-call(s32[6]{0:T(128)S(1)} %stack.24.info_ref, f32[2,256,256]{2,1,0:T(8,128)S(1)} %get-tuple-element.124.ms_ref, f32[2,256,256]{2,1,0:T(8,128)S(1)} %get-tuple-element.125.mk_ref, bf16[2,192,512]{2,1,0:T(8,128)(2,1)S(1)} %collective-permute-done.11.a_ref, ...), custom_call_target="tpu_custom_call" | custom-call | tf_op jit(solution)/shard_map/join/pallas_call | solution.py:700
  70.3 2.1 %collective-permute-done.16.got_ref = bf16[136,1024]{1,0:T(8,128)(2,1)S(1)} collective-permute-done((bf16[136,1024]{1,0:T(8,128)(2,1)S(1)}, bf16[136,1024]{1,0:T(8,128)(2,1)S(1)}, u32[]{:S(2)}, u32[]{:S(2)}) %collective-permute-start.16) | collective-permute-done | bytes 278560 | tf_op jit(solution)/shard_map/ppermute | solution.py:439
  72.5 0.6 grow.3.own_ref
  73.0 4.0 %collective-permute-start.17 = (bf16[264,1024]{1,0:T(8,128)(2,1)S(1)}, bf16[264,1024]{1,0:T(8,128)(2,1)S(1)}, u32[]{:S(2)}, u32[]{:S(2)}) collective-permute-start(bf16[264,1024]{1,0:T(8,128)(2,1)S(1)} %grow.3.own_ref), channel_id=1, source_target_pairs={{0,8},{1,9},{2,10},{3,11},{4,12},{5,13},{6,14},{7,15},{8,0},{9,1},... | collective-permute-start | bytes 1622024 | tf_op jit(solution)/shard_map/ppermute | solution.py:439
  77.0 1.6 %collective-permute-done.17.got_ref = bf16[264,1024]{1,0:T(8,128)(2,1)S(1)} collective-permute-done((bf16[264,1024]{1,0:T(8,128)(2,1)S(1)}, bf16[264,1024]{1,0:T(8,128)(2,1)S(1)}, u32[]{:S(2)}, u32[]{:S(2)}) %collective-permute-start.17) | collective-permute-done | bytes 540704 | tf_op jit(solution)/shard_map/ppermute | solution.py:439
  78.6 1.6 %last.1 = (bf16[512,1024]{1,0:T(8,128)(2,1)}, f32[13,8,13]{2,1,0:T(8,128)}) custom-call(s32[6]{0:T(128)S(1)} %stack.24.info_ref, bf16[264,1024]{1,0:T(8,128)(2,1)S(1)} %grow.3.own_ref, bf16[264,1024]{1,0:T(8,128)(2,1)S(1)} %collective-permute-done.17.got_ref), custom_call_target="tpu_custom_call" | custom-call | tf_op jit(solution)/shard_map/last/pallas_call | solution.py:610
  (20 shorter events, 0.1 us)
Async XLA Ops:
  0.6 23.8 %copy-start.4 = (bf16[16,16,512]{2,1,0:T(8,128)(2,1)S(1)}, bf16[16,16,512]{2,1,0:T(8,128)(2,1)}, u32[]{:S(2)}) copy-start(bf16[16,16,512]{2,1,0:T(8,128)(2,1)} %param.8) | copy-start | bytes 786436
  0.6 23.8 %copy-start.3 = (bf16[16,16,512]{2,1,0:T(8,128)(2,1)S(1)}, bf16[16,16,512]{2,1,0:T(8,128)(2,1)}, u32[]{:S(2)}) copy-start(bf16[16,16,512]{2,1,0:T(8,128)(2,1)} %param.7) | copy-start | bytes 786436
  0.7 23.8 %copy-start = (bf16[16,16,1024]{2,1,0:T(8,128)(2,1)S(1)}, bf16[16,16,1024]{2,1,0:T(8,128)(2,1)}, u32[]{:S(2)}) copy-start(bf16[16,16,1024]{2,1,0:T(8,128)(2,1)} %param.11) | copy-start | bytes 1572868
  0.7 23.8 %copy-start.2 = (bf16[16,16,512]{2,1,0:T(8,128)(2,1)S(1)}, bf16[16,16,512]{2,1,0:T(8,128)(2,1)}, u32[]{:S(2)}) copy-start(bf16[16,16,512]{2,1,0:T(8,128)(2,1)} %param.6) | copy-start | bytes 786436
  2.8 14.0 %collective-permute-start = (bf16[2,96,512]{2,1,0:T(8,128)(2,1)S(1)}, bf16[2,96,512]{2,1,0:T(8,128)(2,1)S(1)}, u32[]{:S(2)}, u32[]{:S(2)}) collective-permute-start(bf16[2,96,512]{2,1,0:T(8,128)(2,1)S(1)} %get-tuple-element.70), channel_id=1, source_target_pairs={{0,1},{1,2},{2,3},{3,4},{4,5},{5,6},{6,7},{7,0},{8,9},{9,10},{10,1... | collective-permute-start | bytes 589832 | tf_op jit(solution)/shard_map/ppermute | solution.py:564
  4.9 11.9 %collective-permute-start.1 = (bf16[2,96,512]{2,1,0:T(8,128)(2,1)S(1)}, bf16[2,96,512]{2,1,0:T(8,128)(2,1)S(1)}, u32[]{:S(2)}, u32[]{:S(2)}) collective-permute-start(bf16[2,96,512]{2,1,0:T(8,128)(2,1)S(1)} %get-tuple-element.71), channel_id=1, source_target_pairs={{0,7},{1,0},{2,1},{3,2},{4,3},{5,4},{6,5},{7,6},{8,15},{9,8},{10,9... | collective-permute-start | bytes 589832 | tf_op jit(solution)/shard_map/ppermute | solution.py:565
  8.0 8.8 %collective-permute-start.2 = (bf16[2,96,512]{2,1,0:T(8,128)(2,1)S(1)}, bf16[2,96,512]{2,1,0:T(8,128)(2,1)S(1)}, u32[]{:S(2)}, u32[]{:S(2)}) collective-permute-start(bf16[2,96,512]{2,1,0:T(8,128)(2,1)S(1)} %get-tuple-element.72), channel_id=1, source_target_pairs={{8,16},{16,8},{9,17},{17,9},{10,18},{18,10},{11,19},{19,11},{12,20... | collective-permute-start | bytes 589832 | tf_op jit(solution)/shard_map/ppermute | solution.py:566
  12.1 0.8 %copy-start.5 = (f32[8,13,13]{2,0,1:T(8,128)S(1)}, f32[8,13,13]{2,0,1:T(8,128)}, u32[]{:S(2)}) copy-start(f32[8,13,13]{2,0,1:T(8,128)} %param.9) | copy-start | bytes 16228
  17.7 6.7 %collective-permute-start.3 = (bf16[2,176,512]{2,1,0:T(8,128)(2,1)S(1)}, bf16[2,176,512]{2,1,0:T(8,128)(2,1)S(1)}, u32[]{:S(2)}, u32[]{:S(2)}) collective-permute-start(bf16[2,176,512]{2,1,0:T(8,128)(2,1)S(1)} %get-tuple-element.77), channel_id=1, source_target_pairs={{0,8},{8,0},{16,24},{24,16},{1,9},{9,1},{17,25},{25,17},{2,10},{10... | collective-permute-start | bytes 1081352 | tf_op jit(solution)/shard_map/ppermute | solution.py:590
  17.8 6.6 %collective-permute-start.4 = (bf16[2,80,512]{2,1,0:T(8,128)(2,1)S(1)}, bf16[2,80,512]{2,1,0:T(8,128)(2,1)S(1)}, u32[]{:S(2)}, u32[]{:S(2)}) collective-permute-start(bf16[2,80,512]{2,1,0:T(8,128)(2,1)S(1)} %get-tuple-element.79), channel_id=1, source_target_pairs={{8,16},{16,8},{9,17},{17,9},{10,18},{18,10},{11,19},{19,11},{12,20... | collective-permute-start | bytes 491528 | tf_op jit(solution)/shard_map/ppermute | solution.py:589
  28.0 3.7 %collective-permute-start.5 = (bf16[256,1024]{1,0:T(8,128)(2,1)S(1)}, bf16[256,1024]{1,0:T(8,128)(2,1)S(1)}, u32[]{:S(2)}, u32[]{:S(2)}) collective-permute-start(bf16[256,1024]{1,0:T(8,128)(2,1)S(1)} %get-tuple-element.82), channel_id=1, source_target_pairs={{0,8},{1,9},{2,10},{3,11},{4,12},{5,13},{6,14},{7,15},{8,0},{9,1},... | collective-permute-start | bytes 1572872 | tf_op jit(solution)/shard_map/ppermute | solution.py:439
  32.4 7.7 %collective-permute-start.6 = (bf16[128,1024]{1,0:T(8,128)(2,1)S(1)}, bf16[128,1024]{1,0:T(8,128)(2,1)S(1)}, u32[]{:S(2)}, u32[]{:S(2)}) collective-permute-start(bf16[128,1024]{1,0:T(8,128)(2,1)S(1)} %get-tuple-element.85), channel_id=1, source_target_pairs={{0,16},{1,17},{2,18},{3,19},{4,20},{5,21},{6,22},{7,23},{8,9},{9,8... | collective-permute-start | bytes 786440 | tf_op jit(solution)/shard_map/ppermute | solution.py:439
  35.9 8.9 %collective-permute-start.8 = (bf16[2,192,256]{2,1,0:T(8,128)(2,1)S(1)}, bf16[2,192,256]{2,1,0:T(8,128)(2,1)S(1)}, u32[]{:S(2)}, u32[]{:S(2)}) collective-permute-start(bf16[2,192,256]{2,1,0:T(8,128)(2,1)S(1)} %get-tuple-element.103), channel_id=1, source_target_pairs={{8,16},{16,8},{9,17},{17,9},{10,18},{18,10},{11,19},{19,11},{12,20... | collective-permute-start | bytes 589832 | tf_op jit(solution)/shard_map/ppermute | solution.py:645
  40.8 4.0 %collective-permute-start.7 = (bf16[64,1024]{1,0:T(8,128)(2,1)S(1)}, bf16[64,1024]{1,0:T(8,128)(2,1)S(1)}, u32[]{:S(2)}, u32[]{:S(2)}) collective-permute-start(bf16[64,1024]{1,0:T(8,128)(2,1)S(1)} %get-tuple-element.95), channel_id=1, source_target_pairs={{0,1},{1,0},{2,3},{3,2},{4,5},{5,4},{6,7},{7,6},{8,24},{9,25},{10,... | collective-permute-start | bytes 393224 | tf_op jit(solution)/shard_map/ppermute | solution.py:439
  40.8 9.9 %copy-start.1 = (bf16[512,1024]{1,0:T(8,128)(2,1)S(1)}, bf16[512,1024]{1,0:T(8,128)(2,1)}, u32[]{:S(2)}) copy-start(bf16[512,1024]{1,0:T(8,128)(2,1)} %w_ref.1) | copy-start | bytes 3145732
  46.1 8.8 %collective-permute-start.11 = (bf16[2,192,512]{2,1,0:T(8,128)(2,1)S(1)}, bf16[2,192,512]{2,1,0:T(8,128)(2,1)S(1)}, u32[]{:S(2)}, u32[]{:S(2)}) collective-permute-start(bf16[2,192,512]{2,1,0:T(8,128)(2,1)S(1)} %get-tuple-element.117), channel_id=1, source_target_pairs={{0,8},{8,0},{16,24},{24,16},{1,9},{9,1},{17,25},{25,17},{2,10},{10... | collective-permute-start | bytes 1179656 | tf_op jit(solution)/shard_map/ppermute | solution.py:675
  46.3 6.5 %collective-permute-start.9 = (bf16[72,1024]{1,0:T(8,128)(2,1)S(1)}, bf16[72,1024]{1,0:T(8,128)(2,1)S(1)}, u32[]{:S(2)}, u32[]{:S(2)}) collective-permute-start(bf16[72,1024]{1,0:T(8,128)(2,1)S(1)} %meet.1.own_ref), channel_id=1, source_target_pairs={{0,2},{1,3},{2,0},{3,1},{4,6},{5,7},{6,4},{7,5},{8,12},{9,13},{10,... | collective-permute-start | bytes 442376 | tf_op jit(solution)/shard_map/ppermute | solution.py:439
  47.9 7.0 %collective-permute-start.12 = (bf16[2,192,256]{2,1,0:T(8,128)(2,1)S(1)}, bf16[2,192,256]{2,1,0:T(8,128)(2,1)S(1)}, u32[]{:S(2)}, u32[]{:S(2)}) collective-permute-start(bf16[2,192,256]{2,1,0:T(8,128)(2,1)S(1)} %get-tuple-element.118), channel_id=1, source_target_pairs={{8,16},{16,8},{9,17},{17,9},{10,18},{18,10},{11,19},{19,11},{12,20... | collective-permute-start | bytes 589832 | tf_op jit(solution)/shard_map/ppermute | solution.py:674
  52.9 5.5 %collective-permute-start.10 = (bf16[72,1024]{1,0:T(8,128)(2,1)S(1)}, bf16[72,1024]{1,0:T(8,128)(2,1)S(1)}, u32[]{:S(2)}, u32[]{:S(2)}) collective-permute-start(bf16[72,1024]{1,0:T(8,128)(2,1)S(1)} %total.2.own_ref), channel_id=1, source_target_pairs={{0,4},{1,5},{2,6},{3,7},{4,0},{5,1},{6,2},{7,3},{8,10},{9,11},{10,... | collective-permute-start | bytes 442376 | tf_op jit(solution)/shard_map/ppermute | solution.py:439
  55.9 7.4 %collective-permute-start.14 = (bf16[2,96,512]{2,1,0:T(8,128)(2,1)S(1)}, bf16[2,96,512]{2,1,0:T(8,128)(2,1)S(1)}, u32[]{:S(2)}, u32[]{:S(2)}) collective-permute-start(bf16[2,96,512]{2,1,0:T(8,128)(2,1)S(1)} %get-tuple-element.120), channel_id=1, source_target_pairs={{0,7},{1,0},{2,1},{3,2},{4,3},{5,4},{6,5},{7,6},{8,15},{9,8},{10,9... | collective-permute-start | bytes 589832 | tf_op jit(solution)/shard_map/ppermute | solution.py:689
  57.6 8.7 %collective-permute-start.15 = (bf16[2,96,512]{2,1,0:T(8,128)(2,1)S(1)}, bf16[2,96,512]{2,1,0:T(8,128)(2,1)S(1)}, u32[]{:S(2)}, u32[]{:S(2)}) collective-permute-start(bf16[2,96,512]{2,1,0:T(8,128)(2,1)S(1)} %get-tuple-element.121), channel_id=1, source_target_pairs={{0,1},{1,2},{2,3},{3,4},{4,5},{5,6},{6,7},{7,0},{8,9},{9,10},{10,1... | collective-permute-start | bytes 589832 | tf_op jit(solution)/shard_map/ppermute | solution.py:690
  58.4 4.4 %collective-permute-start.13 = (bf16[72,1024]{1,0:T(8,128)(2,1)S(1)}, bf16[72,1024]{1,0:T(8,128)(2,1)S(1)}, u32[]{:S(2)}, u32[]{:S(2)}) collective-permute-start(bf16[72,1024]{1,0:T(8,128)(2,1)S(1)} %total.3.own_ref), channel_id=1, source_target_pairs={{0,1},{1,0},{2,3},{3,2},{4,5},{5,4},{6,7},{7,6},{8,24},{9,25},{10,... | collective-permute-start | bytes 442376 | tf_op jit(solution)/shard_map/ppermute | solution.py:439
  66.3 6.1 %collective-permute-start.16 = (bf16[136,1024]{1,0:T(8,128)(2,1)S(1)}, bf16[136,1024]{1,0:T(8,128)(2,1)S(1)}, u32[]{:S(2)}, u32[]{:S(2)}) collective-permute-start(bf16[136,1024]{1,0:T(8,128)(2,1)S(1)} %grow.2.own_ref), channel_id=1, source_target_pairs={{0,16},{1,17},{2,18},{3,19},{4,20},{5,21},{6,22},{7,23},{8,9},{9,8... | collective-permute-start | bytes 835592 | tf_op jit(solution)/shard_map/ppermute | solution.py:439
  73.0 5.5 %collective-permute-start.17 = (bf16[264,1024]{1,0:T(8,128)(2,1)S(1)}, bf16[264,1024]{1,0:T(8,128)(2,1)S(1)}, u32[]{:S(2)}, u32[]{:S(2)}) collective-permute-start(bf16[264,1024]{1,0:T(8,128)(2,1)S(1)} %grow.3.own_ref), channel_id=1, source_target_pairs={{0,8},{1,9},{2,10},{3,11},{4,12},{5,13},{6,14},{7,15},{8,0},{9,1},... | collective-permute-start | bytes 1622024 | tf_op jit(solution)/shard_map/ppermute | solution.py:439

commit v7 on v6

--- a/solution.py
+++ b/solution.py
@@ -419,6 +419,7 @@
 
 def rounds_of(mesh_shape):
     first, *rest = bits_of(mesh_shape)
+    rest[-3], rest[-2] = rest[-2], rest[-3]
     middle, ends = rest[:-2], rest[-2:]
     turned = middle[1:] + middle[:1]
     return [(first, first)] + list(zip(middle, turned)), list(zip(ends, ends[::-1]))
@@ -650,7 +651,11 @@
         got = swap(send, mesh_shape, rounds[number])
     after = backward(2, info_b, p_k, k_k, v_k, *before)
     query_grad, strip_a, strip_b, mid_k, side_k, fold_k = after
-    got, fold_k, get_s = lax.optimization_barrier((got, fold_k, get_s))
+    got, fold_k, strip_a, strip_b, get_s = lax.optimization_barrier(
+        (got, fold_k, strip_a, strip_b, get_s)
+    )
+    get_b = lax.ppermute(strip_b, "lat", pair_b)
+    get_a = lax.ppermute(strip_a, "lat", pair_a)
 
     count = 256
     bias_local = pl.pallas_call(
@@ -670,9 +675,6 @@
     )(info, att_s, att_k, out_weight)
     note = shape((keep.shape[0] + heads, model))
     message = step_call(meet_kernel, "meet", note, keep, got, bias_local)
-    message, strip_a, strip_b = lax.optimization_barrier((message, strip_a, strip_b))
-    get_b = lax.ppermute(strip_b, "lat", pair_b)
-    get_a = lax.ppermute(strip_a, "lat", pair_a)
     got = swap(message, mesh_shape, ends[0])
     kernel = functools.partial(total_kernel, None, count, heads)
     message = step_call(kernel, "total", note, message, got)

time: 81.1 us -> 79.4 us (0.979)
  starting transfers between devices: 30.8 us -> 25.1 us
  waiting for transfers between devices: 16.3 us -> 19.8 us
    ppermute x8, starting transfers between devices: 9.83 us -> 5.59 us  [swap(): return lax.ppermute(x, ('lat', 'lon'), partner_pairs(mesh_shape, bits))]
    ppermute x1, waiting for transfers between devices: 0.01 us -> 3.11 us  [shards(): get_east = lax.ppermute(give_west, 'lon', west)]
    ppermute x1, waiting for transfers between devices: 3 us -> 1.14 us  [shards(): get_west = lax.ppermute(give_east, 'lon', east)]
    ppermute x8, waiting for transfers between devices: 7.87 us -> 9.59 us  [swap(): return lax.ppermute(x, ('lat', 'lon'), partner_pairs(mesh_shape, bits))]
    ppermute x1, starting transfers between devices: 2.78 us -> 1.91 us  [shards(): get_b = lax.ppermute(strip_b, 'lat', pair_b)]
  transfers between devices with their start and end apart: 18 -> 18, of which waited for: 8 -> 9; matrix products, arithmetic and copies ran while one was open for 0% -> 0% of each run, Pallas kernels for 26% -> 28%
where the time goes in v7:
time: 79.4 us; the launch traced here: 78.1 us
  Pallas kernels  31.3 us (39%)
  starting transfers between devices  25.1 us (32%)
  waiting for transfers between devices  19.8 us (25%)
  between operations  0.97 us (1%)
  local copies, waits for them, and re-layouts  0.92 us (1%)
    ppermute x8, waiting for transfers between devices, swap(): return lax.ppermute(x, ('lat', 'lon'), partner_pairs(mesh_shape, bits))  9.59 us
    pallas_call x2, Pallas kernels, backward(): pl.pallas_call(functools.partial(bwd_kernel, sizes, n), in_specs=[smem] +...  7.34 us
    pallas_call x2, Pallas kernels, forward(): pl.pallas_call(functools.partial(fwd_kernel, sizes, n), in_specs=[smem] +...  7.22 us
    ppermute x8, starting transfers between devices, swap(): return lax.ppermute(x, ('lat', 'lon'), partner_pairs(mesh_shape, bits))  5.59 us
    pallas_call x8, Pallas kernels, step_call(): pl.pallas_call(kernel, in_specs=scalars, out_shape=outs, compiler_params=...  4.22 us
    ppermute x1, starting transfers between devices, shards(): from_b = lax.ppermute(own_b, 'lat', pair_b)  4.1 us
    ppermute x1, waiting for transfers between devices, shards(): side_b = lax.ppermute(corner_b, 'lat', pair_b)  4 us
    pallas_call x1, Pallas kernels, shards(): pl.pallas_call(functools.partial(prepare_kernel, lon_dev, cols_pad), in_s...  3.86 us
  transfers between devices with their start and end apart: 18, of which 9 were waited for; matrix products, arithmetic and copies ran while one was open for 0% of the time, Pallas kernels for 28%

profile of v7, /device:TPU:1, one launch (start us, length us, event | category | flops | bytes accessed | tf_op | source)
XLA Modules:
  0.0 78.1 jit_solution(9518478760470530327)
XLA Ops:
  0.6 0.0 copy-start.4
  0.6 0.0 copy-start.3
  0.7 0.1 stack.24.info_ref
  0.8 2.0 %pack.1 = (bf16[2,96,512]{2,1,0:T(8,128)(2,1)S(1)}, bf16[2,96,512]{2,1,0:T(8,128)(2,1)S(1)}, bf16[2,96,512]{2,1,0:T(8,128)(2,1)S(1)}, bf16[2,96,512]{2,1,0:T(8,128)(2,1)S(1)}) custom-call(s32[6]{0:T(128)S(1)} %stack.24.info_ref, bf16[256,512]{1,0:T(8,128)(2,1)} %bitcast.22, bf16[256,512]{1,0:T(8,128)(2,1)} %bitcast.25), custom_call_target="tpu_custom_call" | custom-call | tf_op jit(solution)/shard_map/pack/pallas_call | solution.py:557
  2.8 2.1 %collective-permute-start = (bf16[2,96,512]{2,1,0:T(8,128)(2,1)S(1)}, bf16[2,96,512]{2,1,0:T(8,128)(2,1)S(1)}, u32[]{:S(2)}, u32[]{:S(2)}) collective-permute-start(bf16[2,96,512]{2,1,0:T(8,128)(2,1)S(1)} %get-tuple-element.69), channel_id=1, source_target_pairs={{0,1},{1,2},{2,3},{3,4},{4,5},{5,6},{6,7},{7,0},{8,9},{9,10},{10,1... | collective-permute-start | bytes 589832 | tf_op jit(solution)/shard_map/ppermute | solution.py:565
  4.9 3.1 %collective-permute-start.1 = (bf16[2,96,512]{2,1,0:T(8,128)(2,1)S(1)}, bf16[2,96,512]{2,1,0:T(8,128)(2,1)S(1)}, u32[]{:S(2)}, u32[]{:S(2)}) collective-permute-start(bf16[2,96,512]{2,1,0:T(8,128)(2,1)S(1)} %get-tuple-element.70), channel_id=1, source_target_pairs={{0,7},{1,0},{2,1},{3,2},{4,3},{5,4},{6,5},{7,6},{8,15},{9,8},{10,9... | collective-permute-start | bytes 589832 | tf_op jit(solution)/shard_map/ppermute | solution.py:566
  8.0 4.1 %collective-permute-start.2 = (bf16[2,96,512]{2,1,0:T(8,128)(2,1)S(1)}, bf16[2,96,512]{2,1,0:T(8,128)(2,1)S(1)}, u32[]{:S(2)}, u32[]{:S(2)}) collective-permute-start(bf16[2,96,512]{2,1,0:T(8,128)(2,1)S(1)} %get-tuple-element.71), channel_id=1, source_target_pairs={{8,16},{16,8},{9,17},{17,9},{10,18},{18,10},{11,19},{19,11},{12,20... | collective-permute-start | bytes 589832 | tf_op jit(solution)/shard_map/ppermute | solution.py:567
  12.1 0.8 %copy-done.5 = f32[8,13,13]{2,0,1:T(8,128)S(1)} copy-done((f32[8,13,13]{2,0,1:T(8,128)S(1)}, f32[8,13,13]{2,0,1:T(8,128)}, u32[]{:S(2)}) %copy-start.5) | copy-done | bytes 5432
  12.9 3.9 %prepare.1 = (f32[512,512]{1,0:T(8,128)S(1)}, bf16[256,512]{1,0:T(8,128)(2,1)S(1)}) custom-call(f32[13,8,13]{2,1,0:T(8,128)S(1)} %bitcast.28, bf16[256,1024]{1,0:T(8,128)(2,1)} %bitcast.15, bf16[512,1024]{1,0:T(8,128)(2,1)} %w_ref.1), custom_call_target="tpu_custom_call" | custom-call | tf_op jit(solution)/shard_map/prepare/pallas_call | solution.py:569
  16.8 0.9 %corner.1 = (bf16[2,176,512]{2,1,0:T(8,128)(2,1)S(1)}, bf16[2,80,512]{2,1,0:T(8,128)(2,1)S(1)}) custom-call(s32[6]{0:T(128)S(1)} %stack.24.info_ref, bf16[2,96,512]{2,1,0:T(8,128)(2,1)S(1)} %collective-permute-done.w_ref, bf16[2,96,512]{2,1,0:T(8,128)(2,1)S(1)} %collective-permute-done.1.e_ref, bf16[2,96,512]{2,1,0:T(8,128)(2,1)S(1)} %get-tuple-element.75.own_ref), custom_call_target="tpu_custom_call" | custom-call | tf_op jit(solution)/shard_map/corner/pallas_call | solution.py:583
  17.7 0.1 collective-permute-start.3
  17.8 2.6 %collective-permute-start.4 = (bf16[2,80,512]{2,1,0:T(8,128)(2,1)S(1)}, bf16[2,80,512]{2,1,0:T(8,128)(2,1)S(1)}, u32[]{:S(2)}, u32[]{:S(2)}) collective-permute-start(bf16[2,80,512]{2,1,0:T(8,128)(2,1)S(1)} %get-tuple-element.78), channel_id=1, source_target_pairs={{8,16},{16,8},{9,17},{17,9},{10,18},{18,10},{11,19},{19,11},{12,20... | collective-permute-start | bytes 491528 | tf_op jit(solution)/shard_map/ppermute | solution.py:590
  20.4 4.0 %collective-permute-done.4.c_ref = bf16[2,80,512]{2,1,0:T(8,128)(2,1)S(1)} collective-permute-done((bf16[2,80,512]{2,1,0:T(8,128)(2,1)S(1)}, bf16[2,80,512]{2,1,0:T(8,128)(2,1)S(1)}, u32[]{:S(2)}, u32[]{:S(2)}) %collective-permute-start.4) | collective-permute-done | bytes 163872 | tf_op jit(solution)/shard_map/ppermute | solution.py:590
  24.4 3.6 %attend_fwd.3 = (bf16[256,256]{1,0:T(8,128)(2,1)S(1)}, bf16[256,1024]{1,0:T(8,128)(2,1)S(1)}, f32[4,512,256]{2,1,0:T(8,128)S(1)}, bf16[896,256]{1,0:T(8,128)(2,1)S(1)}, bf16[896,256]{1,0:T(8,128)(2,1)S(1)}) custom-call(s32[6]{0:T(128)S(1)} %stack.24.info_ref, bf16[256,512]{1,0:T(8,128)(2,1)S(1)} %bitcast.18, bf16[256,512]{1,0:T(8,128)(2,1)S(1)} %bitcast.23, ...), custom_call_target="tpu_custom_call" | custom-call | tf_op jit(solution)/shard_map/attend_fwd/pallas_call | solution.py:596
  28.1 0.1 collective-permute-start.5
  28.1 3.6 %attend_fwd.2 = (bf16[256,256]{1,0:T(8,128)(2,1)S(1)}, f32[256,1024]{1,0:T(8,128)S(1)}, f32[4,512,256]{2,1,0:T(8,128)S(1)}, bf16[896,256]{1,0:T(8,128)(2,1)S(1)}, bf16[896,256]{1,0:T(8,128)(2,1)S(1)}) custom-call(s32[6]{0:T(128)S(1)} %stack.24.info_ref, bf16[256,512]{1,0:T(8,128)(2,1)S(1)} %bitcast.19, bf16[256,512]{1,0:T(8,128)(2,1)S(1)} %bitcast.24, ...), custom_call_target="tpu_custom_call" | custom-call | tf_op jit(solution)/shard_map/attend_fwd/pallas_call | solution.py:596
  31.8 0.7 halve.2
  32.5 0.6 collective-permute-start.6
  33.1 3.4 %attend_bwd.2 = (bf16[256,256]{1,0:T(8,128)(2,1)S(1)}, bf16[2,192,256]{2,1,0:T(8,128)(2,1)S(1)}, bf16[2,192,256]{2,1,0:T(8,128)(2,1)S(1)}, f32[2,256,256]{2,1,0:...) custom-call(s32[6]{0:T(128)S(1)} %stack.24.info_ref, bf16[256,512]{1,0:T(8,128)(2,1)S(1)} %bitcast.20, ...), custom_call_target="tpu_custom_call" | custom-call | tf_op jit(solution)/shard_map/attend_bwd/pallas_call | solution.py:628
  36.5 3.6 %collective-permute-start.8 = (bf16[2,192,256]{2,1,0:T(8,128)(2,1)S(1)}, bf16[2,192,256]{2,1,0:T(8,128)(2,1)S(1)}, u32[]{:S(2)}, u32[]{:S(2)}) collective-permute-start(bf16[2,192,256]{2,1,0:T(8,128)(2,1)S(1)} %get-tuple-element.104), channel_id=1, source_target_pairs={{8,16},{16,8},{9,17},{17,9},{10,18},{18,10},{11,19},{19,11},{12,20... | collective-permute-start | bytes 589832 | tf_op jit(solution)/shard_map/ppermute | solution.py:646
  40.2 0.6 halve.3
  40.8 0.1 collective-permute-start.7
  40.9 0.0 copy-start.1
  40.9 3.9 %attend_bwd.3 = (bf16[256,512]{1,0:T(8,128)(2,1)}, bf16[2,192,512]{2,1,0:T(8,128)(2,1)S(1)}, bf16[2,192,256]{2,1,0:T(8,128)(2,1)S(1)}, f32[2,256,256]{2,1,0:T(8,...) custom-call(s32[6]{0:T(128)S(1)} %stack.24.info_ref, bf16[256,512]{1,0:T(8,128)(2,1)S(1)} %bitcast.21, ...), custom_call_target="tpu_custom_call" | custom-call | tf_op jit(solution)/shard_map/attend_bwd/pallas_call | solution.py:628
  44.8 0.1 collective-permute-done.7.got_ref
  44.9 0.1 collective-permute-start.11
  45.0 1.2 %bias_fold.1.bias_ref = f32[8,256]{1,0:T(8,128)S(1)} custom-call(s32[6]{0:T(128)S(1)} %stack.24.info_ref, f32[416,128]{1,0:T(8,128)S(1)} %get-tuple-element.106.xs_ref, f32[416,128]{1,0:T(8,128)S(1)} %get-tuple-element.107.xk_ref), custom_call_target="tpu_custom_call" | custom-call | tf_op jit(solution)/shard_map/bias_fold/pallas_call | solution.py:661
  46.2 0.1 meet.1.own_ref
  46.3 2.2 %collective-permute-start.9 = (bf16[72,1024]{1,0:T(8,128)(2,1)S(1)}, bf16[72,1024]{1,0:T(8,128)(2,1)S(1)}, u32[]{:S(2)}, u32[]{:S(2)}) collective-permute-start(bf16[72,1024]{1,0:T(8,128)(2,1)S(1)} %meet.1.own_ref), channel_id=1, source_target_pairs={{0,1},{1,0},{2,3},{3,2},{4,5},{5,4},{6,7},{7,6},{8,12},{9,13},{10,... | collective-permute-start | bytes 442376 | tf_op jit(solution)/shard_map/ppermute | solution.py:440
  48.5 1.9 %collective-permute-start.12 = (bf16[2,192,256]{2,1,0:T(8,128)(2,1)S(1)}, bf16[2,192,256]{2,1,0:T(8,128)(2,1)S(1)}, u32[]{:S(2)}, u32[]{:S(2)}) collective-permute-start(bf16[2,192,256]{2,1,0:T(8,128)(2,1)S(1)} %get-tuple-element.116), channel_id=1, source_target_pairs={{8,16},{16,8},{9,17},{17,9},{10,18},{18,10},{11,19},{19,11},{12,20... | collective-permute-start | bytes 589832 | tf_op jit(solution)/shard_map/ppermute | solution.py:657
  50.5 1.8 %project.1 = bf16[256,1024]{1,0:T(8,128)(2,1)} custom-call(s32[6]{0:T(128)S(1)} %stack.24.info_ref, bf16[256,256]{1,0:T(8,128)(2,1)S(1)} %get-tuple-element.108.s_ref, bf16[256,256]{1,0:T(8,128)(2,1)S(1)} %get-tuple-element.109.k_ref, bf16[512,1024]{1,0:T(8,128)(2,1)S(1)} %copy-done.1), custom_call_target="tpu_custom_call" | custom-call | tf_op jit(solution)/shard_map/project/pallas_call | solution.py:669
  52.2 0.6 collective-permute-done.9.got_ref
  52.9 0.7 collective-permute-start.10
  53.5 2.0 %collective-permute-done.12.bk_ref = bf16[2,192,256]{2,1,0:T(8,128)(2,1)S(1)} collective-permute-done((bf16[2,192,256]{2,1,0:T(8,128)(2,1)S(1)}, bf16[2,192,256]{2,1,0:T(8,128)(2,1)S(1)}, u32[]{:S(2)}, u32[]{:S(2)}) %collective-permute-start.12) | collective-permute-done | bytes 196640 | tf_op jit(solution)/shard_map/ppermute | solution.py:657
  55.5 1.0 %side.1 = (bf16[2,96,512]{2,1,0:T(8,128)(2,1)S(1)}, bf16[2,96,512]{2,1,0:T(8,128)(2,1)S(1)}) custom-call(s32[6]{0:T(128)S(1)} %stack.24.info_ref, f32[2,256,256]{2,1,0:T(8,128)S(1)} %get-tuple-element.113.ss_ref, f32[2,256,256]{2,1,0:T(8,128)S(1)} %get-tuple-element.114.sk_ref, bf16[2,192,512]{2,1,0:T(8,128)(2,1)S(1)} %collective-permute-done.11.a_ref, ...), custom_call_target="tpu_custom_call" | custom-call | tf_op jit(solution)/shard_map/side/pallas_call | solution.py:683
  56.5 1.8 %collective-permute-start.14 = (bf16[2,96,512]{2,1,0:T(8,128)(2,1)S(1)}, bf16[2,96,512]{2,1,0:T(8,128)(2,1)S(1)}, u32[]{:S(2)}, u32[]{:S(2)}) collective-permute-start(bf16[2,96,512]{2,1,0:T(8,128)(2,1)S(1)} %get-tuple-element.118), channel_id=1, source_target_pairs={{0,7},{1,0},{2,1},{3,2},{4,3},{5,4},{6,5},{7,6},{8,15},{9,8},{10,9... | collective-permute-start | bytes 589832 | tf_op jit(solution)/shard_map/ppermute | solution.py:691
  58.4 0.7 collective-permute-start.13
  59.2 3.6 %collective-permute-done.13.got_ref = bf16[72,1024]{1,0:T(8,128)(2,1)S(1)} collective-permute-done((bf16[72,1024]{1,0:T(8,128)(2,1)S(1)}, bf16[72,1024]{1,0:T(8,128)(2,1)S(1)}, u32[]{:S(2)}, u32[]{:S(2)}) %collective-permute-start.13) | collective-permute-done | bytes 147488 | tf_op jit(solution)/shard_map/ppermute | solution.py:440
  62.8 0.6 grow.2.own_ref
  63.3 3.1 %collective-permute-done.14.e_ref = bf16[2,96,512]{2,1,0:T(8,128)(2,1)S(1)} collective-permute-done((bf16[2,96,512]{2,1,0:T(8,128)(2,1)S(1)}, bf16[2,96,512]{2,1,0:T(8,128)(2,1)S(1)}, u32[]{:S(2)}, u32[]{:S(2)}) %collective-permute-start.14) | collective-permute-done | bytes 196640 | tf_op jit(solution)/shard_map/ppermute | solution.py:691
  66.4 1.1 %collective-permute-done.15.w_ref = bf16[2,96,512]{2,1,0:T(8,128)(2,1)S(1)} collective-permute-done((bf16[2,96,512]{2,1,0:T(8,128)(2,1)S(1)}, bf16[2,96,512]{2,1,0:T(8,128)(2,1)S(1)}, u32[]{:S(2)}, u32[]{:S(2)}) %collective-permute-start.15) | collective-permute-done | bytes 196640 | tf_op jit(solution)/shard_map/ppermute | solution.py:692
  67.6 0.2 collective-permute-start.16
  67.7 1.8 %join.1 = (bf16[256,512]{1,0:T(8,128)(2,1)}, bf16[256,512]{1,0:T(8,128)(2,1)}) custom-call(s32[6]{0:T(128)S(1)} %stack.24.info_ref, f32[2,256,256]{2,1,0:T(8,128)S(1)} %get-tuple-element.122.ms_ref, f32[2,256,256]{2,1,0:T(8,128)S(1)} %get-tuple-element.123.mk_ref, bf16[2,192,512]{2,1,0:T(8,128)(2,1)S(1)} %collective-permute-done.11.a_ref, ...), custom_call_target="tpu_custom_call" | custom-call | tf_op jit(solution)/shard_map/join/pallas_call | solution.py:702
  69.5 3.7 %collective-permute-done.16.got_ref = bf16[136,1024]{1,0:T(8,128)(2,1)S(1)} collective-permute-done((bf16[136,1024]{1,0:T(8,128)(2,1)S(1)}, bf16[136,1024]{1,0:T(8,128)(2,1)S(1)}, u32[]{:S(2)}, u32[]{:S(2)}) %collective-permute-start.16) | collective-permute-done | bytes 278560 | tf_op jit(solution)/shard_map/ppermute | solution.py:440
  73.3 0.6 grow.3.own_ref
  73.9 1.0 %collective-permute-start.17 = (bf16[264,1024]{1,0:T(8,128)(2,1)S(1)}, bf16[264,1024]{1,0:T(8,128)(2,1)S(1)}, u32[]{:S(2)}, u32[]{:S(2)}) collective-permute-start(bf16[264,1024]{1,0:T(8,128)(2,1)S(1)} %grow.3.own_ref), channel_id=1, source_target_pairs={{0,8},{1,9},{2,10},{3,11},{4,12},{5,13},{6,14},{7,15},{8,0},{9,1},... | collective-permute-start | bytes 1622024 | tf_op jit(solution)/shard_map/ppermute | solution.py:440
  74.9 1.6 %collective-permute-done.17.got_ref = bf16[264,1024]{1,0:T(8,128)(2,1)S(1)} collective-permute-done((bf16[264,1024]{1,0:T(8,128)(2,1)S(1)}, bf16[264,1024]{1,0:T(8,128)(2,1)S(1)}, u32[]{:S(2)}, u32[]{:S(2)}) %collective-permute-start.17) | collective-permute-done | bytes 540704 | tf_op jit(solution)/shard_map/ppermute | solution.py:440
  76.5 1.6 %last.1 = (bf16[512,1024]{1,0:T(8,128)(2,1)}, f32[13,8,13]{2,1,0:T(8,128)}) custom-call(s32[6]{0:T(128)S(1)} %stack.24.info_ref, bf16[264,1024]{1,0:T(8,128)(2,1)S(1)} %grow.3.own_ref, bf16[264,1024]{1,0:T(8,128)(2,1)S(1)} %collective-permute-done.17.got_ref), custom_call_target="tpu_custom_call" | custom-call | tf_op jit(solution)/shard_map/last/pallas_call | solution.py:611
  (20 shorter events, 0.1 us)
Async XLA Ops:
  0.6 23.8 %copy-start.4 = (bf16[16,16,512]{2,1,0:T(8,128)(2,1)S(1)}, bf16[16,16,512]{2,1,0:T(8,128)(2,1)}, u32[]{:S(2)}) copy-start(bf16[16,16,512]{2,1,0:T(8,128)(2,1)} %param.8) | copy-start | bytes 786436
  0.6 23.8 %copy-start.3 = (bf16[16,16,512]{2,1,0:T(8,128)(2,1)S(1)}, bf16[16,16,512]{2,1,0:T(8,128)(2,1)}, u32[]{:S(2)}) copy-start(bf16[16,16,512]{2,1,0:T(8,128)(2,1)} %param.7) | copy-start | bytes 786436
  0.7 23.8 %copy-start = (bf16[16,16,1024]{2,1,0:T(8,128)(2,1)S(1)}, bf16[16,16,1024]{2,1,0:T(8,128)(2,1)}, u32[]{:S(2)}) copy-start(bf16[16,16,1024]{2,1,0:T(8,128)(2,1)} %param.11) | copy-start | bytes 1572868
  0.7 23.8 %copy-start.2 = (bf16[16,16,512]{2,1,0:T(8,128)(2,1)S(1)}, bf16[16,16,512]{2,1,0:T(8,128)(2,1)}, u32[]{:S(2)}) copy-start(bf16[16,16,512]{2,1,0:T(8,128)(2,1)} %param.6) | copy-start | bytes 786436
  2.8 14.0 %collective-permute-start = (bf16[2,96,512]{2,1,0:T(8,128)(2,1)S(1)}, bf16[2,96,512]{2,1,0:T(8,128)(2,1)S(1)}, u32[]{:S(2)}, u32[]{:S(2)}) collective-permute-start(bf16[2,96,512]{2,1,0:T(8,128)(2,1)S(1)} %get-tuple-element.69), channel_id=1, source_target_pairs={{0,1},{1,2},{2,3},{3,4},{4,5},{5,6},{6,7},{7,0},{8,9},{9,10},{10,1... | collective-permute-start | bytes 589832 | tf_op jit(solution)/shard_map/ppermute | solution.py:565
  4.9 11.9 %collective-permute-start.1 = (bf16[2,96,512]{2,1,0:T(8,128)(2,1)S(1)}, bf16[2,96,512]{2,1,0:T(8,128)(2,1)S(1)}, u32[]{:S(2)}, u32[]{:S(2)}) collective-permute-start(bf16[2,96,512]{2,1,0:T(8,128)(2,1)S(1)} %get-tuple-element.70), channel_id=1, source_target_pairs={{0,7},{1,0},{2,1},{3,2},{4,3},{5,4},{6,5},{7,6},{8,15},{9,8},{10,9... | collective-permute-start | bytes 589832 | tf_op jit(solution)/shard_map/ppermute | solution.py:566
  8.0 8.8 %collective-permute-start.2 = (bf16[2,96,512]{2,1,0:T(8,128)(2,1)S(1)}, bf16[2,96,512]{2,1,0:T(8,128)(2,1)S(1)}, u32[]{:S(2)}, u32[]{:S(2)}) collective-permute-start(bf16[2,96,512]{2,1,0:T(8,128)(2,1)S(1)} %get-tuple-element.71), channel_id=1, source_target_pairs={{8,16},{16,8},{9,17},{17,9},{10,18},{18,10},{11,19},{19,11},{12,20... | collective-permute-start | bytes 589832 | tf_op jit(solution)/shard_map/ppermute | solution.py:567
  12.1 0.8 %copy-start.5 = (f32[8,13,13]{2,0,1:T(8,128)S(1)}, f32[8,13,13]{2,0,1:T(8,128)}, u32[]{:S(2)}) copy-start(f32[8,13,13]{2,0,1:T(8,128)} %param.9) | copy-start | bytes 16228
  17.7 6.7 %collective-permute-start.3 = (bf16[2,176,512]{2,1,0:T(8,128)(2,1)S(1)}, bf16[2,176,512]{2,1,0:T(8,128)(2,1)S(1)}, u32[]{:S(2)}, u32[]{:S(2)}) collective-permute-start(bf16[2,176,512]{2,1,0:T(8,128)(2,1)S(1)} %get-tuple-element.76), channel_id=1, source_target_pairs={{0,8},{8,0},{16,24},{24,16},{1,9},{9,1},{17,25},{25,17},{2,10},{10... | collective-permute-start | bytes 1081352 | tf_op jit(solution)/shard_map/ppermute | solution.py:591
  17.8 6.6 %collective-permute-start.4 = (bf16[2,80,512]{2,1,0:T(8,128)(2,1)S(1)}, bf16[2,80,512]{2,1,0:T(8,128)(2,1)S(1)}, u32[]{:S(2)}, u32[]{:S(2)}) collective-permute-start(bf16[2,80,512]{2,1,0:T(8,128)(2,1)S(1)} %get-tuple-element.78), channel_id=1, source_target_pairs={{8,16},{16,8},{9,17},{17,9},{10,18},{18,10},{11,19},{19,11},{12,20... | collective-permute-start | bytes 491528 | tf_op jit(solution)/shard_map/ppermute | solution.py:590
  28.1 3.7 %collective-permute-start.5 = (bf16[256,1024]{1,0:T(8,128)(2,1)S(1)}, bf16[256,1024]{1,0:T(8,128)(2,1)S(1)}, u32[]{:S(2)}, u32[]{:S(2)}) collective-permute-start(bf16[256,1024]{1,0:T(8,128)(2,1)S(1)} %get-tuple-element.81), channel_id=1, source_target_pairs={{0,8},{1,9},{2,10},{3,11},{4,12},{5,13},{6,14},{7,15},{8,0},{9,1},... | collective-permute-start | bytes 1572872 | tf_op jit(solution)/shard_map/ppermute | solution.py:440
  32.5 7.7 %collective-permute-start.6 = (bf16[128,1024]{1,0:T(8,128)(2,1)S(1)}, bf16[128,1024]{1,0:T(8,128)(2,1)S(1)}, u32[]{:S(2)}, u32[]{:S(2)}) collective-permute-start(bf16[128,1024]{1,0:T(8,128)(2,1)S(1)} %get-tuple-element.84), channel_id=1, source_target_pairs={{0,16},{1,17},{2,18},{3,19},{4,20},{5,21},{6,22},{7,23},{8,10},{9,... | collective-permute-start | bytes 786440 | tf_op jit(solution)/shard_map/ppermute | solution.py:440
  36.5 8.3 %collective-permute-start.8 = (bf16[2,192,256]{2,1,0:T(8,128)(2,1)S(1)}, bf16[2,192,256]{2,1,0:T(8,128)(2,1)S(1)}, u32[]{:S(2)}, u32[]{:S(2)}) collective-permute-start(bf16[2,192,256]{2,1,0:T(8,128)(2,1)S(1)} %get-tuple-element.104), channel_id=1, source_target_pairs={{8,16},{16,8},{9,17},{17,9},{10,18},{18,10},{11,19},{19,11},{12,20... | collective-permute-start | bytes 589832 | tf_op jit(solution)/shard_map/ppermute | solution.py:646
  40.8 4.1 %collective-permute-start.7 = (bf16[64,1024]{1,0:T(8,128)(2,1)S(1)}, bf16[64,1024]{1,0:T(8,128)(2,1)S(1)}, u32[]{:S(2)}, u32[]{:S(2)}) collective-permute-start(bf16[64,1024]{1,0:T(8,128)(2,1)S(1)} %get-tuple-element.94), channel_id=1, source_target_pairs={{0,2},{1,3},{2,0},{3,1},{4,6},{5,7},{6,4},{7,5},{8,24},{9,25},{10,... | collective-permute-start | bytes 393224 | tf_op jit(solution)/shard_map/ppermute | solution.py:440
  40.9 9.6 %copy-start.1 = (bf16[512,1024]{1,0:T(8,128)(2,1)S(1)}, bf16[512,1024]{1,0:T(8,128)(2,1)}, u32[]{:S(2)}) copy-start(bf16[512,1024]{1,0:T(8,128)(2,1)} %w_ref.1) | copy-start | bytes 3145732
  44.9 10.6 %collective-permute-start.11 = (bf16[2,192,512]{2,1,0:T(8,128)(2,1)S(1)}, bf16[2,192,512]{2,1,0:T(8,128)(2,1)S(1)}, u32[]{:S(2)}, u32[]{:S(2)}) collective-permute-start(bf16[2,192,512]{2,1,0:T(8,128)(2,1)S(1)} %get-tuple-element.115), channel_id=1, source_target_pairs={{0,8},{8,0},{16,24},{24,16},{1,9},{9,1},{17,25},{25,17},{2,10},{10... | collective-permute-start | bytes 1179656 | tf_op jit(solution)/shard_map/ppermute | solution.py:658
  46.3 6.5 %collective-permute-start.9 = (bf16[72,1024]{1,0:T(8,128)(2,1)S(1)}, bf16[72,1024]{1,0:T(8,128)(2,1)S(1)}, u32[]{:S(2)}, u32[]{:S(2)}) collective-permute-start(bf16[72,1024]{1,0:T(8,128)(2,1)S(1)} %meet.1.own_ref), channel_id=1, source_target_pairs={{0,1},{1,0},{2,3},{3,2},{4,5},{5,4},{6,7},{7,6},{8,12},{9,13},{10,... | collective-permute-start | bytes 442376 | tf_op jit(solution)/shard_map/ppermute | solution.py:440
  48.5 7.0 %collective-permute-start.12 = (bf16[2,192,256]{2,1,0:T(8,128)(2,1)S(1)}, bf16[2,192,256]{2,1,0:T(8,128)(2,1)S(1)}, u32[]{:S(2)}, u32[]{:S(2)}) collective-permute-start(bf16[2,192,256]{2,1,0:T(8,128)(2,1)S(1)} %get-tuple-element.116), channel_id=1, source_target_pairs={{8,16},{16,8},{9,17},{17,9},{10,18},{18,10},{11,19},{19,11},{12,20... | collective-permute-start | bytes 589832 | tf_op jit(solution)/shard_map/ppermute | solution.py:657
  52.9 5.5 %collective-permute-start.10 = (bf16[72,1024]{1,0:T(8,128)(2,1)S(1)}, bf16[72,1024]{1,0:T(8,128)(2,1)S(1)}, u32[]{:S(2)}, u32[]{:S(2)}) collective-permute-start(bf16[72,1024]{1,0:T(8,128)(2,1)S(1)} %total.2.own_ref), channel_id=1, source_target_pairs={{0,4},{1,5},{2,6},{3,7},{4,0},{5,1},{6,2},{7,3},{8,9},{9,8},{10,11... | collective-permute-start | bytes 442376 | tf_op jit(solution)/shard_map/ppermute | solution.py:440
  56.5 9.9 %collective-permute-start.14 = (bf16[2,96,512]{2,1,0:T(8,128)(2,1)S(1)}, bf16[2,96,512]{2,1,0:T(8,128)(2,1)S(1)}, u32[]{:S(2)}, u32[]{:S(2)}) collective-permute-start(bf16[2,96,512]{2,1,0:T(8,128)(2,1)S(1)} %get-tuple-element.118), channel_id=1, source_target_pairs={{0,7},{1,0},{2,1},{3,2},{4,3},{5,4},{6,5},{7,6},{8,15},{9,8},{10,9... | collective-permute-start | bytes 589832 | tf_op jit(solution)/shard_map/ppermute | solution.py:691
  58.3 9.2 %collective-permute-start.15 = (bf16[2,96,512]{2,1,0:T(8,128)(2,1)S(1)}, bf16[2,96,512]{2,1,0:T(8,128)(2,1)S(1)}, u32[]{:S(2)}, u32[]{:S(2)}) collective-permute-start(bf16[2,96,512]{2,1,0:T(8,128)(2,1)S(1)} %get-tuple-element.119), channel_id=1, source_target_pairs={{0,1},{1,2},{2,3},{3,4},{4,5},{5,6},{6,7},{7,0},{8,9},{9,10},{10,1... | collective-permute-start | bytes 589832 | tf_op jit(solution)/shard_map/ppermute | solution.py:692
  58.4 4.4 %collective-permute-start.13 = (bf16[72,1024]{1,0:T(8,128)(2,1)S(1)}, bf16[72,1024]{1,0:T(8,128)(2,1)S(1)}, u32[]{:S(2)}, u32[]{:S(2)}) collective-permute-start(bf16[72,1024]{1,0:T(8,128)(2,1)S(1)} %total.3.own_ref), channel_id=1, source_target_pairs={{0,2},{1,3},{2,0},{3,1},{4,6},{5,7},{6,4},{7,5},{8,24},{9,25},{10,... | collective-permute-start | bytes 442376 | tf_op jit(solution)/shard_map/ppermute | solution.py:440
  67.6 5.7 %collective-permute-start.16 = (bf16[136,1024]{1,0:T(8,128)(2,1)S(1)}, bf16[136,1024]{1,0:T(8,128)(2,1)S(1)}, u32[]{:S(2)}, u32[]{:S(2)}) collective-permute-start(bf16[136,1024]{1,0:T(8,128)(2,1)S(1)} %grow.2.own_ref), channel_id=1, source_target_pairs={{0,16},{1,17},{2,18},{3,19},{4,20},{5,21},{6,22},{7,23},{8,10},{9,... | collective-permute-start | bytes 835592 | tf_op jit(solution)/shard_map/ppermute | solution.py:440
  73.9 2.6 %collective-permute-start.17 = (bf16[264,1024]{1,0:T(8,128)(2,1)S(1)}, bf16[264,1024]{1,0:T(8,128)(2,1)S(1)}, u32[]{:S(2)}, u32[]{:S(2)}) collective-permute-start(bf16[264,1024]{1,0:T(8,128)(2,1)S(1)} %grow.3.own_ref), channel_id=1, source_target_pairs={{0,8},{1,9},{2,10},{3,11},{4,12},{5,13},{6,14},{7,15},{8,0},{9,1},... | collective-permute-start | bytes 1622024 | tf_op jit(solution)/shard_map/ppermute | solution.py:440

commit v8 on v7

--- a/solution.py
+++ b/solution.py
@@ -678,7 +678,6 @@
     got = swap(message, mesh_shape, ends[0])
     kernel = functools.partial(total_kernel, None, count, heads)
     message = step_call(kernel, "total", note, message, got)
-    message, block_out = lax.optimization_barrier((message, block_out))
     got = swap(message, mesh_shape, ends[1])
     give_west, give_east = pl.pallas_call(
         functools.partial(side_kernel, lat_dev, lon_dev, cols_pad),
@@ -696,7 +695,9 @@
 
     for number in range(len(rounds) - 1, 0, -1):
         if number == 1:
-            message, get_east, get_west = lax.optimization_barrier((message, get_east, get_west))
+            message, get_east, get_west, block_out = lax.optimization_barrier(
+                (message, get_east, get_west, block_out)
+            )
         got = swap(message, mesh_shape, rounds[number])
         if number == 1:
             key_grad, value_grad = pl.pallas_call(

time: 79.4 us -> 79.5 us (level)
  no operation moved by 1% of the time
where the time goes in v8:
time: 79.5 us; the launch traced here: 78.1 us
  Pallas kernels  31.3 us (39%)
  starting transfers between devices  24.8 us (31%)
  waiting for transfers between devices  20.2 us (25%)
  between operations  0.95 us (1%)
  local copies, waits for them, and re-layouts  0.92 us (1%)
    ppermute x8, waiting for transfers between devices, swap(): return lax.ppermute(x, ('lat', 'lon'), partner_pairs(mesh_shape, bits))  9.58 us
    pallas_call x2, Pallas kernels, backward(): pl.pallas_call(functools.partial(bwd_kernel, sizes, n), in_specs=[smem] +...  7.34 us
    pallas_call x2, Pallas kernels, forward(): pl.pallas_call(functools.partial(fwd_kernel, sizes, n), in_specs=[smem] +...  7.22 us
    ppermute x8, starting transfers between devices, swap(): return lax.ppermute(x, ('lat', 'lon'), partner_pairs(mesh_shape, bits))  5.23 us
    pallas_call x8, Pallas kernels, step_call(): pl.pallas_call(kernel, in_specs=scalars, out_shape=outs, compiler_params=...  4.22 us
    ppermute x1, starting transfers between devices, shards(): from_b = lax.ppermute(own_b, 'lat', pair_b)  4.1 us
    ppermute x1, waiting for transfers between devices, shards(): side_b = lax.ppermute(corner_b, 'lat', pair_b)  4 us
    pallas_call x1, Pallas kernels, shards(): pl.pallas_call(functools.partial(prepare_kernel, lon_dev, cols_pad), in_s...  3.86 us
  transfers between devices with their start and end apart: 18, of which 9 were waited for; matrix products, arithmetic and copies ran while one was open for 0% of the time, Pallas kernels for 28%

profile of v8, /device:TPU:1, one launch (start us, length us, event | category | flops | bytes accessed | tf_op | source)
XLA Modules:
  0.0 78.1 jit_solution(11006083415313459769)
XLA Ops:
  0.6 0.0 copy-start.4
  0.6 0.0 copy-start.3
  0.7 0.0 copy-start
  0.7 0.1 stack.24.info_ref
  0.8 2.0 %pack.1 = (bf16[2,96,512]{2,1,0:T(8,128)(2,1)S(1)}, bf16[2,96,512]{2,1,0:T(8,128)(2,1)S(1)}, bf16[2,96,512]{2,1,0:T(8,128)(2,1)S(1)}, bf16[2,96,512]{2,1,0:T(8,128)(2,1)S(1)}) custom-call(s32[6]{0:T(128)S(1)} %stack.24.info_ref, bf16[256,512]{1,0:T(8,128)(2,1)} %bitcast.22, bf16[256,512]{1,0:T(8,128)(2,1)} %bitcast.25), custom_call_target="tpu_custom_call" | custom-call | tf_op jit(solution)/shard_map/pack/pallas_call | solution.py:557
  2.8 2.1 %collective-permute-start = (bf16[2,96,512]{2,1,0:T(8,128)(2,1)S(1)}, bf16[2,96,512]{2,1,0:T(8,128)(2,1)S(1)}, u32[]{:S(2)}, u32[]{:S(2)}) collective-permute-start(bf16[2,96,512]{2,1,0:T(8,128)(2,1)S(1)} %get-tuple-element.68), channel_id=1, source_target_pairs={{0,1},{1,2},{2,3},{3,4},{4,5},{5,6},{6,7},{7,0},{8,9},{9,10},{10,1... | collective-permute-start | bytes 589832 | tf_op jit(solution)/shard_map/ppermute | solution.py:565
  4.9 3.1 %collective-permute-start.1 = (bf16[2,96,512]{2,1,0:T(8,128)(2,1)S(1)}, bf16[2,96,512]{2,1,0:T(8,128)(2,1)S(1)}, u32[]{:S(2)}, u32[]{:S(2)}) collective-permute-start(bf16[2,96,512]{2,1,0:T(8,128)(2,1)S(1)} %get-tuple-element.69), channel_id=1, source_target_pairs={{0,7},{1,0},{2,1},{3,2},{4,3},{5,4},{6,5},{7,6},{8,15},{9,8},{10,9... | collective-permute-start | bytes 589832 | tf_op jit(solution)/shard_map/ppermute | solution.py:566
  8.0 4.1 %collective-permute-start.2 = (bf16[2,96,512]{2,1,0:T(8,128)(2,1)S(1)}, bf16[2,96,512]{2,1,0:T(8,128)(2,1)S(1)}, u32[]{:S(2)}, u32[]{:S(2)}) collective-permute-start(bf16[2,96,512]{2,1,0:T(8,128)(2,1)S(1)} %get-tuple-element.70), channel_id=1, source_target_pairs={{8,16},{16,8},{9,17},{17,9},{10,18},{18,10},{11,19},{19,11},{12,20... | collective-permute-start | bytes 589832 | tf_op jit(solution)/shard_map/ppermute | solution.py:567
  12.1 0.8 %copy-done.5 = f32[8,13,13]{2,0,1:T(8,128)S(1)} copy-done((f32[8,13,13]{2,0,1:T(8,128)S(1)}, f32[8,13,13]{2,0,1:T(8,128)}, u32[]{:S(2)}) %copy-start.5) | copy-done | bytes 5432
  12.9 3.9 %prepare.1 = (f32[512,512]{1,0:T(8,128)S(1)}, bf16[256,512]{1,0:T(8,128)(2,1)S(1)}) custom-call(f32[13,8,13]{2,1,0:T(8,128)S(1)} %bitcast.28, bf16[256,1024]{1,0:T(8,128)(2,1)} %bitcast.15, bf16[512,1024]{1,0:T(8,128)(2,1)} %w_ref.1), custom_call_target="tpu_custom_call" | custom-call | tf_op jit(solution)/shard_map/prepare/pallas_call | solution.py:569
  16.8 0.9 %corner.1 = (bf16[2,176,512]{2,1,0:T(8,128)(2,1)S(1)}, bf16[2,80,512]{2,1,0:T(8,128)(2,1)S(1)}) custom-call(s32[6]{0:T(128)S(1)} %stack.24.info_ref, bf16[2,96,512]{2,1,0:T(8,128)(2,1)S(1)} %collective-permute-done.w_ref, bf16[2,96,512]{2,1,0:T(8,128)(2,1)S(1)} %collective-permute-done.1.e_ref, bf16[2,96,512]{2,1,0:T(8,128)(2,1)S(1)} %get-tuple-element.74.own_ref), custom_call_target="tpu_custom_call" | custom-call | tf_op jit(solution)/shard_map/corner/pallas_call | solution.py:583
  17.7 0.1 collective-permute-start.3
  17.8 2.6 %collective-permute-start.4 = (bf16[2,80,512]{2,1,0:T(8,128)(2,1)S(1)}, bf16[2,80,512]{2,1,0:T(8,128)(2,1)S(1)}, u32[]{:S(2)}, u32[]{:S(2)}) collective-permute-start(bf16[2,80,512]{2,1,0:T(8,128)(2,1)S(1)} %get-tuple-element.77), channel_id=1, source_target_pairs={{8,16},{16,8},{9,17},{17,9},{10,18},{18,10},{11,19},{19,11},{12,20... | collective-permute-start | bytes 491528 | tf_op jit(solution)/shard_map/ppermute | solution.py:590
  20.4 4.0 %collective-permute-done.4.c_ref = bf16[2,80,512]{2,1,0:T(8,128)(2,1)S(1)} collective-permute-done((bf16[2,80,512]{2,1,0:T(8,128)(2,1)S(1)}, bf16[2,80,512]{2,1,0:T(8,128)(2,1)S(1)}, u32[]{:S(2)}, u32[]{:S(2)}) %collective-permute-start.4) | collective-permute-done | bytes 163872 | tf_op jit(solution)/shard_map/ppermute | solution.py:590
  24.4 3.6 %attend_fwd.3 = (bf16[256,256]{1,0:T(8,128)(2,1)S(1)}, bf16[256,1024]{1,0:T(8,128)(2,1)S(1)}, f32[4,512,256]{2,1,0:T(8,128)S(1)}, bf16[896,256]{1,0:T(8,128)(2,1)S(1)}, bf16[896,256]{1,0:T(8,128)(2,1)S(1)}) custom-call(s32[6]{0:T(128)S(1)} %stack.24.info_ref, bf16[256,512]{1,0:T(8,128)(2,1)S(1)} %bitcast.18, bf16[256,512]{1,0:T(8,128)(2,1)S(1)} %bitcast.23, ...), custom_call_target="tpu_custom_call" | custom-call | tf_op jit(solution)/shard_map/attend_fwd/pallas_call | solution.py:596
  28.1 0.1 collective-permute-start.5
  28.1 3.6 %attend_fwd.2 = (bf16[256,256]{1,0:T(8,128)(2,1)S(1)}, f32[256,1024]{1,0:T(8,128)S(1)}, f32[4,512,256]{2,1,0:T(8,128)S(1)}, bf16[896,256]{1,0:T(8,128)(2,1)S(1)}, bf16[896,256]{1,0:T(8,128)(2,1)S(1)}) custom-call(s32[6]{0:T(128)S(1)} %stack.24.info_ref, bf16[256,512]{1,0:T(8,128)(2,1)S(1)} %bitcast.19, bf16[256,512]{1,0:T(8,128)(2,1)S(1)} %bitcast.24, ...), custom_call_target="tpu_custom_call" | custom-call | tf_op jit(solution)/shard_map/attend_fwd/pallas_call | solution.py:596
  31.8 0.7 halve.2
  32.5 0.6 collective-permute-start.6
  33.1 3.4 %attend_bwd.2 = (bf16[256,256]{1,0:T(8,128)(2,1)S(1)}, bf16[2,192,256]{2,1,0:T(8,128)(2,1)S(1)}, bf16[2,192,256]{2,1,0:T(8,128)(2,1)S(1)}, f32[2,256,256]{2,1,0:...) custom-call(s32[6]{0:T(128)S(1)} %stack.24.info_ref, bf16[256,512]{1,0:T(8,128)(2,1)S(1)} %bitcast.20, ...), custom_call_target="tpu_custom_call" | custom-call | tf_op jit(solution)/shard_map/attend_bwd/pallas_call | solution.py:628
  36.5 3.6 %collective-permute-start.8 = (bf16[2,192,256]{2,1,0:T(8,128)(2,1)S(1)}, bf16[2,192,256]{2,1,0:T(8,128)(2,1)S(1)}, u32[]{:S(2)}, u32[]{:S(2)}) collective-permute-start(bf16[2,192,256]{2,1,0:T(8,128)(2,1)S(1)} %get-tuple-element.103), channel_id=1, source_target_pairs={{8,16},{16,8},{9,17},{17,9},{10,18},{18,10},{11,19},{19,11},{12,20... | collective-permute-start | bytes 589832 | tf_op jit(solution)/shard_map/ppermute | solution.py:646
  40.2 0.6 halve.3
  40.8 0.1 collective-permute-start.7
  40.9 3.9 %attend_bwd.3 = (bf16[256,512]{1,0:T(8,128)(2,1)}, bf16[2,192,512]{2,1,0:T(8,128)(2,1)S(1)}, bf16[2,192,256]{2,1,0:T(8,128)(2,1)S(1)}, f32[2,256,256]{2,1,0:T(8,...) custom-call(s32[6]{0:T(128)S(1)} %stack.24.info_ref, bf16[256,512]{1,0:T(8,128)(2,1)S(1)} %bitcast.21, ...), custom_call_target="tpu_custom_call" | custom-call | tf_op jit(solution)/shard_map/attend_bwd/pallas_call | solution.py:628
  44.8 0.1 collective-permute-done.7.got_ref
  44.9 0.1 collective-permute-start.11
  45.0 1.2 %bias_fold.1.bias_ref = f32[8,256]{1,0:T(8,128)S(1)} custom-call(s32[6]{0:T(128)S(1)} %stack.24.info_ref, f32[416,128]{1,0:T(8,128)S(1)} %get-tuple-element.105.xs_ref, f32[416,128]{1,0:T(8,128)S(1)} %get-tuple-element.106.xk_ref), custom_call_target="tpu_custom_call" | custom-call | tf_op jit(solution)/shard_map/bias_fold/pallas_call | solution.py:661
  46.2 0.1 meet.1.own_ref
  46.3 2.3 %collective-permute-start.9 = (bf16[72,1024]{1,0:T(8,128)(2,1)S(1)}, bf16[72,1024]{1,0:T(8,128)(2,1)S(1)}, u32[]{:S(2)}, u32[]{:S(2)}) collective-permute-start(bf16[72,1024]{1,0:T(8,128)(2,1)S(1)} %meet.1.own_ref), channel_id=1, source_target_pairs={{0,1},{1,0},{2,3},{3,2},{4,5},{5,4},{6,7},{7,6},{8,12},{9,13},{10,... | collective-permute-start | bytes 442376 | tf_op jit(solution)/shard_map/ppermute | solution.py:440
  48.6 1.9 %collective-permute-start.12 = (bf16[2,192,256]{2,1,0:T(8,128)(2,1)S(1)}, bf16[2,192,256]{2,1,0:T(8,128)(2,1)S(1)}, u32[]{:S(2)}, u32[]{:S(2)}) collective-permute-start(bf16[2,192,256]{2,1,0:T(8,128)(2,1)S(1)} %get-tuple-element.110), channel_id=1, source_target_pairs={{8,16},{16,8},{9,17},{17,9},{10,18},{18,10},{11,19},{19,11},{12,20... | collective-permute-start | bytes 589832 | tf_op jit(solution)/shard_map/ppermute | solution.py:657
  50.5 2.4 %collective-permute-done.9.got_ref = bf16[72,1024]{1,0:T(8,128)(2,1)S(1)} collective-permute-done((bf16[72,1024]{1,0:T(8,128)(2,1)S(1)}, bf16[72,1024]{1,0:T(8,128)(2,1)S(1)}, u32[]{:S(2)}, u32[]{:S(2)}) %collective-permute-start.9) | collective-permute-done | bytes 147488 | tf_op jit(solution)/shard_map/ppermute | solution.py:440
  52.9 0.3 collective-permute-start.10
  53.1 2.4 %collective-permute-done.12.bk_ref = bf16[2,192,256]{2,1,0:T(8,128)(2,1)S(1)} collective-permute-done((bf16[2,192,256]{2,1,0:T(8,128)(2,1)S(1)}, bf16[2,192,256]{2,1,0:T(8,128)(2,1)S(1)}, u32[]{:S(2)}, u32[]{:S(2)}) %collective-permute-start.12) | collective-permute-done | bytes 196640 | tf_op jit(solution)/shard_map/ppermute | solution.py:657
  55.5 1.0 %side.1 = (bf16[2,96,512]{2,1,0:T(8,128)(2,1)S(1)}, bf16[2,96,512]{2,1,0:T(8,128)(2,1)S(1)}) custom-call(s32[6]{0:T(128)S(1)} %stack.24.info_ref, f32[2,256,256]{2,1,0:T(8,128)S(1)} %get-tuple-element.107.ss_ref, f32[2,256,256]{2,1,0:T(8,128)S(1)} %get-tuple-element.108.sk_ref, bf16[2,192,512]{2,1,0:T(8,128)(2,1)S(1)} %collective-permute-done.11.a_ref, ...), custom_call_target="tpu_custom_call" | custom-call | tf_op jit(solution)/shard_map/side/pallas_call | solution.py:682
  56.5 1.9 %collective-permute-start.14 = (bf16[2,96,512]{2,1,0:T(8,128)(2,1)S(1)}, bf16[2,96,512]{2,1,0:T(8,128)(2,1)S(1)}, u32[]{:S(2)}, u32[]{:S(2)}) collective-permute-start(bf16[2,96,512]{2,1,0:T(8,128)(2,1)S(1)} %get-tuple-element.112), channel_id=1, source_target_pairs={{0,7},{1,0},{2,1},{3,2},{4,3},{5,4},{6,5},{7,6},{8,15},{9,8},{10,9... | collective-permute-start | bytes 589832 | tf_op jit(solution)/shard_map/ppermute | solution.py:690
  58.5 0.7 collective-permute-start.13
  59.2 1.8 %project.1 = bf16[256,1024]{1,0:T(8,128)(2,1)} custom-call(s32[6]{0:T(128)S(1)} %stack.24.info_ref, bf16[256,256]{1,0:T(8,128)(2,1)S(1)} %get-tuple-element.115.s_ref, bf16[256,256]{1,0:T(8,128)(2,1)S(1)} %get-tuple-element.116.k_ref, bf16[512,1024]{1,0:T(8,128)(2,1)S(1)} %copy-done.1), custom_call_target="tpu_custom_call" | custom-call | tf_op jit(solution)/shard_map/project/pallas_call | solution.py:669
  61.0 1.8 %collective-permute-done.13.got_ref = bf16[72,1024]{1,0:T(8,128)(2,1)S(1)} collective-permute-done((bf16[72,1024]{1,0:T(8,128)(2,1)S(1)}, bf16[72,1024]{1,0:T(8,128)(2,1)S(1)}, u32[]{:S(2)}, u32[]{:S(2)}) %collective-permute-start.13) | collective-permute-done | bytes 147488 | tf_op jit(solution)/shard_map/ppermute | solution.py:440
  62.8 0.6 grow.2.own_ref
  63.4 3.0 %collective-permute-done.14.e_ref = bf16[2,96,512]{2,1,0:T(8,128)(2,1)S(1)} collective-permute-done((bf16[2,96,512]{2,1,0:T(8,128)(2,1)S(1)}, bf16[2,96,512]{2,1,0:T(8,128)(2,1)S(1)}, u32[]{:S(2)}, u32[]{:S(2)}) %collective-permute-start.14) | collective-permute-done | bytes 196640 | tf_op jit(solution)/shard_map/ppermute | solution.py:690
  66.4 1.3 %collective-permute-done.15.w_ref = bf16[2,96,512]{2,1,0:T(8,128)(2,1)S(1)} collective-permute-done((bf16[2,96,512]{2,1,0:T(8,128)(2,1)S(1)}, bf16[2,96,512]{2,1,0:T(8,128)(2,1)S(1)}, u32[]{:S(2)}, u32[]{:S(2)}) %collective-permute-start.15) | collective-permute-done | bytes 196640 | tf_op jit(solution)/shard_map/ppermute | solution.py:691
  67.6 0.2 collective-permute-start.16
  67.8 1.8 %join.1 = (bf16[256,512]{1,0:T(8,128)(2,1)}, bf16[256,512]{1,0:T(8,128)(2,1)}) custom-call(s32[6]{0:T(128)S(1)} %stack.24.info_ref, f32[2,256,256]{2,1,0:T(8,128)S(1)} %get-tuple-element.120.ms_ref, f32[2,256,256]{2,1,0:T(8,128)S(1)} %get-tuple-element.121.mk_ref, bf16[2,192,512]{2,1,0:T(8,128)(2,1)S(1)} %collective-permute-done.11.a_ref, ...), custom_call_target="tpu_custom_call" | custom-call | tf_op jit(solution)/shard_map/join/pallas_call | solution.py:703
  69.6 3.7 %collective-permute-done.16.got_ref = bf16[136,1024]{1,0:T(8,128)(2,1)S(1)} collective-permute-done((bf16[136,1024]{1,0:T(8,128)(2,1)S(1)}, bf16[136,1024]{1,0:T(8,128)(2,1)S(1)}, u32[]{:S(2)}, u32[]{:S(2)}) %collective-permute-start.16) | collective-permute-done | bytes 278560 | tf_op jit(solution)/shard_map/ppermute | solution.py:440
  73.3 0.6 grow.3.own_ref
  73.9 1.0 %collective-permute-start.17 = (bf16[264,1024]{1,0:T(8,128)(2,1)S(1)}, bf16[264,1024]{1,0:T(8,128)(2,1)S(1)}, u32[]{:S(2)}, u32[]{:S(2)}) collective-permute-start(bf16[264,1024]{1,0:T(8,128)(2,1)S(1)} %grow.3.own_ref), channel_id=1, source_target_pairs={{0,8},{1,9},{2,10},{3,11},{4,12},{5,13},{6,14},{7,15},{8,0},{9,1},... | collective-permute-start | bytes 1622024 | tf_op jit(solution)/shard_map/ppermute | solution.py:440
  74.9 1.6 %collective-permute-done.17.got_ref = bf16[264,1024]{1,0:T(8,128)(2,1)S(1)} collective-permute-done((bf16[264,1024]{1,0:T(8,128)(2,1)S(1)}, bf16[264,1024]{1,0:T(8,128)(2,1)S(1)}, u32[]{:S(2)}, u32[]{:S(2)}) %collective-permute-start.17) | collective-permute-done | bytes 540704 | tf_op jit(solution)/shard_map/ppermute | solution.py:440
  76.5 1.6 %last.1 = (bf16[512,1024]{1,0:T(8,128)(2,1)}, f32[13,8,13]{2,1,0:T(8,128)}) custom-call(s32[6]{0:T(128)S(1)} %stack.24.info_ref, bf16[264,1024]{1,0:T(8,128)(2,1)S(1)} %grow.3.own_ref, bf16[264,1024]{1,0:T(8,128)(2,1)S(1)} %collective-permute-done.17.got_ref), custom_call_target="tpu_custom_call" | custom-call | tf_op jit(solution)/shard_map/last/pallas_call | solution.py:611
  (20 shorter events, 0.1 us)
Async XLA Ops:
  0.6 23.8 %copy-start.4 = (bf16[16,16,512]{2,1,0:T(8,128)(2,1)S(1)}, bf16[16,16,512]{2,1,0:T(8,128)(2,1)}, u32[]{:S(2)}) copy-start(bf16[16,16,512]{2,1,0:T(8,128)(2,1)} %param.8) | copy-start | bytes 786436
  0.6 23.8 %copy-start.3 = (bf16[16,16,512]{2,1,0:T(8,128)(2,1)S(1)}, bf16[16,16,512]{2,1,0:T(8,128)(2,1)}, u32[]{:S(2)}) copy-start(bf16[16,16,512]{2,1,0:T(8,128)(2,1)} %param.7) | copy-start | bytes 786436
  0.7 23.8 %copy-start = (bf16[16,16,1024]{2,1,0:T(8,128)(2,1)S(1)}, bf16[16,16,1024]{2,1,0:T(8,128)(2,1)}, u32[]{:S(2)}) copy-start(bf16[16,16,1024]{2,1,0:T(8,128)(2,1)} %param.11) | copy-start | bytes 1572868
  0.7 23.8 %copy-start.2 = (bf16[16,16,512]{2,1,0:T(8,128)(2,1)S(1)}, bf16[16,16,512]{2,1,0:T(8,128)(2,1)}, u32[]{:S(2)}) copy-start(bf16[16,16,512]{2,1,0:T(8,128)(2,1)} %param.6) | copy-start | bytes 786436
  2.8 14.0 %collective-permute-start = (bf16[2,96,512]{2,1,0:T(8,128)(2,1)S(1)}, bf16[2,96,512]{2,1,0:T(8,128)(2,1)S(1)}, u32[]{:S(2)}, u32[]{:S(2)}) collective-permute-start(bf16[2,96,512]{2,1,0:T(8,128)(2,1)S(1)} %get-tuple-element.68), channel_id=1, source_target_pairs={{0,1},{1,2},{2,3},{3,4},{4,5},{5,6},{6,7},{7,0},{8,9},{9,10},{10,1... | collective-permute-start | bytes 589832 | tf_op jit(solution)/shard_map/ppermute | solution.py:565
  4.9 11.9 %collective-permute-start.1 = (bf16[2,96,512]{2,1,0:T(8,128)(2,1)S(1)}, bf16[2,96,512]{2,1,0:T(8,128)(2,1)S(1)}, u32[]{:S(2)}, u32[]{:S(2)}) collective-permute-start(bf16[2,96,512]{2,1,0:T(8,128)(2,1)S(1)} %get-tuple-element.69), channel_id=1, source_target_pairs={{0,7},{1,0},{2,1},{3,2},{4,3},{5,4},{6,5},{7,6},{8,15},{9,8},{10,9... | collective-permute-start | bytes 589832 | tf_op jit(solution)/shard_map/ppermute | solution.py:566
  8.0 8.8 %collective-permute-start.2 = (bf16[2,96,512]{2,1,0:T(8,128)(2,1)S(1)}, bf16[2,96,512]{2,1,0:T(8,128)(2,1)S(1)}, u32[]{:S(2)}, u32[]{:S(2)}) collective-permute-start(bf16[2,96,512]{2,1,0:T(8,128)(2,1)S(1)} %get-tuple-element.70), channel_id=1, source_target_pairs={{8,16},{16,8},{9,17},{17,9},{10,18},{18,10},{11,19},{19,11},{12,20... | collective-permute-start | bytes 589832 | tf_op jit(solution)/shard_map/ppermute | solution.py:567
  12.1 0.8 %copy-start.5 = (f32[8,13,13]{2,0,1:T(8,128)S(1)}, f32[8,13,13]{2,0,1:T(8,128)}, u32[]{:S(2)}) copy-start(f32[8,13,13]{2,0,1:T(8,128)} %param.9) | copy-start | bytes 16228
  17.7 6.7 %collective-permute-start.3 = (bf16[2,176,512]{2,1,0:T(8,128)(2,1)S(1)}, bf16[2,176,512]{2,1,0:T(8,128)(2,1)S(1)}, u32[]{:S(2)}, u32[]{:S(2)}) collective-permute-start(bf16[2,176,512]{2,1,0:T(8,128)(2,1)S(1)} %get-tuple-element.75), channel_id=1, source_target_pairs={{0,8},{8,0},{16,24},{24,16},{1,9},{9,1},{17,25},{25,17},{2,10},{10... | collective-permute-start | bytes 1081352 | tf_op jit(solution)/shard_map/ppermute | solution.py:591
  17.8 6.6 %collective-permute-start.4 = (bf16[2,80,512]{2,1,0:T(8,128)(2,1)S(1)}, bf16[2,80,512]{2,1,0:T(8,128)(2,1)S(1)}, u32[]{:S(2)}, u32[]{:S(2)}) collective-permute-start(bf16[2,80,512]{2,1,0:T(8,128)(2,1)S(1)} %get-tuple-element.77), channel_id=1, source_target_pairs={{8,16},{16,8},{9,17},{17,9},{10,18},{18,10},{11,19},{19,11},{12,20... | collective-permute-start | bytes 491528 | tf_op jit(solution)/shard_map/ppermute | solution.py:590
  28.1 3.7 %collective-permute-start.5 = (bf16[256,1024]{1,0:T(8,128)(2,1)S(1)}, bf16[256,1024]{1,0:T(8,128)(2,1)S(1)}, u32[]{:S(2)}, u32[]{:S(2)}) collective-permute-start(bf16[256,1024]{1,0:T(8,128)(2,1)S(1)} %get-tuple-element.80), channel_id=1, source_target_pairs={{0,8},{1,9},{2,10},{3,11},{4,12},{5,13},{6,14},{7,15},{8,0},{9,1},... | collective-permute-start | bytes 1572872 | tf_op jit(solution)/shard_map/ppermute | solution.py:440
  32.5 7.7 %collective-permute-start.6 = (bf16[128,1024]{1,0:T(8,128)(2,1)S(1)}, bf16[128,1024]{1,0:T(8,128)(2,1)S(1)}, u32[]{:S(2)}, u32[]{:S(2)}) collective-permute-start(bf16[128,1024]{1,0:T(8,128)(2,1)S(1)} %get-tuple-element.83), channel_id=1, source_target_pairs={{0,16},{1,17},{2,18},{3,19},{4,20},{5,21},{6,22},{7,23},{8,10},{9,... | collective-permute-start | bytes 786440 | tf_op jit(solution)/shard_map/ppermute | solution.py:440
  36.5 8.3 %collective-permute-start.8 = (bf16[2,192,256]{2,1,0:T(8,128)(2,1)S(1)}, bf16[2,192,256]{2,1,0:T(8,128)(2,1)S(1)}, u32[]{:S(2)}, u32[]{:S(2)}) collective-permute-start(bf16[2,192,256]{2,1,0:T(8,128)(2,1)S(1)} %get-tuple-element.103), channel_id=1, source_target_pairs={{8,16},{16,8},{9,17},{17,9},{10,18},{18,10},{11,19},{19,11},{12,20... | collective-permute-start | bytes 589832 | tf_op jit(solution)/shard_map/ppermute | solution.py:646
  40.8 4.1 %collective-permute-start.7 = (bf16[64,1024]{1,0:T(8,128)(2,1)S(1)}, bf16[64,1024]{1,0:T(8,128)(2,1)S(1)}, u32[]{:S(2)}, u32[]{:S(2)}) collective-permute-start(bf16[64,1024]{1,0:T(8,128)(2,1)S(1)} %get-tuple-element.93), channel_id=1, source_target_pairs={{0,2},{1,3},{2,0},{3,1},{4,6},{5,7},{6,4},{7,5},{8,24},{9,25},{10,... | collective-permute-start | bytes 393224 | tf_op jit(solution)/shard_map/ppermute | solution.py:440
  44.8 14.4 %copy-start.1 = (bf16[512,1024]{1,0:T(8,128)(2,1)S(1)}, bf16[512,1024]{1,0:T(8,128)(2,1)}, u32[]{:S(2)}) copy-start(bf16[512,1024]{1,0:T(8,128)(2,1)} %w_ref.1) | copy-start | bytes 3145732
  44.9 10.6 %collective-permute-start.11 = (bf16[2,192,512]{2,1,0:T(8,128)(2,1)S(1)}, bf16[2,192,512]{2,1,0:T(8,128)(2,1)S(1)}, u32[]{:S(2)}, u32[]{:S(2)}) collective-permute-start(bf16[2,192,512]{2,1,0:T(8,128)(2,1)S(1)} %get-tuple-element.109), channel_id=1, source_target_pairs={{0,8},{8,0},{16,24},{24,16},{1,9},{9,1},{17,25},{25,17},{2,10},{10... | collective-permute-start | bytes 1179656 | tf_op jit(solution)/shard_map/ppermute | solution.py:658
  46.3 6.5 %collective-permute-start.9 = (bf16[72,1024]{1,0:T(8,128)(2,1)S(1)}, bf16[72,1024]{1,0:T(8,128)(2,1)S(1)}, u32[]{:S(2)}, u32[]{:S(2)}) collective-permute-start(bf16[72,1024]{1,0:T(8,128)(2,1)S(1)} %meet.1.own_ref), channel_id=1, source_target_pairs={{0,1},{1,0},{2,3},{3,2},{4,5},{5,4},{6,7},{7,6},{8,12},{9,13},{10,... | collective-permute-start | bytes 442376 | tf_op jit(solution)/shard_map/ppermute | solution.py:440
  48.6 7.0 %collective-permute-start.12 = (bf16[2,192,256]{2,1,0:T(8,128)(2,1)S(1)}, bf16[2,192,256]{2,1,0:T(8,128)(2,1)S(1)}, u32[]{:S(2)}, u32[]{:S(2)}) collective-permute-start(bf16[2,192,256]{2,1,0:T(8,128)(2,1)S(1)} %get-tuple-element.110), channel_id=1, source_target_pairs={{8,16},{16,8},{9,17},{17,9},{10,18},{18,10},{11,19},{19,11},{12,20... | collective-permute-start | bytes 589832 | tf_op jit(solution)/shard_map/ppermute | solution.py:657
  52.9 5.5 %collective-permute-start.10 = (bf16[72,1024]{1,0:T(8,128)(2,1)S(1)}, bf16[72,1024]{1,0:T(8,128)(2,1)S(1)}, u32[]{:S(2)}, u32[]{:S(2)}) collective-permute-start(bf16[72,1024]{1,0:T(8,128)(2,1)S(1)} %total.2.own_ref), channel_id=1, source_target_pairs={{0,4},{1,5},{2,6},{3,7},{4,0},{5,1},{6,2},{7,3},{8,9},{9,8},{10,11... | collective-permute-start | bytes 442376 | tf_op jit(solution)/shard_map/ppermute | solution.py:440
  56.5 9.8 %collective-permute-start.14 = (bf16[2,96,512]{2,1,0:T(8,128)(2,1)S(1)}, bf16[2,96,512]{2,1,0:T(8,128)(2,1)S(1)}, u32[]{:S(2)}, u32[]{:S(2)}) collective-permute-start(bf16[2,96,512]{2,1,0:T(8,128)(2,1)S(1)} %get-tuple-element.112), channel_id=1, source_target_pairs={{0,7},{1,0},{2,1},{3,2},{4,3},{5,4},{6,5},{7,6},{8,15},{9,8},{10,9... | collective-permute-start | bytes 589832 | tf_op jit(solution)/shard_map/ppermute | solution.py:690
  58.4 9.2 %collective-permute-start.15 = (bf16[2,96,512]{2,1,0:T(8,128)(2,1)S(1)}, bf16[2,96,512]{2,1,0:T(8,128)(2,1)S(1)}, u32[]{:S(2)}, u32[]{:S(2)}) collective-permute-start(bf16[2,96,512]{2,1,0:T(8,128)(2,1)S(1)} %get-tuple-element.113), channel_id=1, source_target_pairs={{0,1},{1,2},{2,3},{3,4},{4,5},{5,6},{6,7},{7,0},{8,9},{9,10},{10,1... | collective-permute-start | bytes 589832 | tf_op jit(solution)/shard_map/ppermute | solution.py:691
  58.5 4.4 %collective-permute-start.13 = (bf16[72,1024]{1,0:T(8,128)(2,1)S(1)}, bf16[72,1024]{1,0:T(8,128)(2,1)S(1)}, u32[]{:S(2)}, u32[]{:S(2)}) collective-permute-start(bf16[72,1024]{1,0:T(8,128)(2,1)S(1)} %total.3.own_ref), channel_id=1, source_target_pairs={{0,2},{1,3},{2,0},{3,1},{4,6},{5,7},{6,4},{7,5},{8,24},{9,25},{10,... | collective-permute-start | bytes 442376 | tf_op jit(solution)/shard_map/ppermute | solution.py:440
  67.6 5.7 %collective-permute-start.16 = (bf16[136,1024]{1,0:T(8,128)(2,1)S(1)}, bf16[136,1024]{1,0:T(8,128)(2,1)S(1)}, u32[]{:S(2)}, u32[]{:S(2)}) collective-permute-start(bf16[136,1024]{1,0:T(8,128)(2,1)S(1)} %grow.2.own_ref), channel_id=1, source_target_pairs={{0,16},{1,17},{2,18},{3,19},{4,20},{5,21},{6,22},{7,23},{8,10},{9,... | collective-permute-start | bytes 835592 | tf_op jit(solution)/shard_map/ppermute | solution.py:440
  73.9 2.6 %collective-permute-start.17 = (bf16[264,1024]{1,0:T(8,128)(2,1)S(1)}, bf16[264,1024]{1,0:T(8,128)(2,1)S(1)}, u32[]{:S(2)}, u32[]{:S(2)}) collective-permute-start(bf16[264,1024]{1,0:T(8,128)(2,1)S(1)} %grow.3.own_ref), channel_id=1, source_target_pairs={{0,8},{1,9},{2,10},{3,11},{4,12},{5,13},{6,14},{7,15},{8,0},{9,1},... | collective-permute-start | bytes 1622024 | tf_op jit(solution)/shard_map/ppermute | solution.py:440
